TPU v7x, 32 devices: a whole 2x2x4 slice. The times are simulated.
32 devices in a mesh: groups: 2 (over y), gx: 4 (over z), gy: 2 (over x), gz: 2 (over core).
Axes of the slice: x: 2, y: 2, z: 4, core: 2. Of those that a mesh axis runs over, the one named last changes fastest.
Arguments:
- adjoint_one_start: float32 [8, 2, 64, 256], P(('groups', 'gx'), 'gy', 'gz'), parts along dimension 0, may hold values from -6 to 6
- adjoint_two_start: float32 [8, 2, 64, 256], P(('groups', 'gx'), 'gy', 'gz'), parts along dimension 0, may hold values from -6 to 6
- couple_panel: float32 [8, 2, 256, 512], P(('groups', 'gx'), 'gy'), parts along dimension 0, may hold values from -0.21875 to 0.21875
- pair_panel: float32 [8, 2, 512, 256], P(('groups', 'gx'), 'gy'), parts along dimension 0, may hold values from -0.25 to 0.25
- lift_panel: float32 [8, 2, 256, 1024], P(('groups', 'gx'), 'gy'), parts along dimension 0, may hold values from -0.25 to 0.25
- root_panel: float32 [8, 2, 1024, 256], P(('groups', 'gx'), 'gy'), parts along dimension 0, may hold values from -0.125 to 0.125
- back_panel: float32 [8, 2, 1024, 256], P(('groups', 'gx'), 'gy'), parts along dimension 0, may hold values from -0.09375 to 0.09375
- mass_two: float32 [8, 2, 256], P(('groups', 'gx'), 'gy'), parts along dimension 0, may hold values from 0.5 to 1.5
- probe_cells: int32 [128], P(('groups', 'gz')), parts along dimension 0, may hold values from 0 to 2047
- probe_weight: float32 [18, 64], P('groups', 'gz'), parts along dimension 0, may hold values from -48 to 48
Outputs:
- adjoint_one: float32 [8, 2, 64, 256], P(('groups', 'gx'), 'gy', 'gz'), parts along dimension 0
- adjoint_two: float32 [8, 2, 64, 256], P(('groups', 'gx'), 'gy', 'gz'), parts along dimension 0
There are 2 independent parts, one for each index of `groups`. A program takes and returns all parts, laid end to end along the dimension named above; each array names one. Nothing has to cross between parts.
All inputs are finite; a program needn't handle non-finite values.
Results may differ from a plain program's by a relative error of at most 0.00022.
Values sent between devices are 32-bit elements; how exact they have to be, the bound alone decides.
No kernel may reach another device: no remote copies, remote signals or barrier semaphores. Data moves between devices by JAX's collectives and lax.ppermute only.
A program may use at most 64 MiB of HBM per device.

v0:
```python
import jax
import jax.numpy as jnp
from jax import lax
from jax.sharding import PartitionSpec as P


def from_partner(value, axis, bit):
    mask = 2**bit
    pairs = [(source, source ^ mask) for source in range(lax.axis_size(axis))]
    return lax.ppermute(value, axis, pairs)


def place_block(block, slot, count):
    picks = (jnp.arange(count) == slot).astype(jnp.float32)
    grown = block[:, None, :] * picks[None, :, None]
    return grown.reshape(block.shape[0], count * block.shape[1])


def order_pair(mine, other, bit_value):
    return jnp.where(
        bit_value == 0,
        jnp.concatenate([mine, other], axis=-1),
        jnp.concatenate([other, mine], axis=-1),
    )


def matmul(left, right):
    return jnp.dot(left, right, precision=lax.Precision.HIGHEST, preferred_element_type=jnp.float32)


def shards(
    adjoint_one_start,
    adjoint_two_start,
    couple_panel,
    pair_panel,
    lift_panel,
    root_panel,
    back_panel,
    mass_two,
    probe_cells,
    probe_weight,
):
    couple = couple_panel[0, 0]
    pair_cols = pair_panel[0, 0]
    lift = lift_panel[0, 0]
    root_cols = root_panel[0, 0]
    back = back_panel[0, 0]
    mass = mass_two[0, 0]
    width = couple.shape[0]
    x_bit = lax.axis_index("gx") % 2
    y_bit = lax.axis_index("gy") % 2
    owner = lax.axis_index("gx") * lax.axis_size("gy") + lax.axis_index("gy")
    targets = owner * width + jnp.arange(width, dtype=jnp.int32)
    probe_mask = (probe_cells[:, None] == targets[None, :]).astype(jnp.float32)
    quarter = 2 * y_bit + x_bit

    def advance(step, carry):
        adj_one, adj_two = carry
        weights = lax.dynamic_index_in_dim(probe_weight, step, 0, keepdims=False)
        source = weights[:, None] * probe_mask
        mass_part = place_block(adj_two * mass[None, :], quarter, 4)
        terms_one = matmul(adj_one, couple) + place_block(source, x_bit, 2)
        sums_one = terms_one + from_partner(terms_one, "gx", 0)
        half_one = matmul(sums_one, pair_cols)
        terms_two = matmul(half_one, lift) + mass_part
        partial_two = terms_two + from_partner(terms_two, "gx", 0)
        sums_two = partial_two + from_partner(partial_two, "gy", 0)
        adj_two = matmul(sums_two, root_cols)
        other_quarter = from_partner(adj_two, "gx", 0)
        joined = order_pair(adj_two, other_quarter, x_bit)
        other_half = from_partner(joined, "gy", 0)
        whole_two = order_pair(joined, other_half, y_bit)
        adj_one = half_one - matmul(whole_two, back)
        return (adj_one, adj_two)

    start = (adjoint_one_start[0, 0], adjoint_two_start[0, 0])
    adj_one, adj_two = lax.fori_loop(0, probe_weight.shape[0], advance, start)
    return (adj_one[None, None], adj_two[None, None])


def solution(mesh):
    placed = (
        P(("groups", "gx"), "gy", "gz", None),
        P(("groups", "gx"), "gy", "gz", None),
        P(("groups", "gx"), "gy", None, None),
        P(("groups", "gx"), "gy", None, None),
        P(("groups", "gx"), "gy", None, None),
        P(("groups", "gx"), "gy", None, None),
        P(("groups", "gx"), "gy", None, None),
        P(("groups", "gx"), "gy", None),
        P(("groups", "gz")),
        P("groups", "gz"),
    )
    return jax.shard_map(
        shards,
        mesh=mesh,
        in_specs=placed,
        out_specs=(P(("groups", "gx"), "gy", "gz", None), P(("groups", "gx"), "gy", "gz", None)),
        check_vma=False,
    )
```

profile of v0, /device:TPU:0, one launch (start us, length us, event | category | flops | bytes accessed | tf_op | source)
XLA Modules:
  0.0 255.8 jit_solution(4647008005473060117)
XLA Ops:
  1.4 253.8 %while.18 = (s32[]{:T(128)}, f32[32,256]{1,0:T(8,128)S(1)}, f32[32,256]{1,0:T(8,128)S(1)}, f32[256,512]{1,0:T(8,128)}, f32[9,32]{1,0:T(8,128)}, /*index=5*/s32[]...) while((s32[]{:T(128)}, f32[32,256]{1,0:T(8,128)S(1)}, ...), condition=%wide.region_1.2_spmd.clone, body=%wide.region_0.1_spmd.clone.sunk | while | flops 403013632 | bytes 22998032 | solution.py:77
  39.9 3.3 %collective-permute-done.1 = f32[32,1024]{1,0:T(8,128)S(1)} collective-permute-done((f32[32,1024]{1,0:T(8,128)S(1)}, f32[32,1024]{1,0:T(8,128)S(1)}, u32[]{:S(2)}, u32[]{:S(2)}) %collective-permute-start.1) | collective-permute-done | bytes 131104 | tf_op jit(solution)/shard_map/while/body/eval_jaxpr/ppermute | solution.py:10
  72.9 3.1 %collective-permute-done.2 = f32[32,1024]{1,0:T(8,128)S(1)} collective-permute-done((f32[32,1024]{1,0:T(8,128)S(1)}, f32[32,1024]{1,0:T(8,128)S(1)}, u32[]{:S(2)}, u32[]{:S(2)}) %collective-permute-start.2) | collective-permute-done | bytes 131104 | tf_op jit(solution)/shard_map/while/body/eval_jaxpr/ppermute | solution.py:10
  95.5 4.3 %collective-permute-done.1 = f32[32,1024]{1,0:T(8,128)S(1)} collective-permute-done((f32[32,1024]{1,0:T(8,128)S(1)}, f32[32,1024]{1,0:T(8,128)S(1)}, u32[]{:S(2)}, u32[]{:S(2)}) %collective-permute-start.1) | collective-permute-done | bytes 131104 | tf_op jit(solution)/shard_map/while/body/eval_jaxpr/ppermute | solution.py:10
  100.4 4.4 %collective-permute-done.2 = f32[32,1024]{1,0:T(8,128)S(1)} collective-permute-done((f32[32,1024]{1,0:T(8,128)S(1)}, f32[32,1024]{1,0:T(8,128)S(1)}, u32[]{:S(2)}, u32[]{:S(2)}) %collective-permute-start.2) | collective-permute-done | bytes 131104 | tf_op jit(solution)/shard_map/while/body/eval_jaxpr/ppermute | solution.py:10
  106.2 3.2 %collective-permute-done.3 = f32[32,256]{1,0:T(8,128)S(1)} collective-permute-done((f32[32,256]{1,0:T(8,128)S(1)}, f32[32,256]{1,0:T(8,128)S(1)}, u32[]{:S(2)}, u32[]{:S(2)}) %collective-permute-start.3) | collective-permute-done | bytes 32800 | tf_op jit(solution)/shard_map/while/body/eval_jaxpr/ppermute | solution.py:10
  110.1 3.6 %collective-permute-done.4 = f32[32,512]{1,0:T(8,128)S(1)} collective-permute-done((f32[32,512]{1,0:T(8,128)S(1)}, f32[32,512]{1,0:T(8,128)S(1)}, u32[]{:S(2)}, u32[]{:S(2)}) %collective-permute-start.4) | collective-permute-done | bytes 65568 | tf_op jit(solution)/shard_map/while/body/eval_jaxpr/ppermute | solution.py:10
  117.7 3.8 %collective-permute-done = f32[32,512]{1,0:T(8,128)S(1)} collective-permute-done((f32[32,512]{1,0:T(8,128)S(1)}, f32[32,512]{1,0:T(8,128)S(1)}, u32[]{:S(2)}, u32[]{:S(2)}) %collective-permute-start) | collective-permute-done | bytes 65568 | tf_op jit(solution)/shard_map/while/body/eval_jaxpr/ppermute | solution.py:10
  123.5 4.7 %collective-permute-done.1 = f32[32,1024]{1,0:T(8,128)S(1)} collective-permute-done((f32[32,1024]{1,0:T(8,128)S(1)}, f32[32,1024]{1,0:T(8,128)S(1)}, u32[]{:S(2)}, u32[]{:S(2)}) %collective-permute-start.1) | collective-permute-done | bytes 131104 | tf_op jit(solution)/shard_map/while/body/eval_jaxpr/ppermute | solution.py:10
  129.0 4.3 %collective-permute-done.2 = f32[32,1024]{1,0:T(8,128)S(1)} collective-permute-done((f32[32,1024]{1,0:T(8,128)S(1)}, f32[32,1024]{1,0:T(8,128)S(1)}, u32[]{:S(2)}, u32[]{:S(2)}) %collective-permute-start.2) | collective-permute-done | bytes 131104 | tf_op jit(solution)/shard_map/while/body/eval_jaxpr/ppermute | solution.py:10
  134.6 3.3 %collective-permute-done.3 = f32[32,256]{1,0:T(8,128)S(1)} collective-permute-done((f32[32,256]{1,0:T(8,128)S(1)}, f32[32,256]{1,0:T(8,128)S(1)}, u32[]{:S(2)}, u32[]{:S(2)}) %collective-permute-start.3) | collective-permute-done | bytes 32800 | tf_op jit(solution)/shard_map/while/body/eval_jaxpr/ppermute | solution.py:10
  138.7 3.6 %collective-permute-done.4 = f32[32,512]{1,0:T(8,128)S(1)} collective-permute-done((f32[32,512]{1,0:T(8,128)S(1)}, f32[32,512]{1,0:T(8,128)S(1)}, u32[]{:S(2)}, u32[]{:S(2)}) %collective-permute-start.4) | collective-permute-done | bytes 65568 | tf_op jit(solution)/shard_map/while/body/eval_jaxpr/ppermute | solution.py:10
  146.2 4.0 %collective-permute-done = f32[32,512]{1,0:T(8,128)S(1)} collective-permute-done((f32[32,512]{1,0:T(8,128)S(1)}, f32[32,512]{1,0:T(8,128)S(1)}, u32[]{:S(2)}, u32[]{:S(2)}) %collective-permute-start) | collective-permute-done | bytes 65568 | tf_op jit(solution)/shard_map/while/body/eval_jaxpr/ppermute | solution.py:10
  151.9 4.4 %collective-permute-done.1 = f32[32,1024]{1,0:T(8,128)S(1)} collective-permute-done((f32[32,1024]{1,0:T(8,128)S(1)}, f32[32,1024]{1,0:T(8,128)S(1)}, u32[]{:S(2)}, u32[]{:S(2)}) %collective-permute-start.1) | collective-permute-done | bytes 131104 | tf_op jit(solution)/shard_map/while/body/eval_jaxpr/ppermute | solution.py:10
  157.0 5.0 %collective-permute-done.2 = f32[32,1024]{1,0:T(8,128)S(1)} collective-permute-done((f32[32,1024]{1,0:T(8,128)S(1)}, f32[32,1024]{1,0:T(8,128)S(1)}, u32[]{:S(2)}, u32[]{:S(2)}) %collective-permute-start.2) | collective-permute-done | bytes 131104 | tf_op jit(solution)/shard_map/while/body/eval_jaxpr/ppermute | solution.py:10
  163.3 3.3 %collective-permute-done.3 = f32[32,256]{1,0:T(8,128)S(1)} collective-permute-done((f32[32,256]{1,0:T(8,128)S(1)}, f32[32,256]{1,0:T(8,128)S(1)}, u32[]{:S(2)}, u32[]{:S(2)}) %collective-permute-start.3) | collective-permute-done | bytes 32800 | tf_op jit(solution)/shard_map/while/body/eval_jaxpr/ppermute | solution.py:10
  167.4 3.6 %collective-permute-done.4 = f32[32,512]{1,0:T(8,128)S(1)} collective-permute-done((f32[32,512]{1,0:T(8,128)S(1)}, f32[32,512]{1,0:T(8,128)S(1)}, u32[]{:S(2)}, u32[]{:S(2)}) %collective-permute-start.4) | collective-permute-done | bytes 65568 | tf_op jit(solution)/shard_map/while/body/eval_jaxpr/ppermute | solution.py:10
  174.9 3.5 %collective-permute-done = f32[32,512]{1,0:T(8,128)S(1)} collective-permute-done((f32[32,512]{1,0:T(8,128)S(1)}, f32[32,512]{1,0:T(8,128)S(1)}, u32[]{:S(2)}, u32[]{:S(2)}) %collective-permute-start) | collective-permute-done | bytes 65568 | tf_op jit(solution)/shard_map/while/body/eval_jaxpr/ppermute | solution.py:10
  180.2 4.4 %collective-permute-done.1 = f32[32,1024]{1,0:T(8,128)S(1)} collective-permute-done((f32[32,1024]{1,0:T(8,128)S(1)}, f32[32,1024]{1,0:T(8,128)S(1)}, u32[]{:S(2)}, u32[]{:S(2)}) %collective-permute-start.1) | collective-permute-done | bytes 131104 | tf_op jit(solution)/shard_map/while/body/eval_jaxpr/ppermute | solution.py:10
  185.3 4.3 %collective-permute-done.2 = f32[32,1024]{1,0:T(8,128)S(1)} collective-permute-done((f32[32,1024]{1,0:T(8,128)S(1)}, f32[32,1024]{1,0:T(8,128)S(1)}, u32[]{:S(2)}, u32[]{:S(2)}) %collective-permute-start.2) | collective-permute-done | bytes 131104 | tf_op jit(solution)/shard_map/while/body/eval_jaxpr/ppermute | solution.py:10
  190.9 3.7 %collective-permute-done.3 = f32[32,256]{1,0:T(8,128)S(1)} collective-permute-done((f32[32,256]{1,0:T(8,128)S(1)}, f32[32,256]{1,0:T(8,128)S(1)}, u32[]{:S(2)}, u32[]{:S(2)}) %collective-permute-start.3) | collective-permute-done | bytes 32800 | tf_op jit(solution)/shard_map/while/body/eval_jaxpr/ppermute | solution.py:10
  195.2 4.3 %collective-permute-done.4 = f32[32,512]{1,0:T(8,128)S(1)} collective-permute-done((f32[32,512]{1,0:T(8,128)S(1)}, f32[32,512]{1,0:T(8,128)S(1)}, u32[]{:S(2)}, u32[]{:S(2)}) %collective-permute-start.4) | collective-permute-done | bytes 65568 | tf_op jit(solution)/shard_map/while/body/eval_jaxpr/ppermute | solution.py:10
  203.4 3.5 %collective-permute-done = f32[32,512]{1,0:T(8,128)S(1)} collective-permute-done((f32[32,512]{1,0:T(8,128)S(1)}, f32[32,512]{1,0:T(8,128)S(1)}, u32[]{:S(2)}, u32[]{:S(2)}) %collective-permute-start) | collective-permute-done | bytes 65568 | tf_op jit(solution)/shard_map/while/body/eval_jaxpr/ppermute | solution.py:10
  208.7 4.4 %collective-permute-done.1 = f32[32,1024]{1,0:T(8,128)S(1)} collective-permute-done((f32[32,1024]{1,0:T(8,128)S(1)}, f32[32,1024]{1,0:T(8,128)S(1)}, u32[]{:S(2)}, u32[]{:S(2)}) %collective-permute-start.1) | collective-permute-done | bytes 131104 | tf_op jit(solution)/shard_map/while/body/eval_jaxpr/ppermute | solution.py:10
  213.8 4.3 %collective-permute-done.2 = f32[32,1024]{1,0:T(8,128)S(1)} collective-permute-done((f32[32,1024]{1,0:T(8,128)S(1)}, f32[32,1024]{1,0:T(8,128)S(1)}, u32[]{:S(2)}, u32[]{:S(2)}) %collective-permute-start.2) | collective-permute-done | bytes 131104 | tf_op jit(solution)/shard_map/while/body/eval_jaxpr/ppermute | solution.py:10
  219.4 3.3 %collective-permute-done.3 = f32[32,256]{1,0:T(8,128)S(1)} collective-permute-done((f32[32,256]{1,0:T(8,128)S(1)}, f32[32,256]{1,0:T(8,128)S(1)}, u32[]{:S(2)}, u32[]{:S(2)}) %collective-permute-start.3) | collective-permute-done | bytes 32800 | tf_op jit(solution)/shard_map/while/body/eval_jaxpr/ppermute | solution.py:10
  223.4 3.6 %collective-permute-done.4 = f32[32,512]{1,0:T(8,128)S(1)} collective-permute-done((f32[32,512]{1,0:T(8,128)S(1)}, f32[32,512]{1,0:T(8,128)S(1)}, u32[]{:S(2)}, u32[]{:S(2)}) %collective-permute-start.4) | collective-permute-done | bytes 65568 | tf_op jit(solution)/shard_map/while/body/eval_jaxpr/ppermute | solution.py:10
  231.0 3.5 %collective-permute-done = f32[32,512]{1,0:T(8,128)S(1)} collective-permute-done((f32[32,512]{1,0:T(8,128)S(1)}, f32[32,512]{1,0:T(8,128)S(1)}, u32[]{:S(2)}, u32[]{:S(2)}) %collective-permute-start) | collective-permute-done | bytes 65568 | tf_op jit(solution)/shard_map/while/body/eval_jaxpr/ppermute | solution.py:10
  236.2 4.4 %collective-permute-done.1 = f32[32,1024]{1,0:T(8,128)S(1)} collective-permute-done((f32[32,1024]{1,0:T(8,128)S(1)}, f32[32,1024]{1,0:T(8,128)S(1)}, u32[]{:S(2)}, u32[]{:S(2)}) %collective-permute-start.1) | collective-permute-done | bytes 131104 | tf_op jit(solution)/shard_map/while/body/eval_jaxpr/ppermute | solution.py:10
  241.3 4.3 %collective-permute-done.2 = f32[32,1024]{1,0:T(8,128)S(1)} collective-permute-done((f32[32,1024]{1,0:T(8,128)S(1)}, f32[32,1024]{1,0:T(8,128)S(1)}, u32[]{:S(2)}, u32[]{:S(2)}) %collective-permute-start.2) | collective-permute-done | bytes 131104 | tf_op jit(solution)/shard_map/while/body/eval_jaxpr/ppermute | solution.py:10
  246.9 3.3 %collective-permute-done.3 = f32[32,256]{1,0:T(8,128)S(1)} collective-permute-done((f32[32,256]{1,0:T(8,128)S(1)}, f32[32,256]{1,0:T(8,128)S(1)}, u32[]{:S(2)}, u32[]{:S(2)}) %collective-permute-start.3) | collective-permute-done | bytes 32800 | tf_op jit(solution)/shard_map/while/body/eval_jaxpr/ppermute | solution.py:10
  251.0 3.6 %collective-permute-done.4 = f32[32,512]{1,0:T(8,128)S(1)} collective-permute-done((f32[32,512]{1,0:T(8,128)S(1)}, f32[32,512]{1,0:T(8,128)S(1)}, u32[]{:S(2)}, u32[]{:S(2)}) %collective-permute-start.4) | collective-permute-done | bytes 65568 | tf_op jit(solution)/shard_map/while/body/eval_jaxpr/ppermute | solution.py:10
  (324 shorter events, 133.6 us)
Async XLA Ops:
  3.9 5.3 %collective-permute-start = (f32[32,512]{1,0:T(8,128)S(1)}, f32[32,512]{1,0:T(8,128)S(1)}, u32[]{:S(2)}, u32[]{:S(2)}) collective-permute-start(f32[32,512]{1,0:T(8,128)S(1)} %convolution_add_fusion.4), channel_id=1, source_target_pairs={{0,4},{4,0},{8,12},{12,8},{1,5},{5,1},{9,13},{13,9},{2,6},{6,2},{1... | collective-permute-start | bytes 196616 | tf_op jit(solution)/shard_map/while/body/eval_jaxpr/ppermute | solution.py:10
  10.3 5.0 %collective-permute-start.1 = (f32[32,1024]{1,0:T(8,128)S(1)}, f32[32,1024]{1,0:T(8,128)S(1)}, u32[]{:S(2)}, u32[]{:S(2)}) collective-permute-start(f32[32,1024]{1,0:T(8,128)S(1)} %convolution_add_fusion.5), channel_id=1, source_target_pairs={{0,4},{4,0},{8,12},{12,8},{1,5},{5,1},{9,13},{13,9},{2,6},{6,2},{1... | collective-permute-start | bytes 393224 | tf_op jit(solution)/shard_map/while/body/eval_jaxpr/ppermute | solution.py:10
  15.4 5.0 %collective-permute-start.2 = (f32[32,1024]{1,0:T(8,128)S(1)}, f32[32,1024]{1,0:T(8,128)S(1)}, u32[]{:S(2)}, u32[]{:S(2)}) collective-permute-start(f32[32,1024]{1,0:T(8,128)S(1)} %add.126), channel_id=1, source_target_pairs={{0,2},{2,0},{1,3},{3,1},{4,6},{6,4},{5,7},{7,5},{8,10},{10,8},{9,1... | collective-permute-start | bytes 393224 | tf_op jit(solution)/shard_map/while/body/eval_jaxpr/ppermute | solution.py:10
  25.0 4.3 %collective-permute-start.4 = (f32[32,512]{1,0:T(8,128)S(1)}, f32[32,512]{1,0:T(8,128)S(1)}, u32[]{:S(2)}, u32[]{:S(2)}) collective-permute-start(f32[32,512]{1,0:T(8,128)S(1)} %maximum_select_fusion.6), channel_id=1, source_target_pairs={{0,2},{2,0},{1,3},{3,1},{4,6},{6,4},{5,7},{7,5},{8,10},{10,8},{9,1... | collective-permute-start | bytes 196616 | tf_op jit(solution)/shard_map/while/body/eval_jaxpr/ppermute | solution.py:10
  32.4 4.3 %collective-permute-start = (f32[32,512]{1,0:T(8,128)S(1)}, f32[32,512]{1,0:T(8,128)S(1)}, u32[]{:S(2)}, u32[]{:S(2)}) collective-permute-start(f32[32,512]{1,0:T(8,128)S(1)} %convolution_add_fusion.4), channel_id=1, source_target_pairs={{0,4},{4,0},{8,12},{12,8},{1,5},{5,1},{9,13},{13,9},{2,6},{6,2},{1... | collective-permute-start | bytes 196616 | tf_op jit(solution)/shard_map/while/body/eval_jaxpr/ppermute | solution.py:10
  37.8 5.4 %collective-permute-start.1 = (f32[32,1024]{1,0:T(8,128)S(1)}, f32[32,1024]{1,0:T(8,128)S(1)}, u32[]{:S(2)}, u32[]{:S(2)}) collective-permute-start(f32[32,1024]{1,0:T(8,128)S(1)} %convolution_add_fusion.5), channel_id=1, source_target_pairs={{0,4},{4,0},{8,12},{12,8},{1,5},{5,1},{9,13},{13,9},{2,6},{6,2},{1... | collective-permute-start | bytes 393224 | tf_op jit(solution)/shard_map/while/body/eval_jaxpr/ppermute | solution.py:10
  43.2 5.0 %collective-permute-start.2 = (f32[32,1024]{1,0:T(8,128)S(1)}, f32[32,1024]{1,0:T(8,128)S(1)}, u32[]{:S(2)}, u32[]{:S(2)}) collective-permute-start(f32[32,1024]{1,0:T(8,128)S(1)} %add.126), channel_id=1, source_target_pairs={{0,2},{2,0},{1,3},{3,1},{4,6},{6,4},{5,7},{7,5},{8,10},{10,8},{9,1... | collective-permute-start | bytes 393224 | tf_op jit(solution)/shard_map/while/body/eval_jaxpr/ppermute | solution.py:10
  53.1 4.3 %collective-permute-start.4 = (f32[32,512]{1,0:T(8,128)S(1)}, f32[32,512]{1,0:T(8,128)S(1)}, u32[]{:S(2)}, u32[]{:S(2)}) collective-permute-start(f32[32,512]{1,0:T(8,128)S(1)} %maximum_select_fusion.6), channel_id=1, source_target_pairs={{0,2},{2,0},{1,3},{3,1},{4,6},{6,4},{5,7},{7,5},{8,10},{10,8},{9,1... | collective-permute-start | bytes 196616 | tf_op jit(solution)/shard_map/while/body/eval_jaxpr/ppermute | solution.py:10
  60.5 4.3 %collective-permute-start = (f32[32,512]{1,0:T(8,128)S(1)}, f32[32,512]{1,0:T(8,128)S(1)}, u32[]{:S(2)}, u32[]{:S(2)}) collective-permute-start(f32[32,512]{1,0:T(8,128)S(1)} %convolution_add_fusion.4), channel_id=1, source_target_pairs={{0,4},{4,0},{8,12},{12,8},{1,5},{5,1},{9,13},{13,9},{2,6},{6,2},{1... | collective-permute-start | bytes 196616 | tf_op jit(solution)/shard_map/while/body/eval_jaxpr/ppermute | solution.py:10
  66.0 5.0 %collective-permute-start.1 = (f32[32,1024]{1,0:T(8,128)S(1)}, f32[32,1024]{1,0:T(8,128)S(1)}, u32[]{:S(2)}, u32[]{:S(2)}) collective-permute-start(f32[32,1024]{1,0:T(8,128)S(1)} %convolution_add_fusion.5), channel_id=1, source_target_pairs={{0,4},{4,0},{8,12},{12,8},{1,5},{5,1},{9,13},{13,9},{2,6},{6,2},{1... | collective-permute-start | bytes 393224 | tf_op jit(solution)/shard_map/while/body/eval_jaxpr/ppermute | solution.py:10
  71.0 5.0 %collective-permute-start.2 = (f32[32,1024]{1,0:T(8,128)S(1)}, f32[32,1024]{1,0:T(8,128)S(1)}, u32[]{:S(2)}, u32[]{:S(2)}) collective-permute-start(f32[32,1024]{1,0:T(8,128)S(1)} %add.126), channel_id=1, source_target_pairs={{0,2},{2,0},{1,3},{3,1},{4,6},{6,4},{5,7},{7,5},{8,10},{10,8},{9,1... | collective-permute-start | bytes 393224 | tf_op jit(solution)/shard_map/while/body/eval_jaxpr/ppermute | solution.py:10
  80.8 4.7 %collective-permute-start.4 = (f32[32,512]{1,0:T(8,128)S(1)}, f32[32,512]{1,0:T(8,128)S(1)}, u32[]{:S(2)}, u32[]{:S(2)}) collective-permute-start(f32[32,512]{1,0:T(8,128)S(1)} %maximum_select_fusion.6), channel_id=1, source_target_pairs={{0,2},{2,0},{1,3},{3,1},{4,6},{6,4},{5,7},{7,5},{8,10},{10,8},{9,1... | collective-permute-start | bytes 196616 | tf_op jit(solution)/shard_map/while/body/eval_jaxpr/ppermute | solution.py:10
  88.6 4.3 %collective-permute-start = (f32[32,512]{1,0:T(8,128)S(1)}, f32[32,512]{1,0:T(8,128)S(1)}, u32[]{:S(2)}, u32[]{:S(2)}) collective-permute-start(f32[32,512]{1,0:T(8,128)S(1)} %convolution_add_fusion.4), channel_id=1, source_target_pairs={{0,4},{4,0},{8,12},{12,8},{1,5},{5,1},{9,13},{13,9},{2,6},{6,2},{1... | collective-permute-start | bytes 196616 | tf_op jit(solution)/shard_map/while/body/eval_jaxpr/ppermute | solution.py:10
  94.0 5.7 %collective-permute-start.1 = (f32[32,1024]{1,0:T(8,128)S(1)}, f32[32,1024]{1,0:T(8,128)S(1)}, u32[]{:S(2)}, u32[]{:S(2)}) collective-permute-start(f32[32,1024]{1,0:T(8,128)S(1)} %convolution_add_fusion.5), channel_id=1, source_target_pairs={{0,4},{4,0},{8,12},{12,8},{1,5},{5,1},{9,13},{13,9},{2,6},{6,2},{1... | collective-permute-start | bytes 393224 | tf_op jit(solution)/shard_map/while/body/eval_jaxpr/ppermute | solution.py:10
  99.8 5.0 %collective-permute-start.2 = (f32[32,1024]{1,0:T(8,128)S(1)}, f32[32,1024]{1,0:T(8,128)S(1)}, u32[]{:S(2)}, u32[]{:S(2)}) collective-permute-start(f32[32,1024]{1,0:T(8,128)S(1)} %add.126), channel_id=1, source_target_pairs={{0,2},{2,0},{1,3},{3,1},{4,6},{6,4},{5,7},{7,5},{8,10},{10,8},{9,1... | collective-permute-start | bytes 393224 | tf_op jit(solution)/shard_map/while/body/eval_jaxpr/ppermute | solution.py:10
  109.4 4.3 %collective-permute-start.4 = (f32[32,512]{1,0:T(8,128)S(1)}, f32[32,512]{1,0:T(8,128)S(1)}, u32[]{:S(2)}, u32[]{:S(2)}) collective-permute-start(f32[32,512]{1,0:T(8,128)S(1)} %maximum_select_fusion.6), channel_id=1, source_target_pairs={{0,2},{2,0},{1,3},{3,1},{4,6},{6,4},{5,7},{7,5},{8,10},{10,8},{9,1... | collective-permute-start | bytes 196616 | tf_op jit(solution)/shard_map/while/body/eval_jaxpr/ppermute | solution.py:10
  116.8 4.8 %collective-permute-start = (f32[32,512]{1,0:T(8,128)S(1)}, f32[32,512]{1,0:T(8,128)S(1)}, u32[]{:S(2)}, u32[]{:S(2)}) collective-permute-start(f32[32,512]{1,0:T(8,128)S(1)} %convolution_add_fusion.4), channel_id=1, source_target_pairs={{0,4},{4,0},{8,12},{12,8},{1,5},{5,1},{9,13},{13,9},{2,6},{6,2},{1... | collective-permute-start | bytes 196616 | tf_op jit(solution)/shard_map/while/body/eval_jaxpr/ppermute | solution.py:10
  122.7 5.6 %collective-permute-start.1 = (f32[32,1024]{1,0:T(8,128)S(1)}, f32[32,1024]{1,0:T(8,128)S(1)}, u32[]{:S(2)}, u32[]{:S(2)}) collective-permute-start(f32[32,1024]{1,0:T(8,128)S(1)} %convolution_add_fusion.5), channel_id=1, source_target_pairs={{0,4},{4,0},{8,12},{12,8},{1,5},{5,1},{9,13},{13,9},{2,6},{6,2},{1... | collective-permute-start | bytes 393224 | tf_op jit(solution)/shard_map/while/body/eval_jaxpr/ppermute | solution.py:10
  128.3 5.0 %collective-permute-start.2 = (f32[32,1024]{1,0:T(8,128)S(1)}, f32[32,1024]{1,0:T(8,128)S(1)}, u32[]{:S(2)}, u32[]{:S(2)}) collective-permute-start(f32[32,1024]{1,0:T(8,128)S(1)} %add.126), channel_id=1, source_target_pairs={{0,2},{2,0},{1,3},{3,1},{4,6},{6,4},{5,7},{7,5},{8,10},{10,8},{9,1... | collective-permute-start | bytes 393224 | tf_op jit(solution)/shard_map/while/body/eval_jaxpr/ppermute | solution.py:10
  145.3 4.9 %collective-permute-start = (f32[32,512]{1,0:T(8,128)S(1)}, f32[32,512]{1,0:T(8,128)S(1)}, u32[]{:S(2)}, u32[]{:S(2)}) collective-permute-start(f32[32,512]{1,0:T(8,128)S(1)} %convolution_add_fusion.4), channel_id=1, source_target_pairs={{0,4},{4,0},{8,12},{12,8},{1,5},{5,1},{9,13},{13,9},{2,6},{6,2},{1... | collective-permute-start | bytes 196616 | tf_op jit(solution)/shard_map/while/body/eval_jaxpr/ppermute | solution.py:10
  151.3 5.0 %collective-permute-start.1 = (f32[32,1024]{1,0:T(8,128)S(1)}, f32[32,1024]{1,0:T(8,128)S(1)}, u32[]{:S(2)}, u32[]{:S(2)}) collective-permute-start(f32[32,1024]{1,0:T(8,128)S(1)} %convolution_add_fusion.5), channel_id=1, source_target_pairs={{0,4},{4,0},{8,12},{12,8},{1,5},{5,1},{9,13},{13,9},{2,6},{6,2},{1... | collective-permute-start | bytes 393224 | tf_op jit(solution)/shard_map/while/body/eval_jaxpr/ppermute | solution.py:10
  156.3 5.7 %collective-permute-start.2 = (f32[32,1024]{1,0:T(8,128)S(1)}, f32[32,1024]{1,0:T(8,128)S(1)}, u32[]{:S(2)}, u32[]{:S(2)}) collective-permute-start(f32[32,1024]{1,0:T(8,128)S(1)} %add.126), channel_id=1, source_target_pairs={{0,2},{2,0},{1,3},{3,1},{4,6},{6,4},{5,7},{7,5},{8,10},{10,8},{9,1... | collective-permute-start | bytes 393224 | tf_op jit(solution)/shard_map/while/body/eval_jaxpr/ppermute | solution.py:10
  174.1 4.3 %collective-permute-start = (f32[32,512]{1,0:T(8,128)S(1)}, f32[32,512]{1,0:T(8,128)S(1)}, u32[]{:S(2)}, u32[]{:S(2)}) collective-permute-start(f32[32,512]{1,0:T(8,128)S(1)} %convolution_add_fusion.4), channel_id=1, source_target_pairs={{0,4},{4,0},{8,12},{12,8},{1,5},{5,1},{9,13},{13,9},{2,6},{6,2},{1... | collective-permute-start | bytes 196616 | tf_op jit(solution)/shard_map/while/body/eval_jaxpr/ppermute | solution.py:10
  179.5 5.0 %collective-permute-start.1 = (f32[32,1024]{1,0:T(8,128)S(1)}, f32[32,1024]{1,0:T(8,128)S(1)}, u32[]{:S(2)}, u32[]{:S(2)}) collective-permute-start(f32[32,1024]{1,0:T(8,128)S(1)} %convolution_add_fusion.5), channel_id=1, source_target_pairs={{0,4},{4,0},{8,12},{12,8},{1,5},{5,1},{9,13},{13,9},{2,6},{6,2},{1... | collective-permute-start | bytes 393224 | tf_op jit(solution)/shard_map/while/body/eval_jaxpr/ppermute | solution.py:10
  184.5 5.0 %collective-permute-start.2 = (f32[32,1024]{1,0:T(8,128)S(1)}, f32[32,1024]{1,0:T(8,128)S(1)}, u32[]{:S(2)}, u32[]{:S(2)}) collective-permute-start(f32[32,1024]{1,0:T(8,128)S(1)} %add.126), channel_id=1, source_target_pairs={{0,2},{2,0},{1,3},{3,1},{4,6},{6,4},{5,7},{7,5},{8,10},{10,8},{9,1... | collective-permute-start | bytes 393224 | tf_op jit(solution)/shard_map/while/body/eval_jaxpr/ppermute | solution.py:10
  194.5 5.0 %collective-permute-start.4 = (f32[32,512]{1,0:T(8,128)S(1)}, f32[32,512]{1,0:T(8,128)S(1)}, u32[]{:S(2)}, u32[]{:S(2)}) collective-permute-start(f32[32,512]{1,0:T(8,128)S(1)} %maximum_select_fusion.6), channel_id=1, source_target_pairs={{0,2},{2,0},{1,3},{3,1},{4,6},{6,4},{5,7},{7,5},{8,10},{10,8},{9,1... | collective-permute-start | bytes 196616 | tf_op jit(solution)/shard_map/while/body/eval_jaxpr/ppermute | solution.py:10
  202.6 4.3 %collective-permute-start = (f32[32,512]{1,0:T(8,128)S(1)}, f32[32,512]{1,0:T(8,128)S(1)}, u32[]{:S(2)}, u32[]{:S(2)}) collective-permute-start(f32[32,512]{1,0:T(8,128)S(1)} %convolution_add_fusion.4), channel_id=1, source_target_pairs={{0,4},{4,0},{8,12},{12,8},{1,5},{5,1},{9,13},{13,9},{2,6},{6,2},{1... | collective-permute-start | bytes 196616 | tf_op jit(solution)/shard_map/while/body/eval_jaxpr/ppermute | solution.py:10
  208.1 5.0 %collective-permute-start.1 = (f32[32,1024]{1,0:T(8,128)S(1)}, f32[32,1024]{1,0:T(8,128)S(1)}, u32[]{:S(2)}, u32[]{:S(2)}) collective-permute-start(f32[32,1024]{1,0:T(8,128)S(1)} %convolution_add_fusion.5), channel_id=1, source_target_pairs={{0,4},{4,0},{8,12},{12,8},{1,5},{5,1},{9,13},{13,9},{2,6},{6,2},{1... | collective-permute-start | bytes 393224 | tf_op jit(solution)/shard_map/while/body/eval_jaxpr/ppermute | solution.py:10
  213.1 5.0 %collective-permute-start.2 = (f32[32,1024]{1,0:T(8,128)S(1)}, f32[32,1024]{1,0:T(8,128)S(1)}, u32[]{:S(2)}, u32[]{:S(2)}) collective-permute-start(f32[32,1024]{1,0:T(8,128)S(1)} %add.126), channel_id=1, source_target_pairs={{0,2},{2,0},{1,3},{3,1},{4,6},{6,4},{5,7},{7,5},{8,10},{10,8},{9,1... | collective-permute-start | bytes 393224 | tf_op jit(solution)/shard_map/while/body/eval_jaxpr/ppermute | solution.py:10
  222.7 4.3 %collective-permute-start.4 = (f32[32,512]{1,0:T(8,128)S(1)}, f32[32,512]{1,0:T(8,128)S(1)}, u32[]{:S(2)}, u32[]{:S(2)}) collective-permute-start(f32[32,512]{1,0:T(8,128)S(1)} %maximum_select_fusion.6), channel_id=1, source_target_pairs={{0,2},{2,0},{1,3},{3,1},{4,6},{6,4},{5,7},{7,5},{8,10},{10,8},{9,1... | collective-permute-start | bytes 196616 | tf_op jit(solution)/shard_map/while/body/eval_jaxpr/ppermute | solution.py:10
  235.6 5.0 %collective-permute-start.1 = (f32[32,1024]{1,0:T(8,128)S(1)}, f32[32,1024]{1,0:T(8,128)S(1)}, u32[]{:S(2)}, u32[]{:S(2)}) collective-permute-start(f32[32,1024]{1,0:T(8,128)S(1)} %convolution_add_fusion.5), channel_id=1, source_target_pairs={{0,4},{4,0},{8,12},{12,8},{1,5},{5,1},{9,13},{13,9},{2,6},{6,2},{1... | collective-permute-start | bytes 393224 | tf_op jit(solution)/shard_map/while/body/eval_jaxpr/ppermute | solution.py:10
  240.6 5.0 %collective-permute-start.2 = (f32[32,1024]{1,0:T(8,128)S(1)}, f32[32,1024]{1,0:T(8,128)S(1)}, u32[]{:S(2)}, u32[]{:S(2)}) collective-permute-start(f32[32,1024]{1,0:T(8,128)S(1)} %add.126), channel_id=1, source_target_pairs={{0,2},{2,0},{1,3},{3,1},{4,6},{6,4},{5,7},{7,5},{8,10},{10,8},{9,1... | collective-permute-start | bytes 393224 | tf_op jit(solution)/shard_map/while/body/eval_jaxpr/ppermute | solution.py:10
  (55 other events, 451.2 us)
where the time goes:
time: 257 us; the launch traced here: 256 us
  waiting for transfers between devices  156 us (61%)
  starting transfers between devices  53.3 us (21%)
  matrix products  34.1 us (13%)
  local copies, waits for them, and re-layouts  9.8 us (4%)
    ppermute x45, waiting for transfers between devices, from_partner(): return lax.ppermute(value, axis, pairs)  156 us
    ppermute x45, starting transfers between devices, from_partner(): return lax.ppermute(value, axis, pairs)  53.3 us
    dot_general x45, matrix products, matmul(): jnp.dot(left, right, precision=lax.Precision.HIGHEST, preferred_element_t...  34.1 us
    mul x9, local copies, waits for them, and re-layouts, advance(): source = weights[:, None] * probe_mask  6.22 us
  transfers between devices with their start and end apart: 45, of which 45 were waited for; matrix products, arithmetic and copies ran while one was open for 0% of the time, Pallas kernels for 0%

commit v1 on v0

v1 whole, which is shorter than its diff:
```python
import jax
import jax.numpy as jnp
from jax import lax
from jax.experimental import pallas as pl
from jax.experimental.pallas import tpu as pltpu
from jax.sharding import PartitionSpec as P

F32 = jnp.float32
BF16 = jnp.bfloat16


def from_partner(value, axis):
    pairs = [(source, source ^ 1) for source in range(lax.axis_size(axis))]
    return lax.ppermute(value, axis, pairs)


def exact_dot(left, right):
    return jnp.dot(left, right, precision=lax.Precision.HIGHEST, preferred_element_type=F32)


def halves_of(value):
    high = value.astype(BF16)
    return high, (value - high.astype(F32)).astype(BF16)


def store_split(high_ref, low_ref, where, value):
    high, low = halves_of(value)
    high_ref[where] = high
    low_ref[where] = low


def tall_kernel(place, own, *refs):
    high_ref, low_ref = refs[6:]
    quarter, core = place[0], place[1]
    half = own.shape[0] // 2
    store_split(high_ref, low_ref, quarter, own[...])
    for tile in range(1, 4):
        for part in range(2):
            rows = pl.ds(pl.multiple_of((core ^ part) * half, half), half)
            store_split(high_ref, low_ref, (quarter ^ tile, rows, slice(None)), refs[2 * (tile - 1) + part][...])


def wide_kernel(place, own, *refs):
    high_ref, low_ref = refs[6:]
    quarter, core = place[0], place[1]
    width = own.shape[0]
    rows = pl.ds(pl.multiple_of(quarter * width, width), width)
    for block in range(4):
        store_split(high_ref, low_ref, (block, rows, slice(None)), own[:, block * width:(block + 1) * width])
    for tile in range(1, 4):
        rows = pl.ds(pl.multiple_of((quarter ^ tile) * width, width), width)
        for part in range(2):
            piece = refs[2 * (tile - 1) + part]
            for block in range(2):
                store_split(
                    high_ref,
                    low_ref,
                    (2 * (core ^ part) + block, rows, slice(None)),
                    piece[:, block * width:(block + 1) * width],
                )


def edge_kernel(place, *refs):
    high_ref, low_ref = refs[8:]
    quarter, core = place[0], place[1]
    rows = refs[0].shape[0] // 2
    for tile in range(4):
        for part in range(2):
            piece = refs[2 * tile + part]
            for bit in range(2):
                start = bit * 2 * rows + (core ^ part) * rows
                store_split(
                    high_ref,
                    low_ref,
                    (quarter ^ tile, pl.ds(pl.multiple_of(start, rows), rows), slice(None)),
                    piece[bit * rows:(bit + 1) * rows, :],
                )


def split_call(kernel, place, shape, arrays):
    out = jax.ShapeDtypeStruct(shape, BF16)
    vmem = pl.BlockSpec(memory_space=pltpu.VMEM)
    return pl.pallas_call(
        kernel,
        in_specs=[pl.BlockSpec(memory_space=pltpu.SMEM)] + [vmem] * len(arrays),
        out_specs=(vmem, vmem),
        out_shape=(out, out),
        compiler_params=pltpu.CompilerParams(vmem_limit_bytes=24 * 2**20),
    )(place, *arrays)


def product(left, high, low):
    rows = left.shape[0]
    left_high, left_low = halves_of(left)
    both = jnp.dot(jnp.concatenate([left_high, left_low], axis=0), high, preferred_element_type=F32)
    rest = jnp.dot(left_high, low, preferred_element_type=F32)
    return both[:rows] + both[rows:] + rest


def march_kernel(place, s0, s1, s2, s3, weight, eh, el, lh, ll, rh, rl, bh, bl, one_ref, two_ref, starts, picks, mass):
    quarter = place[0]
    rows, width = one_ref.shape
    for tile, state in enumerate((s0, s1, s2, s3)):
        where = quarter ^ tile
        starts[0, where] = state[:rows, :width]
        starts[1, where] = state[:rows, width:2 * width]
        picks[where] = state[:rows, 2 * width:]
        mass[where] = state[rows:, :width]
    scale = jnp.concatenate([mass[tile][:1, :] for tile in range(4)], axis=1)
    picked = jnp.concatenate([picks[tile] for tile in range(4)], axis=1)

    def advance(step, carry):
        one, two = carry
        half = jnp.concatenate(
            [product(one[:, (tile // 2) * 2 * width:(tile // 2 + 1) * 2 * width], eh[tile], el[tile]) for tile in range(4)],
            axis=1,
        )
        half = half + weight[step] * picked
        sums = jnp.concatenate([product(half, lh[block], ll[block]) for block in range(4)], axis=1) + two * scale
        two = jnp.concatenate([product(sums, rh[tile], rl[tile]) for tile in range(4)], axis=1)
        back = jnp.concatenate([product(two, bh[tile], bl[tile]) for tile in range(4)], axis=1)
        return half - back, two

    first = tuple(jnp.concatenate([starts[which, tile] for tile in range(4)], axis=1) for which in range(2))
    one, two = lax.fori_loop(0, weight.shape[0], advance, first)
    for tile in range(4):
        starts[0, tile] = one[:, tile * width:(tile + 1) * width]
        starts[1, tile] = two[:, tile * width:(tile + 1) * width]
    one_ref[...] = starts[0, quarter]
    two_ref[...] = starts[1, quarter]


def shards(
    adjoint_one_start,
    adjoint_two_start,
    couple_panel,
    pair_panel,
    lift_panel,
    root_panel,
    back_panel,
    mass_two,
    probe_cells,
    probe_weight,
):
    couple = couple_panel[0, 0]
    pair_cols = pair_panel[0, 0]
    lift = lift_panel[0, 0]
    root = root_panel[0, 0]
    back = back_panel[0, 0]
    mass = mass_two[0, 0]
    width = couple.shape[0]
    rows = probe_cells.shape[0]
    column, row, core = lax.axis_index("gx"), lax.axis_index("gy"), lax.axis_index("gz")
    x_bit, y_bit = column % 2, row % 2
    quarter = 2 * y_bit + x_bit
    place = jnp.stack([quarter, core]).astype(jnp.int32)

    def half_rows(panel):
        size = panel.shape[0] // 2
        return lax.dynamic_slice_in_dim(panel, core * size, size, 0)

    owners = (column - x_bit + jnp.arange(2)) * lax.axis_size("gy") + row
    targets = (owners[:, None] * width + jnp.arange(width)[None, :]).reshape(-1)
    chosen = (probe_cells[:, None] == targets[None, :]).astype(F32)
    picked = exact_dot(chosen, pair_cols)
    state = jnp.concatenate([adjoint_one_start[0, 0], adjoint_two_start[0, 0], picked], axis=1)
    state = jnp.concatenate([state, jnp.broadcast_to(jnp.pad(mass, (0, 2 * width)), (8, 3 * width))], axis=0)

    couple_mine = half_rows(couple)
    couple_other = from_partner(couple_mine, "gx")
    own = {
        "S": state,
        "L": lax.dynamic_slice_in_dim(lift, core * 2 * width, 2 * width, 1),
        "R": half_rows(root),
        "B": half_rows(back),
    }
    first = jnp.where(x_bit == 0, couple_mine, couple_other)
    second = jnp.where(x_bit == 0, couple_other, couple_mine)
    own["E"] = exact_dot(jnp.concatenate([first, second], axis=0), pair_cols)

    across_x = {name: from_partner(own[name], "gx") for name in ("S", "R", "B", "E", "L")}
    across_y = {name: from_partner(own[name], "gy") for name in ("L", "E", "S", "R", "B")}
    diagonal = {name: from_partner(across_y[name], "gx") for name in ("E", "L")}
    diagonal.update({name: from_partner(across_x[name], "gy") for name in ("S", "R", "B")})

    def both(name):
        arrays = []
        for tile in (across_x, across_y, diagonal):
            arrays += [tile[name], from_partner(tile[name], "gz")]
        return arrays

    edge_high, edge_low = split_call(
        edge_kernel, place, (4, 2 * width, width), [own["E"], from_partner(own["E"], "gz")] + both("E")
    )
    lift_high, lift_low = split_call(wide_kernel, place, (4, 4 * width, width), [lift] + both("L"))
    root_high, root_low = split_call(tall_kernel, place, (4, 4 * width, width), [root] + both("R"))
    back_high, back_low = split_call(tall_kernel, place, (4, 4 * width, width), [back] + both("B"))

    vmem = pl.BlockSpec(memory_space=pltpu.VMEM)
    one, two = pl.pallas_call(
        march_kernel,
        in_specs=[pl.BlockSpec(memory_space=pltpu.SMEM)] + [vmem] * 13,
        out_specs=(vmem, vmem),
        out_shape=(jax.ShapeDtypeStruct((rows, width), F32),) * 2,
        scratch_shapes=[
            pltpu.VMEM((2, 4, rows, width), F32),
            pltpu.VMEM((4, rows, width), F32),
            pltpu.VMEM((4, 8, width), F32),
        ],
        compiler_params=pltpu.CompilerParams(vmem_limit_bytes=40 * 2**20),
    )(
        place,
        state,
        across_x["S"],
        across_y["S"],
        diagonal["S"],
        probe_weight[:, :, None],
        edge_high,
        edge_low,
        lift_high,
        lift_low,
        root_high,
        root_low,
        back_high,
        back_low,
    )
    return (one[None, None], two[None, None])


def solution(mesh):
    placed = (
        P(("groups", "gx"), "gy", "gz", None),
        P(("groups", "gx"), "gy", "gz", None),
        P(("groups", "gx"), "gy", None, None),
        P(("groups", "gx"), "gy", None, None),
        P(("groups", "gx"), "gy", None, None),
        P(("groups", "gx"), "gy", None, None),
        P(("groups", "gx"), "gy", None, None),
        P(("groups", "gx"), "gy", None),
        P(("groups", "gz")),
        P("groups", "gz"),
    )
    return jax.shard_map(
        shards,
        mesh=mesh,
        in_specs=placed,
        out_specs=(P(("groups", "gx"), "gy", "gz", None), P(("groups", "gx"), "gy", "gz", None)),
        check_vma=False,
    )
```

time: 257 us -> 150 us (0.58)
  waiting for transfers between devices: 156 us -> 64.1 us
  Pallas kernels: 0 us -> 33.4 us
  matrix products: 34.1 us -> 0.9 us
  starting transfers between devices: 53.3 us -> 20.9 us
  local copies, waits for them, and re-layouts: 9.8 us -> 26.8 us
    ppermute x45 -> x29, waiting for transfers between devices: 156 us -> 64.1 us  [from_partner(): return lax.ppermute(value, axis, pairs)]
    pallas_call x0 -> x5, Pallas kernels: none -> 33.4 us  [the longest x1 26.4 us: shards(): pl.pallas_call(march_kernel, in_specs=[pl.BlockSpec(memory_space=pltpu.SM...]
    dot_general x45 -> x2, matrix products: 34.1 us -> 0.9 us  [exact_dot(): jnp.dot(left, right, precision=lax.Precision.HIGHEST, preferred_element_t...]
    ppermute x45 -> x29, starting transfers between devices: 53.3 us -> 20.9 us  [from_partner(): return lax.ppermute(value, axis, pairs)]
    unnamed x12 -> x85, local copies, waits for them, and re-layouts: 1.34 us -> 20.6 us
    mul x27 -> x0, local copies, waits for them, and re-layouts: 6.64 us -> none  [the longest x9 6.22 us: advance(): source = weights[:, None] * probe_mask]
    dynamic_slice x0 -> x4, local copies, waits for them, and re-layouts: none -> 5.43 us  [the longest x3 3.4 us: half_rows(): return lax.dynamic_slice_in_dim(panel, core * size, size, 0)]
  transfers between devices with their start and end apart: 45 -> 29, of which waited for: 45 -> 8; matrix products, arithmetic and copies ran while one was open for 0% -> 5% of each run, Pallas kernels for 0% -> 5%
where the time goes in v1:
time: 150 us; the launch traced here: 149 us
  waiting for transfers between devices  64.1 us (43%)
  Pallas kernels  33.4 us (22%)
  local copies, waits for them, and re-layouts  26.8 us (18%)
  starting transfers between devices  20.9 us (14%)
  other arithmetic  1.81 us (1%)
    ppermute x29, waiting for transfers between devices, from_partner(): return lax.ppermute(value, axis, pairs)  64.1 us
    pallas_call x1, Pallas kernels, shards(): pl.pallas_call(march_kernel, in_specs=[pl.BlockSpec(memory_space=pltpu.SM...  26.4 us
    ppermute x29, starting transfers between devices, from_partner(): return lax.ppermute(value, axis, pairs)  20.9 us
    unnamed x85, local copies, waits for them, and re-layouts  20.6 us
    pallas_call x4, Pallas kernels, split_call(): pl.pallas_call(kernel, in_specs=[pl.BlockSpec(memory_space=pltpu.SMEM)] +...  6.99 us
    dynamic_slice x3, local copies, waits for them, and re-layouts, half_rows(): return lax.dynamic_slice_in_dim(panel, core * size, size, 0)  3.4 us
  transfers between devices with their start and end apart: 29, of which 8 were waited for; matrix products, arithmetic and copies ran while one was open for 5% of the time, Pallas kernels for 5%

profile of v1, /device:TPU:0, one launch (start us, length us, event | category | flops | bytes accessed | tf_op | source)
XLA Modules:
  0.0 149.0 jit_solution(2387258281605309686)
XLA Ops:
  0.7 2.0 %dynamic-slice_bitcast_fusion.2 = f32[256,512]{1,0:T(8,128)} fusion(f32[1,1,256,1024]{3,2,1,0:T(8,128)} %param.14, s32[]{:T(128)S(6)} %select_n.37), kind=kLoop, calls=%fused_computation.9 | loop fusion | bytes 1048580 | tf_op jit(solution)/shard_map/dynamic_slice | solution.py:173
  2.7 2.9 %collective-permute-start.13 = (f32[256,512]{1,0:T(8,128)}, f32[256,512]{1,0:T(8,128)S(1)}, u32[]{:S(2)}, u32[]{:S(2)}) collective-permute-start(f32[256,512]{1,0:T(8,128)} %dynamic-slice_bitcast_fusion.2), channel_id=1, source_target_pairs={{0,2},{2,0},{1,3},{3,1},{4,6},{6,4},{5,7},{7,5},{8,10},{10,8},{9,1... | collective-permute-start | bytes 1572872 | tf_op jit(solution)/shard_map/ppermute | solution.py:14
  5.7 1.6 %collective-permute-start.11 = (f32[256,512]{1,0:T(8,128)}, f32[256,512]{1,0:T(8,128)}, u32[]{:S(2)}, u32[]{:S(2)}) collective-permute-start(f32[256,512]{1,0:T(8,128)} %dynamic-slice_bitcast_fusion.2), channel_id=1, source_target_pairs={{0,4},{4,0},{8,12},{12,8},{1,5},{5,1},{9,13},{13,9},{2,6},{6,2},{1... | collective-permute-start | bytes 1572872 | tf_op jit(solution)/shard_map/ppermute | solution.py:14
  7.3 1.9 %dynamic-slice_bitcast_fusion.1 = f32[512,256]{1,0:T(8,128)} fusion(f32[1,1,1024,256]{3,2,1,0:T(8,128)} %param.15, s32[]{:T(128)S(6)} %select_n.37), kind=kLoop, calls=%fused_computation.8 | loop fusion | bytes 1048580 | tf_op jit(solution)/shard_map/dynamic_slice | solution.py:160
  10.3 1.6 %collective-permute-start.3 = (f32[128,512]{1,0:T(8,128)}, f32[128,512]{1,0:T(8,128)S(1)}, u32[]{:S(2)}, u32[]{:S(2)}) collective-permute-start(f32[128,512]{1,0:T(8,128)} %dynamic-slice_bitcast_fusion.3), channel_id=1, source_target_pairs={{0,4},{4,0},{8,12},{12,8},{1,5},{5,1},{9,13},{13,9},{2,6},{6,2},{1... | collective-permute-start | bytes 786440 | tf_op jit(solution)/shard_map/ppermute | solution.py:14
  14.3 24.6 %collective-permute-done.s1 = f32[40,768]{1,0:T(8,128)} collective-permute-done((f32[40,768]{1,0:T(8,128)}, f32[40,768]{1,0:T(8,128)}, u32[]{:S(2)}, u32[]{:S(2)}) %collective-permute-start) | collective-permute-done | bytes 122912 | tf_op jit(solution)/shard_map/ppermute | solution.py:14
  39.3 1.7 %collective-permute-start.23 = (f32[512,256]{1,0:T(8,128)}, f32[512,256]{1,0:T(8,128)}, u32[]{:S(2)}, u32[]{:S(2)}) collective-permute-start(f32[512,256]{1,0:T(8,128)} %dynamic-slice_bitcast_fusion), channel_id=1, source_target_pairs={{0,4},{4,0},{8,12},{12,8},{1,5},{5,1},{9,13},{13,9},{2,6},{6,2},{1... | collective-permute-start | bytes 1572872 | tf_op jit(solution)/shard_map/ppermute | solution.py:14
  41.0 1.5 %collective-permute-start.25 = (f32[512,256]{1,0:T(8,128)}, f32[512,256]{1,0:T(8,128)}, u32[]{:S(2)}, u32[]{:S(2)}) collective-permute-start(f32[512,256]{1,0:T(8,128)} %dynamic-slice_bitcast_fusion), channel_id=1, source_target_pairs={{0,2},{2,0},{1,3},{3,1},{4,6},{6,4},{5,7},{7,5},{8,10},{10,8},{9,1... | collective-permute-start | bytes 1572872 | tf_op jit(solution)/shard_map/ppermute | solution.py:14
  42.5 1.0 broadcast_select_fusion.1
  45.0 8.9 %collective-permute-done.19.refs_2_ = f32[512,256]{1,0:T(8,128)S(1)} collective-permute-done((f32[512,256]{1,0:T(8,128)}, f32[512,256]{1,0:T(8,128)S(1)}, u32[]{:S(2)}, u32[]{:S(2)}) %collective-permute-start.19) | collective-permute-done | bytes 524320 | tf_op jit(solution)/shard_map/ppermute | solution.py:14
  54.5 1.7 %collective-permute-start.15 = (f32[256,512]{1,0:T(8,128)S(1)}, f32[256,512]{1,0:T(8,128)S(1)}, u32[]{:S(2)}, u32[]{:S(2)}) collective-permute-start(f32[256,512]{1,0:T(8,128)S(1)} %collective-permute-done.13.refs_2_), channel_id=1, source_target_pairs={{0,4},{4,0},{8,12},{12,8},{1,5},{5,1},{9,13},{13,9},{2,6},{6,2},{1... | collective-permute-start | bytes 1572872 | tf_op jit(solution)/shard_map/ppermute | solution.py:14
  56.2 9.1 %collective-permute-done.25.refs_2_ = f32[512,256]{1,0:T(8,128)} collective-permute-done((f32[512,256]{1,0:T(8,128)}, f32[512,256]{1,0:T(8,128)}, u32[]{:S(2)}, u32[]{:S(2)}) %collective-permute-start.25) | collective-permute-done | bytes 524320 | tf_op jit(solution)/shard_map/ppermute | solution.py:14
  65.3 3.0 %collective-permute-done.7.refs_4_ = f32[256,256]{1,0:T(8,128)S(1)} collective-permute-done((f32[256,256]{1,0:T(8,128)S(1)}, f32[256,256]{1,0:T(8,128)S(1)}, u32[]{:S(2)}, u32[]{:S(2)}) %collective-permute-start.7) | collective-permute-done | bytes 262176 | tf_op jit(solution)/shard_map/ppermute | solution.py:14
  68.3 1.6 %collective-permute-start.9 = (f32[256,256]{1,0:T(8,128)S(1)}, f32[256,256]{1,0:T(8,128)S(1)}, u32[]{:S(2)}, u32[]{:S(2)}) collective-permute-start(f32[256,256]{1,0:T(8,128)S(1)} %collective-permute-done.7.refs_4_), channel_id=1, source_target_pairs={{0,4},{4,0},{8,12},{12,8},{1,5},{5,1},{9,13},{13,9},{2,6},{6,2},{1... | collective-permute-start | bytes 786440 | tf_op jit(solution)/shard_map/ppermute | solution.py:14
  72.5 2.1 %collective-permute-done.9.refs_6_ = f32[256,256]{1,0:T(8,128)S(1)} collective-permute-done((f32[256,256]{1,0:T(8,128)S(1)}, f32[256,256]{1,0:T(8,128)S(1)}, u32[]{:S(2)}, u32[]{:S(2)}) %collective-permute-start.9) | collective-permute-done | bytes 262176 | tf_op jit(solution)/shard_map/ppermute | solution.py:14
  75.4 1.0 collective-permute-start.21
  79.2 1.0 collective-permute-start.27
  81.8 8.6 %collective-permute-done.21.refs_4_ = f32[512,256]{1,0:T(8,128)S(1)} collective-permute-done((f32[512,256]{1,0:T(8,128)}, f32[512,256]{1,0:T(8,128)S(1)}, u32[]{:S(2)}, u32[]{:S(2)}) %collective-permute-start.21) | collective-permute-done | bytes 524320 | tf_op jit(solution)/shard_map/ppermute | solution.py:14
  94.1 7.2 %collective-permute-done.27.refs_4_ = f32[512,256]{1,0:T(8,128)} collective-permute-done((f32[512,256]{1,0:T(8,128)}, f32[512,256]{1,0:T(8,128)}, u32[]{:S(2)}, u32[]{:S(2)}) %collective-permute-start.27) | collective-permute-done | bytes 524320 | tf_op jit(solution)/shard_map/ppermute | solution.py:14
  103.3 1.0 collective-permute-start.1
  105.1 1.0 collective-permute-start.2
  107.1 1.1 copy-done.24
  108.2 0.9 copy-done.26
  109.1 0.9 copy-done.28
  110.1 0.9 copy-done.30
  111.0 0.9 copy-done.32
  112.0 0.9 copy-done.34
  114.8 1.9 %shard_map.114 = (bf16[4,1024,256]{2,1,0:T(8,128)(2,1)S(1)}, bf16[4,1024,256]{2,1,0:T(8,128)(2,1)S(1)}) custom-call(s32[2]{0:T(128)S(1)} %pad_add_fusion.place, f32[256,1024]{1,0:T(8,128)S(1)} %bitcast.29, f32[256,512]{1,0:T(8,128)} %collective-permute-done.11.refs_0_, f32[256,512]{1,0:T(8,128)S(1)} %copy-done.12, ...), custom_call_target="tpu_custom_call" | custom-call | tf_op jit(solution)/shard_map/pallas_call | solution.py:83
  116.9 1.8 %shard_map.115 = (bf16[4,1024,256]{2,1,0:T(8,128)(2,1)S(1)}, bf16[4,1024,256]{2,1,0:T(8,128)(2,1)S(1)}) custom-call(s32[2]{0:T(128)S(1)} %pad_add_fusion.place, f32[1024,256]{1,0:T(8,128)S(1)} %bitcast.30, f32[512,256]{1,0:T(8,128)} %collective-permute-done.17.refs_0_, f32[512,256]{1,0:T(8,128)S(1)} %copy-done.16, f32[512,256]{1,0:T(8,128)S(1)} %copy-done.6, ...), custom_call_target="tpu_custom_call" | custom-call | tf_op jit(solution)/shard_map/pallas_call | solution.py:83
  118.7 2.6 %shard_map.116 = (bf16[4,1024,256]{2,1,0:T(8,128)(2,1)S(1)}, bf16[4,1024,256]{2,1,0:T(8,128)(2,1)S(1)}) custom-call(s32[2]{0:T(128)S(1)} %pad_add_fusion.place, f32[1024,256]{1,0:T(8,128)S(1)} %bitcast.31, f32[512,256]{1,0:T(8,128)} %collective-permute-done.23.refs_0_, f32[512,256]{1,0:T(8,128)} %collective-permute-done.24.refs_1_, ...), custom_call_target="tpu_custom_call" | custom-call | tf_op jit(solution)/shard_map/pallas_call | solution.py:83
  121.3 1.3 copy-done.4
  122.6 26.4 %shard_map.117 = (f32[32,256]{1,0:T(8,128)}, f32[32,256]{1,0:T(8,128)}) custom-call(s32[2]{0:T(128)S(1)} %pad_add_fusion.place, f32[40,768]{1,0:T(8,128)} %pad_maximum_fusion.s0, f32[40,768]{1,0:T(8,128)} %collective-permute-done.s1, f32[40,768]{1,0:T(8,128)} %collective-permute-done.1.s2, f32[40,768]{1,0:T(8,128)} %collective-permute-done.2.s3, ...), custom_call_target="tpu_custom_call" | custom-call | tf_op jit(solution)/shard_map/pallas_call | solution.py:200
  (130 shorter events, 23.2 us)
Async XLA Ops:
  0.7 11.6 %copy-start.39 = (f32[1,1,32,256]{3,2,1,0:T(8,128)S(1)}, f32[1,1,32,256]{3,2,1,0:T(8,128)}, u32[]{:S(2)}) copy-start(f32[1,1,32,256]{3,2,1,0:T(8,128)} %param.10) | copy-start | bytes 98308
  0.7 12.7 %copy-start.3 = (f32[1,1,1024,256]{3,2,1,0:T(8,128)S(1)}, f32[1,1,1024,256]{3,2,1,0:T(8,128)}, u32[]{:S(2)}) copy-start(f32[1,1,1024,256]{3,2,1,0:T(8,128)} %param.16) | copy-start | bytes 3145732
  2.7 38.2 %collective-permute-start.13 = (f32[256,512]{1,0:T(8,128)}, f32[256,512]{1,0:T(8,128)S(1)}, u32[]{:S(2)}, u32[]{:S(2)}) collective-permute-start(f32[256,512]{1,0:T(8,128)} %dynamic-slice_bitcast_fusion.2), channel_id=1, source_target_pairs={{0,2},{2,0},{1,3},{3,1},{4,6},{6,4},{5,7},{7,5},{8,10},{10,8},{9,1... | collective-permute-start | bytes 1572872 | tf_op jit(solution)/shard_map/ppermute | solution.py:14
  5.7 38.4 %collective-permute-start.11 = (f32[256,512]{1,0:T(8,128)}, f32[256,512]{1,0:T(8,128)}, u32[]{:S(2)}, u32[]{:S(2)}) collective-permute-start(f32[256,512]{1,0:T(8,128)} %dynamic-slice_bitcast_fusion.2), channel_id=1, source_target_pairs={{0,4},{4,0},{8,12},{12,8},{1,5},{5,1},{9,13},{13,9},{2,6},{6,2},{1... | collective-permute-start | bytes 1572872 | tf_op jit(solution)/shard_map/ppermute | solution.py:14
  9.1 35.6 %collective-permute-start.17 = (f32[512,256]{1,0:T(8,128)}, f32[512,256]{1,0:T(8,128)}, u32[]{:S(2)}, u32[]{:S(2)}) collective-permute-start(f32[512,256]{1,0:T(8,128)} %dynamic-slice_bitcast_fusion.1), channel_id=1, source_target_pairs={{0,4},{4,0},{8,12},{12,8},{1,5},{5,1},{9,13},{13,9},{2,6},{6,2},{1... | collective-permute-start | bytes 1572872 | tf_op jit(solution)/shard_map/ppermute | solution.py:14
  10.3 29.0 %collective-permute-start.3 = (f32[128,512]{1,0:T(8,128)}, f32[128,512]{1,0:T(8,128)S(1)}, u32[]{:S(2)}, u32[]{:S(2)}) collective-permute-start(f32[128,512]{1,0:T(8,128)} %dynamic-slice_bitcast_fusion.3), channel_id=1, source_target_pairs={{0,4},{4,0},{8,12},{12,8},{1,5},{5,1},{9,13},{13,9},{2,6},{6,2},{1... | collective-permute-start | bytes 786440 | tf_op jit(solution)/shard_map/ppermute | solution.py:14
  13.0 25.9 %collective-permute-start = (f32[40,768]{1,0:T(8,128)}, f32[40,768]{1,0:T(8,128)}, u32[]{:S(2)}, u32[]{:S(2)}) collective-permute-start(f32[40,768]{1,0:T(8,128)} %pad_maximum_fusion.s0), channel_id=1, source_target_pairs={{0,4},{4,0},{8,12},{12,8},{1,5},{5,1},{9,13},{13,9},{2,6},{6,2},{1... | collective-permute-start | bytes 368648 | tf_op jit(solution)/shard_map/ppermute | solution.py:14
  14.3 100.4 %copy-start.1 = (f32[1,1,256,1024]{3,2,1,0:T(8,128)S(1)}, f32[1,1,256,1024]{3,2,1,0:T(8,128)}, u32[]{:S(2)}) copy-start(f32[1,1,256,1024]{3,2,1,0:T(8,128)} %param.14) | copy-start | bytes 3145732
  38.9 15.1 %collective-permute-start.19 = (f32[512,256]{1,0:T(8,128)}, f32[512,256]{1,0:T(8,128)S(1)}, u32[]{:S(2)}, u32[]{:S(2)}) collective-permute-start(f32[512,256]{1,0:T(8,128)} %dynamic-slice_bitcast_fusion.1), channel_id=1, source_target_pairs={{0,2},{2,0},{1,3},{3,1},{4,6},{6,4},{5,7},{7,5},{8,10},{10,8},{9,1... | collective-permute-start | bytes 1572872 | tf_op jit(solution)/shard_map/ppermute | solution.py:14
  39.3 15.2 %collective-permute-start.23 = (f32[512,256]{1,0:T(8,128)}, f32[512,256]{1,0:T(8,128)}, u32[]{:S(2)}, u32[]{:S(2)}) collective-permute-start(f32[512,256]{1,0:T(8,128)} %dynamic-slice_bitcast_fusion), channel_id=1, source_target_pairs={{0,4},{4,0},{8,12},{12,8},{1,5},{5,1},{9,13},{13,9},{2,6},{6,2},{1... | collective-permute-start | bytes 1572872 | tf_op jit(solution)/shard_map/ppermute | solution.py:14
  41.0 24.3 %collective-permute-start.25 = (f32[512,256]{1,0:T(8,128)}, f32[512,256]{1,0:T(8,128)}, u32[]{:S(2)}, u32[]{:S(2)}) collective-permute-start(f32[512,256]{1,0:T(8,128)} %dynamic-slice_bitcast_fusion), channel_id=1, source_target_pairs={{0,2},{2,0},{1,3},{3,1},{4,6},{6,4},{5,7},{7,5},{8,10},{10,8},{9,1... | collective-permute-start | bytes 1572872 | tf_op jit(solution)/shard_map/ppermute | solution.py:14
  44.1 24.2 %collective-permute-start.7 = (f32[256,256]{1,0:T(8,128)S(1)}, f32[256,256]{1,0:T(8,128)S(1)}, u32[]{:S(2)}, u32[]{:S(2)}) collective-permute-start(f32[256,256]{1,0:T(8,128)S(1)} %fusion.refs_0_), channel_id=1, source_target_pairs={{0,2},{2,0},{1,3},{3,1},{4,6},{6,4},{5,7},{7,5},{8,10},{10,8},{9,1... | collective-permute-start | bytes 786440 | tf_op jit(solution)/shard_map/ppermute | solution.py:14
  44.7 25.2 %collective-permute-start.5 = (f32[256,256]{1,0:T(8,128)S(1)}, f32[256,256]{1,0:T(8,128)S(1)}, u32[]{:S(2)}, u32[]{:S(2)}) collective-permute-start(f32[256,256]{1,0:T(8,128)S(1)} %fusion.refs_0_), channel_id=1, source_target_pairs={{0,4},{4,0},{8,12},{12,8},{1,5},{5,1},{9,13},{13,9},{2,6},{6,2},{1... | collective-permute-start | bytes 786440 | tf_op jit(solution)/shard_map/ppermute | solution.py:14
  53.9 16.7 %collective-permute-start.4 = (f32[256,256]{1,0:T(8,128)S(1)}, f32[256,256]{1,0:T(8,128)S(1)}, u32[]{:S(2)}, u32[]{:S(2)}) collective-permute-start(f32[256,256]{1,0:T(8,128)S(1)} %fusion.refs_0_), channel_id=1, source_target_pairs={{0,1},{1,0},{2,3},{3,2},{4,5},{5,4},{6,7},{7,6},{8,9},{9,8},{10,11... | collective-permute-start | bytes 786440 | tf_op jit(solution)/shard_map/ppermute | solution.py:14
  54.5 22.9 %collective-permute-start.15 = (f32[256,512]{1,0:T(8,128)S(1)}, f32[256,512]{1,0:T(8,128)S(1)}, u32[]{:S(2)}, u32[]{:S(2)}) collective-permute-start(f32[256,512]{1,0:T(8,128)S(1)} %collective-permute-done.13.refs_2_), channel_id=1, source_target_pairs={{0,4},{4,0},{8,12},{12,8},{1,5},{5,1},{9,13},{13,9},{2,6},{6,2},{1... | collective-permute-start | bytes 1572872 | tf_op jit(solution)/shard_map/ppermute | solution.py:14
  65.3 13.1 %collective-permute-start.14 = (f32[256,512]{1,0:T(8,128)S(1)}, f32[256,512]{1,0:T(8,128)S(1)}, u32[]{:S(2)}, u32[]{:S(2)}) collective-permute-start(f32[256,512]{1,0:T(8,128)S(1)} %collective-permute-done.13.refs_2_), channel_id=1, source_target_pairs={{0,1},{1,0},{2,3},{3,2},{4,5},{5,4},{6,7},{7,6},{8,9},{9,8},{10,11... | collective-permute-start | bytes 1572872 | tf_op jit(solution)/shard_map/ppermute | solution.py:14
  68.3 6.4 %collective-permute-start.9 = (f32[256,256]{1,0:T(8,128)S(1)}, f32[256,256]{1,0:T(8,128)S(1)}, u32[]{:S(2)}, u32[]{:S(2)}) collective-permute-start(f32[256,256]{1,0:T(8,128)S(1)} %collective-permute-done.7.refs_4_), channel_id=1, source_target_pairs={{0,4},{4,0},{8,12},{12,8},{1,5},{5,1},{9,13},{13,9},{2,6},{6,2},{1... | collective-permute-start | bytes 786440 | tf_op jit(solution)/shard_map/ppermute | solution.py:14
  69.9 4.8 %collective-permute-start.6 = (f32[256,256]{1,0:T(8,128)S(1)}, f32[256,256]{1,0:T(8,128)S(1)}, u32[]{:S(2)}, u32[]{:S(2)}) collective-permute-start(f32[256,256]{1,0:T(8,128)S(1)} %collective-permute-done.5.refs_2_), channel_id=1, source_target_pairs={{0,1},{1,0},{2,3},{3,2},{4,5},{5,4},{6,7},{7,6},{8,9},{9,8},{10,11... | collective-permute-start | bytes 786440 | tf_op jit(solution)/shard_map/ppermute | solution.py:14
  71.3 5.1 %collective-permute-start.8 = (f32[256,256]{1,0:T(8,128)S(1)}, f32[256,256]{1,0:T(8,128)S(1)}, u32[]{:S(2)}, u32[]{:S(2)}) collective-permute-start(f32[256,256]{1,0:T(8,128)S(1)} %collective-permute-done.7.refs_4_), channel_id=1, source_target_pairs={{0,1},{1,0},{2,3},{3,2},{4,5},{5,4},{6,7},{7,6},{8,9},{9,8},{10,11... | collective-permute-start | bytes 786440 | tf_op jit(solution)/shard_map/ppermute | solution.py:14
  74.7 5.6 %collective-permute-start.12 = (f32[256,512]{1,0:T(8,128)}, f32[256,512]{1,0:T(8,128)S(1)}, u32[]{:S(2)}, u32[]{:S(2)}) collective-permute-start(f32[256,512]{1,0:T(8,128)} %collective-permute-done.11.refs_0_), channel_id=1, source_target_pairs={{0,1},{1,0},{2,3},{3,2},{4,5},{5,4},{6,7},{7,6},{8,9},{9,8},{10,11... | collective-permute-start | bytes 1572872 | tf_op jit(solution)/shard_map/ppermute | solution.py:14
  75.4 14.9 %collective-permute-start.21 = (f32[512,256]{1,0:T(8,128)}, f32[512,256]{1,0:T(8,128)S(1)}, u32[]{:S(2)}, u32[]{:S(2)}) collective-permute-start(f32[512,256]{1,0:T(8,128)} %collective-permute-done.17.refs_0_), channel_id=1, source_target_pairs={{0,2},{2,0},{1,3},{3,1},{4,6},{6,4},{5,7},{7,5},{8,10},{10,8},{9,1... | collective-permute-start | bytes 1572872 | tf_op jit(solution)/shard_map/ppermute | solution.py:14
  77.1 14.0 %collective-permute-start.18 = (f32[512,256]{1,0:T(8,128)}, f32[512,256]{1,0:T(8,128)S(1)}, u32[]{:S(2)}, u32[]{:S(2)}) collective-permute-start(f32[512,256]{1,0:T(8,128)} %collective-permute-done.17.refs_0_), channel_id=1, source_target_pairs={{0,1},{1,0},{2,3},{3,2},{4,5},{5,4},{6,7},{7,6},{8,9},{9,8},{10,11... | collective-permute-start | bytes 1572872 | tf_op jit(solution)/shard_map/ppermute | solution.py:14
  77.3 16.0 %collective-permute-start.20 = (f32[512,256]{1,0:T(8,128)S(1)}, f32[512,256]{1,0:T(8,128)S(1)}, u32[]{:S(2)}, u32[]{:S(2)}) collective-permute-start(f32[512,256]{1,0:T(8,128)S(1)} %collective-permute-done.19.refs_2_), channel_id=1, source_target_pairs={{0,1},{1,0},{2,3},{3,2},{4,5},{5,4},{6,7},{7,6},{8,9},{9,8},{10,11... | collective-permute-start | bytes 1572872 | tf_op jit(solution)/shard_map/ppermute | solution.py:14
  79.2 22.1 %collective-permute-start.27 = (f32[512,256]{1,0:T(8,128)}, f32[512,256]{1,0:T(8,128)}, u32[]{:S(2)}, u32[]{:S(2)}) collective-permute-start(f32[512,256]{1,0:T(8,128)} %collective-permute-done.23.refs_0_), channel_id=1, source_target_pairs={{0,2},{2,0},{1,3},{3,1},{4,6},{6,4},{5,7},{7,5},{8,10},{10,8},{9,1... | collective-permute-start | bytes 1572872 | tf_op jit(solution)/shard_map/ppermute | solution.py:14
  81.1 20.2 %collective-permute-start.10 = (f32[256,256]{1,0:T(8,128)S(1)}, f32[256,256]{1,0:T(8,128)S(1)}, u32[]{:S(2)}, u32[]{:S(2)}) collective-permute-start(f32[256,256]{1,0:T(8,128)S(1)} %collective-permute-done.9.refs_6_), channel_id=1, source_target_pairs={{0,1},{1,0},{2,3},{3,2},{4,5},{5,4},{6,7},{7,6},{8,9},{9,8},{10,11... | collective-permute-start | bytes 786440 | tf_op jit(solution)/shard_map/ppermute | solution.py:14
  90.3 12.2 %collective-permute-start.16 = (f32[256,512]{1,0:T(8,128)S(1)}, f32[256,512]{1,0:T(8,128)S(1)}, u32[]{:S(2)}, u32[]{:S(2)}) collective-permute-start(f32[256,512]{1,0:T(8,128)S(1)} %collective-permute-done.15.refs_4_), channel_id=1, source_target_pairs={{0,1},{1,0},{2,3},{3,2},{4,5},{5,4},{6,7},{7,6},{8,9},{9,8},{10,11... | collective-permute-start | bytes 1572872 | tf_op jit(solution)/shard_map/ppermute | solution.py:14
  92.0 12.4 %collective-permute-start.22 = (f32[512,256]{1,0:T(8,128)S(1)}, f32[512,256]{1,0:T(8,128)S(1)}, u32[]{:S(2)}, u32[]{:S(2)}) collective-permute-start(f32[512,256]{1,0:T(8,128)S(1)} %collective-permute-done.21.refs_4_), channel_id=1, source_target_pairs={{0,1},{1,0},{2,3},{3,2},{4,5},{5,4},{6,7},{7,6},{8,9},{9,8},{10,11... | collective-permute-start | bytes 1572872 | tf_op jit(solution)/shard_map/ppermute | solution.py:14
  94.1 24.6 %collective-permute-start.24 = (f32[512,256]{1,0:T(8,128)}, f32[512,256]{1,0:T(8,128)}, u32[]{:S(2)}, u32[]{:S(2)}) collective-permute-start(f32[512,256]{1,0:T(8,128)} %collective-permute-done.23.refs_0_), channel_id=1, source_target_pairs={{0,1},{1,0},{2,3},{3,2},{4,5},{5,4},{6,7},{7,6},{8,9},{9,8},{10,11... | collective-permute-start | bytes 1572872 | tf_op jit(solution)/shard_map/ppermute | solution.py:14
  101.3 17.4 %collective-permute-start.26 = (f32[512,256]{1,0:T(8,128)}, f32[512,256]{1,0:T(8,128)}, u32[]{:S(2)}, u32[]{:S(2)}) collective-permute-start(f32[512,256]{1,0:T(8,128)} %collective-permute-done.25.refs_2_), channel_id=1, source_target_pairs={{0,1},{1,0},{2,3},{3,2},{4,5},{5,4},{6,7},{7,6},{8,9},{9,8},{10,11... | collective-permute-start | bytes 1572872 | tf_op jit(solution)/shard_map/ppermute | solution.py:14
  102.0 16.7 %collective-permute-start.28 = (f32[512,256]{1,0:T(8,128)}, f32[512,256]{1,0:T(8,128)}, u32[]{:S(2)}, u32[]{:S(2)}) collective-permute-start(f32[512,256]{1,0:T(8,128)} %collective-permute-done.27.refs_4_), channel_id=1, source_target_pairs={{0,1},{1,0},{2,3},{3,2},{4,5},{5,4},{6,7},{7,6},{8,9},{9,8},{10,11... | collective-permute-start | bytes 1572872 | tf_op jit(solution)/shard_map/ppermute | solution.py:14
  103.3 19.3 %collective-permute-start.1 = (f32[40,768]{1,0:T(8,128)}, f32[40,768]{1,0:T(8,128)}, u32[]{:S(2)}, u32[]{:S(2)}) collective-permute-start(f32[40,768]{1,0:T(8,128)} %pad_maximum_fusion.s0), channel_id=1, source_target_pairs={{0,2},{2,0},{1,3},{3,1},{4,6},{6,4},{5,7},{7,5},{8,10},{10,8},{9,1... | collective-permute-start | bytes 368648 | tf_op jit(solution)/shard_map/ppermute | solution.py:14
  105.1 17.4 %collective-permute-start.2 = (f32[40,768]{1,0:T(8,128)}, f32[40,768]{1,0:T(8,128)}, u32[]{:S(2)}, u32[]{:S(2)}) collective-permute-start(f32[40,768]{1,0:T(8,128)} %collective-permute-done.s1), channel_id=1, source_target_pairs={{0,2},{2,0},{1,3},{3,1},{4,6},{6,4},{5,7},{7,5},{8,10},{10,8},{9,1... | collective-permute-start | bytes 368648 | tf_op jit(solution)/shard_map/ppermute | solution.py:14
  (39 other events, 117.7 us)

commit v2 on v1

v2 whole, which is shorter than its diff:
```python
import jax
import jax.numpy as jnp
from jax import lax
from jax.experimental import pallas as pl
from jax.experimental.pallas import tpu as pltpu
from jax.sharding import PartitionSpec as P

F32 = jnp.float32
BF16 = jnp.bfloat16


def from_partner(value, axis):
    pairs = [(source, source ^ 1) for source in range(lax.axis_size(axis))]
    return lax.ppermute(value, axis, pairs)


def after(value, *earlier):
    return lax.optimization_barrier((value,) + earlier)[0]


def exact_dot(left, right):
    return jnp.dot(left, right, precision=lax.Precision.HIGHEST, preferred_element_type=F32)


def halves_of(value):
    high = value.astype(BF16)
    return high, (value - high.astype(F32)).astype(BF16)


def store_split(high_ref, low_ref, where, value):
    high, low = halves_of(value)
    high_ref[where] = high
    low_ref[where] = low


def start_copies(sources, targets, sems):
    copies = [pltpu.make_async_copy(source, target, sems.at[i]) for i, (source, target) in enumerate(zip(sources, targets))]
    for copy in copies:
        copy.start()
    return copies


def split_tall_half(place, part, piece, high_ref, low_ref, lead):
    width = piece.shape[1]
    for block in range(2):
        target = (2 * (place[1] ^ part) + block) ^ place[0]
        rows = pl.ds(pl.multiple_of(target * width, width), width)
        store_split(high_ref, low_ref, lead + (rows, slice(None)), piece[block * width:(block + 1) * width, :])


def tall_kernel(place, own, *refs):
    pieces, (high_ref, low_ref, whole, halves, sems) = refs[:4], refs[4:]
    copies = start_copies((own,) + pieces, [whole] + [halves.at[i] for i in range(4)], sems)
    width = whole.shape[1]
    copies[0].wait()
    for block in range(4):
        rows = pl.ds(pl.multiple_of((block ^ place[0]) * width, width), width)
        store_split(high_ref, low_ref, (0, rows, slice(None)), whole[block * width:(block + 1) * width, :])
    for index in range(4):
        copies[1 + index].wait()
        split_tall_half(place, index % 2, halves.at[index], high_ref, low_ref, (1 + index // 2,))


def wide_kernel(place, own, *refs):
    pieces, (high_ref, low_ref, whole, halves, sems) = refs[:6], refs[6:]
    copies = start_copies((own,) + pieces, [whole] + [halves.at[i] for i in range(6)], sems)
    width = whole.shape[0]
    copies[0].wait()
    for block in range(4):
        store_split(
            high_ref, low_ref, (block ^ place[0], slice(0, width), slice(None)), whole[:, block * width:(block + 1) * width]
        )
    for index in range(6):
        copies[1 + index].wait()
        tile, part = 1 + index // 2, index % 2
        for block in range(2):
            store_split(
                high_ref,
                low_ref,
                ((2 * (place[1] ^ part) + block) ^ place[0], slice(tile * width, (tile + 1) * width), slice(None)),
                halves[index, :, block * width:(block + 1) * width],
            )


def edge_kernel(place, *refs):
    pieces, (high_ref, low_ref, halves, sems) = refs[:8], refs[8:]
    copies = start_copies(pieces, [halves.at[i] for i in range(8)], sems)
    rows = halves.shape[1] // 2
    for index in range(8):
        copies[index].wait()
        for bit in range(2):
            start = (bit ^ (place[0] % 2)) * 2 * rows + (place[1] ^ (index % 2)) * rows
            store_split(
                high_ref,
                low_ref,
                (index // 2, pl.ds(pl.multiple_of(start, rows), rows), slice(None)),
                halves[index, bit * rows:(bit + 1) * rows, :],
            )


def split_call(kernel, place, shape, arrays, scratch):
    out = jax.ShapeDtypeStruct(shape, BF16)
    vmem = pl.BlockSpec(memory_space=pltpu.VMEM)
    return pl.pallas_call(
        kernel,
        in_specs=[pl.BlockSpec(memory_space=pltpu.SMEM)] + [pl.BlockSpec(memory_space=pltpu.HBM)] * len(arrays),
        out_specs=(vmem, vmem),
        out_shape=(out, out),
        scratch_shapes=[pltpu.VMEM(size, F32) for size in scratch] + [pltpu.SemaphoreType.DMA((len(arrays),))],
        compiler_params=pltpu.CompilerParams(vmem_limit_bytes=14 * 2**20),
    )(place, *arrays)


def product(left, high, low):
    rows = left.shape[0]
    left_high, left_low = halves_of(left)
    both = jnp.dot(jnp.concatenate([left_high, left_low], axis=0), high, preferred_element_type=F32)
    rest = jnp.dot(left_high, low, preferred_element_type=F32)
    return both[:rows] + both[rows:] + rest


def march_kernel(place, s0, s1, s2, s3, weight, eh, el, lh, ll, rh, rl, bh, bl, r_mine, r_other, b_mine, b_other, *refs):
    one_ref, two_ref, last_rh, last_rl, last_bh, last_bl, halves, sems = refs
    rows, width = one_ref.shape
    copies = start_copies((r_mine, r_other, b_mine, b_other), [halves.at[i] for i in range(4)], sems)
    states = (s0, s1, s2, s3)
    one = jnp.concatenate([state[:rows, :width] for state in states], axis=1)
    two = jnp.concatenate([state[:rows, width:2 * width] for state in states], axis=1)
    picked = jnp.concatenate([state[:rows, 2 * width:] for state in states], axis=1)
    scale = jnp.concatenate([state[rows:rows + 1, :width] for state in states], axis=1)
    for index in range(4):
        copies[index].wait()
        high_ref, low_ref = ((last_rh, last_rl), (last_bh, last_bl))[index // 2]
        split_tall_half(place, index % 2, halves.at[index], high_ref, low_ref, ())

    def tall(left, high, low, last_high, last_low):
        blocks = [product(left, high[tile], low[tile]) for tile in range(3)]
        return jnp.concatenate(blocks + [product(left, last_high[...], last_low[...])], axis=1)

    def advance(step, carry):
        one, two = carry
        half = jnp.concatenate(
            [product(one[:, (tile // 2) * 2 * width:(tile // 2 + 1) * 2 * width], eh[tile], el[tile]) for tile in range(4)],
            axis=1,
        )
        half = half + weight[step] * picked
        sums = jnp.concatenate([product(half, lh[block], ll[block]) for block in range(4)], axis=1) + two * scale
        two = tall(sums, rh, rl, last_rh, last_rl)
        return half - tall(two, bh, bl, last_bh, last_bl), two

    one, two = lax.fori_loop(0, weight.shape[0], advance, (one, two))
    one_ref[...] = one[:, :width]
    two_ref[...] = two[:, :width]


def shards(
    adjoint_one_start,
    adjoint_two_start,
    couple_panel,
    pair_panel,
    lift_panel,
    root_panel,
    back_panel,
    mass_two,
    probe_cells,
    probe_weight,
):
    couple = couple_panel[0, 0]
    pair_cols = pair_panel[0, 0]
    lift = lift_panel[0, 0]
    root = root_panel[0, 0]
    back = back_panel[0, 0]
    mass = mass_two[0, 0]
    width = couple.shape[0]
    rows = probe_cells.shape[0]
    column, row, core = lax.axis_index("gx"), lax.axis_index("gy"), lax.axis_index("gz")
    x_bit, y_bit = column % 2, row % 2
    place = jnp.stack([2 * y_bit + x_bit, core]).astype(jnp.int32)

    def half_rows(panel):
        size = panel.shape[0] // 2
        return lax.dynamic_slice_in_dim(panel, core * size, size, 0)

    owners = (column - x_bit + jnp.arange(2)) * lax.axis_size("gy") + row
    targets = (owners[:, None] * width + jnp.arange(width)[None, :]).reshape(-1)
    chosen = (probe_cells[:, None] == targets[None, :]).astype(F32)
    picked = exact_dot(chosen, pair_cols)
    state = jnp.concatenate([adjoint_one_start[0, 0], adjoint_two_start[0, 0], picked], axis=1)
    state = jnp.concatenate([state, jnp.broadcast_to(jnp.pad(mass, (0, 2 * width)), (8, 3 * width))], axis=0)
    lift_half = lax.dynamic_slice_in_dim(lift, core * 2 * width, 2 * width, 1)
    root_half = half_rows(root)
    back_half = half_rows(back)

    couple_mine = half_rows(couple)
    couple_other = from_partner(couple_mine, "gx")
    state_x = from_partner(state, "gx")
    state_y = from_partner(state, "gy")
    lift_y = from_partner(lift_half, "gy")

    first = jnp.where(x_bit == 0, couple_mine, couple_other)
    second = jnp.where(x_bit == 0, couple_other, couple_mine)
    edge_half = exact_dot(jnp.concatenate([first, second], axis=0), pair_cols)

    lift_x = from_partner(after(lift_half, couple_other), "gx")
    back_y = from_partner(after(back_half, state_y), "gy")
    root_x = from_partner(after(root_half, state_x), "gx")
    edge_y = from_partner(after(edge_half, lift_y), "gy")
    back_x = from_partner(after(back_half, lift_x), "gx")
    root_y = from_partner(after(root_half, back_y), "gy")
    edge_x = from_partner(after(edge_half, root_x), "gx")
    state_d = from_partner(after(state_x, edge_y), "gy")
    lift_d = from_partner(after(lift_x, root_y), "gy")
    edge_d = from_partner(after(edge_y, back_x), "gx")
    back_d = from_partner(after(back_y, edge_x), "gx")
    root_d = from_partner(after(root_x, state_d), "gy")

    def both(*values):
        arrays = []
        for value in values:
            arrays += [value, from_partner(value, "gz")]
        return arrays

    tall_scratch = [(4 * width, width), (4, 2 * width, width)]
    back_high, back_low = split_call(tall_kernel, place, (3, 4 * width, width), [back] + both(back_x, back_y), tall_scratch)
    root_high, root_low = split_call(tall_kernel, place, (3, 4 * width, width), [root] + both(root_x, root_y), tall_scratch)
    edge_high, edge_low = split_call(
        edge_kernel, place, (4, 2 * width, width), both(edge_half, edge_x, edge_y, edge_d), [(8, width, width)]
    )
    lift_high, lift_low = split_call(
        wide_kernel, place, (4, 4 * width, width), [lift] + both(lift_x, lift_y, lift_d), [(width, 4 * width), (6, width, 2 * width)]
    )

    vmem = pl.BlockSpec(memory_space=pltpu.VMEM)
    one, two = pl.pallas_call(
        march_kernel,
        in_specs=[pl.BlockSpec(memory_space=pltpu.SMEM)] + [vmem] * 13 + [pl.BlockSpec(memory_space=pltpu.HBM)] * 4,
        out_specs=(vmem, vmem),
        out_shape=(jax.ShapeDtypeStruct((rows, width), F32),) * 2,
        scratch_shapes=[pltpu.VMEM((4 * width, width), BF16)] * 4
        + [pltpu.VMEM((4, 2 * width, width), F32), pltpu.SemaphoreType.DMA((4,))],
        compiler_params=pltpu.CompilerParams(vmem_limit_bytes=14 * 2**20),
    )(
        place,
        state,
        state_x,
        state_y,
        state_d,
        probe_weight[:, :, None],
        edge_high,
        edge_low,
        lift_high,
        lift_low,
        root_high,
        root_low,
        back_high,
        back_low,
        *both(root_d, back_d),
    )
    return (one[None, None], two[None, None])


def solution(mesh):
    placed = (
        P(("groups", "gx"), "gy", "gz", None),
        P(("groups", "gx"), "gy", "gz", None),
        P(("groups", "gx"), "gy", None, None),
        P(("groups", "gx"), "gy", None, None),
        P(("groups", "gx"), "gy", None, None),
        P(("groups", "gx"), "gy", None, None),
        P(("groups", "gx"), "gy", None, None),
        P(("groups", "gx"), "gy", None),
        P(("groups", "gz")),
        P("groups", "gz"),
    )
    return jax.shard_map(
        shards,
        mesh=mesh,
        in_specs=placed,
        out_specs=(P(("groups", "gx"), "gy", "gz", None), P(("groups", "gx"), "gy", "gz", None)),
        check_vma=False,
    )
```

time: 150 us -> 128 us (0.85)
  waiting for transfers between devices: 64.1 us -> 44.7 us
  local copies, waits for them, and re-layouts: 26.8 us -> 23.9 us
    ppermute x29, waiting for transfers between devices: 64.1 us -> 44.7 us  [from_partner(): return lax.ppermute(value, axis, pairs)]
    unnamed x85 -> x89, local copies, waits for them, and re-layouts: 20.6 us -> 17.1 us
  transfers between devices with their start and end apart: 29 -> 29, of which waited for: 8 -> 10; matrix products, arithmetic and copies ran while one was open for 5% -> 6% of each run, Pallas kernels for 5% -> 5%
where the time goes in v2:
time: 128 us
  waiting for transfers between devices  44.7 us (35%)
  Pallas kernels  32.8 us (26%)
  local copies, waits for them, and re-layouts  23.9 us (19%)
  starting transfers between devices  21.5 us (17%)
  other arithmetic  2.09 us (2%)
  matrix products  1.56 us (1%)
    ppermute x29, waiting for transfers between devices, from_partner(): return lax.ppermute(value, axis, pairs)  44.7 us
    pallas_call x1, Pallas kernels, shards(): pl.pallas_call(march_kernel, in_specs=[pl.BlockSpec(memory_space=pltpu.SM...  26.7 us
    ppermute x29, starting transfers between devices, from_partner(): return lax.ppermute(value, axis, pairs)  21.5 us
    unnamed x89, local copies, waits for them, and re-layouts  17.1 us
    pallas_call x4, Pallas kernels, split_call(): pl.pallas_call(kernel, in_specs=[pl.BlockSpec(memory_space=pltpu.SMEM)] +...  6.09 us
    dynamic_slice x3, local copies, waits for them, and re-layouts, half_rows(): return lax.dynamic_slice_in_dim(panel, core * size, size, 0)  4.39 us
  transfers between devices with their start and end apart: 29, of which 10 were waited for; matrix products, arithmetic and copies ran while one was open for 6% of the time, Pallas kernels for 5%

profile of v2, /device:TPU:0, one launch (start us, length us, event | category | flops | bytes accessed | tf_op | source)
XLA Modules:
  0.0 127.6 jit_solution(6783582458882582399)
XLA Ops:
  1.7 1.0 fusion.5
  2.7 0.9 pad_maximum_fusion.s0
  3.6 3.0 %collective-permute-start.1 = (f32[40,768]{1,0:T(8,128)S(1)}, f32[40,768]{1,0:T(8,128)S(1)}, u32[]{:S(2)}, u32[]{:S(2)}) collective-permute-start(f32[40,768]{1,0:T(8,128)S(1)} %pad_maximum_fusion.s0), channel_id=1, source_target_pairs={{0,2},{2,0},{1,3},{3,1},{4,6},{6,4},{5,7},{7,5},{8,10},{10,8},{9,1... | collective-permute-start | bytes 368648 | tf_op jit(solution)/shard_map/ppermute | solution.py:14
  6.6 1.6 %collective-permute-start = (f32[40,768]{1,0:T(8,128)S(1)}, f32[40,768]{1,0:T(8,128)S(1)}, u32[]{:S(2)}, u32[]{:S(2)}) collective-permute-start(f32[40,768]{1,0:T(8,128)S(1)} %pad_maximum_fusion.s0), channel_id=1, source_target_pairs={{0,4},{4,0},{8,12},{12,8},{1,5},{5,1},{9,13},{13,9},{2,6},{6,2},{1... | collective-permute-start | bytes 368648 | tf_op jit(solution)/shard_map/ppermute | solution.py:14
  8.1 1.7 %dynamic-slice_bitcast_fusion.3 = f32[128,512]{1,0:T(8,128)} fusion(f32[1,1,256,512]{3,2,1,0:T(8,128)} %param.12, s32[]{:T(128)S(6)} %select_n.34), kind=kLoop, calls=%fused_computation.10 | loop fusion | bytes 524292 | tf_op jit(solution)/shard_map/dynamic_slice | solution.py:182
  10.3 0.9 dynamic-slice_bitcast_fusion.2
  11.2 1.9 %dynamic-slice_bitcast_fusion = f32[512,256]{1,0:T(8,128)} fusion(f32[1,1,1024,256]{3,2,1,0:T(8,128)} %param.16, s32[]{:T(128)S(6)} %select_n.37), kind=kLoop, calls=%fused_computation.7 | loop fusion | bytes 1048580 | tf_op jit(solution)/shard_map/dynamic_slice | solution.py:182
  14.0 2.0 %collective-permute-start.17 = (f32[512,256]{1,0:T(8,128)}, f32[512,256]{1,0:T(8,128)S(1)}, u32[]{:S(2)}, u32[]{:S(2)}) collective-permute-start(f32[512,256]{1,0:T(8,128)} %dynamic-slice_bitcast_fusion), channel_id=1, source_target_pairs={{0,2},{2,0},{1,3},{3,1},{4,6},{6,4},{5,7},{7,5},{8,10},{10,8},{9,1... | collective-permute-start | bytes 1572872 | tf_op jit(solution)/shard_map/ppermute | solution.py:14
  16.0 1.6 %collective-permute-start.7 = (f32[512,256]{1,0:T(8,128)}, f32[512,256]{1,0:T(8,128)S(1)}, u32[]{:S(2)}, u32[]{:S(2)}) collective-permute-start(f32[512,256]{1,0:T(8,128)} %dynamic-slice_bitcast_fusion.1), channel_id=1, source_target_pairs={{0,4},{4,0},{8,12},{12,8},{1,5},{5,1},{9,13},{13,9},{2,6},{6,2},{1... | collective-permute-start | bytes 1572872 | tf_op jit(solution)/shard_map/ppermute | solution.py:14
  17.8 0.9 collective-permute-start.11
  18.7 1.1 broadcast_select_fusion.1
  20.4 5.8 %collective-permute-done.3.refs_2_ = f32[256,512]{1,0:T(8,128)S(1)} collective-permute-done((f32[256,512]{1,0:T(8,128)}, f32[256,512]{1,0:T(8,128)S(1)}, u32[]{:S(2)}, u32[]{:S(2)}) %collective-permute-start.3) | collective-permute-done | bytes 524320 | tf_op jit(solution)/shard_map/ppermute | solution.py:14
  26.3 11.1 %collective-permute-done.17.refs_2_ = f32[512,256]{1,0:T(8,128)S(1)} collective-permute-done((f32[512,256]{1,0:T(8,128)}, f32[512,256]{1,0:T(8,128)S(1)}, u32[]{:S(2)}, u32[]{:S(2)}) %collective-permute-start.17) | collective-permute-done | bytes 524320 | tf_op jit(solution)/shard_map/ppermute | solution.py:14
  37.6 2.0 %collective-permute-start.8 = (f32[256,256]{1,0:T(8,128)S(1)}, f32[256,256]{1,0:T(8,128)S(1)}, u32[]{:S(2)}, u32[]{:S(2)}) collective-permute-start(f32[256,256]{1,0:T(8,128)S(1)} %fusion.refs_0_), channel_id=1, source_target_pairs={{0,4},{4,0},{8,12},{12,8},{1,5},{5,1},{9,13},{13,9},{2,6},{6,2},{1... | collective-permute-start | bytes 786440 | tf_op jit(solution)/shard_map/ppermute | solution.py:14
  39.6 2.8 %collective-permute-done.11.refs_0_ = f32[256,512]{1,0:T(8,128)} collective-permute-done((f32[256,512]{1,0:T(8,128)}, f32[256,512]{1,0:T(8,128)}, u32[]{:S(2)}, u32[]{:S(2)}) %collective-permute-start.11) | collective-permute-done | bytes 524320 | tf_op jit(solution)/shard_map/ppermute | solution.py:14
  42.4 1.6 %collective-permute-start.12 = (f32[512,256]{1,0:T(8,128)S(1)}, f32[512,256]{1,0:T(8,128)S(1)}, u32[]{:S(2)}, u32[]{:S(2)}) collective-permute-start(f32[512,256]{1,0:T(8,128)S(1)} %copy-done.42), channel_id=1, source_target_pairs={{0,4},{4,0},{8,12},{12,8},{1,5},{5,1},{9,13},{13,9},{2,6},{6,2},{1... | collective-permute-start | bytes 1572872 | tf_op jit(solution)/shard_map/ppermute | solution.py:14
  44.1 3.8 %collective-permute-done.8.refs_2_ = f32[256,256]{1,0:T(8,128)S(1)} collective-permute-done((f32[256,256]{1,0:T(8,128)S(1)}, f32[256,256]{1,0:T(8,128)S(1)}, u32[]{:S(2)}, u32[]{:S(2)}) %collective-permute-start.8) | collective-permute-done | bytes 262176 | tf_op jit(solution)/shard_map/ppermute | solution.py:14
  49.1 5.8 %collective-permute-done.5.s3 = f32[40,768]{1,0:T(8,128)S(1)} collective-permute-done((f32[40,768]{1,0:T(8,128)S(1)}, f32[40,768]{1,0:T(8,128)S(1)}, u32[]{:S(2)}, u32[]{:S(2)}) %collective-permute-start.5) | collective-permute-done | bytes 122912 | tf_op jit(solution)/shard_map/ppermute | solution.py:14
  55.6 1.6 %collective-permute-start.27 = (f32[512,256]{1,0:T(8,128)S(1)}, f32[512,256]{1,0:T(8,128)}, u32[]{:S(2)}, u32[]{:S(2)}) collective-permute-start(f32[512,256]{1,0:T(8,128)S(1)} %collective-permute-done.17.refs_2_), channel_id=1, source_target_pairs={{0,4},{4,0},{8,12},{12,8},{1,5},{5,1},{9,13},{13,9},{2,6},{6,2},{1... | collective-permute-start | bytes 1572872 | tf_op jit(solution)/shard_map/ppermute | solution.py:14
  62.4 1.5 %collective-permute-start.19 = (f32[256,512]{1,0:T(8,128)}, f32[256,512]{1,0:T(8,128)}, u32[]{:S(2)}, u32[]{:S(2)}) collective-permute-start(f32[256,512]{1,0:T(8,128)} %collective-permute-done.11.refs_0_), channel_id=1, source_target_pairs={{0,2},{2,0},{1,3},{3,1},{4,6},{6,4},{5,7},{7,5},{8,10},{10,8},{9,1... | collective-permute-start | bytes 1572872 | tf_op jit(solution)/shard_map/ppermute | solution.py:14
  68.2 1.3 %collective-permute-start.13 = (f32[256,256]{1,0:T(8,128)S(1)}, f32[256,256]{1,0:T(8,128)S(1)}, u32[]{:S(2)}, u32[]{:S(2)}) collective-permute-start(f32[256,256]{1,0:T(8,128)S(1)} %collective-permute-done.4.refs_4_), channel_id=1, source_target_pairs={{0,4},{4,0},{8,12},{12,8},{1,5},{5,1},{9,13},{13,9},{2,6},{6,2},{1... | collective-permute-start | bytes 786440 | tf_op jit(solution)/shard_map/ppermute | solution.py:14
  70.2 5.6 %collective-permute-done.13.refs_6_ = f32[256,256]{1,0:T(8,128)S(1)} collective-permute-done((f32[256,256]{1,0:T(8,128)S(1)}, f32[256,256]{1,0:T(8,128)S(1)}, u32[]{:S(2)}, u32[]{:S(2)}) %collective-permute-start.13) | collective-permute-done | bytes 262176 | tf_op jit(solution)/shard_map/ppermute | solution.py:14
  77.0 8.5 %collective-permute-done.19.refs_4_ = f32[256,512]{1,0:T(8,128)} collective-permute-done((f32[256,512]{1,0:T(8,128)}, f32[256,512]{1,0:T(8,128)}, u32[]{:S(2)}, u32[]{:S(2)}) %collective-permute-start.19) | collective-permute-done | bytes 524320 | tf_op jit(solution)/shard_map/ppermute | solution.py:14
  89.8 1.0 copy-done.7
  90.9 1.0 copy-done.9
  91.9 1.0 copy-done.15
  93.0 1.0 copy-done.17
  94.0 1.3 %shard_map.115 = (bf16[3,1024,256]{2,1,0:T(8,128)(2,1)S(1)}, bf16[3,1024,256]{2,1,0:T(8,128)(2,1)S(1)}) custom-call(s32[2]{0:T(128)S(1)} %pad_add_fusion.place, f32[1024,256]{1,0:T(8,128)S(1)} %bitcast.30, f32[512,256]{1,0:T(8,128)S(1)} %copy-done.7, f32[512,256]{1,0:T(8,128)S(1)} %copy-done.15, f32[512,256]{1,0:T(8,128)S(1)} %copy-done.9, ...), custom_call_target="tpu_custom_call" | custom-call | tf_op jit(solution)/shard_map/pallas_call | solution.py:104
  95.9 1.3 %shard_map.116 = (bf16[3,1024,256]{2,1,0:T(8,128)(2,1)S(1)}, bf16[3,1024,256]{2,1,0:T(8,128)(2,1)S(1)}) custom-call(s32[2]{0:T(128)S(1)} %pad_add_fusion.place, f32[1024,256]{1,0:T(8,128)S(1)} %bitcast.31, f32[512,256]{1,0:T(8,128)S(1)} %copy-done.11, f32[512,256]{1,0:T(8,128)S(1)} %copy-done.19, f32[512,256]{1,0:T(8,128)S(1)} %copy-done.5, ...), custom_call_target="tpu_custom_call" | custom-call | tf_op jit(solution)/shard_map/pallas_call | solution.py:104
  97.3 1.0 shard_map.113
  98.4 2.4 %shard_map.114 = (bf16[4,1024,256]{2,1,0:T(8,128)(2,1)S(1)}, bf16[4,1024,256]{2,1,0:T(8,128)(2,1)S(1)}) custom-call(s32[2]{0:T(128)S(1)} %pad_add_fusion.place, f32[256,1024]{1,0:T(8,128)S(1)} %bitcast.29, f32[256,512]{1,0:T(8,128)} %collective-permute-done.11.refs_0_, f32[256,512]{1,0:T(8,128)} %collective-permute-done.15.refs_1_, ...), custom_call_target="tpu_custom_call" | custom-call | tf_op jit(solution)/shard_map/pallas_call | solution.py:104
  100.9 26.7 %shard_map.117 = (f32[32,256]{1,0:T(8,128)}, f32[32,256]{1,0:T(8,128)}) custom-call(s32[2]{0:T(128)S(1)} %pad_add_fusion.place, f32[40,768]{1,0:T(8,128)S(1)} %copy-done.21, f32[40,768]{1,0:T(8,128)S(1)} %copy-done.39, f32[40,768]{1,0:T(8,128)S(1)} %copy-done.37, f32[40,768]{1,0:T(8,128)S(1)} %copy-done.41, f32[9,32,1]{2,1,0:T(8,128)S(1)} %copy.12.weight, ...), custom_call_target="tpu_custom_call" | custom-call | tf_op jit(solution)/shard_map/pallas_call | solution.py:234
  (134 shorter events, 21.8 us)
Async XLA Ops:
  3.6 10.4 %collective-permute-start.1 = (f32[40,768]{1,0:T(8,128)S(1)}, f32[40,768]{1,0:T(8,128)S(1)}, u32[]{:S(2)}, u32[]{:S(2)}) collective-permute-start(f32[40,768]{1,0:T(8,128)S(1)} %pad_maximum_fusion.s0), channel_id=1, source_target_pairs={{0,2},{2,0},{1,3},{3,1},{4,6},{6,4},{5,7},{7,5},{8,10},{10,8},{9,1... | collective-permute-start | bytes 368648 | tf_op jit(solution)/shard_map/ppermute | solution.py:14
  6.6 9.4 %collective-permute-start = (f32[40,768]{1,0:T(8,128)S(1)}, f32[40,768]{1,0:T(8,128)S(1)}, u32[]{:S(2)}, u32[]{:S(2)}) collective-permute-start(f32[40,768]{1,0:T(8,128)S(1)} %pad_maximum_fusion.s0), channel_id=1, source_target_pairs={{0,4},{4,0},{8,12},{12,8},{1,5},{5,1},{9,13},{13,9},{2,6},{6,2},{1... | collective-permute-start | bytes 368648 | tf_op jit(solution)/shard_map/ppermute | solution.py:14
  9.8 8.0 %collective-permute-start.2 = (f32[128,512]{1,0:T(8,128)}, f32[128,512]{1,0:T(8,128)}, u32[]{:S(2)}, u32[]{:S(2)}) collective-permute-start(f32[128,512]{1,0:T(8,128)} %dynamic-slice_bitcast_fusion.3), channel_id=1, source_target_pairs={{0,4},{4,0},{8,12},{12,8},{1,5},{5,1},{9,13},{13,9},{2,6},{6,2},{1... | collective-permute-start | bytes 786440 | tf_op jit(solution)/shard_map/ppermute | solution.py:14
  11.2 15.1 %collective-permute-start.3 = (f32[256,512]{1,0:T(8,128)}, f32[256,512]{1,0:T(8,128)S(1)}, u32[]{:S(2)}, u32[]{:S(2)}) collective-permute-start(f32[256,512]{1,0:T(8,128)} %dynamic-slice_bitcast_fusion.2), channel_id=1, source_target_pairs={{0,2},{2,0},{1,3},{3,1},{4,6},{6,4},{5,7},{7,5},{8,10},{10,8},{9,1... | collective-permute-start | bytes 1572872 | tf_op jit(solution)/shard_map/ppermute | solution.py:14
  14.0 23.5 %copy-start.43 = (f32[512,256]{1,0:T(8,128)S(1)}, f32[512,256]{1,0:T(8,128)}, u32[]{:S(2)}) copy-start(f32[512,256]{1,0:T(8,128)} %dynamic-slice_bitcast_fusion.1) | copy-start | bytes 1572868
  14.0 28.4 %copy-start.42 = (f32[512,256]{1,0:T(8,128)S(1)}, f32[512,256]{1,0:T(8,128)}, u32[]{:S(2)}) copy-start(f32[512,256]{1,0:T(8,128)} %dynamic-slice_bitcast_fusion) | copy-start | bytes 1572868
  14.0 23.5 %collective-permute-start.17 = (f32[512,256]{1,0:T(8,128)}, f32[512,256]{1,0:T(8,128)S(1)}, u32[]{:S(2)}, u32[]{:S(2)}) collective-permute-start(f32[512,256]{1,0:T(8,128)} %dynamic-slice_bitcast_fusion), channel_id=1, source_target_pairs={{0,2},{2,0},{1,3},{3,1},{4,6},{6,4},{5,7},{7,5},{8,10},{10,8},{9,1... | collective-permute-start | bytes 1572872 | tf_op jit(solution)/shard_map/ppermute | solution.py:14
  16.0 72.9 %copy-start.38 = (f32[40,768]{1,0:T(8,128)}, f32[40,768]{1,0:T(8,128)S(1)}, u32[]{:S(2)}) copy-start(f32[40,768]{1,0:T(8,128)S(1)} %collective-permute-done.s1) | copy-start | bytes 368644
  16.0 21.6 %collective-permute-start.7 = (f32[512,256]{1,0:T(8,128)}, f32[512,256]{1,0:T(8,128)S(1)}, u32[]{:S(2)}, u32[]{:S(2)}) collective-permute-start(f32[512,256]{1,0:T(8,128)} %dynamic-slice_bitcast_fusion.1), channel_id=1, source_target_pairs={{0,4},{4,0},{8,12},{12,8},{1,5},{5,1},{9,13},{13,9},{2,6},{6,2},{1... | collective-permute-start | bytes 1572872 | tf_op jit(solution)/shard_map/ppermute | solution.py:14
  17.8 24.5 %collective-permute-start.11 = (f32[256,512]{1,0:T(8,128)}, f32[256,512]{1,0:T(8,128)}, u32[]{:S(2)}, u32[]{:S(2)}) collective-permute-start(f32[256,512]{1,0:T(8,128)} %dynamic-slice_bitcast_fusion.2), channel_id=1, source_target_pairs={{0,4},{4,0},{8,12},{12,8},{1,5},{5,1},{9,13},{13,9},{2,6},{6,2},{1... | collective-permute-start | bytes 1572872 | tf_op jit(solution)/shard_map/ppermute | solution.py:14
  26.2 17.8 %collective-permute-start.4 = (f32[256,256]{1,0:T(8,128)S(1)}, f32[256,256]{1,0:T(8,128)S(1)}, u32[]{:S(2)}, u32[]{:S(2)}) collective-permute-start(f32[256,256]{1,0:T(8,128)S(1)} %fusion.refs_0_), channel_id=1, source_target_pairs={{0,2},{2,0},{1,3},{3,1},{4,6},{6,4},{5,7},{7,5},{8,10},{10,8},{9,1... | collective-permute-start | bytes 786440 | tf_op jit(solution)/shard_map/ppermute | solution.py:14
  26.3 21.6 %collective-permute-start.6 = (f32[256,256]{1,0:T(8,128)S(1)}, f32[256,256]{1,0:T(8,128)S(1)}, u32[]{:S(2)}, u32[]{:S(2)}) collective-permute-start(f32[256,256]{1,0:T(8,128)S(1)} %fusion.refs_0_), channel_id=1, source_target_pairs={{0,1},{1,0},{2,3},{3,2},{4,5},{5,4},{6,7},{7,6},{8,9},{9,8},{10,11... | collective-permute-start | bytes 786440 | tf_op jit(solution)/shard_map/ppermute | solution.py:14
  37.5 20.5 %collective-permute-start.18 = (f32[512,256]{1,0:T(8,128)S(1)}, f32[512,256]{1,0:T(8,128)S(1)}, u32[]{:S(2)}, u32[]{:S(2)}) collective-permute-start(f32[512,256]{1,0:T(8,128)S(1)} %copy-done.43), channel_id=1, source_target_pairs={{0,2},{2,0},{1,3},{3,1},{4,6},{6,4},{5,7},{7,5},{8,10},{10,8},{9,1... | collective-permute-start | bytes 1572872 | tf_op jit(solution)/shard_map/ppermute | solution.py:14
  37.6 10.4 %collective-permute-start.8 = (f32[256,256]{1,0:T(8,128)S(1)}, f32[256,256]{1,0:T(8,128)S(1)}, u32[]{:S(2)}, u32[]{:S(2)}) collective-permute-start(f32[256,256]{1,0:T(8,128)S(1)} %fusion.refs_0_), channel_id=1, source_target_pairs={{0,4},{4,0},{8,12},{12,8},{1,5},{5,1},{9,13},{13,9},{2,6},{6,2},{1... | collective-permute-start | bytes 786440 | tf_op jit(solution)/shard_map/ppermute | solution.py:14
  42.4 15.6 %collective-permute-start.12 = (f32[512,256]{1,0:T(8,128)S(1)}, f32[512,256]{1,0:T(8,128)S(1)}, u32[]{:S(2)}, u32[]{:S(2)}) collective-permute-start(f32[512,256]{1,0:T(8,128)S(1)} %copy-done.42), channel_id=1, source_target_pairs={{0,4},{4,0},{8,12},{12,8},{1,5},{5,1},{9,13},{13,9},{2,6},{6,2},{1... | collective-permute-start | bytes 1572872 | tf_op jit(solution)/shard_map/ppermute | solution.py:14
  44.0 10.9 %collective-permute-start.5 = (f32[40,768]{1,0:T(8,128)S(1)}, f32[40,768]{1,0:T(8,128)S(1)}, u32[]{:S(2)}, u32[]{:S(2)}) collective-permute-start(f32[40,768]{1,0:T(8,128)S(1)} %collective-permute-done.s1), channel_id=1, source_target_pairs={{0,2},{2,0},{1,3},{3,1},{4,6},{6,4},{5,7},{7,5},{8,10},{10,8},{9,1... | collective-permute-start | bytes 368648 | tf_op jit(solution)/shard_map/ppermute | solution.py:14
  47.9 13.7 %collective-permute-start.24 = (f32[512,256]{1,0:T(8,128)S(1)}, f32[512,256]{1,0:T(8,128)S(1)}, u32[]{:S(2)}, u32[]{:S(2)}) collective-permute-start(f32[512,256]{1,0:T(8,128)S(1)} %collective-permute-done.17.refs_2_), channel_id=1, source_target_pairs={{0,1},{1,0},{2,3},{3,2},{4,5},{5,4},{6,7},{7,6},{8,9},{9,8},{10,11... | collective-permute-start | bytes 1572872 | tf_op jit(solution)/shard_map/ppermute | solution.py:14
  48.6 15.2 %collective-permute-start.21 = (f32[512,256]{1,0:T(8,128)S(1)}, f32[512,256]{1,0:T(8,128)S(1)}, u32[]{:S(2)}, u32[]{:S(2)}) collective-permute-start(f32[512,256]{1,0:T(8,128)S(1)} %collective-permute-done.7.refs_0_), channel_id=1, source_target_pairs={{0,1},{1,0},{2,3},{3,2},{4,5},{5,4},{6,7},{7,6},{8,9},{9,8},{10,11... | collective-permute-start | bytes 1572872 | tf_op jit(solution)/shard_map/ppermute | solution.py:14
  55.6 12.6 %collective-permute-start.27 = (f32[512,256]{1,0:T(8,128)S(1)}, f32[512,256]{1,0:T(8,128)}, u32[]{:S(2)}, u32[]{:S(2)}) collective-permute-start(f32[512,256]{1,0:T(8,128)S(1)} %collective-permute-done.17.refs_2_), channel_id=1, source_target_pairs={{0,4},{4,0},{8,12},{12,8},{1,5},{5,1},{9,13},{13,9},{2,6},{6,2},{1... | collective-permute-start | bytes 1572872 | tf_op jit(solution)/shard_map/ppermute | solution.py:14
  58.0 1.5 %collective-permute-start.10 = (f32[256,256]{1,0:T(8,128)S(1)}, f32[256,256]{1,0:T(8,128)S(1)}, u32[]{:S(2)}, u32[]{:S(2)}) collective-permute-start(f32[256,256]{1,0:T(8,128)S(1)} %collective-permute-done.4.refs_4_), channel_id=1, source_target_pairs={{0,1},{1,0},{2,3},{3,2},{4,5},{5,4},{6,7},{7,6},{8,9},{9,8},{10,11... | collective-permute-start | bytes 786440 | tf_op jit(solution)/shard_map/ppermute | solution.py:14
  58.0 7.5 %collective-permute-start.9 = (f32[256,256]{1,0:T(8,128)S(1)}, f32[256,256]{1,0:T(8,128)S(1)}, u32[]{:S(2)}, u32[]{:S(2)}) collective-permute-start(f32[256,256]{1,0:T(8,128)S(1)} %collective-permute-done.8.refs_2_), channel_id=1, source_target_pairs={{0,1},{1,0},{2,3},{3,2},{4,5},{5,4},{6,7},{7,6},{8,9},{9,8},{10,11... | collective-permute-start | bytes 786440 | tf_op jit(solution)/shard_map/ppermute | solution.py:14
  60.3 16.3 %collective-permute-start.25 = (f32[512,256]{1,0:T(8,128)S(1)}, f32[512,256]{1,0:T(8,128)}, u32[]{:S(2)}, u32[]{:S(2)}) collective-permute-start(f32[512,256]{1,0:T(8,128)S(1)} %collective-permute-done.7.refs_0_), channel_id=1, source_target_pairs={{0,2},{2,0},{1,3},{3,1},{4,6},{6,4},{5,7},{7,5},{8,10},{10,8},{9,1... | collective-permute-start | bytes 1572872 | tf_op jit(solution)/shard_map/ppermute | solution.py:14
  62.4 23.2 %collective-permute-start.19 = (f32[256,512]{1,0:T(8,128)}, f32[256,512]{1,0:T(8,128)}, u32[]{:S(2)}, u32[]{:S(2)}) collective-permute-start(f32[256,512]{1,0:T(8,128)} %collective-permute-done.11.refs_0_), channel_id=1, source_target_pairs={{0,2},{2,0},{1,3},{3,1},{4,6},{6,4},{5,7},{7,5},{8,10},{10,8},{9,1... | collective-permute-start | bytes 1572872 | tf_op jit(solution)/shard_map/ppermute | solution.py:14
  64.7 20.9 %collective-permute-start.22 = (f32[512,256]{1,0:T(8,128)S(1)}, f32[512,256]{1,0:T(8,128)S(1)}, u32[]{:S(2)}, u32[]{:S(2)}) collective-permute-start(f32[512,256]{1,0:T(8,128)S(1)} %collective-permute-done.18.refs_2_), channel_id=1, source_target_pairs={{0,1},{1,0},{2,3},{3,2},{4,5},{5,4},{6,7},{7,6},{8,9},{9,8},{10,11... | collective-permute-start | bytes 1572872 | tf_op jit(solution)/shard_map/ppermute | solution.py:14
  66.2 20.6 %collective-permute-start.23 = (f32[512,256]{1,0:T(8,128)S(1)}, f32[512,256]{1,0:T(8,128)S(1)}, u32[]{:S(2)}, u32[]{:S(2)}) collective-permute-start(f32[512,256]{1,0:T(8,128)S(1)} %collective-permute-done.12.refs_0_), channel_id=1, source_target_pairs={{0,1},{1,0},{2,3},{3,2},{4,5},{5,4},{6,7},{7,6},{8,9},{9,8},{10,11... | collective-permute-start | bytes 1572872 | tf_op jit(solution)/shard_map/ppermute | solution.py:14
  68.2 7.6 %collective-permute-start.13 = (f32[256,256]{1,0:T(8,128)S(1)}, f32[256,256]{1,0:T(8,128)S(1)}, u32[]{:S(2)}, u32[]{:S(2)}) collective-permute-start(f32[256,256]{1,0:T(8,128)S(1)} %collective-permute-done.4.refs_4_), channel_id=1, source_target_pairs={{0,4},{4,0},{8,12},{12,8},{1,5},{5,1},{9,13},{13,9},{2,6},{6,2},{1... | collective-permute-start | bytes 786440 | tf_op jit(solution)/shard_map/ppermute | solution.py:14
  75.8 11.9 %collective-permute-start.14 = (f32[256,256]{1,0:T(8,128)S(1)}, f32[256,256]{1,0:T(8,128)S(1)}, u32[]{:S(2)}, u32[]{:S(2)}) collective-permute-start(f32[256,256]{1,0:T(8,128)S(1)} %collective-permute-done.13.refs_6_), channel_id=1, source_target_pairs={{0,1},{1,0},{2,3},{3,2},{4,5},{5,4},{6,7},{7,6},{8,9},{9,8},{10,11... | collective-permute-start | bytes 786440 | tf_op jit(solution)/shard_map/ppermute | solution.py:14
  76.5 21.8 %collective-permute-start.16 = (f32[256,512]{1,0:T(8,128)S(1)}, f32[256,512]{1,0:T(8,128)}, u32[]{:S(2)}, u32[]{:S(2)}) collective-permute-start(f32[256,512]{1,0:T(8,128)S(1)} %collective-permute-done.3.refs_2_), channel_id=1, source_target_pairs={{0,1},{1,0},{2,3},{3,2},{4,5},{5,4},{6,7},{7,6},{8,9},{9,8},{10,11... | collective-permute-start | bytes 1572872 | tf_op jit(solution)/shard_map/ppermute | solution.py:14
  85.6 12.8 %collective-permute-start.15 = (f32[256,512]{1,0:T(8,128)}, f32[256,512]{1,0:T(8,128)}, u32[]{:S(2)}, u32[]{:S(2)}) collective-permute-start(f32[256,512]{1,0:T(8,128)} %collective-permute-done.11.refs_0_), channel_id=1, source_target_pairs={{0,1},{1,0},{2,3},{3,2},{4,5},{5,4},{6,7},{7,6},{8,9},{9,8},{10,11... | collective-permute-start | bytes 1572872 | tf_op jit(solution)/shard_map/ppermute | solution.py:14
  86.4 12.0 %collective-permute-start.20 = (f32[256,512]{1,0:T(8,128)}, f32[256,512]{1,0:T(8,128)}, u32[]{:S(2)}, u32[]{:S(2)}) collective-permute-start(f32[256,512]{1,0:T(8,128)} %collective-permute-done.19.refs_4_), channel_id=1, source_target_pairs={{0,1},{1,0},{2,3},{3,2},{4,5},{5,4},{6,7},{7,6},{8,9},{9,8},{10,11... | collective-permute-start | bytes 1572872 | tf_op jit(solution)/shard_map/ppermute | solution.py:14
  87.7 13.1 %collective-permute-start.28 = (f32[512,256]{1,0:T(8,128)}, f32[512,256]{1,0:T(8,128)}, u32[]{:S(2)}, u32[]{:S(2)}) collective-permute-start(f32[512,256]{1,0:T(8,128)} %collective-permute-done.27.b_mine), channel_id=1, source_target_pairs={{0,1},{1,0},{2,3},{3,2},{4,5},{5,4},{6,7},{7,6},{8,9},{9,8},{10,11... | collective-permute-start | bytes 1572872 | tf_op jit(solution)/shard_map/ppermute | solution.py:14
  88.4 12.4 %collective-permute-start.26 = (f32[512,256]{1,0:T(8,128)}, f32[512,256]{1,0:T(8,128)}, u32[]{:S(2)}, u32[]{:S(2)}) collective-permute-start(f32[512,256]{1,0:T(8,128)} %collective-permute-done.25.r_mine), channel_id=1, source_target_pairs={{0,1},{1,0},{2,3},{3,2},{4,5},{5,4},{6,7},{7,6},{8,9},{9,8},{10,11... | collective-permute-start | bytes 1572872 | tf_op jit(solution)/shard_map/ppermute | solution.py:14
  (41 other events, 81.1 us)

commit v3 on v0

v3 whole, which is shorter than its diff:
```python
import jax
import jax.numpy as jnp
from jax import lax
from jax.experimental import pallas as pl
from jax.experimental.pallas import tpu as pltpu
from jax.sharding import PartitionSpec as P

F32 = jnp.float32
BF16 = jnp.bfloat16


def from_partner(value, axis):
    pairs = [(source, source ^ 1) for source in range(lax.axis_size(axis))]
    return lax.ppermute(value, axis, pairs)


def after(value, *earlier):
    return lax.optimization_barrier((value,) + earlier)[0]


def exact_dot(left, right):
    return jnp.dot(left, right, precision=lax.Precision.HIGHEST, preferred_element_type=F32)


def halves_of(value):
    high = value.astype(BF16)
    return high, (value - high.astype(F32)).astype(BF16)


def store_split(high_ref, low_ref, where, value):
    high, low = halves_of(value)
    high_ref[where] = high
    low_ref[where] = low


def cut_kernel(place, *refs):
    count = (len(refs) - 1) // 2
    panels, halves, sems = refs[:count], refs[count:2 * count], refs[-1]
    copies = []
    for index, (panel, half) in enumerate(zip(panels, halves)):
        rows, columns = half.shape
        if columns < panel.shape[1]:
            source = panel.at[:, pl.ds(pl.multiple_of(place[1] * columns, columns), columns)]
        else:
            source = panel.at[pl.ds(pl.multiple_of(place[1] * rows, rows), rows), :]
        copies.append(pltpu.make_async_copy(source, half, sems.at[index]))
    for copy in copies:
        copy.start()
    for copy in copies:
        copy.wait()


def cut_call(place, panels, shapes):
    hbm = [pltpu.with_memory_space_constraint(panel, pltpu.HBM) for panel in panels]
    return pl.pallas_call(
        cut_kernel,
        in_specs=[pl.BlockSpec(memory_space=pltpu.SMEM)] + [pl.BlockSpec(memory_space=pl.ANY)] * len(panels),
        out_specs=[pl.BlockSpec(memory_space=pl.ANY)] * len(panels),
        out_shape=[jax.ShapeDtypeStruct(shape, F32) for shape in shapes],
        scratch_shapes=[pltpu.SemaphoreType.DMA((len(panels),))],
        compiler_params=pltpu.CompilerParams(vmem_limit_bytes=2**20),
    )(place, *hbm)


def column_of(row):
    shape = (row.shape[1], row.shape[1])
    same = lax.broadcasted_iota(jnp.int32, shape, 0) == lax.broadcasted_iota(jnp.int32, shape, 1)
    return jnp.sum(jnp.where(same, row, 0.0), axis=1, keepdims=True)


def state_kernel(place, cells, one, two, pair_cols, mass, state_ref):
    rows, width = one.shape
    cell = column_of(cells[...].astype(F32))
    number = lax.broadcasted_iota(jnp.int32, (rows, width), 1)
    chosen = [(cell == (number + place[2 + side]).astype(F32)).astype(F32) for side in range(2)]
    state_ref[:rows, :width] = one[...]
    state_ref[:rows, width:2 * width] = two[...]
    state_ref[:rows, 2 * width:] = exact_dot(jnp.concatenate(chosen, axis=1), pair_cols[...])
    state_ref[rows:, :width] = jnp.broadcast_to(mass[...], (8, width))
    state_ref[rows:, width:] = jnp.zeros((8, 2 * width), F32)


def panel_kernel(place, mine, other, pair_cols, panel_ref):
    rows = mine.shape[0]
    for step, couple in enumerate((mine, other)):
        start = ((place[0] % 2) ^ step) * rows
        panel_ref[pl.ds(pl.multiple_of(start, rows), rows), :] = exact_dot(couple[...], pair_cols[...])


def small_call(kernel, shape, *values):
    vmem = pl.BlockSpec(memory_space=pltpu.VMEM)
    return pl.pallas_call(
        kernel,
        in_specs=[pl.BlockSpec(memory_space=pltpu.SMEM)] + [vmem] * (len(values) - 1),
        out_specs=vmem,
        out_shape=jax.ShapeDtypeStruct(shape, F32),
        compiler_params=pltpu.CompilerParams(vmem_limit_bytes=6 * 2**20),
    )(*values)


def split_tall(place, pieces, high_ref, low_ref):
    width = high_ref.shape[1]
    blocks = 4 // len(pieces)
    for part, piece in enumerate(pieces):
        for block in range(blocks):
            number = block if len(pieces) == 1 else 2 * (place[1] ^ part) + block
            rows = pl.ds(pl.multiple_of((number ^ place[0]) * width, width), width)
            store_split(high_ref, low_ref, (rows, slice(None)), piece[block * width:(block + 1) * width, :])


def tall_kernel(place, *refs):
    split_tall(place, refs[:-2], *refs[-2:])


def wide_kernel(place, *refs):
    pieces, (high_ref, low_ref) = refs[:-2], refs[-2:]
    width = high_ref.shape[1]
    blocks = 4 // len(pieces)
    for part, piece in enumerate(pieces):
        for block in range(blocks):
            number = block if len(pieces) == 1 else 2 * (place[1] ^ part) + block
            rows = pl.ds(pl.multiple_of((number ^ place[0]) * width, width), width)
            store_split(high_ref, low_ref, (rows, slice(None)), piece[:, block * width:(block + 1) * width])


def edge_kernel(place, *refs):
    pieces, (high_ref, low_ref) = refs[:-2], refs[-2:]
    rows = pieces[0].shape[0] // 2
    for part, piece in enumerate(pieces):
        for bit in range(2):
            start = (bit ^ (place[0] % 2)) * 2 * rows + (place[1] ^ part) * rows
            where = (pl.ds(pl.multiple_of(start, rows), rows), slice(None))
            store_split(high_ref, low_ref, where, piece[bit * rows:(bit + 1) * rows, :])


def split_call(kernel, place, rows, *pieces):
    out = jax.ShapeDtypeStruct((rows, pieces[0].shape[1]), BF16)
    if kernel is wide_kernel:
        out = jax.ShapeDtypeStruct((rows, pieces[0].shape[0]), BF16)
    vmem = pl.BlockSpec(memory_space=pltpu.VMEM)
    return pl.pallas_call(
        kernel,
        in_specs=[pl.BlockSpec(memory_space=pltpu.SMEM)] + [vmem] * len(pieces),
        out_specs=(vmem, vmem),
        out_shape=(pltpu.VMEM(out.shape, BF16),) * 2,
        compiler_params=pltpu.CompilerParams(vmem_limit_bytes=4 * 2**20),
    )(place, *pieces)


def product(left, high, low):
    rows = left.shape[0]
    left_high, left_low = halves_of(left)
    both = jnp.dot(jnp.concatenate([left_high, left_low], axis=0), high, preferred_element_type=F32)
    rest = jnp.dot(left_high, low, preferred_element_type=F32)
    return both[:rows] + both[rows:] + rest


def march_kernel(place, s0, s1, s2, s3, weight, *refs):
    edge, lift, root, back = refs[:8], refs[8:16], refs[16:22], refs[22:28]
    r_mine, r_other, b_mine, b_other, one_ref, two_ref, last_rh, last_rl, last_bh, last_bl = refs[28:]
    rows, width = one_ref.shape
    states = (s0, s1, s2, s3)
    one = jnp.concatenate([state[:rows, :width] for state in states], axis=1)
    two = jnp.concatenate([state[:rows, width:2 * width] for state in states], axis=1)
    picked = jnp.concatenate([state[:rows, 2 * width:] for state in states], axis=1)
    scale = jnp.concatenate([state[rows:rows + 1, :width] for state in states], axis=1)
    split_tall(place, (r_mine, r_other), last_rh, last_rl)
    split_tall(place, (b_mine, b_other), last_bh, last_bl)
    root = root + (last_rh, last_rl)
    back = back + (last_bh, last_bl)

    def tall(left, panels):
        return jnp.concatenate([product(left, panels[2 * tile][...], panels[2 * tile + 1][...]) for tile in range(4)], axis=1)

    def column_block(block, part):
        return jnp.concatenate([lift[2 * tile + part][block * width:(block + 1) * width, :] for tile in range(4)], axis=0)

    def advance(step, carry):
        one, two = carry
        half = jnp.concatenate(
            [
                product(one[:, side * 2 * width:(side + 1) * 2 * width], edge[2 * tile][...], edge[2 * tile + 1][...])
                for side in range(2)
                for tile in (2 * side, 2 * side + 1)
            ],
            axis=1,
        )
        half = half + column_of(weight[pl.ds(step, 1), :]) * picked
        sums = jnp.concatenate([product(half, column_block(block, 0), column_block(block, 1)) for block in range(4)], axis=1)
        two = tall(sums + two * scale, root)
        return half - tall(two, back), two

    one, two = lax.fori_loop(0, weight.shape[0], advance, (one, two))
    one_ref[...] = one[:, :width]
    two_ref[...] = two[:, :width]


def shards(
    adjoint_one_start,
    adjoint_two_start,
    couple_panel,
    pair_panel,
    lift_panel,
    root_panel,
    back_panel,
    mass_two,
    probe_cells,
    probe_weight,
):
    couple = couple_panel[0, 0]
    pair_cols = pair_panel[0, 0]
    lift = lift_panel[0, 0]
    root = root_panel[0, 0]
    back = back_panel[0, 0]
    width = couple.shape[0]
    rows = probe_cells.shape[0]
    column, row, core = lax.axis_index("gx"), lax.axis_index("gy"), lax.axis_index("gz")
    x_bit, y_bit = column % 2, row % 2
    first_cell = ((column - x_bit) * lax.axis_size("gy") + row) * width
    place = jnp.stack([2 * y_bit + x_bit, core, first_cell, first_cell + lax.axis_size("gy") * width]).astype(jnp.int32)

    couple_mine, lift_half = cut_call(place, (couple, lift), ((width // 2, 2 * width), (width, 2 * width)))
    couple_other = from_partner(couple_mine, "gx")
    lift_y = from_partner(lift_half, "gy")
    root_half, back_half = cut_call(after(place, lift_half), (root, back), ((2 * width, width),) * 2)
    lift_x = from_partner(lift_half, "gx")
    back_y = from_partner(back_half, "gy")

    cells = probe_cells[None, :]
    state = small_call(
        state_kernel,
        (rows + 8, 3 * width),
        after(place, root_half),
        cells,
        adjoint_one_start[0, 0],
        adjoint_two_start[0, 0],
        pair_cols,
        mass_two[0],
    )
    edge_half = small_call(panel_kernel, (width, width), place, couple_mine, couple_other, pair_cols)

    token = [couple_other]

    def arrive(value, *done):
        value = after(value, token[0], *done)
        token[0] = value
        return value

    def send(value, axis):
        return from_partner(after(value, token[0]), axis)

    def split(kernel, rows, value):
        return split_call(kernel, place, rows, value, from_partner(value, "gz"))

    tall, wide, edge = (tall_kernel, 4 * width), (wide_kernel, 4 * width), (edge_kernel, 2 * width)
    lift_own = split_call(wide_kernel, place, wide[1], after(lift, couple_other))
    root_own = split_call(tall_kernel, place, tall[1], after(root, couple_other))
    back_own = split_call(tall_kernel, place, tall[1], after(back, couple_other))

    state_x = send(state, "gx")
    root_x = send(root_half, "gx")
    lift_y = arrive(lift_y, lift_own[0], root_own[0], back_own[0])
    edge_own = split(*edge, edge_half)
    edge_y = send(edge_half, "gy")
    state_y = send(state, "gy")
    lift_x = arrive(lift_x, edge_own[0])
    lift_y_split = split(*wide, lift_y)
    back_x = send(back_half, "gx")
    back_y = arrive(back_y, lift_y_split[0])
    lift_x_split = split(*wide, lift_x)
    root_y = send(root_half, "gy")
    edge_y = arrive(edge_y, lift_x_split[0])
    back_y_split = split(*tall, back_y)
    root_x = arrive(root_x, back_y_split[0])
    edge_y_split = split(*edge, edge_y)
    edge_x = send(edge_half, "gx")
    state_y = arrive(state_y)
    state_d = send(state_x, "gy")
    back_x = arrive(back_x, edge_y_split[0])
    root_x_split = split(*tall, root_x)
    edge_d = send(edge_y, "gx")
    root_y = arrive(root_y, root_x_split[0])
    lift_d = send(lift_x, "gy")
    back_x_split = split(*tall, back_x)
    state_d = arrive(state_d)
    root_d = send(root_x, "gy")
    edge_x = arrive(edge_x, back_x_split[0])
    root_y_split = split(*tall, root_y)
    back_d = send(back_y, "gx")
    edge_d = arrive(edge_d, root_y_split[0])
    edge_x_split = split(*edge, edge_x)
    lift_d = arrive(lift_d, edge_x_split[0])
    edge_d_split = split(*edge, edge_d)
    back_d = arrive(back_d, edge_d_split[0])
    lift_d_split = split(*wide, lift_d)
    root_d = arrive(root_d, lift_d_split[0])

    vmem = pl.BlockSpec(memory_space=pltpu.VMEM)
    panels = edge_own + edge_x_split + edge_y_split + edge_d_split + lift_own + lift_x_split + lift_y_split + lift_d_split
    panels += root_own + root_x_split + root_y_split + back_own + back_x_split + back_y_split
    panels = tuple(pltpu.with_memory_space_constraint(panel, pltpu.VMEM) for panel in panels)
    panels += (root_d, from_partner(root_d, "gz"), back_d, from_partner(back_d, "gz"))
    one, two = pl.pallas_call(
        march_kernel,
        in_specs=[pl.BlockSpec(memory_space=pltpu.SMEM)] + [vmem] * (5 + len(panels)),
        out_specs=(vmem, vmem),
        out_shape=(jax.ShapeDtypeStruct((rows, width), F32),) * 2,
        scratch_shapes=[pltpu.VMEM((4 * width, width), BF16)] * 4,
        compiler_params=pltpu.CompilerParams(vmem_limit_bytes=12 * 2**20),
    )(place, state, state_x, state_y, state_d, probe_weight, *panels)
    return (one[None, None], two[None, None])


def solution(mesh):
    placed = (
        P(("groups", "gx"), "gy", "gz", None),
        P(("groups", "gx"), "gy", "gz", None),
        P(("groups", "gx"), "gy", None, None),
        P(("groups", "gx"), "gy", None, None),
        P(("groups", "gx"), "gy", None, None),
        P(("groups", "gx"), "gy", None, None),
        P(("groups", "gx"), "gy", None, None),
        P(("groups", "gx"), "gy", None),
        P(("groups", "gz")),
        P("groups", "gz"),
    )
    return jax.shard_map(
        shards,
        mesh=mesh,
        in_specs=placed,
        out_specs=(P(("groups", "gx"), "gy", "gz", None), P(("groups", "gx"), "gy", "gz", None)),
        check_vma=False,
    )
```

time: 257 us -> 136 us (0.53)
  waiting for transfers between devices: 156 us -> 69.9 us
  Pallas kernels: 0 us -> 40.6 us
  matrix products: 34.1 us -> 0 us
  starting transfers between devices: 53.3 us -> 22.5 us
  local copies, waits for them, and re-layouts: 9.8 us -> 1.4 us
    ppermute x45 -> x29, waiting for transfers between devices: 156 us -> 69.9 us  [from_partner(): return lax.ppermute(value, axis, pairs)]
    pallas_call x0 -> x19, Pallas kernels: none -> 40.6 us  [the longest x1 25.6 us: shards(): pl.pallas_call(march_kernel, in_specs=[pl.BlockSpec(memory_space=pltpu.SM...]
    dot_general x45 -> x0, matrix products: 34.1 us -> none  [matmul(): jnp.dot(left, right, precision=lax.Precision.HIGHEST, preferred_element_t...]
    ppermute x45 -> x29, starting transfers between devices: 53.3 us -> 22.5 us  [from_partner(): return lax.ppermute(value, axis, pairs)]
    mul x27 -> x0, local copies, waits for them, and re-layouts: 6.64 us -> none  [the longest x9 6.22 us: advance(): source = weights[:, None] * probe_mask]
  transfers between devices with their start and end apart: 45 -> 29, of which waited for: 45 -> 15; matrix products, arithmetic and copies ran while one was open for 0% -> 0% of each run, Pallas kernels for 0% -> 10%
where the time goes in v3:
time: 136 us; the launch traced here: 135 us
  waiting for transfers between devices  69.9 us (51%)
  Pallas kernels  40.6 us (30%)
  starting transfers between devices  22.5 us (17%)
  local copies, waits for them, and re-layouts  1.4 us (1%)
    ppermute x29, waiting for transfers between devices, from_partner(): return lax.ppermute(value, axis, pairs)  69.9 us
    pallas_call x1, Pallas kernels, shards(): pl.pallas_call(march_kernel, in_specs=[pl.BlockSpec(memory_space=pltpu.SM...  25.6 us
    ppermute x29, starting transfers between devices, from_partner(): return lax.ppermute(value, axis, pairs)  22.5 us
    pallas_call x14, Pallas kernels, split_call(): pl.pallas_call(kernel, in_specs=[pl.BlockSpec(memory_space=pltpu.SMEM)] +...  9.5 us
    pallas_call x2, Pallas kernels, cut_call(): pl.pallas_call(cut_kernel, in_specs=[pl.BlockSpec(memory_space=pltpu.SMEM...  3.45 us
  transfers between devices with their start and end apart: 29, of which 15 were waited for; matrix products, arithmetic and copies ran while one was open for 0% of the time, Pallas kernels for 10%

profile of v3, /device:TPU:0, one launch (start us, length us, event | category | flops | bytes accessed | tf_op | source)
XLA Modules:
  0.0 135.5 jit_solution(10012231465976365411)
XLA Ops:
  0.7 1.7 %shard_map.113 = (f32[128,512]{1,0:T(8,128)S(1)}, f32[256,512]{1,0:T(8,128)S(1)}) custom-call(s32[4]{0:T(128)S(1)} %pad_add_fusion.place, f32[256,512]{1,0:T(8,128)} %bitcast.27, f32[256,1024]{1,0:T(8,128)} %bitcast.19), custom_call_target="tpu_custom_call" | custom-call | tf_op jit(solution)/shard_map/pallas_call | solution.py:55
  2.4 3.0 %collective-permute-start.2 = (f32[256,512]{1,0:T(8,128)S(1)}, f32[256,512]{1,0:T(8,128)S(1)}, u32[]{:S(2)}, u32[]{:S(2)}) collective-permute-start(f32[256,512]{1,0:T(8,128)S(1)} %get-tuple-element.67), channel_id=1, source_target_pairs={{0,2},{2,0},{1,3},{3,1},{4,6},{6,4},{5,7},{7,5},{8,10},{10,8},{9,1... | collective-permute-start | bytes 1572872 | tf_op jit(solution)/shard_map/ppermute | solution.py:14
  5.4 1.6 %collective-permute-start = (f32[128,512]{1,0:T(8,128)S(1)}, f32[128,512]{1,0:T(8,128)S(1)}, u32[]{:S(2)}, u32[]{:S(2)}) collective-permute-start(f32[128,512]{1,0:T(8,128)S(1)} %get-tuple-element.71.mine), channel_id=1, source_target_pairs={{0,4},{4,0},{8,12},{12,8},{1,5},{5,1},{9,13},{13,9},{2,6},{6,2},{1... | collective-permute-start | bytes 786440 | tf_op jit(solution)/shard_map/ppermute | solution.py:14
  7.5 1.8 %shard_map.114 = (f32[512,256]{1,0:T(8,128)S(1)}, f32[512,256]{1,0:T(8,128)S(1)}) custom-call(s32[4]{0:T(128)S(1)} %pad_add_fusion.place, f32[1024,256]{1,0:T(8,128)} %bitcast.15, f32[1024,256]{1,0:T(8,128)} %bitcast.17), custom_call_target="tpu_custom_call" | custom-call | tf_op jit(solution)/shard_map/pallas_call | solution.py:55
  9.2 5.4 %collective-permute-done.other = f32[128,512]{1,0:T(8,128)S(1)} collective-permute-done((f32[128,512]{1,0:T(8,128)S(1)}, f32[128,512]{1,0:T(8,128)S(1)}, u32[]{:S(2)}, u32[]{:S(2)}) %collective-permute-start) | collective-permute-done | bytes 262176 | tf_op jit(solution)/shard_map/ppermute | solution.py:14
  17.4 1.7 %collective-permute-start.6 = (f32[512,256]{1,0:T(8,128)S(1)}, f32[512,256]{1,0:T(8,128)S(1)}, u32[]{:S(2)}, u32[]{:S(2)}) collective-permute-start(f32[512,256]{1,0:T(8,128)S(1)} %get-tuple-element.95), channel_id=1, source_target_pairs={{0,2},{2,0},{1,3},{3,1},{4,6},{6,4},{5,7},{7,5},{8,10},{10,8},{9,1... | collective-permute-start | bytes 1572872 | tf_op jit(solution)/shard_map/ppermute | solution.py:14
  19.1 1.2 shard_map.119.refs_0_
  20.6 1.3 collective-permute-done.8.refs_1_
  22.5 1.9 %collective-permute-done.7.refs_0_ = f32[256,512]{1,0:T(8,128)S(1)} collective-permute-done((f32[256,512]{1,0:T(8,128)S(1)}, f32[256,512]{1,0:T(8,128)S(1)}, u32[]{:S(2)}, u32[]{:S(2)}) %collective-permute-start.7) | collective-permute-done | bytes 524320 | tf_op jit(solution)/shard_map/ppermute | solution.py:14
  24.4 0.7 shard_map.121
  25.1 6.5 %collective-permute-done.6.refs_0_ = f32[512,256]{1,0:T(8,128)S(1)} collective-permute-done((f32[512,256]{1,0:T(8,128)S(1)}, f32[512,256]{1,0:T(8,128)S(1)}, u32[]{:S(2)}, u32[]{:S(2)}) %collective-permute-start.6) | collective-permute-done | bytes 524320 | tf_op jit(solution)/shard_map/ppermute | solution.py:14
  31.7 1.8 %collective-permute-start.4 = (f32[512,256]{1,0:T(8,128)S(1)}, f32[512,256]{1,0:T(8,128)S(1)}, u32[]{:S(2)}, u32[]{:S(2)}) collective-permute-start(f32[512,256]{1,0:T(8,128)S(1)} %get-tuple-element.94), channel_id=1, source_target_pairs={{0,4},{4,0},{8,12},{12,8},{1,5},{5,1},{9,13},{13,9},{2,6},{6,2},{1... | collective-permute-start | bytes 1572872 | tf_op jit(solution)/shard_map/ppermute | solution.py:14
  33.5 1.5 %collective-permute-start.5 = (f32[256,256]{1,0:T(8,128)S(1)}, f32[256,256]{1,0:T(8,128)S(1)}, u32[]{:S(2)}, u32[]{:S(2)}) collective-permute-start(f32[256,256]{1,0:T(8,128)S(1)} %shard_map.119.refs_0_), channel_id=1, source_target_pairs={{0,2},{2,0},{1,3},{3,1},{4,6},{6,4},{5,7},{7,5},{8,10},{10,8},{9,1... | collective-permute-start | bytes 786440 | tf_op jit(solution)/shard_map/ppermute | solution.py:14
  36.2 5.8 %collective-permute-done.5.refs_0_ = f32[256,256]{1,0:T(8,128)S(1)} collective-permute-done((f32[256,256]{1,0:T(8,128)S(1)}, f32[256,256]{1,0:T(8,128)S(1)}, u32[]{:S(2)}, u32[]{:S(2)}) %collective-permute-start.5) | collective-permute-done | bytes 262176 | tf_op jit(solution)/shard_map/ppermute | solution.py:14
  42.0 0.7 shard_map.123
  42.7 3.7 %collective-permute-done.4.refs_0_ = f32[512,256]{1,0:T(8,128)S(1)} collective-permute-done((f32[512,256]{1,0:T(8,128)S(1)}, f32[512,256]{1,0:T(8,128)S(1)}, u32[]{:S(2)}, u32[]{:S(2)}) %collective-permute-start.4) | collective-permute-done | bytes 524320 | tf_op jit(solution)/shard_map/ppermute | solution.py:14
  46.4 1.8 %collective-permute-start.13 = (f32[512,256]{1,0:T(8,128)S(1)}, f32[512,256]{1,0:T(8,128)S(1)}, u32[]{:S(2)}, u32[]{:S(2)}) collective-permute-start(f32[512,256]{1,0:T(8,128)S(1)} %get-tuple-element.94), channel_id=1, source_target_pairs={{0,2},{2,0},{1,3},{3,1},{4,6},{6,4},{5,7},{7,5},{8,10},{10,8},{9,1... | collective-permute-start | bytes 1572872 | tf_op jit(solution)/shard_map/ppermute | solution.py:14
  48.8 1.0 shard_map.115.s0
  50.8 12.6 %collective-permute-done.3.s2 = f32[40,768]{1,0:T(8,128)S(1)} collective-permute-done((f32[40,768]{1,0:T(8,128)S(1)}, f32[40,768]{1,0:T(8,128)S(1)}, u32[]{:S(2)}, u32[]{:S(2)}) %collective-permute-start.3) | collective-permute-done | bytes 122912 | tf_op jit(solution)/shard_map/ppermute | solution.py:14
  63.4 1.8 %collective-permute-start.17 = (f32[256,256]{1,0:T(8,128)S(1)}, f32[256,256]{1,0:T(8,128)S(1)}, u32[]{:S(2)}, u32[]{:S(2)}) collective-permute-start(f32[256,256]{1,0:T(8,128)S(1)} %shard_map.119.refs_0_), channel_id=1, source_target_pairs={{0,4},{4,0},{8,12},{12,8},{1,5},{5,1},{9,13},{13,9},{2,6},{6,2},{1... | collective-permute-start | bytes 786440 | tf_op jit(solution)/shard_map/ppermute | solution.py:14
  66.2 1.5 %collective-permute-start.23 = (f32[256,512]{1,0:T(8,128)S(1)}, f32[256,512]{1,0:T(8,128)S(1)}, u32[]{:S(2)}, u32[]{:S(2)}) collective-permute-start(f32[256,512]{1,0:T(8,128)S(1)} %collective-permute-done.7.refs_0_), channel_id=1, source_target_pairs={{0,2},{2,0},{1,3},{3,1},{4,6},{6,4},{5,7},{7,5},{8,10},{10,8},{9,1... | collective-permute-start | bytes 1572872 | tf_op jit(solution)/shard_map/ppermute | solution.py:14
  68.2 6.6 %collective-permute-done.1.s1 = f32[40,768]{1,0:T(8,128)S(1)} collective-permute-done((f32[40,768]{1,0:T(8,128)S(1)}, f32[40,768]{1,0:T(8,128)S(1)}, u32[]{:S(2)}, u32[]{:S(2)}) %collective-permute-start.1) | collective-permute-done | bytes 122912 | tf_op jit(solution)/shard_map/ppermute | solution.py:14
  74.8 1.7 %collective-permute-start.12 = (f32[40,768]{1,0:T(8,128)S(1)}, f32[40,768]{1,0:T(8,128)S(1)}, u32[]{:S(2)}, u32[]{:S(2)}) collective-permute-start(f32[40,768]{1,0:T(8,128)S(1)} %collective-permute-done.1.s1), channel_id=1, source_target_pairs={{0,2},{2,0},{1,3},{3,1},{4,6},{6,4},{5,7},{7,5},{8,10},{10,8},{9,1... | collective-permute-start | bytes 368648 | tf_op jit(solution)/shard_map/ppermute | solution.py:14
  76.5 6.5 %collective-permute-done.12.s3 = f32[40,768]{1,0:T(8,128)S(1)} collective-permute-done((f32[40,768]{1,0:T(8,128)S(1)}, f32[40,768]{1,0:T(8,128)S(1)}, u32[]{:S(2)}, u32[]{:S(2)}) %collective-permute-start.12) | collective-permute-done | bytes 122912 | tf_op jit(solution)/shard_map/ppermute | solution.py:14
  84.1 1.8 %collective-permute-start.26 = (f32[512,256]{1,0:T(8,128)S(1)}, f32[512,256]{1,0:T(8,128)S(1)}, u32[]{:S(2)}, u32[]{:S(2)}) collective-permute-start(f32[512,256]{1,0:T(8,128)S(1)} %collective-permute-done.6.refs_0_), channel_id=1, source_target_pairs={{0,4},{4,0},{8,12},{12,8},{1,5},{5,1},{9,13},{13,9},{2,6},{6,2},{1... | collective-permute-start | bytes 1572872 | tf_op jit(solution)/shard_map/ppermute | solution.py:14
  87.2 5.7 %collective-permute-done.20.refs_0_ = f32[256,256]{1,0:T(8,128)S(1)} collective-permute-done((f32[256,256]{1,0:T(8,128)S(1)}, f32[256,256]{1,0:T(8,128)S(1)}, u32[]{:S(2)}, u32[]{:S(2)}) %collective-permute-start.20) | collective-permute-done | bytes 262176 | tf_op jit(solution)/shard_map/ppermute | solution.py:14
  93.0 1.5 %collective-permute-start.25 = (f32[512,256]{1,0:T(8,128)S(1)}, f32[512,256]{1,0:T(8,128)S(1)}, u32[]{:S(2)}, u32[]{:S(2)}) collective-permute-start(f32[512,256]{1,0:T(8,128)S(1)} %collective-permute-done.4.refs_0_), channel_id=1, source_target_pairs={{0,2},{2,0},{1,3},{3,1},{4,6},{6,4},{5,7},{7,5},{8,10},{10,8},{9,1... | collective-permute-start | bytes 1572872 | tf_op jit(solution)/shard_map/ppermute | solution.py:14
  94.7 1.3 collective-permute-done.22.refs_1_
  96.6 7.1 %collective-permute-done.26.refs_30_ = f32[512,256]{1,0:T(8,128)S(1)} collective-permute-done((f32[512,256]{1,0:T(8,128)S(1)}, f32[512,256]{1,0:T(8,128)S(1)}, u32[]{:S(2)}, u32[]{:S(2)}) %collective-permute-start.26) | collective-permute-done | bytes 524320 | tf_op jit(solution)/shard_map/ppermute | solution.py:14
  104.5 2.8 %collective-permute-done.25.refs_28_ = f32[512,256]{1,0:T(8,128)S(1)} collective-permute-done((f32[512,256]{1,0:T(8,128)S(1)}, f32[512,256]{1,0:T(8,128)S(1)}, u32[]{:S(2)}, u32[]{:S(2)}) %collective-permute-start.25) | collective-permute-done | bytes 524320 | tf_op jit(solution)/shard_map/ppermute | solution.py:14
  107.3 1.9 %collective-permute-done.27.refs_29_ = f32[512,256]{1,0:T(8,128)S(1)} collective-permute-done((f32[512,256]{1,0:T(8,128)S(1)}, f32[512,256]{1,0:T(8,128)S(1)}, u32[]{:S(2)}, u32[]{:S(2)}) %collective-permute-start.27) | collective-permute-done | bytes 524320 | tf_op jit(solution)/shard_map/ppermute | solution.py:14
  109.9 25.6 %shard_map.131 = (f32[32,256]{1,0:T(8,128)}, f32[32,256]{1,0:T(8,128)}) custom-call(s32[4]{0:T(128)S(1)} %pad_add_fusion.place, f32[40,768]{1,0:T(8,128)S(1)} %shard_map.115.s0, f32[40,768]{1,0:T(8,128)S(1)} %collective-permute-done.1.s1, f32[40,768]{1,0:T(8,128)S(1)} %collective-permute-done.3.s2, f32[40,768]{1,0:T(8,128)S(1)} %collective-permute-done.12.s3, ...), custom_call_target="tpu_custom_call" | custom-call | tf_op jit(solution)/shard_map/pallas_call | solution.py:303
  (64 shorter events, 13.0 us)
Async XLA Ops:
  2.4 14.9 %collective-permute-start.2 = (f32[256,512]{1,0:T(8,128)S(1)}, f32[256,512]{1,0:T(8,128)S(1)}, u32[]{:S(2)}, u32[]{:S(2)}) collective-permute-start(f32[256,512]{1,0:T(8,128)S(1)} %get-tuple-element.67), channel_id=1, source_target_pairs={{0,2},{2,0},{1,3},{3,1},{4,6},{6,4},{5,7},{7,5},{8,10},{10,8},{9,1... | collective-permute-start | bytes 1572872 | tf_op jit(solution)/shard_map/ppermute | solution.py:14
  5.4 9.2 %collective-permute-start = (f32[128,512]{1,0:T(8,128)S(1)}, f32[128,512]{1,0:T(8,128)S(1)}, u32[]{:S(2)}, u32[]{:S(2)}) collective-permute-start(f32[128,512]{1,0:T(8,128)S(1)} %get-tuple-element.71.mine), channel_id=1, source_target_pairs={{0,4},{4,0},{8,12},{12,8},{1,5},{5,1},{9,13},{13,9},{2,6},{6,2},{1... | collective-permute-start | bytes 786440 | tf_op jit(solution)/shard_map/ppermute | solution.py:14
  7.0 17.4 %collective-permute-start.7 = (f32[256,512]{1,0:T(8,128)S(1)}, f32[256,512]{1,0:T(8,128)S(1)}, u32[]{:S(2)}, u32[]{:S(2)}) collective-permute-start(f32[256,512]{1,0:T(8,128)S(1)} %get-tuple-element.67), channel_id=1, source_target_pairs={{0,4},{4,0},{8,12},{12,8},{1,5},{5,1},{9,13},{13,9},{2,6},{6,2},{1... | collective-permute-start | bytes 1572872 | tf_op jit(solution)/shard_map/ppermute | solution.py:14
  7.5 7.2 %copy-start.2 = (f32[1,1,256,1024]{3,2,1,0:T(8,128)S(1)}, f32[1,1,256,1024]{3,2,1,0:T(8,128)}, u32[]{:S(2)}) copy-start(f32[1,1,256,1024]{3,2,1,0:T(8,128)} %param.14) | copy-start | bytes 3145732
  9.2 6.9 %copy-start.1 = (f32[1,1,1024,256]{3,2,1,0:T(8,128)S(1)}, f32[1,1,1024,256]{3,2,1,0:T(8,128)}, u32[]{:S(2)}) copy-start(f32[1,1,1024,256]{3,2,1,0:T(8,128)} %param.16) | copy-start | bytes 3145732
  17.3 7.1 %collective-permute-start.9 = (f32[256,512]{1,0:T(8,128)S(1)}, f32[256,512]{1,0:T(8,128)S(1)}, u32[]{:S(2)}, u32[]{:S(2)}) collective-permute-start(f32[256,512]{1,0:T(8,128)S(1)} %collective-permute-done.2.refs_0_), channel_id=1, source_target_pairs={{0,1},{1,0},{2,3},{3,2},{4,5},{5,4},{6,7},{7,6},{8,9},{9,8},{10,11... | collective-permute-start | bytes 1572872 | tf_op jit(solution)/shard_map/ppermute | solution.py:14
  17.4 14.3 %collective-permute-start.6 = (f32[512,256]{1,0:T(8,128)S(1)}, f32[512,256]{1,0:T(8,128)S(1)}, u32[]{:S(2)}, u32[]{:S(2)}) collective-permute-start(f32[512,256]{1,0:T(8,128)S(1)} %get-tuple-element.95), channel_id=1, source_target_pairs={{0,2},{2,0},{1,3},{3,1},{4,6},{6,4},{5,7},{7,5},{8,10},{10,8},{9,1... | collective-permute-start | bytes 1572872 | tf_op jit(solution)/shard_map/ppermute | solution.py:14
  20.3 1.6 %collective-permute-start.8 = (f32[256,256]{1,0:T(8,128)S(1)}, f32[256,256]{1,0:T(8,128)S(1)}, u32[]{:S(2)}, u32[]{:S(2)}) collective-permute-start(f32[256,256]{1,0:T(8,128)S(1)} %shard_map.119.refs_0_), channel_id=1, source_target_pairs={{0,1},{1,0},{2,3},{3,2},{4,5},{5,4},{6,7},{7,6},{8,9},{9,8},{10,11... | collective-permute-start | bytes 786440 | tf_op jit(solution)/shard_map/ppermute | solution.py:14
  24.4 11.0 %collective-permute-start.10 = (f32[256,512]{1,0:T(8,128)S(1)}, f32[256,512]{1,0:T(8,128)S(1)}, u32[]{:S(2)}, u32[]{:S(2)}) collective-permute-start(f32[256,512]{1,0:T(8,128)S(1)} %collective-permute-done.7.refs_0_), channel_id=1, source_target_pairs={{0,1},{1,0},{2,3},{3,2},{4,5},{5,4},{6,7},{7,6},{8,9},{9,8},{10,11... | collective-permute-start | bytes 1572872 | tf_op jit(solution)/shard_map/ppermute | solution.py:14
  31.7 10.3 %collective-permute-start.11 = (f32[512,256]{1,0:T(8,128)S(1)}, f32[512,256]{1,0:T(8,128)S(1)}, u32[]{:S(2)}, u32[]{:S(2)}) collective-permute-start(f32[512,256]{1,0:T(8,128)S(1)} %collective-permute-done.6.refs_0_), channel_id=1, source_target_pairs={{0,1},{1,0},{2,3},{3,2},{4,5},{5,4},{6,7},{7,6},{8,9},{9,8},{10,11... | collective-permute-start | bytes 1572872 | tf_op jit(solution)/shard_map/ppermute | solution.py:14
  31.7 14.7 %collective-permute-start.4 = (f32[512,256]{1,0:T(8,128)S(1)}, f32[512,256]{1,0:T(8,128)S(1)}, u32[]{:S(2)}, u32[]{:S(2)}) collective-permute-start(f32[512,256]{1,0:T(8,128)S(1)} %get-tuple-element.94), channel_id=1, source_target_pairs={{0,4},{4,0},{8,12},{12,8},{1,5},{5,1},{9,13},{13,9},{2,6},{6,2},{1... | collective-permute-start | bytes 1572872 | tf_op jit(solution)/shard_map/ppermute | solution.py:14
  33.5 8.4 %collective-permute-start.5 = (f32[256,256]{1,0:T(8,128)S(1)}, f32[256,256]{1,0:T(8,128)S(1)}, u32[]{:S(2)}, u32[]{:S(2)}) collective-permute-start(f32[256,256]{1,0:T(8,128)S(1)} %shard_map.119.refs_0_), channel_id=1, source_target_pairs={{0,2},{2,0},{1,3},{3,1},{4,6},{6,4},{5,7},{7,5},{8,10},{10,8},{9,1... | collective-permute-start | bytes 786440 | tf_op jit(solution)/shard_map/ppermute | solution.py:14
  35.0 28.4 %collective-permute-start.14 = (f32[512,256]{1,0:T(8,128)S(1)}, f32[512,256]{1,0:T(8,128)S(1)}, u32[]{:S(2)}, u32[]{:S(2)}) collective-permute-start(f32[512,256]{1,0:T(8,128)S(1)} %get-tuple-element.95), channel_id=1, source_target_pairs={{0,4},{4,0},{8,12},{12,8},{1,5},{5,1},{9,13},{13,9},{2,6},{6,2},{1... | collective-permute-start | bytes 1572872 | tf_op jit(solution)/shard_map/ppermute | solution.py:14
  42.0 6.2 %copy-start.5 = (f32[1,1,32,256]{3,2,1,0:T(8,128)S(1)}, f32[1,1,32,256]{3,2,1,0:T(8,128)}, u32[]{:S(2)}) copy-start(f32[1,1,32,256]{3,2,1,0:T(8,128)} %param.11) | copy-start | bytes 98308
  42.0 8.2 %collective-permute-start.15 = (f32[256,256]{1,0:T(8,128)S(1)}, f32[256,256]{1,0:T(8,128)S(1)}, u32[]{:S(2)}, u32[]{:S(2)}) collective-permute-start(f32[256,256]{1,0:T(8,128)S(1)} %collective-permute-done.5.refs_0_), channel_id=1, source_target_pairs={{0,1},{1,0},{2,3},{3,2},{4,5},{5,4},{6,7},{7,6},{8,9},{9,8},{10,11... | collective-permute-start | bytes 786440 | tf_op jit(solution)/shard_map/ppermute | solution.py:14
  46.4 18.8 %collective-permute-start.16 = (f32[512,256]{1,0:T(8,128)S(1)}, f32[512,256]{1,0:T(8,128)S(1)}, u32[]{:S(2)}, u32[]{:S(2)}) collective-permute-start(f32[512,256]{1,0:T(8,128)S(1)} %collective-permute-done.4.refs_0_), channel_id=1, source_target_pairs={{0,1},{1,0},{2,3},{3,2},{4,5},{5,4},{6,7},{7,6},{8,9},{9,8},{10,11... | collective-permute-start | bytes 1572872 | tf_op jit(solution)/shard_map/ppermute | solution.py:14
  46.4 19.5 %collective-permute-start.13 = (f32[512,256]{1,0:T(8,128)S(1)}, f32[512,256]{1,0:T(8,128)S(1)}, u32[]{:S(2)}, u32[]{:S(2)}) collective-permute-start(f32[512,256]{1,0:T(8,128)S(1)} %get-tuple-element.94), channel_id=1, source_target_pairs={{0,2},{2,0},{1,3},{3,1},{4,6},{6,4},{5,7},{7,5},{8,10},{10,8},{9,1... | collective-permute-start | bytes 1572872 | tf_op jit(solution)/shard_map/ppermute | solution.py:14
  49.8 13.6 %collective-permute-start.3 = (f32[40,768]{1,0:T(8,128)S(1)}, f32[40,768]{1,0:T(8,128)S(1)}, u32[]{:S(2)}, u32[]{:S(2)}) collective-permute-start(f32[40,768]{1,0:T(8,128)S(1)} %shard_map.115.s0), channel_id=1, source_target_pairs={{0,2},{2,0},{1,3},{3,1},{4,6},{6,4},{5,7},{7,5},{8,10},{10,8},{9,1... | collective-permute-start | bytes 368648 | tf_op jit(solution)/shard_map/ppermute | solution.py:14
  63.4 19.6 %collective-permute-start.18 = (f32[512,256]{1,0:T(8,128)S(1)}, f32[512,256]{1,0:T(8,128)S(1)}, u32[]{:S(2)}, u32[]{:S(2)}) collective-permute-start(f32[512,256]{1,0:T(8,128)S(1)} %collective-permute-done.14.refs_0_), channel_id=1, source_target_pairs={{0,1},{1,0},{2,3},{3,2},{4,5},{5,4},{6,7},{7,6},{8,9},{9,8},{10,11... | collective-permute-start | bytes 1572872 | tf_op jit(solution)/shard_map/ppermute | solution.py:14
  63.4 20.3 %collective-permute-start.17 = (f32[256,256]{1,0:T(8,128)S(1)}, f32[256,256]{1,0:T(8,128)S(1)}, u32[]{:S(2)}, u32[]{:S(2)}) collective-permute-start(f32[256,256]{1,0:T(8,128)S(1)} %shard_map.119.refs_0_), channel_id=1, source_target_pairs={{0,4},{4,0},{8,12},{12,8},{1,5},{5,1},{9,13},{13,9},{2,6},{6,2},{1... | collective-permute-start | bytes 786440 | tf_op jit(solution)/shard_map/ppermute | solution.py:14
  65.9 20.6 %collective-permute-start.21 = (f32[512,256]{1,0:T(8,128)S(1)}, f32[512,256]{1,0:T(8,128)S(1)}, u32[]{:S(2)}, u32[]{:S(2)}) collective-permute-start(f32[512,256]{1,0:T(8,128)S(1)} %collective-permute-done.13.refs_0_), channel_id=1, source_target_pairs={{0,1},{1,0},{2,3},{3,2},{4,5},{5,4},{6,7},{7,6},{8,9},{9,8},{10,11... | collective-permute-start | bytes 1572872 | tf_op jit(solution)/shard_map/ppermute | solution.py:14
  66.2 26.7 %collective-permute-start.23 = (f32[256,512]{1,0:T(8,128)S(1)}, f32[256,512]{1,0:T(8,128)S(1)}, u32[]{:S(2)}, u32[]{:S(2)}) collective-permute-start(f32[256,512]{1,0:T(8,128)S(1)} %collective-permute-done.7.refs_0_), channel_id=1, source_target_pairs={{0,2},{2,0},{1,3},{3,1},{4,6},{6,4},{5,7},{7,5},{8,10},{10,8},{9,1... | collective-permute-start | bytes 1572872 | tf_op jit(solution)/shard_map/ppermute | solution.py:14
  67.7 7.1 %collective-permute-start.1 = (f32[40,768]{1,0:T(8,128)S(1)}, f32[40,768]{1,0:T(8,128)S(1)}, u32[]{:S(2)}, u32[]{:S(2)}) collective-permute-start(f32[40,768]{1,0:T(8,128)S(1)} %shard_map.115.s0), channel_id=1, source_target_pairs={{0,4},{4,0},{8,12},{12,8},{1,5},{5,1},{9,13},{13,9},{2,6},{6,2},{1... | collective-permute-start | bytes 368648 | tf_op jit(solution)/shard_map/ppermute | solution.py:14
  74.8 8.2 %collective-permute-start.12 = (f32[40,768]{1,0:T(8,128)S(1)}, f32[40,768]{1,0:T(8,128)S(1)}, u32[]{:S(2)}, u32[]{:S(2)}) collective-permute-start(f32[40,768]{1,0:T(8,128)S(1)} %collective-permute-done.1.s1), channel_id=1, source_target_pairs={{0,2},{2,0},{1,3},{3,1},{4,6},{6,4},{5,7},{7,5},{8,10},{10,8},{9,1... | collective-permute-start | bytes 368648 | tf_op jit(solution)/shard_map/ppermute | solution.py:14
  83.7 2.2 %collective-permute-start.19 = (f32[256,256]{1,0:T(8,128)S(1)}, f32[256,256]{1,0:T(8,128)S(1)}, u32[]{:S(2)}, u32[]{:S(2)}) collective-permute-start(f32[256,256]{1,0:T(8,128)S(1)} %collective-permute-done.17.refs_0_), channel_id=1, source_target_pairs={{0,1},{1,0},{2,3},{3,2},{4,5},{5,4},{6,7},{7,6},{8,9},{9,8},{10,11... | collective-permute-start | bytes 786440 | tf_op jit(solution)/shard_map/ppermute | solution.py:14
  83.8 9.2 %collective-permute-start.20 = (f32[256,256]{1,0:T(8,128)S(1)}, f32[256,256]{1,0:T(8,128)S(1)}, u32[]{:S(2)}, u32[]{:S(2)}) collective-permute-start(f32[256,256]{1,0:T(8,128)S(1)} %collective-permute-done.5.refs_0_), channel_id=1, source_target_pairs={{0,4},{4,0},{8,12},{12,8},{1,5},{5,1},{9,13},{13,9},{2,6},{6,2},{1... | collective-permute-start | bytes 786440 | tf_op jit(solution)/shard_map/ppermute | solution.py:14
  84.1 19.7 %collective-permute-start.26 = (f32[512,256]{1,0:T(8,128)S(1)}, f32[512,256]{1,0:T(8,128)S(1)}, u32[]{:S(2)}, u32[]{:S(2)}) collective-permute-start(f32[512,256]{1,0:T(8,128)S(1)} %collective-permute-done.6.refs_0_), channel_id=1, source_target_pairs={{0,4},{4,0},{8,12},{12,8},{1,5},{5,1},{9,13},{13,9},{2,6},{6,2},{1... | collective-permute-start | bytes 1572872 | tf_op jit(solution)/shard_map/ppermute | solution.py:14
  93.0 10.8 %collective-permute-start.24 = (f32[256,512]{1,0:T(8,128)S(1)}, f32[256,512]{1,0:T(8,128)S(1)}, u32[]{:S(2)}, u32[]{:S(2)}) collective-permute-start(f32[256,512]{1,0:T(8,128)S(1)} %collective-permute-done.23.refs_0_), channel_id=1, source_target_pairs={{0,1},{1,0},{2,3},{3,2},{4,5},{5,4},{6,7},{7,6},{8,9},{9,8},{10,11... | collective-permute-start | bytes 1572872 | tf_op jit(solution)/shard_map/ppermute | solution.py:14
  93.0 14.3 %collective-permute-start.25 = (f32[512,256]{1,0:T(8,128)S(1)}, f32[512,256]{1,0:T(8,128)S(1)}, u32[]{:S(2)}, u32[]{:S(2)}) collective-permute-start(f32[512,256]{1,0:T(8,128)S(1)} %collective-permute-done.4.refs_0_), channel_id=1, source_target_pairs={{0,2},{2,0},{1,3},{3,1},{4,6},{6,4},{5,7},{7,5},{8,10},{10,8},{9,1... | collective-permute-start | bytes 1572872 | tf_op jit(solution)/shard_map/ppermute | solution.py:14
  94.5 1.5 %collective-permute-start.22 = (f32[256,256]{1,0:T(8,128)S(1)}, f32[256,256]{1,0:T(8,128)S(1)}, u32[]{:S(2)}, u32[]{:S(2)}) collective-permute-start(f32[256,256]{1,0:T(8,128)S(1)} %collective-permute-done.20.refs_0_), channel_id=1, source_target_pairs={{0,1},{1,0},{2,3},{3,2},{4,5},{5,4},{6,7},{7,6},{8,9},{9,8},{10,11... | collective-permute-start | bytes 786440 | tf_op jit(solution)/shard_map/ppermute | solution.py:14
  103.7 3.6 %collective-permute-start.28 = (f32[512,256]{1,0:T(8,128)S(1)}, f32[512,256]{1,0:T(8,128)S(1)}, u32[]{:S(2)}, u32[]{:S(2)}) collective-permute-start(f32[512,256]{1,0:T(8,128)S(1)} %collective-permute-done.26.refs_30_), channel_id=1, source_target_pairs={{0,1},{1,0},{2,3},{3,2},{4,5},{5,4},{6,7},{7,6},{8,9},{9,8},{10,11... | collective-permute-start | bytes 1572872 | tf_op jit(solution)/shard_map/ppermute | solution.py:14
  107.3 1.9 %collective-permute-start.27 = (f32[512,256]{1,0:T(8,128)S(1)}, f32[512,256]{1,0:T(8,128)S(1)}, u32[]{:S(2)}, u32[]{:S(2)}) collective-permute-start(f32[512,256]{1,0:T(8,128)S(1)} %collective-permute-done.25.refs_28_), channel_id=1, source_target_pairs={{0,1},{1,0},{2,3},{3,2},{4,5},{5,4},{6,7},{7,6},{8,9},{9,8},{10,11... | collective-permute-start | bytes 1572872 | tf_op jit(solution)/shard_map/ppermute | solution.py:14
  (6 other events, 17.4 us)

commit v4 on v3

--- a/solution.py
+++ b/solution.py
@@ -31,6 +31,9 @@
     high, low = halves_of(value)
     high_ref[where] = high
     low_ref[where] = low
+
+
+CHEAP = pl.CostEstimate(flops=1, transcendentals=0, bytes_accessed=1)
 
 
 def cut_kernel(place, *refs):
@@ -58,6 +61,7 @@
         out_specs=[pl.BlockSpec(memory_space=pl.ANY)] * len(panels),
         out_shape=[jax.ShapeDtypeStruct(shape, F32) for shape in shapes],
         scratch_shapes=[pltpu.SemaphoreType.DMA((len(panels),))],
+        cost_estimate=CHEAP,
         compiler_params=pltpu.CompilerParams(vmem_limit_bytes=2**20),
     )(place, *hbm)
 
@@ -68,23 +72,19 @@
     return jnp.sum(jnp.where(same, row, 0.0), axis=1, keepdims=True)
 
 
-def state_kernel(place, cells, one, two, pair_cols, mass, state_ref):
+def edge_state_kernel(place, mine, other, pair_cols, cells, one, two, mass, edge_ref):
+    half = mine.shape[0]
     rows, width = one.shape
+    for step, couple in enumerate((mine, other)):
+        start = ((place[0] % 2) ^ step) * half
+        edge_ref[pl.ds(pl.multiple_of(start, half), half), :] = exact_dot(couple[...], pair_cols[...])
     cell = column_of(cells[...].astype(F32))
     number = lax.broadcasted_iota(jnp.int32, (rows, width), 1)
     chosen = [(cell == (number + place[2 + side]).astype(F32)).astype(F32) for side in range(2)]
-    state_ref[:rows, :width] = one[...]
-    state_ref[:rows, width:2 * width] = two[...]
-    state_ref[:rows, 2 * width:] = exact_dot(jnp.concatenate(chosen, axis=1), pair_cols[...])
-    state_ref[rows:, :width] = jnp.broadcast_to(mass[...], (8, width))
-    state_ref[rows:, width:] = jnp.zeros((8, 2 * width), F32)
-
-
-def panel_kernel(place, mine, other, pair_cols, panel_ref):
-    rows = mine.shape[0]
-    for step, couple in enumerate((mine, other)):
-        start = ((place[0] % 2) ^ step) * rows
-        panel_ref[pl.ds(pl.multiple_of(start, rows), rows), :] = exact_dot(couple[...], pair_cols[...])
+    picked = exact_dot(jnp.concatenate(chosen, axis=1), pair_cols[...])
+    for index, value in enumerate((one[...], two[...], picked)):
+        edge_ref[2 * half + index * rows:2 * half + (index + 1) * rows, :] = value
+    edge_ref[2 * half + 3 * rows:, :] = jnp.broadcast_to(mass[...], (8, width))
 
 
 def small_call(kernel, shape, *values):
@@ -94,6 +94,7 @@
         in_specs=[pl.BlockSpec(memory_space=pltpu.SMEM)] + [vmem] * (len(values) - 1),
         out_specs=vmem,
         out_shape=jax.ShapeDtypeStruct(shape, F32),
+        cost_estimate=CHEAP,
         compiler_params=pltpu.CompilerParams(vmem_limit_bytes=6 * 2**20),
     )(*values)
 
@@ -125,7 +126,7 @@
 
 def edge_kernel(place, *refs):
     pieces, (high_ref, low_ref) = refs[:-2], refs[-2:]
-    rows = pieces[0].shape[0] // 2
+    rows = pieces[0].shape[1] // 2
     for part, piece in enumerate(pieces):
         for bit in range(2):
             start = (bit ^ (place[0] % 2)) * 2 * rows + (place[1] ^ part) * rows
@@ -143,6 +144,7 @@
         in_specs=[pl.BlockSpec(memory_space=pltpu.SMEM)] + [vmem] * len(pieces),
         out_specs=(vmem, vmem),
         out_shape=(pltpu.VMEM(out.shape, BF16),) * 2,
+        cost_estimate=CHEAP,
         compiler_params=pltpu.CompilerParams(vmem_limit_bytes=4 * 2**20),
     )(place, *pieces)
 
@@ -155,15 +157,16 @@
     return both[:rows] + both[rows:] + rest
 
 
-def march_kernel(place, s0, s1, s2, s3, weight, *refs):
+def march_kernel(s0, s1, s2, s3, weight, place, *refs):
     edge, lift, root, back = refs[:8], refs[8:16], refs[16:22], refs[22:28]
     r_mine, r_other, b_mine, b_other, one_ref, two_ref, last_rh, last_rl, last_bh, last_bl = refs[28:]
     rows, width = one_ref.shape
-    states = (s0, s1, s2, s3)
-    one = jnp.concatenate([state[:rows, :width] for state in states], axis=1)
-    two = jnp.concatenate([state[:rows, width:2 * width] for state in states], axis=1)
-    picked = jnp.concatenate([state[:rows, 2 * width:] for state in states], axis=1)
-    scale = jnp.concatenate([state[rows:rows + 1, :width] for state in states], axis=1)
+
+    def below(index, count):
+        start = width + index * rows
+        return jnp.concatenate([tile[start:start + count, :] for tile in (s0, s1, s2, s3)], axis=1)
+
+    one, two, picked, scale = below(0, rows), below(1, rows), below(2, rows), below(3, 1)
     split_tall(place, (r_mine, r_other), last_rh, last_rl)
     split_tall(place, (b_mine, b_other), last_bh, last_bl)
     root = root + (last_rh, last_rl)
@@ -219,81 +222,54 @@
     first_cell = ((column - x_bit) * lax.axis_size("gy") + row) * width
     place = jnp.stack([2 * y_bit + x_bit, core, first_cell, first_cell + lax.axis_size("gy") * width]).astype(jnp.int32)
 
+    def split(kernel, size, value):
+        return split_call(kernel, place, size, value, from_partner(value, "gz"))
+
+    tall, wide, edge = (tall_kernel, 4 * width), (wide_kernel, 4 * width), (edge_kernel, 2 * width)
+
     couple_mine, lift_half = cut_call(place, (couple, lift), ((width // 2, 2 * width), (width, 2 * width)))
+    back_half, root_half = cut_call(after(place, lift_half), (back, root), ((2 * width, width),) * 2)
     couple_other = from_partner(couple_mine, "gx")
     lift_y = from_partner(lift_half, "gy")
-    root_half, back_half = cut_call(after(place, lift_half), (root, back), ((2 * width, width),) * 2)
     lift_x = from_partner(lift_half, "gx")
     back_y = from_partner(back_half, "gy")
-
-    cells = probe_cells[None, :]
-    state = small_call(
-        state_kernel,
-        (rows + 8, 3 * width),
-        after(place, root_half),
-        cells,
+    lift_own = split_call(wide_kernel, place, wide[1], after(lift, root_half))
+    root_own = split_call(tall_kernel, place, tall[1], after(root, root_half))
+    back_own = split_call(tall_kernel, place, tall[1], after(back, root_half))
+    edge_half = small_call(
+        edge_state_kernel,
+        (width + 3 * rows + 8, width),
+        after(place, lift_own[0], root_own[0], back_own[0]),
+        couple_mine,
+        couple_other,
+        pair_cols,
+        probe_cells[None, :],
         adjoint_one_start[0, 0],
         adjoint_two_start[0, 0],
-        pair_cols,
         mass_two[0],
     )
-    edge_half = small_call(panel_kernel, (width, width), place, couple_mine, couple_other, pair_cols)
-
-    token = [couple_other]
-
-    def arrive(value, *done):
-        value = after(value, token[0], *done)
-        token[0] = value
-        return value
-
-    def send(value, axis):
-        return from_partner(after(value, token[0]), axis)
-
-    def split(kernel, rows, value):
-        return split_call(kernel, place, rows, value, from_partner(value, "gz"))
-
-    tall, wide, edge = (tall_kernel, 4 * width), (wide_kernel, 4 * width), (edge_kernel, 2 * width)
-    lift_own = split_call(wide_kernel, place, wide[1], after(lift, couple_other))
-    root_own = split_call(tall_kernel, place, tall[1], after(root, couple_other))
-    back_own = split_call(tall_kernel, place, tall[1], after(back, couple_other))
-
-    state_x = send(state, "gx")
-    root_x = send(root_half, "gx")
-    lift_y = arrive(lift_y, lift_own[0], root_own[0], back_own[0])
+    root_x = from_partner(after(root_half, couple_other), "gx")
+    edge_y = from_partner(after(edge_half, lift_y), "gy")
     edge_own = split(*edge, edge_half)
-    edge_y = send(edge_half, "gy")
-    state_y = send(state, "gy")
-    lift_x = arrive(lift_x, edge_own[0])
+    back_x = from_partner(after(back_half, lift_x, edge_own[0]), "gx")
     lift_y_split = split(*wide, lift_y)
-    back_x = send(back_half, "gx")
-    back_y = arrive(back_y, lift_y_split[0])
+    root_y = from_partner(after(root_half, back_y, lift_y_split[0]), "gy")
     lift_x_split = split(*wide, lift_x)
-    root_y = send(root_half, "gy")
-    edge_y = arrive(edge_y, lift_x_split[0])
+    edge_x = from_partner(after(edge_half, root_x, lift_x_split[0]), "gx")
     back_y_split = split(*tall, back_y)
-    root_x = arrive(root_x, back_y_split[0])
+    lift_d = from_partner(after(lift_x, edge_y, back_y_split[0]), "gy")
     edge_y_split = split(*edge, edge_y)
-    edge_x = send(edge_half, "gx")
-    state_y = arrive(state_y)
-    state_d = send(state_x, "gy")
-    back_x = arrive(back_x, edge_y_split[0])
+    edge_d = from_partner(after(edge_y, back_x, edge_y_split[0]), "gx")
     root_x_split = split(*tall, root_x)
-    edge_d = send(edge_y, "gx")
-    root_y = arrive(root_y, root_x_split[0])
-    lift_d = send(lift_x, "gy")
+    root_d = from_partner(after(root_x, root_y, root_x_split[0]), "gy")
+    root_y_split = split(*tall, root_y)
+    back_d = from_partner(after(back_y, edge_x, root_y_split[0]), "gx")
     back_x_split = split(*tall, back_x)
-    state_d = arrive(state_d)
-    root_d = send(root_x, "gy")
-    edge_x = arrive(edge_x, back_x_split[0])
-    root_y_split = split(*tall, root_y)
-    back_d = send(back_y, "gx")
-    edge_d = arrive(edge_d, root_y_split[0])
     edge_x_split = split(*edge, edge_x)
-    lift_d = arrive(lift_d, edge_x_split[0])
+    lift_d_split = split(*wide, lift_d)
     edge_d_split = split(*edge, edge_d)
-    back_d = arrive(back_d, edge_d_split[0])
-    lift_d_split = split(*wide, lift_d)
-    root_d = arrive(root_d, lift_d_split[0])
+    back_d = after(back_d, back_x_split[0], edge_x_split[0])
+    root_d = after(root_d, lift_d_split[0], edge_d_split[0])
 
     vmem = pl.BlockSpec(memory_space=pltpu.VMEM)
     panels = edge_own + edge_x_split + edge_y_split + edge_d_split + lift_own + lift_x_split + lift_y_split + lift_d_split
@@ -302,12 +278,12 @@
     panels += (root_d, from_partner(root_d, "gz"), back_d, from_partner(back_d, "gz"))
     one, two = pl.pallas_call(
         march_kernel,
-        in_specs=[pl.BlockSpec(memory_space=pltpu.SMEM)] + [vmem] * (5 + len(panels)),
+        in_specs=[vmem] * 5 + [pl.BlockSpec(memory_space=pltpu.SMEM)] + [vmem] * len(panels),
         out_specs=(vmem, vmem),
         out_shape=(jax.ShapeDtypeStruct((rows, width), F32),) * 2,
         scratch_shapes=[pltpu.VMEM((4 * width, width), BF16)] * 4,
         compiler_params=pltpu.CompilerParams(vmem_limit_bytes=12 * 2**20),
-    )(place, state, state_x, state_y, state_d, probe_weight, *panels)
+    )(edge_half, edge_x, edge_y, edge_d, probe_weight, place, *panels)
     return (one[None, None], two[None, None])
 
 

time: 136 us -> 111 us (0.82)
  waiting for transfers between devices: 69.9 us -> 47.3 us
  starting transfers between devices: 22.5 us -> 20.7 us
    ppermute x29 -> x26, waiting for transfers between devices: 69.9 us -> 47.3 us  [from_partner(): return lax.ppermute(value, axis, pairs)]
    ppermute x29 -> x26, starting transfers between devices: 22.5 us -> 20.7 us  [from_partner(): return lax.ppermute(value, axis, pairs)]
  transfers between devices with their start and end apart: 29 -> 26, of which waited for: 15 -> 11; matrix products, arithmetic and copies ran while one was open for 0% -> 0% of each run, Pallas kernels for 10% -> 12%
where the time goes in v4:
time: 111 us; the launch traced here: 110 us
  waiting for transfers between devices  47.3 us (43%)
  Pallas kernels  40 us (36%)
  starting transfers between devices  20.7 us (19%)
  local copies, waits for them, and re-layouts  1.39 us (1%)
    ppermute x26, waiting for transfers between devices, from_partner(): return lax.ppermute(value, axis, pairs)  47.3 us
    pallas_call x1, Pallas kernels, shards(): pl.pallas_call(march_kernel, in_specs=[vmem] * 5 + [pl.BlockSpec(memory_s...  25.6 us
    ppermute x26, starting transfers between devices, from_partner(): return lax.ppermute(value, axis, pairs)  20.7 us
    pallas_call x14, Pallas kernels, split_call(): pl.pallas_call(kernel, in_specs=[pl.BlockSpec(memory_space=pltpu.SMEM)] +...  9.5 us
    pallas_call x2, Pallas kernels, cut_call(): pl.pallas_call(cut_kernel, in_specs=[pl.BlockSpec(memory_space=pltpu.SMEM...  3.45 us
  transfers between devices with their start and end apart: 26, of which 11 were waited for; matrix products, arithmetic and copies ran while one was open for 0% of the time, Pallas kernels for 12%

profile of v4, /device:TPU:0, one launch (start us, length us, event | category | flops | bytes accessed | tf_op | source)
XLA Modules:
  0.0 110.4 jit_solution(4151448030770508285)
XLA Ops:
  0.7 1.7 %shard_map.113 = (f32[128,512]{1,0:T(8,128)S(1)}, f32[256,512]{1,0:T(8,128)S(1)}) custom-call(s32[4]{0:T(128)S(1)} %pad_add_fusion.place, f32[256,512]{1,0:T(8,128)} %bitcast.26, f32[256,1024]{1,0:T(8,128)} %bitcast.19), custom_call_target="tpu_custom_call" | custom-call | flops 1 | bytes 1 | tf_op jit(solution)/shard_map/pallas_call | solution.py:58
  2.4 3.0 %collective-permute-start.5 = (f32[256,512]{1,0:T(8,128)S(1)}, f32[256,512]{1,0:T(8,128)S(1)}, u32[]{:S(2)}, u32[]{:S(2)}) collective-permute-start(f32[256,512]{1,0:T(8,128)S(1)} %get-tuple-element.52), channel_id=1, source_target_pairs={{0,2},{2,0},{1,3},{3,1},{4,6},{6,4},{5,7},{7,5},{8,10},{10,8},{9,1... | collective-permute-start | bytes 1572872 | tf_op jit(solution)/shard_map/ppermute | solution.py:14
  5.4 1.8 %shard_map.114 = (f32[512,256]{1,0:T(8,128)S(1)}, f32[512,256]{1,0:T(8,128)S(1)}) custom-call(s32[4]{0:T(128)S(1)} %pad_add_fusion.place, f32[1024,256]{1,0:T(8,128)} %bitcast.17, f32[1024,256]{1,0:T(8,128)} %bitcast.15), custom_call_target="tpu_custom_call" | custom-call | flops 1 | bytes 1 | tf_op jit(solution)/shard_map/pallas_call | solution.py:58
  7.3 2.1 %collective-permute-start = (f32[128,512]{1,0:T(8,128)S(1)}, f32[128,512]{1,0:T(8,128)S(1)}, u32[]{:S(2)}, u32[]{:S(2)}) collective-permute-start(f32[128,512]{1,0:T(8,128)S(1)} %get-tuple-element.62.mine), channel_id=1, source_target_pairs={{0,4},{4,0},{8,12},{12,8},{1,5},{5,1},{9,13},{13,9},{2,6},{6,2},{1... | collective-permute-start | bytes 786440 | tf_op jit(solution)/shard_map/ppermute | solution.py:14
  9.4 8.8 %collective-permute-done.5.refs_0_ = f32[256,512]{1,0:T(8,128)S(1)} collective-permute-done((f32[256,512]{1,0:T(8,128)S(1)}, f32[256,512]{1,0:T(8,128)S(1)}, u32[]{:S(2)}, u32[]{:S(2)}) %collective-permute-start.5) | collective-permute-done | bytes 524320 | tf_op jit(solution)/shard_map/ppermute | solution.py:14
  18.2 0.7 shard_map.115
  18.9 0.7 shard_map.116
  19.7 0.7 shard_map.117
  20.4 2.2 %collective-permute-start.1 = (f32[512,256]{1,0:T(8,128)S(1)}, f32[512,256]{1,0:T(8,128)S(1)}, u32[]{:S(2)}, u32[]{:S(2)}) collective-permute-start(f32[512,256]{1,0:T(8,128)S(1)} %get-tuple-element.89), channel_id=1, source_target_pairs={{0,4},{4,0},{8,12},{12,8},{1,5},{5,1},{9,13},{13,9},{2,6},{6,2},{1... | collective-permute-start | bytes 1572872 | tf_op jit(solution)/shard_map/ppermute | solution.py:14
  23.3 1.5 %shard_map.118.refs_0_.s0 = f32[360,256]{1,0:T(8,128)S(1)} custom-call(s32[4]{0:T(128)S(1)} %pad_add_fusion.place, f32[128,512]{1,0:T(8,128)S(1)} %get-tuple-element.62.mine, f32[128,512]{1,0:T(8,128)S(1)} %collective-permute-done.other, f32[512,256]{1,0:T(8,128)S(1)} %bitcast.21, s32[1,32]{1,0:T(1,128)S(1)} %bitcast.25, f32[32,256]{1,0:T(8,128)S(1)} %bitcast.22, ...), custom_call_target="tpu_custom_call" | custom-call | flops 1 | bytes 1 | tf_op jit(solution)/shard_map/pallas_call | solution.py:92
  25.1 3.5 %collective-permute-done.14.refs_0_ = f32[512,256]{1,0:T(8,128)S(1)} collective-permute-done((f32[512,256]{1,0:T(8,128)S(1)}, f32[512,256]{1,0:T(8,128)S(1)}, u32[]{:S(2)}, u32[]{:S(2)}) %collective-permute-start.14) | collective-permute-done | bytes 524320 | tf_op jit(solution)/shard_map/ppermute | solution.py:14
  28.6 1.7 %collective-permute-start.6 = (f32[360,256]{1,0:T(8,128)S(1)}, f32[360,256]{1,0:T(8,128)S(1)}, u32[]{:S(2)}, u32[]{:S(2)}) collective-permute-start(f32[360,256]{1,0:T(8,128)S(1)} %shard_map.118.refs_0_.s0), channel_id=1, source_target_pairs={{0,2},{2,0},{1,3},{3,1},{4,6},{6,4},{5,7},{7,5},{8,10},{10,8},{9,1... | collective-permute-start | bytes 1105928 | tf_op jit(solution)/shard_map/ppermute | solution.py:14
  30.6 0.7 shard_map.124
  32.3 5.3 %collective-permute-done.1.refs_0_ = f32[512,256]{1,0:T(8,128)S(1)} collective-permute-done((f32[512,256]{1,0:T(8,128)S(1)}, f32[512,256]{1,0:T(8,128)S(1)}, u32[]{:S(2)}, u32[]{:S(2)}) %collective-permute-start.1) | collective-permute-done | bytes 524320 | tf_op jit(solution)/shard_map/ppermute | solution.py:14
  37.6 1.7 %collective-permute-start.8 = (f32[512,256]{1,0:T(8,128)S(1)}, f32[512,256]{1,0:T(8,128)S(1)}, u32[]{:S(2)}, u32[]{:S(2)}) collective-permute-start(f32[512,256]{1,0:T(8,128)S(1)} %get-tuple-element.69), channel_id=1, source_target_pairs={{0,4},{4,0},{8,12},{12,8},{1,5},{5,1},{9,13},{13,9},{2,6},{6,2},{1... | collective-permute-start | bytes 1572872 | tf_op jit(solution)/shard_map/ppermute | solution.py:14
  40.5 0.7 shard_map.125
  41.2 1.8 %collective-permute-start.16 = (f32[256,512]{1,0:T(8,128)S(1)}, f32[256,512]{1,0:T(8,128)S(1)}, u32[]{:S(2)}, u32[]{:S(2)}) collective-permute-start(f32[256,512]{1,0:T(8,128)S(1)} %collective-permute-done.2.refs_0_), channel_id=1, source_target_pairs={{0,2},{2,0},{1,3},{3,1},{4,6},{6,4},{5,7},{7,5},{8,10},{10,8},{9,1... | collective-permute-start | bytes 1572872 | tf_op jit(solution)/shard_map/ppermute | solution.py:14
  43.0 8.2 %collective-permute-done.19.refs_0_ = f32[512,256]{1,0:T(8,128)S(1)} collective-permute-done((f32[512,256]{1,0:T(8,128)S(1)}, f32[512,256]{1,0:T(8,128)S(1)}, u32[]{:S(2)}, u32[]{:S(2)}) %collective-permute-start.19) | collective-permute-done | bytes 524320 | tf_op jit(solution)/shard_map/ppermute | solution.py:14
  51.7 0.7 shard_map.119
  52.4 1.9 %collective-permute-start.4 = (f32[360,256]{1,0:T(8,128)S(1)}, f32[360,256]{1,0:T(8,128)S(1)}, u32[]{:S(2)}, u32[]{:S(2)}) collective-permute-start(f32[360,256]{1,0:T(8,128)S(1)} %shard_map.118.refs_0_.s0), channel_id=1, source_target_pairs={{0,4},{4,0},{8,12},{12,8},{1,5},{5,1},{9,13},{13,9},{2,6},{6,2},{1... | collective-permute-start | bytes 1105928 | tf_op jit(solution)/shard_map/ppermute | solution.py:14
  55.2 0.7 shard_map.127
  55.9 6.1 %collective-permute-done.16.refs_0_ = f32[256,512]{1,0:T(8,128)S(1)} collective-permute-done((f32[256,512]{1,0:T(8,128)S(1)}, f32[256,512]{1,0:T(8,128)S(1)}, u32[]{:S(2)}, u32[]{:S(2)}) %collective-permute-start.16) | collective-permute-done | bytes 524320 | tf_op jit(solution)/shard_map/ppermute | solution.py:14
  62.1 1.7 %collective-permute-start.22 = (f32[512,256]{1,0:T(8,128)S(1)}, f32[512,256]{1,0:T(8,128)S(1)}, u32[]{:S(2)}, u32[]{:S(2)}) collective-permute-start(f32[512,256]{1,0:T(8,128)S(1)} %collective-permute-done.1.refs_0_), channel_id=1, source_target_pairs={{0,2},{2,0},{1,3},{3,1},{4,6},{6,4},{5,7},{7,5},{8,10},{10,8},{9,1... | collective-permute-start | bytes 1572872 | tf_op jit(solution)/shard_map/ppermute | solution.py:14
  63.8 0.7 shard_map.128
  64.5 1.6 %collective-permute-start.24 = (f32[512,256]{1,0:T(8,128)S(1)}, f32[512,256]{1,0:T(8,128)S(1)}, u32[]{:S(2)}, u32[]{:S(2)}) collective-permute-start(f32[512,256]{1,0:T(8,128)S(1)} %collective-permute-done.14.refs_0_), channel_id=1, source_target_pairs={{0,4},{4,0},{8,12},{12,8},{1,5},{5,1},{9,13},{13,9},{2,6},{6,2},{1... | collective-permute-start | bytes 1572872 | tf_op jit(solution)/shard_map/ppermute | solution.py:14
  66.2 5.7 %collective-permute-done.10.refs_0_.s3 = f32[360,256]{1,0:T(8,128)S(1)} collective-permute-done((f32[360,256]{1,0:T(8,128)S(1)}, f32[360,256]{1,0:T(8,128)S(1)}, u32[]{:S(2)}, u32[]{:S(2)}) %collective-permute-start.10) | collective-permute-done | bytes 368672 | tf_op jit(solution)/shard_map/ppermute | solution.py:14
  72.4 0.7 shard_map.129
  74.8 0.7 shard_map.126
  75.5 0.9 collective-permute-done.22.refs_28_
  76.4 5.8 %collective-permute-done.24.refs_30_ = f32[512,256]{1,0:T(8,128)S(1)} collective-permute-done((f32[512,256]{1,0:T(8,128)S(1)}, f32[512,256]{1,0:T(8,128)S(1)}, u32[]{:S(2)}, u32[]{:S(2)}) %collective-permute-start.24) | collective-permute-done | bytes 524320 | tf_op jit(solution)/shard_map/ppermute | solution.py:14
  82.2 1.9 %collective-permute-done.25.refs_31_ = f32[512,256]{1,0:T(8,128)S(1)} collective-permute-done((f32[512,256]{1,0:T(8,128)S(1)}, f32[512,256]{1,0:T(8,128)S(1)}, u32[]{:S(2)}, u32[]{:S(2)}) %collective-permute-start.25) | collective-permute-done | bytes 524320 | tf_op jit(solution)/shard_map/ppermute | solution.py:14
  84.8 25.6 %shard_map.130 = (f32[32,256]{1,0:T(8,128)}, f32[32,256]{1,0:T(8,128)}) custom-call(f32[360,256]{1,0:T(8,128)S(1)} %shard_map.118.refs_0_.s0, f32[360,256]{1,0:T(8,128)S(1)} %collective-permute-done.4.refs_0_.s1, f32[360,256]{1,0:T(8,128)S(1)} %collective-permute-done.6.refs_0_.s2, f32[360,256]{1,0:T(8,128)S(1)} %collective-permute-done.10.refs_0_.s3, ...), custom_call_target="tpu_custom_call" | custom-call | tf_op jit(solution)/shard_map/pallas_call | solution.py:279
  (57 shorter events, 7.9 us)
Async XLA Ops:
  2.4 15.8 %collective-permute-start.5 = (f32[256,512]{1,0:T(8,128)S(1)}, f32[256,512]{1,0:T(8,128)S(1)}, u32[]{:S(2)}, u32[]{:S(2)}) collective-permute-start(f32[256,512]{1,0:T(8,128)S(1)} %get-tuple-element.52), channel_id=1, source_target_pairs={{0,2},{2,0},{1,3},{3,1},{4,6},{6,4},{5,7},{7,5},{8,10},{10,8},{9,1... | collective-permute-start | bytes 1572872 | tf_op jit(solution)/shard_map/ppermute | solution.py:14
  5.4 12.8 %copy-start.2 = (f32[1,1,256,1024]{3,2,1,0:T(8,128)S(1)}, f32[1,1,256,1024]{3,2,1,0:T(8,128)}, u32[]{:S(2)}) copy-start(f32[1,1,256,1024]{3,2,1,0:T(8,128)} %param.14) | copy-start | bytes 3145732
  7.2 11.7 %copy-start = (f32[1,1,1024,256]{3,2,1,0:T(8,128)S(1)}, f32[1,1,1024,256]{3,2,1,0:T(8,128)}, u32[]{:S(2)}) copy-start(f32[1,1,1024,256]{3,2,1,0:T(8,128)} %param.15) | copy-start | bytes 3145732
  7.2 21.4 %collective-permute-start.14 = (f32[512,256]{1,0:T(8,128)S(1)}, f32[512,256]{1,0:T(8,128)S(1)}, u32[]{:S(2)}, u32[]{:S(2)}) collective-permute-start(f32[512,256]{1,0:T(8,128)S(1)} %get-tuple-element.69), channel_id=1, source_target_pairs={{0,2},{2,0},{1,3},{3,1},{4,6},{6,4},{5,7},{7,5},{8,10},{10,8},{9,1... | collective-permute-start | bytes 1572872 | tf_op jit(solution)/shard_map/ppermute | solution.py:14
  7.3 13.1 %collective-permute-start = (f32[128,512]{1,0:T(8,128)S(1)}, f32[128,512]{1,0:T(8,128)S(1)}, u32[]{:S(2)}, u32[]{:S(2)}) collective-permute-start(f32[128,512]{1,0:T(8,128)S(1)} %get-tuple-element.62.mine), channel_id=1, source_target_pairs={{0,4},{4,0},{8,12},{12,8},{1,5},{5,1},{9,13},{13,9},{2,6},{6,2},{1... | collective-permute-start | bytes 786440 | tf_op jit(solution)/shard_map/ppermute | solution.py:14
  9.4 19.2 %collective-permute-start.2 = (f32[256,512]{1,0:T(8,128)S(1)}, f32[256,512]{1,0:T(8,128)S(1)}, u32[]{:S(2)}, u32[]{:S(2)}) collective-permute-start(f32[256,512]{1,0:T(8,128)S(1)} %get-tuple-element.52), channel_id=1, source_target_pairs={{0,4},{4,0},{8,12},{12,8},{1,5},{5,1},{9,13},{13,9},{2,6},{6,2},{1... | collective-permute-start | bytes 1572872 | tf_op jit(solution)/shard_map/ppermute | solution.py:14
  18.2 12.2 %collective-permute-start.13 = (f32[256,512]{1,0:T(8,128)S(1)}, f32[256,512]{1,0:T(8,128)S(1)}, u32[]{:S(2)}, u32[]{:S(2)}) collective-permute-start(f32[256,512]{1,0:T(8,128)S(1)} %collective-permute-done.5.refs_0_), channel_id=1, source_target_pairs={{0,1},{1,0},{2,3},{3,2},{4,5},{5,4},{6,7},{7,6},{8,9},{9,8},{10,11... | collective-permute-start | bytes 1572872 | tf_op jit(solution)/shard_map/ppermute | solution.py:14
  18.2 1.4 %copy-start.1 = (f32[1,1,1024,256]{3,2,1,0:T(8,128)S(1)}, f32[1,1,1024,256]{3,2,1,0:T(8,128)}, u32[]{:S(2)}) copy-start(f32[1,1,1024,256]{3,2,1,0:T(8,128)} %param.16) | copy-start | bytes 3145732
  19.6 3.0 %copy-start.3 = (f32[1,1,512,256]{3,2,1,0:T(8,128)S(1)}, f32[1,1,512,256]{3,2,1,0:T(8,128)}, u32[]{:S(2)}) copy-start(f32[1,1,512,256]{3,2,1,0:T(8,128)} %param.13) | copy-start | bytes 1572868
  19.6 3.0 %copy-start.4 = (f32[1,1,32,256]{3,2,1,0:T(8,128)S(1)}, f32[1,1,32,256]{3,2,1,0:T(8,128)}, u32[]{:S(2)}) copy-start(f32[1,1,32,256]{3,2,1,0:T(8,128)} %param.10) | copy-start | bytes 98308
  19.7 3.0 %copy-start.5 = (f32[1,1,32,256]{3,2,1,0:T(8,128)S(1)}, f32[1,1,32,256]{3,2,1,0:T(8,128)}, u32[]{:S(2)}) copy-start(f32[1,1,32,256]{3,2,1,0:T(8,128)} %param.11) | copy-start | bytes 98308
  20.4 17.2 %collective-permute-start.1 = (f32[512,256]{1,0:T(8,128)S(1)}, f32[512,256]{1,0:T(8,128)S(1)}, u32[]{:S(2)}, u32[]{:S(2)}) collective-permute-start(f32[512,256]{1,0:T(8,128)S(1)} %get-tuple-element.89), channel_id=1, source_target_pairs={{0,4},{4,0},{8,12},{12,8},{1,5},{5,1},{9,13},{13,9},{2,6},{6,2},{1... | collective-permute-start | bytes 1572872 | tf_op jit(solution)/shard_map/ppermute | solution.py:14
  24.8 6.5 %collective-permute-start.7 = (f32[360,256]{1,0:T(8,128)S(1)}, f32[360,256]{1,0:T(8,128)S(1)}, u32[]{:S(2)}, u32[]{:S(2)}) collective-permute-start(f32[360,256]{1,0:T(8,128)S(1)} %shard_map.118.refs_0_.s0), channel_id=1, source_target_pairs={{0,1},{1,0},{2,3},{3,2},{4,5},{5,4},{6,7},{7,6},{8,9},{9,8},{10,11... | collective-permute-start | bytes 1105928 | tf_op jit(solution)/shard_map/ppermute | solution.py:14
  28.6 11.4 %collective-permute-start.15 = (f32[512,256]{1,0:T(8,128)S(1)}, f32[512,256]{1,0:T(8,128)S(1)}, u32[]{:S(2)}, u32[]{:S(2)}) collective-permute-start(f32[512,256]{1,0:T(8,128)S(1)} %collective-permute-done.14.refs_0_), channel_id=1, source_target_pairs={{0,1},{1,0},{2,3},{3,2},{4,5},{5,4},{6,7},{7,6},{8,9},{9,8},{10,11... | collective-permute-start | bytes 1572872 | tf_op jit(solution)/shard_map/ppermute | solution.py:14
  28.6 11.4 %collective-permute-start.6 = (f32[360,256]{1,0:T(8,128)S(1)}, f32[360,256]{1,0:T(8,128)S(1)}, u32[]{:S(2)}, u32[]{:S(2)}) collective-permute-start(f32[360,256]{1,0:T(8,128)S(1)} %shard_map.118.refs_0_.s0), channel_id=1, source_target_pairs={{0,2},{2,0},{1,3},{3,1},{4,6},{6,4},{5,7},{7,5},{8,10},{10,8},{9,1... | collective-permute-start | bytes 1105928 | tf_op jit(solution)/shard_map/ppermute | solution.py:14
  30.3 10.9 %collective-permute-start.3 = (f32[256,512]{1,0:T(8,128)S(1)}, f32[256,512]{1,0:T(8,128)S(1)}, u32[]{:S(2)}, u32[]{:S(2)}) collective-permute-start(f32[256,512]{1,0:T(8,128)S(1)} %collective-permute-done.2.refs_0_), channel_id=1, source_target_pairs={{0,1},{1,0},{2,3},{3,2},{4,5},{5,4},{6,7},{7,6},{8,9},{9,8},{10,11... | collective-permute-start | bytes 1572872 | tf_op jit(solution)/shard_map/ppermute | solution.py:14
  31.3 19.9 %collective-permute-start.19 = (f32[512,256]{1,0:T(8,128)S(1)}, f32[512,256]{1,0:T(8,128)S(1)}, u32[]{:S(2)}, u32[]{:S(2)}) collective-permute-start(f32[512,256]{1,0:T(8,128)S(1)} %get-tuple-element.89), channel_id=1, source_target_pairs={{0,2},{2,0},{1,3},{3,1},{4,6},{6,4},{5,7},{7,5},{8,10},{10,8},{9,1... | collective-permute-start | bytes 1572872 | tf_op jit(solution)/shard_map/ppermute | solution.py:14
  37.6 13.6 %collective-permute-start.8 = (f32[512,256]{1,0:T(8,128)S(1)}, f32[512,256]{1,0:T(8,128)S(1)}, u32[]{:S(2)}, u32[]{:S(2)}) collective-permute-start(f32[512,256]{1,0:T(8,128)S(1)} %get-tuple-element.69), channel_id=1, source_target_pairs={{0,4},{4,0},{8,12},{12,8},{1,5},{5,1},{9,13},{13,9},{2,6},{6,2},{1... | collective-permute-start | bytes 1572872 | tf_op jit(solution)/shard_map/ppermute | solution.py:14
  40.0 15.0 %collective-permute-start.18 = (f32[512,256]{1,0:T(8,128)S(1)}, f32[512,256]{1,0:T(8,128)S(1)}, u32[]{:S(2)}, u32[]{:S(2)}) collective-permute-start(f32[512,256]{1,0:T(8,128)S(1)} %collective-permute-done.1.refs_0_), channel_id=1, source_target_pairs={{0,1},{1,0},{2,3},{3,2},{4,5},{5,4},{6,7},{7,6},{8,9},{9,8},{10,11... | collective-permute-start | bytes 1572872 | tf_op jit(solution)/shard_map/ppermute | solution.py:14
  40.0 12.5 %collective-permute-start.9 = (f32[360,256]{1,0:T(8,128)S(1)}, f32[360,256]{1,0:T(8,128)S(1)}, u32[]{:S(2)}, u32[]{:S(2)}) collective-permute-start(f32[360,256]{1,0:T(8,128)S(1)} %collective-permute-done.6.refs_0_.s2), channel_id=1, source_target_pairs={{0,1},{1,0},{2,3},{3,2},{4,5},{5,4},{6,7},{7,6},{8,9},{9,8},{10,11... | collective-permute-start | bytes 1105928 | tf_op jit(solution)/shard_map/ppermute | solution.py:14
  41.2 20.9 %collective-permute-start.16 = (f32[256,512]{1,0:T(8,128)S(1)}, f32[256,512]{1,0:T(8,128)S(1)}, u32[]{:S(2)}, u32[]{:S(2)}) collective-permute-start(f32[256,512]{1,0:T(8,128)S(1)} %collective-permute-done.2.refs_0_), channel_id=1, source_target_pairs={{0,2},{2,0},{1,3},{3,1},{4,6},{6,4},{5,7},{7,5},{8,10},{10,8},{9,1... | collective-permute-start | bytes 1572872 | tf_op jit(solution)/shard_map/ppermute | solution.py:14
  51.2 10.9 %collective-permute-start.20 = (f32[512,256]{1,0:T(8,128)S(1)}, f32[512,256]{1,0:T(8,128)S(1)}, u32[]{:S(2)}, u32[]{:S(2)}) collective-permute-start(f32[512,256]{1,0:T(8,128)S(1)} %collective-permute-done.19.refs_0_), channel_id=1, source_target_pairs={{0,1},{1,0},{2,3},{3,2},{4,5},{5,4},{6,7},{7,6},{8,9},{9,8},{10,11... | collective-permute-start | bytes 1572872 | tf_op jit(solution)/shard_map/ppermute | solution.py:14
  51.2 20.6 %collective-permute-start.21 = (f32[512,256]{1,0:T(8,128)S(1)}, f32[512,256]{1,0:T(8,128)S(1)}, u32[]{:S(2)}, u32[]{:S(2)}) collective-permute-start(f32[512,256]{1,0:T(8,128)S(1)} %collective-permute-done.8.refs_0_), channel_id=1, source_target_pairs={{0,1},{1,0},{2,3},{3,2},{4,5},{5,4},{6,7},{7,6},{8,9},{9,8},{10,11... | collective-permute-start | bytes 1572872 | tf_op jit(solution)/shard_map/ppermute | solution.py:14
  52.4 12.1 %collective-permute-start.4 = (f32[360,256]{1,0:T(8,128)S(1)}, f32[360,256]{1,0:T(8,128)S(1)}, u32[]{:S(2)}, u32[]{:S(2)}) collective-permute-start(f32[360,256]{1,0:T(8,128)S(1)} %shard_map.118.refs_0_.s0), channel_id=1, source_target_pairs={{0,4},{4,0},{8,12},{12,8},{1,5},{5,1},{9,13},{13,9},{2,6},{6,2},{1... | collective-permute-start | bytes 1105928 | tf_op jit(solution)/shard_map/ppermute | solution.py:14
  55.0 16.9 %collective-permute-start.10 = (f32[360,256]{1,0:T(8,128)S(1)}, f32[360,256]{1,0:T(8,128)S(1)}, u32[]{:S(2)}, u32[]{:S(2)}) collective-permute-start(f32[360,256]{1,0:T(8,128)S(1)} %collective-permute-done.6.refs_0_.s2), channel_id=1, source_target_pairs={{0,4},{4,0},{8,12},{12,8},{1,5},{5,1},{9,13},{13,9},{2,6},{6,2},{1... | collective-permute-start | bytes 1105928 | tf_op jit(solution)/shard_map/ppermute | solution.py:14
  62.1 12.7 %collective-permute-start.17 = (f32[256,512]{1,0:T(8,128)S(1)}, f32[256,512]{1,0:T(8,128)S(1)}, u32[]{:S(2)}, u32[]{:S(2)}) collective-permute-start(f32[256,512]{1,0:T(8,128)S(1)} %collective-permute-done.16.refs_0_), channel_id=1, source_target_pairs={{0,1},{1,0},{2,3},{3,2},{4,5},{5,4},{6,7},{7,6},{8,9},{9,8},{10,11... | collective-permute-start | bytes 1572872 | tf_op jit(solution)/shard_map/ppermute | solution.py:14
  62.1 14.3 %collective-permute-start.22 = (f32[512,256]{1,0:T(8,128)S(1)}, f32[512,256]{1,0:T(8,128)S(1)}, u32[]{:S(2)}, u32[]{:S(2)}) collective-permute-start(f32[512,256]{1,0:T(8,128)S(1)} %collective-permute-done.1.refs_0_), channel_id=1, source_target_pairs={{0,2},{2,0},{1,3},{3,1},{4,6},{6,4},{5,7},{7,5},{8,10},{10,8},{9,1... | collective-permute-start | bytes 1572872 | tf_op jit(solution)/shard_map/ppermute | solution.py:14
  64.5 17.7 %collective-permute-start.24 = (f32[512,256]{1,0:T(8,128)S(1)}, f32[512,256]{1,0:T(8,128)S(1)}, u32[]{:S(2)}, u32[]{:S(2)}) collective-permute-start(f32[512,256]{1,0:T(8,128)S(1)} %collective-permute-done.14.refs_0_), channel_id=1, source_target_pairs={{0,4},{4,0},{8,12},{12,8},{1,5},{5,1},{9,13},{13,9},{2,6},{6,2},{1... | collective-permute-start | bytes 1572872 | tf_op jit(solution)/shard_map/ppermute | solution.py:14
  71.9 1.7 %collective-permute-start.11 = (f32[360,256]{1,0:T(8,128)S(1)}, f32[360,256]{1,0:T(8,128)S(1)}, u32[]{:S(2)}, u32[]{:S(2)}) collective-permute-start(f32[360,256]{1,0:T(8,128)S(1)} %collective-permute-done.4.refs_0_.s1), channel_id=1, source_target_pairs={{0,1},{1,0},{2,3},{3,2},{4,5},{5,4},{6,7},{7,6},{8,9},{9,8},{10,11... | collective-permute-start | bytes 1105928 | tf_op jit(solution)/shard_map/ppermute | solution.py:14
  71.9 2.3 %collective-permute-start.12 = (f32[360,256]{1,0:T(8,128)S(1)}, f32[360,256]{1,0:T(8,128)S(1)}, u32[]{:S(2)}, u32[]{:S(2)}) collective-permute-start(f32[360,256]{1,0:T(8,128)S(1)} %collective-permute-done.10.refs_0_.s3), channel_id=1, source_target_pairs={{0,1},{1,0},{2,3},{3,2},{4,5},{5,4},{6,7},{7,6},{8,9},{9,8},{10,11... | collective-permute-start | bytes 1105928 | tf_op jit(solution)/shard_map/ppermute | solution.py:14
  76.4 5.8 %collective-permute-start.23 = (f32[512,256]{1,0:T(8,128)S(1)}, f32[512,256]{1,0:T(8,128)S(1)}, u32[]{:S(2)}, u32[]{:S(2)}) collective-permute-start(f32[512,256]{1,0:T(8,128)S(1)} %collective-permute-done.22.refs_28_), channel_id=1, source_target_pairs={{0,1},{1,0},{2,3},{3,2},{4,5},{5,4},{6,7},{7,6},{8,9},{9,8},{10,11... | collective-permute-start | bytes 1572872 | tf_op jit(solution)/shard_map/ppermute | solution.py:14
  82.2 1.9 %collective-permute-start.25 = (f32[512,256]{1,0:T(8,128)S(1)}, f32[512,256]{1,0:T(8,128)S(1)}, u32[]{:S(2)}, u32[]{:S(2)}) collective-permute-start(f32[512,256]{1,0:T(8,128)S(1)} %collective-permute-done.24.refs_30_), channel_id=1, source_target_pairs={{0,1},{1,0},{2,3},{3,2},{4,5},{5,4},{6,7},{7,6},{8,9},{9,8},{10,11... | collective-permute-start | bytes 1572872 | tf_op jit(solution)/shard_map/ppermute | solution.py:14
  (3 other events, 2.1 us)

commit v5 on v4

--- a/solution.py
+++ b/solution.py
@@ -157,44 +157,51 @@
     return both[:rows] + both[rows:] + rest
 
 
+def forward_half(one, picked, weights, edge):
+    width = edge[0].shape[1]
+    pairs = [one[:, side * 2 * width:(side + 1) * 2 * width] for side in range(2)]
+    blocks = [product(pairs[tile // 2], edge[2 * tile][...], edge[2 * tile + 1][...]) for tile in range(4)]
+    return jnp.concatenate(blocks, axis=1) + column_of(weights) * picked
+
+
+def tall(left, panels):
+    return jnp.concatenate([product(left, panels[2 * tile][...], panels[2 * tile + 1][...]) for tile in range(4)], axis=1)
+
+
+def forward_two(half, two, scale, lift, root):
+    width = lift[0].shape[1]
+
+    def column_block(block, part):
+        return jnp.concatenate([lift[2 * tile + part][block * width:(block + 1) * width, :] for tile in range(4)], axis=0)
+
+    sums = jnp.concatenate([product(half, column_block(block, 0), column_block(block, 1)) for block in range(4)], axis=1)
+    return tall(sums + two * scale, root)
+
+
+def below(tiles, rows, index, count):
+    start = tiles[0].shape[1] + index * rows
+    return jnp.concatenate([tile[start:start + count, :] for tile in tiles], axis=1)
+
+
 def march_kernel(s0, s1, s2, s3, weight, place, *refs):
     edge, lift, root, back = refs[:8], refs[8:16], refs[16:22], refs[22:28]
-    r_mine, r_other, b_mine, b_other, one_ref, two_ref, last_rh, last_rl, last_bh, last_bl = refs[28:]
+    root_mine, root_other, back_mine, back_other, one_ref, two_ref = refs[28:34]
     rows, width = one_ref.shape
-
-    def below(index, count):
-        start = width + index * rows
-        return jnp.concatenate([tile[start:start + count, :] for tile in (s0, s1, s2, s3)], axis=1)
-
-    one, two, picked, scale = below(0, rows), below(1, rows), below(2, rows), below(3, 1)
-    split_tall(place, (r_mine, r_other), last_rh, last_rl)
-    split_tall(place, (b_mine, b_other), last_bh, last_bl)
-    root = root + (last_rh, last_rl)
-    back = back + (last_bh, last_bl)
-
-    def tall(left, panels):
-        return jnp.concatenate([product(left, panels[2 * tile][...], panels[2 * tile + 1][...]) for tile in range(4)], axis=1)
-
-    def column_block(block, part):
-        return jnp.concatenate([lift[2 * tile + part][block * width:(block + 1) * width, :] for tile in range(4)], axis=0)
+    tiles = (s0, s1, s2, s3)
+    split_tall(place, (root_mine, root_other), *refs[34:36])
+    split_tall(place, (back_mine, back_other), *refs[36:38])
+    root, back = root + refs[34:36], back + refs[36:38]
+    one, two, picked, scale = [below(tiles, rows, index, count) for index, count in enumerate((rows, rows, rows, 1))]
+    half = forward_half(one, picked, weight[0:1, :], edge)
+    two = forward_two(half, two, scale, lift, root)
 
     def advance(step, carry):
-        one, two = carry
-        half = jnp.concatenate(
-            [
-                product(one[:, side * 2 * width:(side + 1) * 2 * width], edge[2 * tile][...], edge[2 * tile + 1][...])
-                for side in range(2)
-                for tile in (2 * side, 2 * side + 1)
-            ],
-            axis=1,
-        )
-        half = half + column_of(weight[pl.ds(step, 1), :]) * picked
-        sums = jnp.concatenate([product(half, column_block(block, 0), column_block(block, 1)) for block in range(4)], axis=1)
-        two = tall(sums + two * scale, root)
-        return half - tall(two, back), two
-
-    one, two = lax.fori_loop(0, weight.shape[0], advance, (one, two))
-    one_ref[...] = one[:, :width]
+        half, two = carry
+        half = forward_half(half - tall(two, back), picked, weight[pl.ds(step, 1), :], edge)
+        return half, forward_two(half, two, scale, lift, root)
+
+    half, two = lax.fori_loop(1, weight.shape[0], advance, (half, two))
+    one_ref[...] = half[:, :width] - product(two, back[0][...], back[1][...])
     two_ref[...] = two[:, :width]
 
 
@@ -222,24 +229,47 @@
     first_cell = ((column - x_bit) * lax.axis_size("gy") + row) * width
     place = jnp.stack([2 * y_bit + x_bit, core, first_cell, first_cell + lax.axis_size("gy") * width]).astype(jnp.int32)
 
-    def split(kernel, size, value):
-        return split_call(kernel, place, size, value, from_partner(value, "gz"))
-
     tall, wide, edge = (tall_kernel, 4 * width), (wide_kernel, 4 * width), (edge_kernel, 2 * width)
 
     couple_mine, lift_half = cut_call(place, (couple, lift), ((width // 2, 2 * width), (width, 2 * width)))
-    back_half, root_half = cut_call(after(place, lift_half), (back, root), ((2 * width, width),) * 2)
+
+    token = [place]
+    waiting = []
+    done = {}
+
+    def arrive(name, value, kernel=None, size=0, ready=()):
+        token[0] = after(value, token[0], *[done[other][0] for other in ready])
+        if kernel is not None:
+            waiting.append((name, kernel, size, token[0]))
+        return token[0]
+
+    def send(value, axis):
+        return from_partner(after(value, token[0]), axis)
+
+    def swap(count=1):
+        for _ in range(count):
+            name, kernel, size, value = waiting.pop(0)
+            done[name] = (kernel, size, value, send(value, "gz"))
+
+    def split(*names):
+        for name in names:
+            kernel, size, *pieces = done[name]
+            done[name] = split_call(kernel, after(place, token[0]), size, *pieces)
+
     couple_other = from_partner(couple_mine, "gx")
     lift_y = from_partner(lift_half, "gy")
     lift_x = from_partner(lift_half, "gx")
-    back_y = from_partner(back_half, "gy")
-    lift_own = split_call(wide_kernel, place, wide[1], after(lift, root_half))
-    root_own = split_call(tall_kernel, place, tall[1], after(root, root_half))
-    back_own = split_call(tall_kernel, place, tall[1], after(back, root_half))
+    back_half, root_half = cut_call(after(place, couple_other), (back, root), ((2 * width, width),) * 2)
+    done["L"] = split_call(wide_kernel, place, wide[1], after(lift, lift_half))
+    done["R"] = split_call(tall_kernel, place, tall[1], after(root, lift_half))
+    done["B"] = split_call(tall_kernel, place, tall[1], after(back, lift_half))
+    couple_other = arrive("C", couple_other)
+    root_x = send(root_half, "gx")
+    back_y = send(back_half, "gy")
     edge_half = small_call(
         edge_state_kernel,
         (width + 3 * rows + 8, width),
-        after(place, lift_own[0], root_own[0], back_own[0]),
+        place,
         couple_mine,
         couple_other,
         pair_cols,
@@ -248,37 +278,54 @@
         adjoint_two_start[0, 0],
         mass_two[0],
     )
-    root_x = from_partner(after(root_half, couple_other), "gx")
-    edge_y = from_partner(after(edge_half, lift_y), "gy")
-    edge_own = split(*edge, edge_half)
-    back_x = from_partner(after(back_half, lift_x, edge_own[0]), "gx")
-    lift_y_split = split(*wide, lift_y)
-    root_y = from_partner(after(root_half, back_y, lift_y_split[0]), "gy")
-    lift_x_split = split(*wide, lift_x)
-    edge_x = from_partner(after(edge_half, root_x, lift_x_split[0]), "gx")
-    back_y_split = split(*tall, back_y)
-    lift_d = from_partner(after(lift_x, edge_y, back_y_split[0]), "gy")
-    edge_y_split = split(*edge, edge_y)
-    edge_d = from_partner(after(edge_y, back_x, edge_y_split[0]), "gx")
-    root_x_split = split(*tall, root_x)
-    root_d = from_partner(after(root_x, root_y, root_x_split[0]), "gy")
-    root_y_split = split(*tall, root_y)
-    back_d = from_partner(after(back_y, edge_x, root_y_split[0]), "gx")
-    back_x_split = split(*tall, back_x)
-    edge_x_split = split(*edge, edge_x)
-    lift_d_split = split(*wide, lift_d)
-    edge_d_split = split(*edge, edge_d)
-    back_d = after(back_d, back_x_split[0], edge_x_split[0])
-    root_d = after(root_d, lift_d_split[0], edge_d_split[0])
-
-    vmem = pl.BlockSpec(memory_space=pltpu.VMEM)
-    panels = edge_own + edge_x_split + edge_y_split + edge_d_split + lift_own + lift_x_split + lift_y_split + lift_d_split
-    panels += root_own + root_x_split + root_y_split + back_own + back_x_split + back_y_split
-    panels = tuple(pltpu.with_memory_space_constraint(panel, pltpu.VMEM) for panel in panels)
+    waiting.append(("E", *edge, edge_half))
+    lift_y = arrive("Ly", lift_y, *wide)
+    edge_y = send(edge_half, "gy")
+    lift_x = arrive("Lx", lift_x, *wide)
+    back_x = send(back_half, "gx")
+    swap()
+    back_y = arrive("By", back_y, *tall, ready=("L",))
+    root_y = send(root_half, "gy")
+    swap()
+    root_x = arrive("Rx", root_x, *tall, ready=("R",))
+    edge_x = send(edge_half, "gx")
+    swap()
+    split("E")
+    edge_y = arrive("Ey", edge_y, *edge, ready=("B",))
+    lift_d = send(lift_x, "gy")
+    swap()
+    split("Ly")
+    back_x = arrive("Bx", back_x, *tall, ready=("E",))
+    edge_d = send(edge_y, "gx")
+    swap()
+    split("Lx")
+    root_y = arrive("Ry", root_y, *tall, ready=("Ly",))
+    root_d = send(root_x, "gy")
+    swap()
+    split("By")
+    edge_x = arrive("Ex", edge_x, *edge, ready=("Lx",))
+    back_d = send(back_y, "gx")
+    swap()
+    split("Rx")
+    lift_d = arrive("Ld", lift_d, *wide, ready=("By",))
+    swap()
+    split("Ey")
+    edge_d = arrive("Ed", edge_d, *edge, ready=("Rx", "Ey"))
+    swap()
+    split("Bx", "Ry")
+    root_d = arrive("Rd", root_d, ready=("Bx", "Ry"))
+    swap(2)
+    split("Ex")
+    back_d = arrive("Bd", back_d, ready=("Ex",))
+    split("Ld", "Ed")
+
+    vmem, smem = pl.BlockSpec(memory_space=pltpu.VMEM), pl.BlockSpec(memory_space=pltpu.SMEM)
+    panels = done["E"] + done["Ex"] + done["Ey"] + done["Ed"] + done["L"] + done["Lx"] + done["Ly"] + done["Ld"]
+    panels += done["R"] + done["Rx"] + done["Ry"] + done["B"] + done["Bx"] + done["By"]
     panels += (root_d, from_partner(root_d, "gz"), back_d, from_partner(back_d, "gz"))
     one, two = pl.pallas_call(
         march_kernel,
-        in_specs=[vmem] * 5 + [pl.BlockSpec(memory_space=pltpu.SMEM)] + [vmem] * len(panels),
+        in_specs=[vmem] * 5 + [smem] + [vmem] * len(panels),
         out_specs=(vmem, vmem),
         out_shape=(jax.ShapeDtypeStruct((rows, width), F32),) * 2,
         scratch_shapes=[pltpu.VMEM((4 * width, width), BF16)] * 4,

time: 111 us -> 106 us (0.955)
  waiting for transfers between devices: 47.3 us -> 42.4 us
  starting transfers between devices: 20.7 us -> 22.7 us
    ppermute x26, waiting for transfers between devices: 47.3 us -> 42.4 us  [from_partner(): return lax.ppermute(value, axis, pairs)]
    ppermute x26, starting transfers between devices: 20.7 us -> 22.7 us  [from_partner(): return lax.ppermute(value, axis, pairs)]
  transfers between devices with their start and end apart: 26 -> 26, of which waited for: 11 -> 13; matrix products, arithmetic and copies ran while one was open for 0% -> 0% of each run, Pallas kernels for 12% -> 12%
where the time goes in v5:
time: 106 us
  waiting for transfers between devices  42.4 us (40%)
  Pallas kernels  39.4 us (37%)
  starting transfers between devices  22.7 us (21%)
    ppermute x26, waiting for transfers between devices, from_partner(): return lax.ppermute(value, axis, pairs)  42.4 us
    pallas_call x1, Pallas kernels, shards(): pl.pallas_call(march_kernel, in_specs=[vmem] * 5 + [smem] + [vmem] * len(...  25 us
    ppermute x26, starting transfers between devices, from_partner(): return lax.ppermute(value, axis, pairs)  22.7 us
    pallas_call x14, Pallas kernels, split_call(): pl.pallas_call(kernel, in_specs=[pl.BlockSpec(memory_space=pltpu.SMEM)] +...  9.51 us
    pallas_call x2, Pallas kernels, cut_call(): pl.pallas_call(cut_kernel, in_specs=[pl.BlockSpec(memory_space=pltpu.SMEM...  3.45 us
  transfers between devices with their start and end apart: 26, of which 13 were waited for; matrix products, arithmetic and copies ran while one was open for 0% of the time, Pallas kernels for 12%

profile of v5, /device:TPU:0, one launch (start us, length us, event | category | flops | bytes accessed | tf_op | source)
XLA Modules:
  0.0 106.3 jit_solution(3049256591107123230)
XLA Ops:
  0.7 1.7 %shard_map.113 = (f32[128,512]{1,0:T(8,128)S(1)}, f32[256,512]{1,0:T(8,128)S(1)}) custom-call(s32[4]{0:T(128)S(1)} %pad_add_fusion.place, f32[256,512]{1,0:T(8,128)} %bitcast.26, f32[256,1024]{1,0:T(8,128)} %bitcast.19), custom_call_target="tpu_custom_call" | custom-call | flops 1 | bytes 1 | tf_op jit(solution)/shard_map/pallas_call | solution.py:58
  2.4 3.1 %collective-permute-start = (f32[128,512]{1,0:T(8,128)S(1)}, f32[128,512]{1,0:T(8,128)S(1)}, u32[]{:S(2)}, u32[]{:S(2)}) collective-permute-start(f32[128,512]{1,0:T(8,128)S(1)} %get-tuple-element.83.mine), channel_id=1, source_target_pairs={{0,4},{4,0},{8,12},{12,8},{1,5},{5,1},{9,13},{13,9},{2,6},{6,2},{1... | collective-permute-start | bytes 786440 | tf_op jit(solution)/shard_map/ppermute | solution.py:14
  5.5 1.5 %collective-permute-start.4 = (f32[256,512]{1,0:T(8,128)S(1)}, f32[256,512]{1,0:T(8,128)S(1)}, u32[]{:S(2)}, u32[]{:S(2)}) collective-permute-start(f32[256,512]{1,0:T(8,128)S(1)} %get-tuple-element.90), channel_id=1, source_target_pairs={{0,2},{2,0},{1,3},{3,1},{4,6},{6,4},{5,7},{7,5},{8,10},{10,8},{9,1... | collective-permute-start | bytes 1572872 | tf_op jit(solution)/shard_map/ppermute | solution.py:14
  7.5 5.2 %collective-permute-done.other = f32[128,512]{1,0:T(8,128)S(1)} collective-permute-done((f32[128,512]{1,0:T(8,128)S(1)}, f32[128,512]{1,0:T(8,128)S(1)}, u32[]{:S(2)}, u32[]{:S(2)}) %collective-permute-start) | collective-permute-done | bytes 262176 | tf_op jit(solution)/shard_map/ppermute | solution.py:14
  12.7 1.8 %shard_map.115 = (f32[512,256]{1,0:T(8,128)S(1)}, f32[512,256]{1,0:T(8,128)S(1)}) custom-call(s32[4]{0:T(128)S(1)} %pad_add_fusion.place, f32[1024,256]{1,0:T(8,128)} %bitcast.17, f32[1024,256]{1,0:T(8,128)} %bitcast.15), custom_call_target="tpu_custom_call" | custom-call | flops 1 | bytes 1 | tf_op jit(solution)/shard_map/pallas_call | solution.py:58
  14.5 2.0 %collective-permute-start.2 = (f32[512,256]{1,0:T(8,128)S(1)}, f32[512,256]{1,0:T(8,128)S(1)}, u32[]{:S(2)}, u32[]{:S(2)}) collective-permute-start(f32[512,256]{1,0:T(8,128)S(1)} %get-tuple-element.101), channel_id=1, source_target_pairs={{0,2},{2,0},{1,3},{3,1},{4,6},{6,4},{5,7},{7,5},{8,10},{10,8},{9,1... | collective-permute-start | bytes 1572872 | tf_op jit(solution)/shard_map/ppermute | solution.py:14
  16.5 1.6 %collective-permute-start.1 = (f32[512,256]{1,0:T(8,128)S(1)}, f32[512,256]{1,0:T(8,128)S(1)}, u32[]{:S(2)}, u32[]{:S(2)}) collective-permute-start(f32[512,256]{1,0:T(8,128)S(1)} %get-tuple-element.100), channel_id=1, source_target_pairs={{0,4},{4,0},{8,12},{12,8},{1,5},{5,1},{9,13},{13,9},{2,6},{6,2},{1... | collective-permute-start | bytes 1572872 | tf_op jit(solution)/shard_map/ppermute | solution.py:14
  18.1 1.5 %shard_map.114.refs_0_.s0 = f32[360,256]{1,0:T(8,128)S(1)} custom-call(s32[4]{0:T(128)S(1)} %pad_add_fusion.place, f32[128,512]{1,0:T(8,128)S(1)} %get-tuple-element.83.mine, f32[128,512]{1,0:T(8,128)S(1)} %collective-permute-done.other, f32[512,256]{1,0:T(8,128)S(1)} %bitcast.21, s32[1,32]{1,0:T(1,128)S(1)} %bitcast.25, f32[32,256]{1,0:T(8,128)S(1)} %bitcast.22, ...), custom_call_target="tpu_custom_call" | custom-call | flops 1 | bytes 1 | tf_op jit(solution)/shard_map/pallas_call | solution.py:92
  19.6 0.8 collective-permute-done.4.refs_0_
  20.4 1.5 %collective-permute-start.8 = (f32[360,256]{1,0:T(8,128)S(1)}, f32[360,256]{1,0:T(8,128)S(1)}, u32[]{:S(2)}, u32[]{:S(2)}) collective-permute-start(f32[360,256]{1,0:T(8,128)S(1)} %shard_map.114.refs_0_.s0), channel_id=1, source_target_pairs={{0,2},{2,0},{1,3},{3,1},{4,6},{6,4},{5,7},{7,5},{8,10},{10,8},{9,1... | collective-permute-start | bytes 1105928 | tf_op jit(solution)/shard_map/ppermute | solution.py:14
  21.9 2.0 %collective-permute-done.3.refs_0_ = f32[256,512]{1,0:T(8,128)S(1)} collective-permute-done((f32[256,512]{1,0:T(8,128)S(1)}, f32[256,512]{1,0:T(8,128)S(1)}, u32[]{:S(2)}, u32[]{:S(2)}) %collective-permute-start.3) | collective-permute-done | bytes 524320 | tf_op jit(solution)/shard_map/ppermute | solution.py:14
  24.6 2.1 %collective-permute-start.7 = (f32[512,256]{1,0:T(8,128)S(1)}, f32[512,256]{1,0:T(8,128)S(1)}, u32[]{:S(2)}, u32[]{:S(2)}) collective-permute-start(f32[512,256]{1,0:T(8,128)S(1)} %get-tuple-element.101), channel_id=1, source_target_pairs={{0,4},{4,0},{8,12},{12,8},{1,5},{5,1},{9,13},{13,9},{2,6},{6,2},{1... | collective-permute-start | bytes 1572872 | tf_op jit(solution)/shard_map/ppermute | solution.py:14
  26.7 4.9 %collective-permute-done.2.refs_0_ = f32[512,256]{1,0:T(8,128)S(1)} collective-permute-done((f32[512,256]{1,0:T(8,128)S(1)}, f32[512,256]{1,0:T(8,128)S(1)}, u32[]{:S(2)}, u32[]{:S(2)}) %collective-permute-start.2) | collective-permute-done | bytes 524320 | tf_op jit(solution)/shard_map/ppermute | solution.py:14
  31.6 3.5 %collective-permute-done.1.refs_0_ = f32[512,256]{1,0:T(8,128)S(1)} collective-permute-done((f32[512,256]{1,0:T(8,128)S(1)}, f32[512,256]{1,0:T(8,128)S(1)}, u32[]{:S(2)}, u32[]{:S(2)}) %collective-permute-start.1) | collective-permute-done | bytes 524320 | tf_op jit(solution)/shard_map/ppermute | solution.py:14
  35.1 2.0 %collective-permute-start.6 = (f32[512,256]{1,0:T(8,128)S(1)}, f32[512,256]{1,0:T(8,128)S(1)}, u32[]{:S(2)}, u32[]{:S(2)}) collective-permute-start(f32[512,256]{1,0:T(8,128)S(1)} %get-tuple-element.100), channel_id=1, source_target_pairs={{0,2},{2,0},{1,3},{3,1},{4,6},{6,4},{5,7},{7,5},{8,10},{10,8},{9,1... | collective-permute-start | bytes 1572872 | tf_op jit(solution)/shard_map/ppermute | solution.py:14
  37.8 1.7 %collective-permute-done.8.refs_0_.s2 = f32[360,256]{1,0:T(8,128)S(1)} collective-permute-done((f32[360,256]{1,0:T(8,128)S(1)}, f32[360,256]{1,0:T(8,128)S(1)}, u32[]{:S(2)}, u32[]{:S(2)}) %collective-permute-start.8) | collective-permute-done | bytes 368672 | tf_op jit(solution)/shard_map/ppermute | solution.py:14
  40.9 5.5 %collective-permute-done.7.refs_0_ = f32[512,256]{1,0:T(8,128)S(1)} collective-permute-done((f32[512,256]{1,0:T(8,128)S(1)}, f32[512,256]{1,0:T(8,128)S(1)}, u32[]{:S(2)}, u32[]{:S(2)}) %collective-permute-start.7) | collective-permute-done | bytes 524320 | tf_op jit(solution)/shard_map/ppermute | solution.py:14
  46.4 2.0 %collective-permute-start.13 = (f32[256,512]{1,0:T(8,128)S(1)}, f32[256,512]{1,0:T(8,128)S(1)}, u32[]{:S(2)}, u32[]{:S(2)}) collective-permute-start(f32[256,512]{1,0:T(8,128)S(1)} %collective-permute-done.3.refs_0_), channel_id=1, source_target_pairs={{0,2},{2,0},{1,3},{3,1},{4,6},{6,4},{5,7},{7,5},{8,10},{10,8},{9,1... | collective-permute-start | bytes 1572872 | tf_op jit(solution)/shard_map/ppermute | solution.py:14
  48.3 0.9 collective-permute-done.6.refs_0_
  49.3 0.7 shard_map.120
  50.0 3.4 %collective-permute-done.5.refs_0_.s1 = f32[360,256]{1,0:T(8,128)S(1)} collective-permute-done((f32[360,256]{1,0:T(8,128)S(1)}, f32[360,256]{1,0:T(8,128)S(1)}, u32[]{:S(2)}, u32[]{:S(2)}) %collective-permute-start.5) | collective-permute-done | bytes 368672 | tf_op jit(solution)/shard_map/ppermute | solution.py:14
  53.4 1.7 %collective-permute-start.12 = (f32[360,256]{1,0:T(8,128)S(1)}, f32[360,256]{1,0:T(8,128)S(1)}, u32[]{:S(2)}, u32[]{:S(2)}) collective-permute-start(f32[360,256]{1,0:T(8,128)S(1)} %collective-permute-done.8.refs_0_.s2), channel_id=1, source_target_pairs={{0,4},{4,0},{8,12},{12,8},{1,5},{5,1},{9,13},{13,9},{2,6},{6,2},{1... | collective-permute-start | bytes 1105928 | tf_op jit(solution)/shard_map/ppermute | solution.py:14
  55.2 0.7 shard_map.121
  56.9 4.0 %collective-permute-done.13.refs_0_ = f32[256,512]{1,0:T(8,128)S(1)} collective-permute-done((f32[256,512]{1,0:T(8,128)S(1)}, f32[256,512]{1,0:T(8,128)S(1)}, u32[]{:S(2)}, u32[]{:S(2)}) %collective-permute-start.13) | collective-permute-done | bytes 524320 | tf_op jit(solution)/shard_map/ppermute | solution.py:14
  60.9 1.7 %collective-permute-start.17 = (f32[512,256]{1,0:T(8,128)S(1)}, f32[512,256]{1,0:T(8,128)S(1)}, u32[]{:S(2)}, u32[]{:S(2)}) collective-permute-start(f32[512,256]{1,0:T(8,128)S(1)} %collective-permute-done.1.refs_0_), channel_id=1, source_target_pairs={{0,2},{2,0},{1,3},{3,1},{4,6},{6,4},{5,7},{7,5},{8,10},{10,8},{9,1... | collective-permute-start | bytes 1572872 | tf_op jit(solution)/shard_map/ppermute | solution.py:14
  62.7 1.6 %collective-permute-start.21 = (f32[512,256]{1,0:T(8,128)S(1)}, f32[512,256]{1,0:T(8,128)S(1)}, u32[]{:S(2)}, u32[]{:S(2)}) collective-permute-start(f32[512,256]{1,0:T(8,128)S(1)} %collective-permute-done.2.refs_0_), channel_id=1, source_target_pairs={{0,4},{4,0},{8,12},{12,8},{1,5},{5,1},{9,13},{13,9},{2,6},{6,2},{1... | collective-permute-start | bytes 1572872 | tf_op jit(solution)/shard_map/ppermute | solution.py:14
  65.7 0.7 shard_map.125
  66.4 0.7 shard_map.126
  67.1 8.1 %collective-permute-done.17.refs_28_ = f32[512,256]{1,0:T(8,128)S(1)} collective-permute-done((f32[512,256]{1,0:T(8,128)S(1)}, f32[512,256]{1,0:T(8,128)S(1)}, u32[]{:S(2)}, u32[]{:S(2)}) %collective-permute-start.17) | collective-permute-done | bytes 524320 | tf_op jit(solution)/shard_map/ppermute | solution.py:14
  77.2 2.0 %collective-permute-done.22.refs_1_ = f32[360,256]{1,0:T(8,128)S(1)} collective-permute-done((f32[360,256]{1,0:T(8,128)S(1)}, f32[360,256]{1,0:T(8,128)S(1)}, u32[]{:S(2)}, u32[]{:S(2)}) %collective-permute-start.22) | collective-permute-done | bytes 368672 | tf_op jit(solution)/shard_map/ppermute | solution.py:14
  79.8 0.7 shard_map.129
  81.3 25.0 %shard_map.130 = (f32[32,256]{1,0:T(8,128)}, f32[32,256]{1,0:T(8,128)}) custom-call(f32[360,256]{1,0:T(8,128)S(1)} %shard_map.114.refs_0_.s0, f32[360,256]{1,0:T(8,128)S(1)} %collective-permute-done.5.refs_0_.s1, f32[360,256]{1,0:T(8,128)S(1)} %collective-permute-done.8.refs_0_.s2, f32[360,256]{1,0:T(8,128)S(1)} %collective-permute-done.12.refs_0_.s3, ...), custom_call_target="tpu_custom_call" | custom-call | tf_op jit(solution)/shard_map/pallas_call | solution.py:326
  (57 shorter events, 9.0 us)
Async XLA Ops:
  2.4 10.2 %collective-permute-start = (f32[128,512]{1,0:T(8,128)S(1)}, f32[128,512]{1,0:T(8,128)S(1)}, u32[]{:S(2)}, u32[]{:S(2)}) collective-permute-start(f32[128,512]{1,0:T(8,128)S(1)} %get-tuple-element.83.mine), channel_id=1, source_target_pairs={{0,4},{4,0},{8,12},{12,8},{1,5},{5,1},{9,13},{13,9},{2,6},{6,2},{1... | collective-permute-start | bytes 786440 | tf_op jit(solution)/shard_map/ppermute | solution.py:14
  5.5 14.8 %collective-permute-start.4 = (f32[256,512]{1,0:T(8,128)S(1)}, f32[256,512]{1,0:T(8,128)S(1)}, u32[]{:S(2)}, u32[]{:S(2)}) collective-permute-start(f32[256,512]{1,0:T(8,128)S(1)} %get-tuple-element.90), channel_id=1, source_target_pairs={{0,2},{2,0},{1,3},{3,1},{4,6},{6,4},{5,7},{7,5},{8,10},{10,8},{9,1... | collective-permute-start | bytes 1572872 | tf_op jit(solution)/shard_map/ppermute | solution.py:14
  7.0 16.9 %collective-permute-start.3 = (f32[256,512]{1,0:T(8,128)S(1)}, f32[256,512]{1,0:T(8,128)S(1)}, u32[]{:S(2)}, u32[]{:S(2)}) collective-permute-start(f32[256,512]{1,0:T(8,128)S(1)} %get-tuple-element.90), channel_id=1, source_target_pairs={{0,4},{4,0},{8,12},{12,8},{1,5},{5,1},{9,13},{13,9},{2,6},{6,2},{1... | collective-permute-start | bytes 1572872 | tf_op jit(solution)/shard_map/ppermute | solution.py:14
  12.6 5.4 %copy-start.5 = (f32[1,1,32,256]{3,2,1,0:T(8,128)S(1)}, f32[1,1,32,256]{3,2,1,0:T(8,128)}, u32[]{:S(2)}) copy-start(f32[1,1,32,256]{3,2,1,0:T(8,128)} %param.11) | copy-start | bytes 98308
  12.7 5.4 %copy-start.7 = (f32[1,1,256]{2,1,0:T(1,128)S(1)}, f32[1,1,256]{2,1,0:T(1,128)}, u32[]{:S(2)}) copy-start(f32[1,1,256]{2,1,0:T(1,128)} %param.17) | copy-start | bytes 3076
  12.7 5.4 %copy-start.8 = (s32[32]{0:T(128)S(1)}, s32[32]{0:T(128)}, u32[]{:S(2)}) copy-start(s32[32]{0:T(128)} %param.18) | copy-start | bytes 388
  14.4 9.4 %copy-start.2 = (f32[1,1,256,1024]{3,2,1,0:T(8,128)S(1)}, f32[1,1,256,1024]{3,2,1,0:T(8,128)}, u32[]{:S(2)}) copy-start(f32[1,1,256,1024]{3,2,1,0:T(8,128)} %param.14) | copy-start | bytes 3145732
  14.5 17.1 %collective-permute-start.2 = (f32[512,256]{1,0:T(8,128)S(1)}, f32[512,256]{1,0:T(8,128)S(1)}, u32[]{:S(2)}, u32[]{:S(2)}) collective-permute-start(f32[512,256]{1,0:T(8,128)S(1)} %get-tuple-element.101), channel_id=1, source_target_pairs={{0,2},{2,0},{1,3},{3,1},{4,6},{6,4},{5,7},{7,5},{8,10},{10,8},{9,1... | collective-permute-start | bytes 1572872 | tf_op jit(solution)/shard_map/ppermute | solution.py:14
  16.5 18.6 %collective-permute-start.1 = (f32[512,256]{1,0:T(8,128)S(1)}, f32[512,256]{1,0:T(8,128)S(1)}, u32[]{:S(2)}, u32[]{:S(2)}) collective-permute-start(f32[512,256]{1,0:T(8,128)S(1)} %get-tuple-element.100), channel_id=1, source_target_pairs={{0,4},{4,0},{8,12},{12,8},{1,5},{5,1},{9,13},{13,9},{2,6},{6,2},{1... | collective-permute-start | bytes 1572872 | tf_op jit(solution)/shard_map/ppermute | solution.py:14
  18.1 19.0 %copy-start = (f32[1,1,1024,256]{3,2,1,0:T(8,128)S(1)}, f32[1,1,1024,256]{3,2,1,0:T(8,128)}, u32[]{:S(2)}) copy-start(f32[1,1,1024,256]{3,2,1,0:T(8,128)} %param.15) | copy-start | bytes 3145732
  19.6 19.9 %copy-start.1 = (f32[1,1,1024,256]{3,2,1,0:T(8,128)S(1)}, f32[1,1,1024,256]{3,2,1,0:T(8,128)}, u32[]{:S(2)}) copy-start(f32[1,1,1024,256]{3,2,1,0:T(8,128)} %param.16) | copy-start | bytes 3145732
  20.4 19.1 %collective-permute-start.8 = (f32[360,256]{1,0:T(8,128)S(1)}, f32[360,256]{1,0:T(8,128)S(1)}, u32[]{:S(2)}, u32[]{:S(2)}) collective-permute-start(f32[360,256]{1,0:T(8,128)S(1)} %shard_map.114.refs_0_.s0), channel_id=1, source_target_pairs={{0,2},{2,0},{1,3},{3,1},{4,6},{6,4},{5,7},{7,5},{8,10},{10,8},{9,1... | collective-permute-start | bytes 1105928 | tf_op jit(solution)/shard_map/ppermute | solution.py:14
  23.9 15.6 %collective-permute-start.9 = (f32[360,256]{1,0:T(8,128)S(1)}, f32[360,256]{1,0:T(8,128)S(1)}, u32[]{:S(2)}, u32[]{:S(2)}) collective-permute-start(f32[360,256]{1,0:T(8,128)S(1)} %shard_map.114.refs_0_.s0), channel_id=1, source_target_pairs={{0,1},{1,0},{2,3},{3,2},{4,5},{5,4},{6,7},{7,6},{8,9},{9,8},{10,11... | collective-permute-start | bytes 1105928 | tf_op jit(solution)/shard_map/ppermute | solution.py:14
  24.6 21.8 %collective-permute-start.7 = (f32[512,256]{1,0:T(8,128)S(1)}, f32[512,256]{1,0:T(8,128)S(1)}, u32[]{:S(2)}, u32[]{:S(2)}) collective-permute-start(f32[512,256]{1,0:T(8,128)S(1)} %get-tuple-element.101), channel_id=1, source_target_pairs={{0,4},{4,0},{8,12},{12,8},{1,5},{5,1},{9,13},{13,9},{2,6},{6,2},{1... | collective-permute-start | bytes 1572872 | tf_op jit(solution)/shard_map/ppermute | solution.py:14
  31.6 14.8 %collective-permute-start.10 = (f32[256,512]{1,0:T(8,128)S(1)}, f32[256,512]{1,0:T(8,128)S(1)}, u32[]{:S(2)}, u32[]{:S(2)}) collective-permute-start(f32[256,512]{1,0:T(8,128)S(1)} %collective-permute-done.4.refs_0_), channel_id=1, source_target_pairs={{0,1},{1,0},{2,3},{3,2},{4,5},{5,4},{6,7},{7,6},{8,9},{9,8},{10,11... | collective-permute-start | bytes 1572872 | tf_op jit(solution)/shard_map/ppermute | solution.py:14
  35.1 14.1 %collective-permute-start.6 = (f32[512,256]{1,0:T(8,128)S(1)}, f32[512,256]{1,0:T(8,128)S(1)}, u32[]{:S(2)}, u32[]{:S(2)}) collective-permute-start(f32[512,256]{1,0:T(8,128)S(1)} %get-tuple-element.100), channel_id=1, source_target_pairs={{0,2},{2,0},{1,3},{3,1},{4,6},{6,4},{5,7},{7,5},{8,10},{10,8},{9,1... | collective-permute-start | bytes 1572872 | tf_op jit(solution)/shard_map/ppermute | solution.py:14
  39.5 13.9 %collective-permute-start.11 = (f32[256,512]{1,0:T(8,128)S(1)}, f32[256,512]{1,0:T(8,128)S(1)}, u32[]{:S(2)}, u32[]{:S(2)}) collective-permute-start(f32[256,512]{1,0:T(8,128)S(1)} %collective-permute-done.3.refs_0_), channel_id=1, source_target_pairs={{0,1},{1,0},{2,3},{3,2},{4,5},{5,4},{6,7},{7,6},{8,9},{9,8},{10,11... | collective-permute-start | bytes 1572872 | tf_op jit(solution)/shard_map/ppermute | solution.py:14
  39.5 13.9 %collective-permute-start.5 = (f32[360,256]{1,0:T(8,128)S(1)}, f32[360,256]{1,0:T(8,128)S(1)}, u32[]{:S(2)}, u32[]{:S(2)}) collective-permute-start(f32[360,256]{1,0:T(8,128)S(1)} %shard_map.114.refs_0_.s0), channel_id=1, source_target_pairs={{0,4},{4,0},{8,12},{12,8},{1,5},{5,1},{9,13},{13,9},{2,6},{6,2},{1... | collective-permute-start | bytes 1105928 | tf_op jit(solution)/shard_map/ppermute | solution.py:14
  46.4 9.5 %collective-permute-start.14 = (f32[512,256]{1,0:T(8,128)S(1)}, f32[512,256]{1,0:T(8,128)S(1)}, u32[]{:S(2)}, u32[]{:S(2)}) collective-permute-start(f32[512,256]{1,0:T(8,128)S(1)} %collective-permute-done.2.refs_0_), channel_id=1, source_target_pairs={{0,1},{1,0},{2,3},{3,2},{4,5},{5,4},{6,7},{7,6},{8,9},{9,8},{10,11... | collective-permute-start | bytes 1572872 | tf_op jit(solution)/shard_map/ppermute | solution.py:14
  46.4 14.6 %collective-permute-start.13 = (f32[256,512]{1,0:T(8,128)S(1)}, f32[256,512]{1,0:T(8,128)S(1)}, u32[]{:S(2)}, u32[]{:S(2)}) collective-permute-start(f32[256,512]{1,0:T(8,128)S(1)} %collective-permute-done.3.refs_0_), channel_id=1, source_target_pairs={{0,2},{2,0},{1,3},{3,1},{4,6},{6,4},{5,7},{7,5},{8,10},{10,8},{9,1... | collective-permute-start | bytes 1572872 | tf_op jit(solution)/shard_map/ppermute | solution.py:14
  49.3 11.7 %collective-permute-start.15 = (f32[512,256]{1,0:T(8,128)S(1)}, f32[512,256]{1,0:T(8,128)S(1)}, u32[]{:S(2)}, u32[]{:S(2)}) collective-permute-start(f32[512,256]{1,0:T(8,128)S(1)} %collective-permute-done.1.refs_0_), channel_id=1, source_target_pairs={{0,1},{1,0},{2,3},{3,2},{4,5},{5,4},{6,7},{7,6},{8,9},{9,8},{10,11... | collective-permute-start | bytes 1572872 | tf_op jit(solution)/shard_map/ppermute | solution.py:14
  53.4 9.3 %collective-permute-start.16 = (f32[360,256]{1,0:T(8,128)S(1)}, f32[360,256]{1,0:T(8,128)S(1)}, u32[]{:S(2)}, u32[]{:S(2)}) collective-permute-start(f32[360,256]{1,0:T(8,128)S(1)} %collective-permute-done.8.refs_0_.s2), channel_id=1, source_target_pairs={{0,1},{1,0},{2,3},{3,2},{4,5},{5,4},{6,7},{7,6},{8,9},{9,8},{10,11... | collective-permute-start | bytes 1105928 | tf_op jit(solution)/shard_map/ppermute | solution.py:14
  53.4 12.2 %collective-permute-start.12 = (f32[360,256]{1,0:T(8,128)S(1)}, f32[360,256]{1,0:T(8,128)S(1)}, u32[]{:S(2)}, u32[]{:S(2)}) collective-permute-start(f32[360,256]{1,0:T(8,128)S(1)} %collective-permute-done.8.refs_0_.s2), channel_id=1, source_target_pairs={{0,4},{4,0},{8,12},{12,8},{1,5},{5,1},{9,13},{13,9},{2,6},{6,2},{1... | collective-permute-start | bytes 1105928 | tf_op jit(solution)/shard_map/ppermute | solution.py:14
  55.9 9.8 %collective-permute-start.18 = (f32[512,256]{1,0:T(8,128)S(1)}, f32[512,256]{1,0:T(8,128)S(1)}, u32[]{:S(2)}, u32[]{:S(2)}) collective-permute-start(f32[512,256]{1,0:T(8,128)S(1)} %collective-permute-done.7.refs_0_), channel_id=1, source_target_pairs={{0,1},{1,0},{2,3},{3,2},{4,5},{5,4},{6,7},{7,6},{8,9},{9,8},{10,11... | collective-permute-start | bytes 1572872 | tf_op jit(solution)/shard_map/ppermute | solution.py:14
  60.9 5.5 %collective-permute-start.19 = (f32[512,256]{1,0:T(8,128)S(1)}, f32[512,256]{1,0:T(8,128)S(1)}, u32[]{:S(2)}, u32[]{:S(2)}) collective-permute-start(f32[512,256]{1,0:T(8,128)S(1)} %collective-permute-done.6.refs_0_), channel_id=1, source_target_pairs={{0,1},{1,0},{2,3},{3,2},{4,5},{5,4},{6,7},{7,6},{8,9},{9,8},{10,11... | collective-permute-start | bytes 1572872 | tf_op jit(solution)/shard_map/ppermute | solution.py:14
  60.9 14.3 %collective-permute-start.17 = (f32[512,256]{1,0:T(8,128)S(1)}, f32[512,256]{1,0:T(8,128)S(1)}, u32[]{:S(2)}, u32[]{:S(2)}) collective-permute-start(f32[512,256]{1,0:T(8,128)S(1)} %collective-permute-done.1.refs_0_), channel_id=1, source_target_pairs={{0,2},{2,0},{1,3},{3,1},{4,6},{6,4},{5,7},{7,5},{8,10},{10,8},{9,1... | collective-permute-start | bytes 1572872 | tf_op jit(solution)/shard_map/ppermute | solution.py:14
  62.7 14.1 %collective-permute-start.21 = (f32[512,256]{1,0:T(8,128)S(1)}, f32[512,256]{1,0:T(8,128)S(1)}, u32[]{:S(2)}, u32[]{:S(2)}) collective-permute-start(f32[512,256]{1,0:T(8,128)S(1)} %collective-permute-done.2.refs_0_), channel_id=1, source_target_pairs={{0,4},{4,0},{8,12},{12,8},{1,5},{5,1},{9,13},{13,9},{2,6},{6,2},{1... | collective-permute-start | bytes 1572872 | tf_op jit(solution)/shard_map/ppermute | solution.py:14
  65.6 10.2 %collective-permute-start.20 = (f32[360,256]{1,0:T(8,128)S(1)}, f32[360,256]{1,0:T(8,128)S(1)}, u32[]{:S(2)}, u32[]{:S(2)}) collective-permute-start(f32[360,256]{1,0:T(8,128)S(1)} %collective-permute-done.5.refs_0_.s1), channel_id=1, source_target_pairs={{0,1},{1,0},{2,3},{3,2},{4,5},{5,4},{6,7},{7,6},{8,9},{9,8},{10,11... | collective-permute-start | bytes 1105928 | tf_op jit(solution)/shard_map/ppermute | solution.py:14
  75.3 5.3 %collective-permute-start.24 = (f32[512,256]{1,0:T(8,128)S(1)}, f32[512,256]{1,0:T(8,128)S(1)}, u32[]{:S(2)}, u32[]{:S(2)}) collective-permute-start(f32[512,256]{1,0:T(8,128)S(1)} %collective-permute-done.17.refs_28_), channel_id=1, source_target_pairs={{0,1},{1,0},{2,3},{3,2},{4,5},{5,4},{6,7},{7,6},{8,9},{9,8},{10,11... | collective-permute-start | bytes 1572872 | tf_op jit(solution)/shard_map/ppermute | solution.py:14
  75.3 4.5 %collective-permute-start.23 = (f32[256,512]{1,0:T(8,128)S(1)}, f32[256,512]{1,0:T(8,128)S(1)}, u32[]{:S(2)}, u32[]{:S(2)}) collective-permute-start(f32[256,512]{1,0:T(8,128)S(1)} %collective-permute-done.13.refs_0_), channel_id=1, source_target_pairs={{0,1},{1,0},{2,3},{3,2},{4,5},{5,4},{6,7},{7,6},{8,9},{9,8},{10,11... | collective-permute-start | bytes 1572872 | tf_op jit(solution)/shard_map/ppermute | solution.py:14
  76.7 3.8 %collective-permute-start.25 = (f32[512,256]{1,0:T(8,128)S(1)}, f32[512,256]{1,0:T(8,128)S(1)}, u32[]{:S(2)}, u32[]{:S(2)}) collective-permute-start(f32[512,256]{1,0:T(8,128)S(1)} %collective-permute-done.21.refs_30_), channel_id=1, source_target_pairs={{0,1},{1,0},{2,3},{3,2},{4,5},{5,4},{6,7},{7,6},{8,9},{9,8},{10,11... | collective-permute-start | bytes 1572872 | tf_op jit(solution)/shard_map/ppermute | solution.py:14
  76.7 2.5 %collective-permute-start.22 = (f32[360,256]{1,0:T(8,128)S(1)}, f32[360,256]{1,0:T(8,128)S(1)}, u32[]{:S(2)}, u32[]{:S(2)}) collective-permute-start(f32[360,256]{1,0:T(8,128)S(1)} %collective-permute-done.12.refs_0_.s3), channel_id=1, source_target_pairs={{0,1},{1,0},{2,3},{3,2},{4,5},{5,4},{6,7},{7,6},{8,9},{9,8},{10,11... | collective-permute-start | bytes 1105928 | tf_op jit(solution)/shard_map/ppermute | solution.py:14
  (3 other events, 11.5 us)

commit v6 on v5

--- a/solution.py
+++ b/solution.py
@@ -31,6 +31,23 @@
     high, low = halves_of(value)
     high_ref[where] = high
     low_ref[where] = low
+
+
+PLAN = (
+    ("take", "Cx"), ("send", "Rx"), ("send", "By"), ("edge", "E"),
+    ("take", "Ly"), ("send", "Ey"),
+    ("take", "Lx", "B"), ("send", "Bx"), ("swap", "E"),
+    ("take", "By", "L"), ("send", "Ry"), ("swap", "Ly"),
+    ("take", "Rx", "R"), ("send", "Ex"), ("swap", "Lx"), ("split", "E"),
+    ("take", "Ey"), ("send", "Ld"), ("swap", "By"), ("split", "Ly"),
+    ("take", "Bx", "E"), ("send", "Ed"), ("swap", "Rx"), ("split", "Lx"),
+    ("take", "Ry", "Ly"), ("send", "Rd"), ("swap", "Ey"),
+    ("take", "Ex", "Lx"), ("send", "Bd"), ("swap", "Bx"), ("split", "By"), ("split", "Rx"),
+    ("take", "Ld"), ("swap", "Ry"), ("swap", "Ld"), ("split", "Ey"),
+    ("take", "Ed", "By", "Rx", "Ey"), ("swap", "Ex"), ("swap", "Ed"), ("split", "Bx"), ("split", "Ry"), ("split", "Ld"),
+    ("take", "Rd", "Ld"), ("swap", "Rd"), ("split", "Ex"), ("split", "Ed"),
+    ("take", "Bd", "Ex", "Ed"), ("swap", "Bd"),
+)
 
 
 CHEAP = pl.CostEstimate(flops=1, transcendentals=0, bytes_accessed=1)
@@ -72,7 +89,7 @@
     return jnp.sum(jnp.where(same, row, 0.0), axis=1, keepdims=True)
 
 
-def edge_state_kernel(place, mine, other, pair_cols, cells, one, two, mass, edge_ref):
+def edge_state_kernel(place, mine, other, pair_cols, cells, one, two, mass, weight, edge_ref, weight_ref):
     half = mine.shape[0]
     rows, width = one.shape
     for step, couple in enumerate((mine, other)):
@@ -85,18 +102,20 @@
     for index, value in enumerate((one[...], two[...], picked)):
         edge_ref[2 * half + index * rows:2 * half + (index + 1) * rows, :] = value
     edge_ref[2 * half + 3 * rows:, :] = jnp.broadcast_to(mass[...], (8, width))
-
-
-def small_call(kernel, shape, *values):
+    weight_ref[...] = weight[...]
+
+
+def edge_call(rows, place, *values):
     vmem = pl.BlockSpec(memory_space=pltpu.VMEM)
+    shapes = ((rows, values[2].shape[1]), values[-1].shape)
     return pl.pallas_call(
-        kernel,
-        in_specs=[pl.BlockSpec(memory_space=pltpu.SMEM)] + [vmem] * (len(values) - 1),
-        out_specs=vmem,
-        out_shape=jax.ShapeDtypeStruct(shape, F32),
+        edge_state_kernel,
+        in_specs=[pl.BlockSpec(memory_space=pltpu.SMEM)] + [vmem] * len(values),
+        out_specs=(vmem, vmem),
+        out_shape=tuple(jax.ShapeDtypeStruct(shape, F32) for shape in shapes),
         cost_estimate=CHEAP,
         compiler_params=pltpu.CompilerParams(vmem_limit_bytes=6 * 2**20),
-    )(*values)
+    )(place, *values)
 
 
 def split_tall(place, pieces, high_ref, low_ref):
@@ -229,100 +248,52 @@
     first_cell = ((column - x_bit) * lax.axis_size("gy") + row) * width
     place = jnp.stack([2 * y_bit + x_bit, core, first_cell, first_cell + lax.axis_size("gy") * width]).astype(jnp.int32)
 
-    tall, wide, edge = (tall_kernel, 4 * width), (wide_kernel, 4 * width), (edge_kernel, 2 * width)
-
-    couple_mine, lift_half = cut_call(place, (couple, lift), ((width // 2, 2 * width), (width, 2 * width)))
-
-    token = [place]
-    waiting = []
-    done = {}
-
-    def arrive(name, value, kernel=None, size=0, ready=()):
-        token[0] = after(value, token[0], *[done[other][0] for other in ready])
-        if kernel is not None:
-            waiting.append((name, kernel, size, token[0]))
-        return token[0]
-
-    def send(value, axis):
-        return from_partner(after(value, token[0]), axis)
-
-    def swap(count=1):
-        for _ in range(count):
-            name, kernel, size, value = waiting.pop(0)
-            done[name] = (kernel, size, value, send(value, "gz"))
-
-    def split(*names):
-        for name in names:
-            kernel, size, *pieces = done[name]
-            done[name] = split_call(kernel, after(place, token[0]), size, *pieces)
-
-    couple_other = from_partner(couple_mine, "gx")
-    lift_y = from_partner(lift_half, "gy")
-    lift_x = from_partner(lift_half, "gx")
-    back_half, root_half = cut_call(after(place, couple_other), (back, root), ((2 * width, width),) * 2)
-    done["L"] = split_call(wide_kernel, place, wide[1], after(lift, lift_half))
-    done["R"] = split_call(tall_kernel, place, tall[1], after(root, lift_half))
-    done["B"] = split_call(tall_kernel, place, tall[1], after(back, lift_half))
-    couple_other = arrive("C", couple_other)
-    root_x = send(root_half, "gx")
-    back_y = send(back_half, "gy")
-    edge_half = small_call(
-        edge_state_kernel,
-        (width + 3 * rows + 8, width),
-        place,
-        couple_mine,
-        couple_other,
-        pair_cols,
-        probe_cells[None, :],
-        adjoint_one_start[0, 0],
-        adjoint_two_start[0, 0],
-        mass_two[0],
-    )
-    waiting.append(("E", *edge, edge_half))
-    lift_y = arrive("Ly", lift_y, *wide)
-    edge_y = send(edge_half, "gy")
-    lift_x = arrive("Lx", lift_x, *wide)
-    back_x = send(back_half, "gx")
-    swap()
-    back_y = arrive("By", back_y, *tall, ready=("L",))
-    root_y = send(root_half, "gy")
-    swap()
-    root_x = arrive("Rx", root_x, *tall, ready=("R",))
-    edge_x = send(edge_half, "gx")
-    swap()
-    split("E")
-    edge_y = arrive("Ey", edge_y, *edge, ready=("B",))
-    lift_d = send(lift_x, "gy")
-    swap()
-    split("Ly")
-    back_x = arrive("Bx", back_x, *tall, ready=("E",))
-    edge_d = send(edge_y, "gx")
-    swap()
-    split("Lx")
-    root_y = arrive("Ry", root_y, *tall, ready=("Ly",))
-    root_d = send(root_x, "gy")
-    swap()
-    split("By")
-    edge_x = arrive("Ex", edge_x, *edge, ready=("Lx",))
-    back_d = send(back_y, "gx")
-    swap()
-    split("Rx")
-    lift_d = arrive("Ld", lift_d, *wide, ready=("By",))
-    swap()
-    split("Ey")
-    edge_d = arrive("Ed", edge_d, *edge, ready=("Rx", "Ey"))
-    swap()
-    split("Bx", "Ry")
-    root_d = arrive("Rd", root_d, ready=("Bx", "Ry"))
-    swap(2)
-    split("Ex")
-    back_d = arrive("Bd", back_d, ready=("Ex",))
-    split("Ld", "Ed")
+    couple_half, lift_half = cut_call(place, (couple, lift), ((width // 2, 2 * width), (width, 2 * width)))
+    value = {"Cx": from_partner(couple_half, "gx"), "Ly": from_partner(lift_half, "gy"), "Lx": from_partner(lift_half, "gx")}
+    back_half, root_half = cut_call(after(place, value["Cx"]), (back, root), ((2 * width, width),) * 2)
+    own = {"L": lift_half, "B": back_half, "R": root_half}
+    kernels = {"L": (wide_kernel, 4 * width), "R": (tall_kernel, 4 * width), "B": (tall_kernel, 4 * width), "E": (edge_kernel, 2 * width)}
+    whole = after(place, lift_half)
+    ready = {
+        name: split_call(kernels[name][0], whole, kernels[name][1], panel)
+        for name, panel in (("L", lift), ("R", root), ("B", back))
+    }
+    other = {}
+    token = place
+    for verb, name, *earlier in PLAN:
+        kind, where = name[0], name[1:]
+        if verb == "take":
+            token = value[name] = after(value[name], token, *[ready[panel][0] for panel in earlier])
+        elif verb == "edge":
+            own["E"], weight = edge_call(
+                width + 3 * rows + 8,
+                place,
+                couple_half,
+                value["Cx"],
+                pair_cols,
+                probe_cells[None, :],
+                adjoint_one_start[0, 0],
+                adjoint_two_start[0, 0],
+                mass_two[0],
+                probe_weight,
+            )
+            value["E"] = own["E"]
+        elif verb == "send":
+            axis = where if where != "d" else "x" if kind in "EB" else "y"
+            source = own[kind] if where != "d" else value[kind + ("y" if axis == "x" else "x")]
+            value[name] = from_partner(after(source, token), "g" + axis)
+        elif verb == "swap":
+            other[name] = from_partner(after(value[name], token), "gz")
+        else:
+            kernel, size = kernels[kind]
+            ready[name] = split_call(kernel, after(place, token), size, value[name], other[name])
 
     vmem, smem = pl.BlockSpec(memory_space=pltpu.VMEM), pl.BlockSpec(memory_space=pltpu.SMEM)
-    panels = done["E"] + done["Ex"] + done["Ey"] + done["Ed"] + done["L"] + done["Lx"] + done["Ly"] + done["Ld"]
-    panels += done["R"] + done["Rx"] + done["Ry"] + done["B"] + done["Bx"] + done["By"]
-    panels += (root_d, from_partner(root_d, "gz"), back_d, from_partner(back_d, "gz"))
+    panels = ()
+    for kind, tiles in (("E", ("", "x", "y", "d")), ("L", ("", "x", "y", "d")), ("R", ("", "x", "y")), ("B", ("", "x", "y"))):
+        for tile in tiles:
+            panels += ready[kind + tile]
+    panels += (value["Rd"], other["Rd"], value["Bd"], other["Bd"])
     one, two = pl.pallas_call(
         march_kernel,
         in_specs=[vmem] * 5 + [smem] + [vmem] * len(panels),
@@ -330,7 +301,7 @@
         out_shape=(jax.ShapeDtypeStruct((rows, width), F32),) * 2,
         scratch_shapes=[pltpu.VMEM((4 * width, width), BF16)] * 4,
         compiler_params=pltpu.CompilerParams(vmem_limit_bytes=12 * 2**20),
-    )(edge_half, edge_x, edge_y, edge_d, probe_weight, place, *panels)
+    )(own["E"], value["Ex"], value["Ey"], value["Ed"], weight, place, *panels)
     return (one[None, None], two[None, None])
 
 

time: 106 us -> 104 us (0.981)
  starting transfers between devices: 22.7 us -> 21.2 us
    ppermute x26, starting transfers between devices: 22.7 us -> 21.2 us  [from_partner(): return lax.ppermute(value, axis, pairs)]
  transfers between devices with their start and end apart: 26 -> 26, of which waited for: 13 -> 12; matrix products, arithmetic and copies ran while one was open for 0% -> 0% of each run, Pallas kernels for 12% -> 12%
where the time goes in v6:
time: 104 us
  waiting for transfers between devices  41.9 us (40%)
  Pallas kernels  39.4 us (38%)
  starting transfers between devices  21.2 us (20%)
    ppermute x26, waiting for transfers between devices, from_partner(): return lax.ppermute(value, axis, pairs)  41.9 us
    pallas_call x1, Pallas kernels, shards(): pl.pallas_call(march_kernel, in_specs=[vmem] * 5 + [smem] + [vmem] * len(...  25 us
    ppermute x26, starting transfers between devices, from_partner(): return lax.ppermute(value, axis, pairs)  21.2 us
    pallas_call x14, Pallas kernels, split_call(): pl.pallas_call(kernel, in_specs=[pl.BlockSpec(memory_space=pltpu.SMEM)] +...  9.5 us
    pallas_call x2, Pallas kernels, cut_call(): pl.pallas_call(cut_kernel, in_specs=[pl.BlockSpec(memory_space=pltpu.SMEM...  3.45 us
  transfers between devices with their start and end apart: 26, of which 12 were waited for; matrix products, arithmetic and copies ran while one was open for 0% of the time, Pallas kernels for 12%

profile of v6, /device:TPU:0, one launch (start us, length us, event | category | flops | bytes accessed | tf_op | source)
XLA Modules:
  0.0 103.6 jit_solution(13012801357651673917)
XLA Ops:
  0.7 1.7 %shard_map.113 = (f32[128,512]{1,0:T(8,128)S(1)}, f32[256,512]{1,0:T(8,128)S(1)}) custom-call(s32[4]{0:T(128)S(1)} %pad_add_fusion.place, f32[256,512]{1,0:T(8,128)} %bitcast.26, f32[256,1024]{1,0:T(8,128)} %bitcast.19), custom_call_target="tpu_custom_call" | custom-call | flops 1 | bytes 1 | tf_op jit(solution)/shard_map/pallas_call | solution.py:75
  2.4 3.1 %collective-permute-start = (f32[128,512]{1,0:T(8,128)S(1)}, f32[128,512]{1,0:T(8,128)S(1)}, u32[]{:S(2)}, u32[]{:S(2)}) collective-permute-start(f32[128,512]{1,0:T(8,128)S(1)} %get-tuple-element.83.mine), channel_id=1, source_target_pairs={{0,4},{4,0},{8,12},{12,8},{1,5},{5,1},{9,13},{13,9},{2,6},{6,2},{1... | collective-permute-start | bytes 786440 | tf_op jit(solution)/shard_map/ppermute | solution.py:14
  5.5 1.5 %collective-permute-start.4 = (f32[256,512]{1,0:T(8,128)S(1)}, f32[256,512]{1,0:T(8,128)S(1)}, u32[]{:S(2)}, u32[]{:S(2)}) collective-permute-start(f32[256,512]{1,0:T(8,128)S(1)} %get-tuple-element.91), channel_id=1, source_target_pairs={{0,2},{2,0},{1,3},{3,1},{4,6},{6,4},{5,7},{7,5},{8,10},{10,8},{9,1... | collective-permute-start | bytes 1572872 | tf_op jit(solution)/shard_map/ppermute | solution.py:14
  7.5 5.2 %collective-permute-done.other = f32[128,512]{1,0:T(8,128)S(1)} collective-permute-done((f32[128,512]{1,0:T(8,128)S(1)}, f32[128,512]{1,0:T(8,128)S(1)}, u32[]{:S(2)}, u32[]{:S(2)}) %collective-permute-start) | collective-permute-done | bytes 262176 | tf_op jit(solution)/shard_map/ppermute | solution.py:14
  12.7 1.8 %shard_map.115 = (f32[512,256]{1,0:T(8,128)S(1)}, f32[512,256]{1,0:T(8,128)S(1)}) custom-call(s32[4]{0:T(128)S(1)} %pad_add_fusion.place, f32[1024,256]{1,0:T(8,128)} %bitcast.15, f32[1024,256]{1,0:T(8,128)} %bitcast.17), custom_call_target="tpu_custom_call" | custom-call | flops 1 | bytes 1 | tf_op jit(solution)/shard_map/pallas_call | solution.py:75
  14.5 2.0 %collective-permute-start.2 = (f32[512,256]{1,0:T(8,128)S(1)}, f32[512,256]{1,0:T(8,128)S(1)}, u32[]{:S(2)}, u32[]{:S(2)}) collective-permute-start(f32[512,256]{1,0:T(8,128)S(1)} %get-tuple-element.102), channel_id=1, source_target_pairs={{0,2},{2,0},{1,3},{3,1},{4,6},{6,4},{5,7},{7,5},{8,10},{10,8},{9,1... | collective-permute-start | bytes 1572872 | tf_op jit(solution)/shard_map/ppermute | solution.py:14
  16.5 1.6 %collective-permute-start.1 = (f32[512,256]{1,0:T(8,128)S(1)}, f32[512,256]{1,0:T(8,128)S(1)}, u32[]{:S(2)}, u32[]{:S(2)}) collective-permute-start(f32[512,256]{1,0:T(8,128)S(1)} %get-tuple-element.101), channel_id=1, source_target_pairs={{0,4},{4,0},{8,12},{12,8},{1,5},{5,1},{9,13},{13,9},{2,6},{6,2},{1... | collective-permute-start | bytes 1572872 | tf_op jit(solution)/shard_map/ppermute | solution.py:14
  18.1 1.5 %shard_map.114 = (f32[360,256]{1,0:T(8,128)S(1)}, f32[9,32]{1,0:T(8,128)S(1)}) custom-call(s32[4]{0:T(128)S(1)} %pad_add_fusion.place, f32[128,512]{1,0:T(8,128)S(1)} %get-tuple-element.83.mine, f32[128,512]{1,0:T(8,128)S(1)} %collective-permute-done.other, f32[512,256]{1,0:T(8,128)S(1)} %bitcast.21, s32[1,32]{1,0:T(1,128)S(1)} %bitcast.25, ...), custom_call_target="tpu_custom_call" | custom-call | flops 1 | bytes 1 | tf_op jit(solution)/shard_map/pallas_call | solution.py:111
  19.6 0.7 collective-permute-done.4.refs_0_
  20.4 1.5 %collective-permute-start.8 = (f32[360,256]{1,0:T(8,128)S(1)}, f32[360,256]{1,0:T(8,128)S(1)}, u32[]{:S(2)}, u32[]{:S(2)}) collective-permute-start(f32[360,256]{1,0:T(8,128)S(1)} %get-tuple-element.106.refs_0_.s0), channel_id=1, source_target_pairs={{0,2},{2,0},{1,3},{3,1},{4,6},{6,4},{5,7},{7,5},{8,10},{10,8},{9,1... | collective-permute-start | bytes 1105928 | tf_op jit(solution)/shard_map/ppermute | solution.py:14
  22.6 1.3 %collective-permute-done.3.refs_0_ = f32[256,512]{1,0:T(8,128)S(1)} collective-permute-done((f32[256,512]{1,0:T(8,128)S(1)}, f32[256,512]{1,0:T(8,128)S(1)}, u32[]{:S(2)}, u32[]{:S(2)}) %collective-permute-start.3) | collective-permute-done | bytes 524320 | tf_op jit(solution)/shard_map/ppermute | solution.py:14
  23.9 2.1 %collective-permute-start.7 = (f32[512,256]{1,0:T(8,128)S(1)}, f32[512,256]{1,0:T(8,128)S(1)}, u32[]{:S(2)}, u32[]{:S(2)}) collective-permute-start(f32[512,256]{1,0:T(8,128)S(1)} %get-tuple-element.102), channel_id=1, source_target_pairs={{0,4},{4,0},{8,12},{12,8},{1,5},{5,1},{9,13},{13,9},{2,6},{6,2},{1... | collective-permute-start | bytes 1572872 | tf_op jit(solution)/shard_map/ppermute | solution.py:14
  26.7 4.9 %collective-permute-done.2.refs_0_ = f32[512,256]{1,0:T(8,128)S(1)} collective-permute-done((f32[512,256]{1,0:T(8,128)S(1)}, f32[512,256]{1,0:T(8,128)S(1)}, u32[]{:S(2)}, u32[]{:S(2)}) %collective-permute-start.2) | collective-permute-done | bytes 524320 | tf_op jit(solution)/shard_map/ppermute | solution.py:14
  31.6 1.5 %collective-permute-start.6 = (f32[512,256]{1,0:T(8,128)S(1)}, f32[512,256]{1,0:T(8,128)S(1)}, u32[]{:S(2)}, u32[]{:S(2)}) collective-permute-start(f32[512,256]{1,0:T(8,128)S(1)} %get-tuple-element.101), channel_id=1, source_target_pairs={{0,2},{2,0},{1,3},{3,1},{4,6},{6,4},{5,7},{7,5},{8,10},{10,8},{9,1... | collective-permute-start | bytes 1572872 | tf_op jit(solution)/shard_map/ppermute | solution.py:14
  33.1 2.0 %collective-permute-done.1.refs_0_ = f32[512,256]{1,0:T(8,128)S(1)} collective-permute-done((f32[512,256]{1,0:T(8,128)S(1)}, f32[512,256]{1,0:T(8,128)S(1)}, u32[]{:S(2)}, u32[]{:S(2)}) %collective-permute-start.1) | collective-permute-done | bytes 524320 | tf_op jit(solution)/shard_map/ppermute | solution.py:14
  35.8 3.7 %collective-permute-done.8.refs_0_.s2 = f32[360,256]{1,0:T(8,128)S(1)} collective-permute-done((f32[360,256]{1,0:T(8,128)S(1)}, f32[360,256]{1,0:T(8,128)S(1)}, u32[]{:S(2)}, u32[]{:S(2)}) %collective-permute-start.8) | collective-permute-done | bytes 368672 | tf_op jit(solution)/shard_map/ppermute | solution.py:14
  39.5 6.8 %collective-permute-done.7.refs_0_ = f32[512,256]{1,0:T(8,128)S(1)} collective-permute-done((f32[512,256]{1,0:T(8,128)S(1)}, f32[512,256]{1,0:T(8,128)S(1)}, u32[]{:S(2)}, u32[]{:S(2)}) %collective-permute-start.7) | collective-permute-done | bytes 524320 | tf_op jit(solution)/shard_map/ppermute | solution.py:14
  46.4 2.0 %collective-permute-start.13 = (f32[256,512]{1,0:T(8,128)S(1)}, f32[256,512]{1,0:T(8,128)S(1)}, u32[]{:S(2)}, u32[]{:S(2)}) collective-permute-start(f32[256,512]{1,0:T(8,128)S(1)} %collective-permute-done.3.refs_0_), channel_id=1, source_target_pairs={{0,2},{2,0},{1,3},{3,1},{4,6},{6,4},{5,7},{7,5},{8,10},{10,8},{9,1... | collective-permute-start | bytes 1572872 | tf_op jit(solution)/shard_map/ppermute | solution.py:14
  48.3 2.4 %collective-permute-done.6.refs_0_ = f32[512,256]{1,0:T(8,128)S(1)} collective-permute-done((f32[512,256]{1,0:T(8,128)S(1)}, f32[512,256]{1,0:T(8,128)S(1)}, u32[]{:S(2)}, u32[]{:S(2)}) %collective-permute-start.6) | collective-permute-done | bytes 524320 | tf_op jit(solution)/shard_map/ppermute | solution.py:14
  51.9 0.7 shard_map.120
  52.6 0.8 collective-permute-done.5.refs_0_.s1
  53.4 1.7 %collective-permute-start.12 = (f32[360,256]{1,0:T(8,128)S(1)}, f32[360,256]{1,0:T(8,128)S(1)}, u32[]{:S(2)}, u32[]{:S(2)}) collective-permute-start(f32[360,256]{1,0:T(8,128)S(1)} %collective-permute-done.8.refs_0_.s2), channel_id=1, source_target_pairs={{0,4},{4,0},{8,12},{12,8},{1,5},{5,1},{9,13},{13,9},{2,6},{6,2},{1... | collective-permute-start | bytes 1105928 | tf_op jit(solution)/shard_map/ppermute | solution.py:14
  55.2 0.7 shard_map.121
  55.9 4.6 %collective-permute-done.13.refs_0_ = f32[256,512]{1,0:T(8,128)S(1)} collective-permute-done((f32[256,512]{1,0:T(8,128)S(1)}, f32[256,512]{1,0:T(8,128)S(1)}, u32[]{:S(2)}, u32[]{:S(2)}) %collective-permute-start.13) | collective-permute-done | bytes 524320 | tf_op jit(solution)/shard_map/ppermute | solution.py:14
  60.5 1.5 %collective-permute-start.17 = (f32[512,256]{1,0:T(8,128)S(1)}, f32[512,256]{1,0:T(8,128)S(1)}, u32[]{:S(2)}, u32[]{:S(2)}) collective-permute-start(f32[512,256]{1,0:T(8,128)S(1)} %collective-permute-done.1.refs_0_), channel_id=1, source_target_pairs={{0,2},{2,0},{1,3},{3,1},{4,6},{6,4},{5,7},{7,5},{8,10},{10,8},{9,1... | collective-permute-start | bytes 1572872 | tf_op jit(solution)/shard_map/ppermute | solution.py:14
  62.5 0.7 shard_map.122
  63.2 0.7 shard_map.123
  65.2 0.7 shard_map.125
  65.9 9.0 %collective-permute-done.17.refs_28_ = f32[512,256]{1,0:T(8,128)S(1)} collective-permute-done((f32[512,256]{1,0:T(8,128)S(1)}, f32[512,256]{1,0:T(8,128)S(1)}, u32[]{:S(2)}, u32[]{:S(2)}) %collective-permute-start.17) | collective-permute-done | bytes 524320 | tf_op jit(solution)/shard_map/ppermute | solution.py:14
  76.7 0.7 shard_map.129
  77.4 0.7 shard_map.128
  78.6 25.0 %shard_map.130 = (f32[32,256]{1,0:T(8,128)}, f32[32,256]{1,0:T(8,128)}) custom-call(f32[360,256]{1,0:T(8,128)S(1)} %get-tuple-element.106.refs_0_.s0, f32[360,256]{1,0:T(8,128)S(1)} %collective-permute-done.5.refs_0_.s1, f32[360,256]{1,0:T(8,128)S(1)} %collective-permute-done.8.refs_0_.s2, f32[360,256]{1,0:T(8,128)S(1)} %collective-permute-done.12.refs_0_.s3, ...), custom_call_target="tpu_custom_call" | custom-call | tf_op jit(solution)/shard_map/pallas_call | solution.py:297
  (57 shorter events, 7.9 us)
Async XLA Ops:
  2.4 10.2 %collective-permute-start = (f32[128,512]{1,0:T(8,128)S(1)}, f32[128,512]{1,0:T(8,128)S(1)}, u32[]{:S(2)}, u32[]{:S(2)}) collective-permute-start(f32[128,512]{1,0:T(8,128)S(1)} %get-tuple-element.83.mine), channel_id=1, source_target_pairs={{0,4},{4,0},{8,12},{12,8},{1,5},{5,1},{9,13},{13,9},{2,6},{6,2},{1... | collective-permute-start | bytes 786440 | tf_op jit(solution)/shard_map/ppermute | solution.py:14
  5.5 14.8 %collective-permute-start.4 = (f32[256,512]{1,0:T(8,128)S(1)}, f32[256,512]{1,0:T(8,128)S(1)}, u32[]{:S(2)}, u32[]{:S(2)}) collective-permute-start(f32[256,512]{1,0:T(8,128)S(1)} %get-tuple-element.91), channel_id=1, source_target_pairs={{0,2},{2,0},{1,3},{3,1},{4,6},{6,4},{5,7},{7,5},{8,10},{10,8},{9,1... | collective-permute-start | bytes 1572872 | tf_op jit(solution)/shard_map/ppermute | solution.py:14
  7.0 16.9 %collective-permute-start.3 = (f32[256,512]{1,0:T(8,128)S(1)}, f32[256,512]{1,0:T(8,128)S(1)}, u32[]{:S(2)}, u32[]{:S(2)}) collective-permute-start(f32[256,512]{1,0:T(8,128)S(1)} %get-tuple-element.91), channel_id=1, source_target_pairs={{0,4},{4,0},{8,12},{12,8},{1,5},{5,1},{9,13},{13,9},{2,6},{6,2},{1... | collective-permute-start | bytes 1572872 | tf_op jit(solution)/shard_map/ppermute | solution.py:14
  12.6 5.4 %copy-start.5 = (f32[1,1,32,256]{3,2,1,0:T(8,128)S(1)}, f32[1,1,32,256]{3,2,1,0:T(8,128)}, u32[]{:S(2)}) copy-start(f32[1,1,32,256]{3,2,1,0:T(8,128)} %param.11) | copy-start | bytes 98308
  12.7 5.4 %copy-start.6 = (f32[9,32]{1,0:T(8,128)S(1)}, f32[9,32]{1,0:T(8,128)}, u32[]{:S(2)}) copy-start(f32[9,32]{1,0:T(8,128)} %weight.1) | copy-start | bytes 3460
  12.7 5.4 %copy-start.7 = (f32[1,1,256]{2,1,0:T(1,128)S(1)}, f32[1,1,256]{2,1,0:T(1,128)}, u32[]{:S(2)}) copy-start(f32[1,1,256]{2,1,0:T(1,128)} %param.17) | copy-start | bytes 3076
  14.5 7.4 %copy-start = (f32[1,1,1024,256]{3,2,1,0:T(8,128)S(1)}, f32[1,1,1024,256]{3,2,1,0:T(8,128)}, u32[]{:S(2)}) copy-start(f32[1,1,1024,256]{3,2,1,0:T(8,128)} %param.16) | copy-start | bytes 3145732
  14.5 17.1 %collective-permute-start.2 = (f32[512,256]{1,0:T(8,128)S(1)}, f32[512,256]{1,0:T(8,128)S(1)}, u32[]{:S(2)}, u32[]{:S(2)}) collective-permute-start(f32[512,256]{1,0:T(8,128)S(1)} %get-tuple-element.102), channel_id=1, source_target_pairs={{0,2},{2,0},{1,3},{3,1},{4,6},{6,4},{5,7},{7,5},{8,10},{10,8},{9,1... | collective-permute-start | bytes 1572872 | tf_op jit(solution)/shard_map/ppermute | solution.py:14
  16.5 18.6 %collective-permute-start.1 = (f32[512,256]{1,0:T(8,128)S(1)}, f32[512,256]{1,0:T(8,128)S(1)}, u32[]{:S(2)}, u32[]{:S(2)}) collective-permute-start(f32[512,256]{1,0:T(8,128)S(1)} %get-tuple-element.101), channel_id=1, source_target_pairs={{0,4},{4,0},{8,12},{12,8},{1,5},{5,1},{9,13},{13,9},{2,6},{6,2},{1... | collective-permute-start | bytes 1572872 | tf_op jit(solution)/shard_map/ppermute | solution.py:14
  18.1 7.8 %copy-start.2 = (f32[1,1,256,1024]{3,2,1,0:T(8,128)S(1)}, f32[1,1,256,1024]{3,2,1,0:T(8,128)}, u32[]{:S(2)}) copy-start(f32[1,1,256,1024]{3,2,1,0:T(8,128)} %param.14) | copy-start | bytes 3145732
  20.4 14.8 %copy-start.1 = (f32[1,1,1024,256]{3,2,1,0:T(8,128)S(1)}, f32[1,1,1024,256]{3,2,1,0:T(8,128)}, u32[]{:S(2)}) copy-start(f32[1,1,1024,256]{3,2,1,0:T(8,128)} %param.15) | copy-start | bytes 3145732
  20.4 19.1 %collective-permute-start.8 = (f32[360,256]{1,0:T(8,128)S(1)}, f32[360,256]{1,0:T(8,128)S(1)}, u32[]{:S(2)}, u32[]{:S(2)}) collective-permute-start(f32[360,256]{1,0:T(8,128)S(1)} %get-tuple-element.106.refs_0_.s0), channel_id=1, source_target_pairs={{0,2},{2,0},{1,3},{3,1},{4,6},{6,4},{5,7},{7,5},{8,10},{10,8},{9,1... | collective-permute-start | bytes 1105928 | tf_op jit(solution)/shard_map/ppermute | solution.py:14
  23.9 22.5 %collective-permute-start.7 = (f32[512,256]{1,0:T(8,128)S(1)}, f32[512,256]{1,0:T(8,128)S(1)}, u32[]{:S(2)}, u32[]{:S(2)}) collective-permute-start(f32[512,256]{1,0:T(8,128)S(1)} %get-tuple-element.102), channel_id=1, source_target_pairs={{0,4},{4,0},{8,12},{12,8},{1,5},{5,1},{9,13},{13,9},{2,6},{6,2},{1... | collective-permute-start | bytes 1572872 | tf_op jit(solution)/shard_map/ppermute | solution.py:14
  31.6 19.1 %collective-permute-start.6 = (f32[512,256]{1,0:T(8,128)S(1)}, f32[512,256]{1,0:T(8,128)S(1)}, u32[]{:S(2)}, u32[]{:S(2)}) collective-permute-start(f32[512,256]{1,0:T(8,128)S(1)} %get-tuple-element.101), channel_id=1, source_target_pairs={{0,2},{2,0},{1,3},{3,1},{4,6},{6,4},{5,7},{7,5},{8,10},{10,8},{9,1... | collective-permute-start | bytes 1572872 | tf_op jit(solution)/shard_map/ppermute | solution.py:14
  33.1 18.3 %collective-permute-start.10 = (f32[256,512]{1,0:T(8,128)S(1)}, f32[256,512]{1,0:T(8,128)S(1)}, u32[]{:S(2)}, u32[]{:S(2)}) collective-permute-start(f32[256,512]{1,0:T(8,128)S(1)} %collective-permute-done.4.refs_0_), channel_id=1, source_target_pairs={{0,1},{1,0},{2,3},{3,2},{4,5},{5,4},{6,7},{7,6},{8,9},{9,8},{10,11... | collective-permute-start | bytes 1572872 | tf_op jit(solution)/shard_map/ppermute | solution.py:14
  35.1 4.4 %collective-permute-start.9 = (f32[360,256]{1,0:T(8,128)S(1)}, f32[360,256]{1,0:T(8,128)S(1)}, u32[]{:S(2)}, u32[]{:S(2)}) collective-permute-start(f32[360,256]{1,0:T(8,128)S(1)} %get-tuple-element.106.refs_0_.s0), channel_id=1, source_target_pairs={{0,1},{1,0},{2,3},{3,2},{4,5},{5,4},{6,7},{7,6},{8,9},{9,8},{10,11... | collective-permute-start | bytes 1105928 | tf_op jit(solution)/shard_map/ppermute | solution.py:14
  39.5 13.9 %collective-permute-start.11 = (f32[256,512]{1,0:T(8,128)S(1)}, f32[256,512]{1,0:T(8,128)S(1)}, u32[]{:S(2)}, u32[]{:S(2)}) collective-permute-start(f32[256,512]{1,0:T(8,128)S(1)} %collective-permute-done.3.refs_0_), channel_id=1, source_target_pairs={{0,1},{1,0},{2,3},{3,2},{4,5},{5,4},{6,7},{7,6},{8,9},{9,8},{10,11... | collective-permute-start | bytes 1572872 | tf_op jit(solution)/shard_map/ppermute | solution.py:14
  39.5 13.9 %collective-permute-start.5 = (f32[360,256]{1,0:T(8,128)S(1)}, f32[360,256]{1,0:T(8,128)S(1)}, u32[]{:S(2)}, u32[]{:S(2)}) collective-permute-start(f32[360,256]{1,0:T(8,128)S(1)} %get-tuple-element.106.refs_0_.s0), channel_id=1, source_target_pairs={{0,4},{4,0},{8,12},{12,8},{1,5},{5,1},{9,13},{13,9},{2,6},{6,2},{1... | collective-permute-start | bytes 1105928 | tf_op jit(solution)/shard_map/ppermute | solution.py:14
  46.4 14.1 %collective-permute-start.13 = (f32[256,512]{1,0:T(8,128)S(1)}, f32[256,512]{1,0:T(8,128)S(1)}, u32[]{:S(2)}, u32[]{:S(2)}) collective-permute-start(f32[256,512]{1,0:T(8,128)S(1)} %collective-permute-done.3.refs_0_), channel_id=1, source_target_pairs={{0,2},{2,0},{1,3},{3,1},{4,6},{6,4},{5,7},{7,5},{8,10},{10,8},{9,1... | collective-permute-start | bytes 1572872 | tf_op jit(solution)/shard_map/ppermute | solution.py:14
  50.7 9.8 %collective-permute-start.14 = (f32[512,256]{1,0:T(8,128)S(1)}, f32[512,256]{1,0:T(8,128)S(1)}, u32[]{:S(2)}, u32[]{:S(2)}) collective-permute-start(f32[512,256]{1,0:T(8,128)S(1)} %collective-permute-done.2.refs_0_), channel_id=1, source_target_pairs={{0,1},{1,0},{2,3},{3,2},{4,5},{5,4},{6,7},{7,6},{8,9},{9,8},{10,11... | collective-permute-start | bytes 1572872 | tf_op jit(solution)/shard_map/ppermute | solution.py:14
  51.4 10.6 %collective-permute-start.15 = (f32[512,256]{1,0:T(8,128)S(1)}, f32[512,256]{1,0:T(8,128)S(1)}, u32[]{:S(2)}, u32[]{:S(2)}) collective-permute-start(f32[512,256]{1,0:T(8,128)S(1)} %collective-permute-done.1.refs_0_), channel_id=1, source_target_pairs={{0,1},{1,0},{2,3},{3,2},{4,5},{5,4},{6,7},{7,6},{8,9},{9,8},{10,11... | collective-permute-start | bytes 1572872 | tf_op jit(solution)/shard_map/ppermute | solution.py:14
  53.4 10.5 %collective-permute-start.16 = (f32[360,256]{1,0:T(8,128)S(1)}, f32[360,256]{1,0:T(8,128)S(1)}, u32[]{:S(2)}, u32[]{:S(2)}) collective-permute-start(f32[360,256]{1,0:T(8,128)S(1)} %collective-permute-done.8.refs_0_.s2), channel_id=1, source_target_pairs={{0,1},{1,0},{2,3},{3,2},{4,5},{5,4},{6,7},{7,6},{8,9},{9,8},{10,11... | collective-permute-start | bytes 1105928 | tf_op jit(solution)/shard_map/ppermute | solution.py:14
  53.4 11.1 %collective-permute-start.12 = (f32[360,256]{1,0:T(8,128)S(1)}, f32[360,256]{1,0:T(8,128)S(1)}, u32[]{:S(2)}, u32[]{:S(2)}) collective-permute-start(f32[360,256]{1,0:T(8,128)S(1)} %collective-permute-done.8.refs_0_.s2), channel_id=1, source_target_pairs={{0,4},{4,0},{8,12},{12,8},{1,5},{5,1},{9,13},{13,9},{2,6},{6,2},{1... | collective-permute-start | bytes 1105928 | tf_op jit(solution)/shard_map/ppermute | solution.py:14
  60.5 4.6 %collective-permute-start.18 = (f32[256,512]{1,0:T(8,128)S(1)}, f32[256,512]{1,0:T(8,128)S(1)}, u32[]{:S(2)}, u32[]{:S(2)}) collective-permute-start(f32[256,512]{1,0:T(8,128)S(1)} %collective-permute-done.13.refs_0_), channel_id=1, source_target_pairs={{0,1},{1,0},{2,3},{3,2},{4,5},{5,4},{6,7},{7,6},{8,9},{9,8},{10,11... | collective-permute-start | bytes 1572872 | tf_op jit(solution)/shard_map/ppermute | solution.py:14
  60.5 14.3 %collective-permute-start.17 = (f32[512,256]{1,0:T(8,128)S(1)}, f32[512,256]{1,0:T(8,128)S(1)}, u32[]{:S(2)}, u32[]{:S(2)}) collective-permute-start(f32[512,256]{1,0:T(8,128)S(1)} %collective-permute-done.1.refs_0_), channel_id=1, source_target_pairs={{0,2},{2,0},{1,3},{3,1},{4,6},{6,4},{5,7},{7,5},{8,10},{10,8},{9,1... | collective-permute-start | bytes 1572872 | tf_op jit(solution)/shard_map/ppermute | solution.py:14
  62.0 14.6 %collective-permute-start.24 = (f32[512,256]{1,0:T(8,128)S(1)}, f32[512,256]{1,0:T(8,128)S(1)}, u32[]{:S(2)}, u32[]{:S(2)}) collective-permute-start(f32[512,256]{1,0:T(8,128)S(1)} %collective-permute-done.2.refs_0_), channel_id=1, source_target_pairs={{0,4},{4,0},{8,12},{12,8},{1,5},{5,1},{9,13},{13,9},{2,6},{6,2},{1... | collective-permute-start | bytes 1572872 | tf_op jit(solution)/shard_map/ppermute | solution.py:14
  64.5 10.3 %collective-permute-start.19 = (f32[360,256]{1,0:T(8,128)S(1)}, f32[360,256]{1,0:T(8,128)S(1)}, u32[]{:S(2)}, u32[]{:S(2)}) collective-permute-start(f32[360,256]{1,0:T(8,128)S(1)} %collective-permute-done.5.refs_0_.s1), channel_id=1, source_target_pairs={{0,1},{1,0},{2,3},{3,2},{4,5},{5,4},{6,7},{7,6},{8,9},{9,8},{10,11... | collective-permute-start | bytes 1105928 | tf_op jit(solution)/shard_map/ppermute | solution.py:14
  64.6 11.4 %collective-permute-start.20 = (f32[360,256]{1,0:T(8,128)S(1)}, f32[360,256]{1,0:T(8,128)S(1)}, u32[]{:S(2)}, u32[]{:S(2)}) collective-permute-start(f32[360,256]{1,0:T(8,128)S(1)} %collective-permute-done.12.refs_0_.s3), channel_id=1, source_target_pairs={{0,1},{1,0},{2,3},{3,2},{4,5},{5,4},{6,7},{7,6},{8,9},{9,8},{10,11... | collective-permute-start | bytes 1105928 | tf_op jit(solution)/shard_map/ppermute | solution.py:14
  65.1 11.6 %collective-permute-start.22 = (f32[512,256]{1,0:T(8,128)S(1)}, f32[512,256]{1,0:T(8,128)S(1)}, u32[]{:S(2)}, u32[]{:S(2)}) collective-permute-start(f32[512,256]{1,0:T(8,128)S(1)} %collective-permute-done.7.refs_0_), channel_id=1, source_target_pairs={{0,1},{1,0},{2,3},{3,2},{4,5},{5,4},{6,7},{7,6},{8,9},{9,8},{10,11... | collective-permute-start | bytes 1572872 | tf_op jit(solution)/shard_map/ppermute | solution.py:14
  74.8 2.6 %collective-permute-start.21 = (f32[512,256]{1,0:T(8,128)S(1)}, f32[512,256]{1,0:T(8,128)S(1)}, u32[]{:S(2)}, u32[]{:S(2)}) collective-permute-start(f32[512,256]{1,0:T(8,128)S(1)} %collective-permute-done.6.refs_0_), channel_id=1, source_target_pairs={{0,1},{1,0},{2,3},{3,2},{4,5},{5,4},{6,7},{7,6},{8,9},{9,8},{10,11... | collective-permute-start | bytes 1572872 | tf_op jit(solution)/shard_map/ppermute | solution.py:14
  74.9 3.3 %collective-permute-start.23 = (f32[512,256]{1,0:T(8,128)S(1)}, f32[512,256]{1,0:T(8,128)S(1)}, u32[]{:S(2)}, u32[]{:S(2)}) collective-permute-start(f32[512,256]{1,0:T(8,128)S(1)} %collective-permute-done.17.refs_28_), channel_id=1, source_target_pairs={{0,1},{1,0},{2,3},{3,2},{4,5},{5,4},{6,7},{7,6},{8,9},{9,8},{10,11... | collective-permute-start | bytes 1572872 | tf_op jit(solution)/shard_map/ppermute | solution.py:14
  76.6 2.0 %collective-permute-start.25 = (f32[512,256]{1,0:T(8,128)S(1)}, f32[512,256]{1,0:T(8,128)S(1)}, u32[]{:S(2)}, u32[]{:S(2)}) collective-permute-start(f32[512,256]{1,0:T(8,128)S(1)} %collective-permute-done.24.refs_30_), channel_id=1, source_target_pairs={{0,1},{1,0},{2,3},{3,2},{4,5},{5,4},{6,7},{7,6},{8,9},{9,8},{10,11... | collective-permute-start | bytes 1572872 | tf_op jit(solution)/shard_map/ppermute | solution.py:14
  (3 other events, 16.3 us)

commit v7 on v6

--- a/solution.py
+++ b/solution.py
@@ -36,17 +36,17 @@
 PLAN = (
     ("take", "Cx"), ("send", "Rx"), ("send", "By"), ("edge", "E"),
     ("take", "Ly"), ("send", "Ey"),
-    ("take", "Lx", "B"), ("send", "Bx"), ("swap", "E"),
+    ("take", "Lx"), ("send", "Bx"), ("swap", "E"),
     ("take", "By", "L"), ("send", "Ry"), ("swap", "Ly"),
-    ("take", "Rx", "R"), ("send", "Ex"), ("swap", "Lx"), ("split", "E"),
-    ("take", "Ey"), ("send", "Ld"), ("swap", "By"), ("split", "Ly"),
-    ("take", "Bx", "E"), ("send", "Ed"), ("swap", "Rx"), ("split", "Lx"),
-    ("take", "Ry", "Ly"), ("send", "Rd"), ("swap", "Ey"),
-    ("take", "Ex", "Lx"), ("send", "Bd"), ("swap", "Bx"), ("split", "By"), ("split", "Rx"),
-    ("take", "Ld"), ("swap", "Ry"), ("swap", "Ld"), ("split", "Ey"),
-    ("take", "Ed", "By", "Rx", "Ey"), ("swap", "Ex"), ("swap", "Ed"), ("split", "Bx"), ("split", "Ry"), ("split", "Ld"),
-    ("take", "Rd", "Ld"), ("swap", "Rd"), ("split", "Ex"), ("split", "Ed"),
-    ("take", "Bd", "Ex", "Ed"), ("swap", "Bd"),
+    ("take", "Rx", "R", "B"), ("send", "Ex"), ("swap", "Lx"), ("split", "E"),
+    ("take", "Ey"), ("send", "Ld"), ("split", "Ly"),
+    ("take", "Bx", "E"), ("send", "Ed"), ("swap", "By"), ("swap", "Rx"), ("split", "Rx"),
+    ("take", "Ry", "Ly"), ("send", "Rd"), ("swap", "Ey"), ("swap", "Bx"), ("split", "Lx"),
+    ("take", "Ex", "Rx"), ("send", "Bd"),
+    ("take", "Ld", "Lx"), ("swap", "Ry"), ("swap", "Ld"), ("split", "By"), ("split", "Ey"), ("split", "Bx"),
+    ("take", "Ed", "Ey"), ("swap", "Ex"), ("swap", "Ed"), ("split", "Ry"), ("split", "Ex"), ("split", "Ld"),
+    ("take", "Rd", "By"), ("swap", "Rd"), ("split", "Ed"),
+    ("take", "Bd", "Ex", "Ld", "Ed"), ("swap", "Bd"),
 )
 
 

time: 104 us -> 103 us (level)
  waiting for transfers between devices: 41.9 us -> 38.9 us
  starting transfers between devices: 21.2 us -> 23.3 us
    ppermute x26, waiting for transfers between devices: 41.9 us -> 38.9 us  [from_partner(): return lax.ppermute(value, axis, pairs)]
    ppermute x26, starting transfers between devices: 21.2 us -> 23.3 us  [from_partner(): return lax.ppermute(value, axis, pairs)]
  transfers between devices with their start and end apart: 26 -> 26, of which waited for: 12 -> 14; matrix products, arithmetic and copies ran while one was open for 0% -> 0% of each run, Pallas kernels for 12% -> 12%
where the time goes in v7:
time: 103 us
  Pallas kernels  39.4 us (38%)
  waiting for transfers between devices  38.9 us (38%)
  starting transfers between devices  23.3 us (23%)
    ppermute x26, waiting for transfers between devices, from_partner(): return lax.ppermute(value, axis, pairs)  38.9 us
    pallas_call x1, Pallas kernels, shards(): pl.pallas_call(march_kernel, in_specs=[vmem] * 5 + [smem] + [vmem] * len(...  25 us
    ppermute x26, starting transfers between devices, from_partner(): return lax.ppermute(value, axis, pairs)  23.3 us
    pallas_call x14, Pallas kernels, split_call(): pl.pallas_call(kernel, in_specs=[pl.BlockSpec(memory_space=pltpu.SMEM)] +...  9.5 us
    pallas_call x2, Pallas kernels, cut_call(): pl.pallas_call(cut_kernel, in_specs=[pl.BlockSpec(memory_space=pltpu.SMEM...  3.45 us
  transfers between devices with their start and end apart: 26, of which 14 were waited for; matrix products, arithmetic and copies ran while one was open for 0% of the time, Pallas kernels for 12%

profile of v7, /device:TPU:0, one launch (start us, length us, event | category | flops | bytes accessed | tf_op | source)
XLA Modules:
  0.0 102.6 jit_solution(780496815229959108)
XLA Ops:
  0.7 1.7 %shard_map.113 = (f32[128,512]{1,0:T(8,128)S(1)}, f32[256,512]{1,0:T(8,128)S(1)}) custom-call(s32[4]{0:T(128)S(1)} %pad_add_fusion.place, f32[256,512]{1,0:T(8,128)} %bitcast.26, f32[256,1024]{1,0:T(8,128)} %bitcast.19), custom_call_target="tpu_custom_call" | custom-call | flops 1 | bytes 1 | tf_op jit(solution)/shard_map/pallas_call | solution.py:75
  2.4 3.1 %collective-permute-start = (f32[128,512]{1,0:T(8,128)S(1)}, f32[128,512]{1,0:T(8,128)S(1)}, u32[]{:S(2)}, u32[]{:S(2)}) collective-permute-start(f32[128,512]{1,0:T(8,128)S(1)} %get-tuple-element.83.mine), channel_id=1, source_target_pairs={{0,4},{4,0},{8,12},{12,8},{1,5},{5,1},{9,13},{13,9},{2,6},{6,2},{1... | collective-permute-start | bytes 786440 | tf_op jit(solution)/shard_map/ppermute | solution.py:14
  5.5 1.5 %collective-permute-start.4 = (f32[256,512]{1,0:T(8,128)S(1)}, f32[256,512]{1,0:T(8,128)S(1)}, u32[]{:S(2)}, u32[]{:S(2)}) collective-permute-start(f32[256,512]{1,0:T(8,128)S(1)} %get-tuple-element.91), channel_id=1, source_target_pairs={{0,2},{2,0},{1,3},{3,1},{4,6},{6,4},{5,7},{7,5},{8,10},{10,8},{9,1... | collective-permute-start | bytes 1572872 | tf_op jit(solution)/shard_map/ppermute | solution.py:14
  7.5 5.2 %collective-permute-done.other = f32[128,512]{1,0:T(8,128)S(1)} collective-permute-done((f32[128,512]{1,0:T(8,128)S(1)}, f32[128,512]{1,0:T(8,128)S(1)}, u32[]{:S(2)}, u32[]{:S(2)}) %collective-permute-start) | collective-permute-done | bytes 262176 | tf_op jit(solution)/shard_map/ppermute | solution.py:14
  12.7 1.8 %shard_map.115 = (f32[512,256]{1,0:T(8,128)S(1)}, f32[512,256]{1,0:T(8,128)S(1)}) custom-call(s32[4]{0:T(128)S(1)} %pad_add_fusion.place, f32[1024,256]{1,0:T(8,128)} %bitcast.17, f32[1024,256]{1,0:T(8,128)} %bitcast.15), custom_call_target="tpu_custom_call" | custom-call | flops 1 | bytes 1 | tf_op jit(solution)/shard_map/pallas_call | solution.py:75
  14.5 2.0 %collective-permute-start.2 = (f32[512,256]{1,0:T(8,128)S(1)}, f32[512,256]{1,0:T(8,128)S(1)}, u32[]{:S(2)}, u32[]{:S(2)}) collective-permute-start(f32[512,256]{1,0:T(8,128)S(1)} %get-tuple-element.102), channel_id=1, source_target_pairs={{0,2},{2,0},{1,3},{3,1},{4,6},{6,4},{5,7},{7,5},{8,10},{10,8},{9,1... | collective-permute-start | bytes 1572872 | tf_op jit(solution)/shard_map/ppermute | solution.py:14
  16.5 1.6 %collective-permute-start.1 = (f32[512,256]{1,0:T(8,128)S(1)}, f32[512,256]{1,0:T(8,128)S(1)}, u32[]{:S(2)}, u32[]{:S(2)}) collective-permute-start(f32[512,256]{1,0:T(8,128)S(1)} %get-tuple-element.101), channel_id=1, source_target_pairs={{0,4},{4,0},{8,12},{12,8},{1,5},{5,1},{9,13},{13,9},{2,6},{6,2},{1... | collective-permute-start | bytes 1572872 | tf_op jit(solution)/shard_map/ppermute | solution.py:14
  18.1 1.5 %shard_map.114 = (f32[360,256]{1,0:T(8,128)S(1)}, f32[9,32]{1,0:T(8,128)S(1)}) custom-call(s32[4]{0:T(128)S(1)} %pad_add_fusion.place, f32[128,512]{1,0:T(8,128)S(1)} %get-tuple-element.83.mine, f32[128,512]{1,0:T(8,128)S(1)} %collective-permute-done.other, f32[512,256]{1,0:T(8,128)S(1)} %bitcast.21, s32[1,32]{1,0:T(1,128)S(1)} %bitcast.25, ...), custom_call_target="tpu_custom_call" | custom-call | flops 1 | bytes 1 | tf_op jit(solution)/shard_map/pallas_call | solution.py:111
  19.6 0.7 collective-permute-done.4.refs_0_
  20.4 1.5 %collective-permute-start.8 = (f32[360,256]{1,0:T(8,128)S(1)}, f32[360,256]{1,0:T(8,128)S(1)}, u32[]{:S(2)}, u32[]{:S(2)}) collective-permute-start(f32[360,256]{1,0:T(8,128)S(1)} %get-tuple-element.106.refs_0_.s0), channel_id=1, source_target_pairs={{0,2},{2,0},{1,3},{3,1},{4,6},{6,4},{5,7},{7,5},{8,10},{10,8},{9,1... | collective-permute-start | bytes 1105928 | tf_op jit(solution)/shard_map/ppermute | solution.py:14
  21.9 2.0 %collective-permute-done.3.refs_0_ = f32[256,512]{1,0:T(8,128)S(1)} collective-permute-done((f32[256,512]{1,0:T(8,128)S(1)}, f32[256,512]{1,0:T(8,128)S(1)}, u32[]{:S(2)}, u32[]{:S(2)}) %collective-permute-start.3) | collective-permute-done | bytes 524320 | tf_op jit(solution)/shard_map/ppermute | solution.py:14
  23.9 2.1 %collective-permute-start.7 = (f32[512,256]{1,0:T(8,128)S(1)}, f32[512,256]{1,0:T(8,128)S(1)}, u32[]{:S(2)}, u32[]{:S(2)}) collective-permute-start(f32[512,256]{1,0:T(8,128)S(1)} %get-tuple-element.102), channel_id=1, source_target_pairs={{0,4},{4,0},{8,12},{12,8},{1,5},{5,1},{9,13},{13,9},{2,6},{6,2},{1... | collective-permute-start | bytes 1572872 | tf_op jit(solution)/shard_map/ppermute | solution.py:14
  26.7 4.9 %collective-permute-done.2.refs_0_ = f32[512,256]{1,0:T(8,128)S(1)} collective-permute-done((f32[512,256]{1,0:T(8,128)S(1)}, f32[512,256]{1,0:T(8,128)S(1)}, u32[]{:S(2)}, u32[]{:S(2)}) %collective-permute-start.2) | collective-permute-done | bytes 524320 | tf_op jit(solution)/shard_map/ppermute | solution.py:14
  31.6 3.5 %collective-permute-done.1.refs_0_ = f32[512,256]{1,0:T(8,128)S(1)} collective-permute-done((f32[512,256]{1,0:T(8,128)S(1)}, f32[512,256]{1,0:T(8,128)S(1)}, u32[]{:S(2)}, u32[]{:S(2)}) %collective-permute-start.1) | collective-permute-done | bytes 524320 | tf_op jit(solution)/shard_map/ppermute | solution.py:14
  35.1 2.0 %collective-permute-start.6 = (f32[512,256]{1,0:T(8,128)S(1)}, f32[512,256]{1,0:T(8,128)S(1)}, u32[]{:S(2)}, u32[]{:S(2)}) collective-permute-start(f32[512,256]{1,0:T(8,128)S(1)} %get-tuple-element.101), channel_id=1, source_target_pairs={{0,2},{2,0},{1,3},{3,1},{4,6},{6,4},{5,7},{7,5},{8,10},{10,8},{9,1... | collective-permute-start | bytes 1572872 | tf_op jit(solution)/shard_map/ppermute | solution.py:14
  38.5 1.0 collective-permute-done.8.refs_0_.s2
  39.5 0.8 collective-permute-start.5
  40.9 5.5 %collective-permute-done.7.refs_0_ = f32[512,256]{1,0:T(8,128)S(1)} collective-permute-done((f32[512,256]{1,0:T(8,128)S(1)}, f32[512,256]{1,0:T(8,128)S(1)}, u32[]{:S(2)}, u32[]{:S(2)}) %collective-permute-start.7) | collective-permute-done | bytes 524320 | tf_op jit(solution)/shard_map/ppermute | solution.py:14
  46.4 2.0 %collective-permute-start.13 = (f32[256,512]{1,0:T(8,128)S(1)}, f32[256,512]{1,0:T(8,128)S(1)}, u32[]{:S(2)}, u32[]{:S(2)}) collective-permute-start(f32[256,512]{1,0:T(8,128)S(1)} %collective-permute-done.3.refs_0_), channel_id=1, source_target_pairs={{0,2},{2,0},{1,3},{3,1},{4,6},{6,4},{5,7},{7,5},{8,10},{10,8},{9,1... | collective-permute-start | bytes 1572872 | tf_op jit(solution)/shard_map/ppermute | solution.py:14
  48.3 0.7 shard_map.120
  49.3 4.1 %collective-permute-done.5.refs_0_.s1 = f32[360,256]{1,0:T(8,128)S(1)} collective-permute-done((f32[360,256]{1,0:T(8,128)S(1)}, f32[360,256]{1,0:T(8,128)S(1)}, u32[]{:S(2)}, u32[]{:S(2)}) %collective-permute-start.5) | collective-permute-done | bytes 368672 | tf_op jit(solution)/shard_map/ppermute | solution.py:14
  53.4 1.7 %collective-permute-start.12 = (f32[360,256]{1,0:T(8,128)S(1)}, f32[360,256]{1,0:T(8,128)S(1)}, u32[]{:S(2)}, u32[]{:S(2)}) collective-permute-start(f32[360,256]{1,0:T(8,128)S(1)} %collective-permute-done.8.refs_0_.s2), channel_id=1, source_target_pairs={{0,4},{4,0},{8,12},{12,8},{1,5},{5,1},{9,13},{13,9},{2,6},{6,2},{1... | collective-permute-start | bytes 1105928 | tf_op jit(solution)/shard_map/ppermute | solution.py:14
  55.2 1.5 %collective-permute-start.17 = (f32[512,256]{1,0:T(8,128)S(1)}, f32[512,256]{1,0:T(8,128)S(1)}, u32[]{:S(2)}, u32[]{:S(2)}) collective-permute-start(f32[512,256]{1,0:T(8,128)S(1)} %collective-permute-done.1.refs_0_), channel_id=1, source_target_pairs={{0,2},{2,0},{1,3},{3,1},{4,6},{6,4},{5,7},{7,5},{8,10},{10,8},{9,1... | collective-permute-start | bytes 1572872 | tf_op jit(solution)/shard_map/ppermute | solution.py:14
  57.4 0.7 shard_map.121
  58.1 3.1 %collective-permute-done.13.refs_0_ = f32[256,512]{1,0:T(8,128)S(1)} collective-permute-done((f32[256,512]{1,0:T(8,128)S(1)}, f32[256,512]{1,0:T(8,128)S(1)}, u32[]{:S(2)}, u32[]{:S(2)}) %collective-permute-start.13) | collective-permute-done | bytes 524320 | tf_op jit(solution)/shard_map/ppermute | solution.py:14
  61.2 2.0 %collective-permute-start.24 = (f32[512,256]{1,0:T(8,128)S(1)}, f32[512,256]{1,0:T(8,128)S(1)}, u32[]{:S(2)}, u32[]{:S(2)}) collective-permute-start(f32[512,256]{1,0:T(8,128)S(1)} %collective-permute-done.2.refs_0_), channel_id=1, source_target_pairs={{0,4},{4,0},{8,12},{12,8},{1,5},{5,1},{9,13},{13,9},{2,6},{6,2},{1... | collective-permute-start | bytes 1572872 | tf_op jit(solution)/shard_map/ppermute | solution.py:14
  65.7 6.5 %collective-permute-done.17.refs_28_ = f32[512,256]{1,0:T(8,128)S(1)} collective-permute-done((f32[512,256]{1,0:T(8,128)S(1)}, f32[512,256]{1,0:T(8,128)S(1)}, u32[]{:S(2)}, u32[]{:S(2)}) %collective-permute-start.17) | collective-permute-done | bytes 524320 | tf_op jit(solution)/shard_map/ppermute | solution.py:14
  74.0 0.7 shard_map.127
  74.7 1.0 collective-permute-done.24.refs_30_
  75.7 0.7 shard_map.129
  76.5 0.7 shard_map.128
  77.7 25.0 %shard_map.130 = (f32[32,256]{1,0:T(8,128)}, f32[32,256]{1,0:T(8,128)}) custom-call(f32[360,256]{1,0:T(8,128)S(1)} %get-tuple-element.106.refs_0_.s0, f32[360,256]{1,0:T(8,128)S(1)} %collective-permute-done.5.refs_0_.s1, f32[360,256]{1,0:T(8,128)S(1)} %collective-permute-done.8.refs_0_.s2, f32[360,256]{1,0:T(8,128)S(1)} %collective-permute-done.12.refs_0_.s3, ...), custom_call_target="tpu_custom_call" | custom-call | tf_op jit(solution)/shard_map/pallas_call | solution.py:297
  (57 shorter events, 9.1 us)
Async XLA Ops:
  2.4 10.2 %collective-permute-start = (f32[128,512]{1,0:T(8,128)S(1)}, f32[128,512]{1,0:T(8,128)S(1)}, u32[]{:S(2)}, u32[]{:S(2)}) collective-permute-start(f32[128,512]{1,0:T(8,128)S(1)} %get-tuple-element.83.mine), channel_id=1, source_target_pairs={{0,4},{4,0},{8,12},{12,8},{1,5},{5,1},{9,13},{13,9},{2,6},{6,2},{1... | collective-permute-start | bytes 786440 | tf_op jit(solution)/shard_map/ppermute | solution.py:14
  5.5 14.8 %collective-permute-start.4 = (f32[256,512]{1,0:T(8,128)S(1)}, f32[256,512]{1,0:T(8,128)S(1)}, u32[]{:S(2)}, u32[]{:S(2)}) collective-permute-start(f32[256,512]{1,0:T(8,128)S(1)} %get-tuple-element.91), channel_id=1, source_target_pairs={{0,2},{2,0},{1,3},{3,1},{4,6},{6,4},{5,7},{7,5},{8,10},{10,8},{9,1... | collective-permute-start | bytes 1572872 | tf_op jit(solution)/shard_map/ppermute | solution.py:14
  7.0 16.9 %collective-permute-start.3 = (f32[256,512]{1,0:T(8,128)S(1)}, f32[256,512]{1,0:T(8,128)S(1)}, u32[]{:S(2)}, u32[]{:S(2)}) collective-permute-start(f32[256,512]{1,0:T(8,128)S(1)} %get-tuple-element.91), channel_id=1, source_target_pairs={{0,4},{4,0},{8,12},{12,8},{1,5},{5,1},{9,13},{13,9},{2,6},{6,2},{1... | collective-permute-start | bytes 1572872 | tf_op jit(solution)/shard_map/ppermute | solution.py:14
  12.7 5.4 %copy-start.5 = (f32[1,1,32,256]{3,2,1,0:T(8,128)S(1)}, f32[1,1,32,256]{3,2,1,0:T(8,128)}, u32[]{:S(2)}) copy-start(f32[1,1,32,256]{3,2,1,0:T(8,128)} %param.11) | copy-start | bytes 98308
  12.7 5.4 %copy-start.6 = (f32[9,32]{1,0:T(8,128)S(1)}, f32[9,32]{1,0:T(8,128)}, u32[]{:S(2)}) copy-start(f32[9,32]{1,0:T(8,128)} %weight.1) | copy-start | bytes 3460
  12.7 5.4 %copy-start.7 = (f32[1,1,256]{2,1,0:T(1,128)S(1)}, f32[1,1,256]{2,1,0:T(1,128)}, u32[]{:S(2)}) copy-start(f32[1,1,256]{2,1,0:T(1,128)} %param.17) | copy-start | bytes 3076
  14.5 11.5 %copy-start.2 = (f32[1,1,256,1024]{3,2,1,0:T(8,128)S(1)}, f32[1,1,256,1024]{3,2,1,0:T(8,128)}, u32[]{:S(2)}) copy-start(f32[1,1,256,1024]{3,2,1,0:T(8,128)} %param.14) | copy-start | bytes 3145732
  14.5 17.1 %collective-permute-start.2 = (f32[512,256]{1,0:T(8,128)S(1)}, f32[512,256]{1,0:T(8,128)S(1)}, u32[]{:S(2)}, u32[]{:S(2)}) collective-permute-start(f32[512,256]{1,0:T(8,128)S(1)} %get-tuple-element.102), channel_id=1, source_target_pairs={{0,2},{2,0},{1,3},{3,1},{4,6},{6,4},{5,7},{7,5},{8,10},{10,8},{9,1... | collective-permute-start | bytes 1572872 | tf_op jit(solution)/shard_map/ppermute | solution.py:14
  16.5 18.6 %collective-permute-start.1 = (f32[512,256]{1,0:T(8,128)S(1)}, f32[512,256]{1,0:T(8,128)S(1)}, u32[]{:S(2)}, u32[]{:S(2)}) collective-permute-start(f32[512,256]{1,0:T(8,128)S(1)} %get-tuple-element.101), channel_id=1, source_target_pairs={{0,4},{4,0},{8,12},{12,8},{1,5},{5,1},{9,13},{13,9},{2,6},{6,2},{1... | collective-permute-start | bytes 1572872 | tf_op jit(solution)/shard_map/ppermute | solution.py:14
  18.1 19.0 %copy-start = (f32[1,1,1024,256]{3,2,1,0:T(8,128)S(1)}, f32[1,1,1024,256]{3,2,1,0:T(8,128)}, u32[]{:S(2)}) copy-start(f32[1,1,1024,256]{3,2,1,0:T(8,128)} %param.15) | copy-start | bytes 3145732
  20.4 17.4 %copy-start.1 = (f32[1,1,1024,256]{3,2,1,0:T(8,128)S(1)}, f32[1,1,1024,256]{3,2,1,0:T(8,128)}, u32[]{:S(2)}) copy-start(f32[1,1,1024,256]{3,2,1,0:T(8,128)} %param.16) | copy-start | bytes 3145732
  20.4 19.1 %collective-permute-start.8 = (f32[360,256]{1,0:T(8,128)S(1)}, f32[360,256]{1,0:T(8,128)S(1)}, u32[]{:S(2)}, u32[]{:S(2)}) collective-permute-start(f32[360,256]{1,0:T(8,128)S(1)} %get-tuple-element.106.refs_0_.s0), channel_id=1, source_target_pairs={{0,2},{2,0},{1,3},{3,1},{4,6},{6,4},{5,7},{7,5},{8,10},{10,8},{9,1... | collective-permute-start | bytes 1105928 | tf_op jit(solution)/shard_map/ppermute | solution.py:14
  23.9 15.6 %collective-permute-start.9 = (f32[360,256]{1,0:T(8,128)S(1)}, f32[360,256]{1,0:T(8,128)S(1)}, u32[]{:S(2)}, u32[]{:S(2)}) collective-permute-start(f32[360,256]{1,0:T(8,128)S(1)} %get-tuple-element.106.refs_0_.s0), channel_id=1, source_target_pairs={{0,1},{1,0},{2,3},{3,2},{4,5},{5,4},{6,7},{7,6},{8,9},{9,8},{10,11... | collective-permute-start | bytes 1105928 | tf_op jit(solution)/shard_map/ppermute | solution.py:14
  23.9 22.5 %collective-permute-start.7 = (f32[512,256]{1,0:T(8,128)S(1)}, f32[512,256]{1,0:T(8,128)S(1)}, u32[]{:S(2)}, u32[]{:S(2)}) collective-permute-start(f32[512,256]{1,0:T(8,128)S(1)} %get-tuple-element.102), channel_id=1, source_target_pairs={{0,4},{4,0},{8,12},{12,8},{1,5},{5,1},{9,13},{13,9},{2,6},{6,2},{1... | collective-permute-start | bytes 1572872 | tf_op jit(solution)/shard_map/ppermute | solution.py:14
  31.6 14.8 %collective-permute-start.10 = (f32[256,512]{1,0:T(8,128)S(1)}, f32[256,512]{1,0:T(8,128)S(1)}, u32[]{:S(2)}, u32[]{:S(2)}) collective-permute-start(f32[256,512]{1,0:T(8,128)S(1)} %collective-permute-done.4.refs_0_), channel_id=1, source_target_pairs={{0,1},{1,0},{2,3},{3,2},{4,5},{5,4},{6,7},{7,6},{8,9},{9,8},{10,11... | collective-permute-start | bytes 1572872 | tf_op jit(solution)/shard_map/ppermute | solution.py:14
  35.1 14.1 %collective-permute-start.6 = (f32[512,256]{1,0:T(8,128)S(1)}, f32[512,256]{1,0:T(8,128)S(1)}, u32[]{:S(2)}, u32[]{:S(2)}) collective-permute-start(f32[512,256]{1,0:T(8,128)S(1)} %get-tuple-element.101), channel_id=1, source_target_pairs={{0,2},{2,0},{1,3},{3,1},{4,6},{6,4},{5,7},{7,5},{8,10},{10,8},{9,1... | collective-permute-start | bytes 1572872 | tf_op jit(solution)/shard_map/ppermute | solution.py:14
  39.5 13.9 %collective-permute-start.14 = (f32[256,512]{1,0:T(8,128)S(1)}, f32[256,512]{1,0:T(8,128)S(1)}, u32[]{:S(2)}, u32[]{:S(2)}) collective-permute-start(f32[256,512]{1,0:T(8,128)S(1)} %collective-permute-done.3.refs_0_), channel_id=1, source_target_pairs={{0,1},{1,0},{2,3},{3,2},{4,5},{5,4},{6,7},{7,6},{8,9},{9,8},{10,11... | collective-permute-start | bytes 1572872 | tf_op jit(solution)/shard_map/ppermute | solution.py:14
  39.5 13.9 %collective-permute-start.5 = (f32[360,256]{1,0:T(8,128)S(1)}, f32[360,256]{1,0:T(8,128)S(1)}, u32[]{:S(2)}, u32[]{:S(2)}) collective-permute-start(f32[360,256]{1,0:T(8,128)S(1)} %get-tuple-element.106.refs_0_.s0), channel_id=1, source_target_pairs={{0,4},{4,0},{8,12},{12,8},{1,5},{5,1},{9,13},{13,9},{2,6},{6,2},{1... | collective-permute-start | bytes 1105928 | tf_op jit(solution)/shard_map/ppermute | solution.py:14
  46.4 8.8 %collective-permute-start.11 = (f32[512,256]{1,0:T(8,128)S(1)}, f32[512,256]{1,0:T(8,128)S(1)}, u32[]{:S(2)}, u32[]{:S(2)}) collective-permute-start(f32[512,256]{1,0:T(8,128)S(1)} %collective-permute-done.1.refs_0_), channel_id=1, source_target_pairs={{0,1},{1,0},{2,3},{3,2},{4,5},{5,4},{6,7},{7,6},{8,9},{9,8},{10,11... | collective-permute-start | bytes 1572872 | tf_op jit(solution)/shard_map/ppermute | solution.py:14
  46.4 14.8 %collective-permute-start.13 = (f32[256,512]{1,0:T(8,128)S(1)}, f32[256,512]{1,0:T(8,128)S(1)}, u32[]{:S(2)}, u32[]{:S(2)}) collective-permute-start(f32[256,512]{1,0:T(8,128)S(1)} %collective-permute-done.3.refs_0_), channel_id=1, source_target_pairs={{0,2},{2,0},{1,3},{3,1},{4,6},{6,4},{5,7},{7,5},{8,10},{10,8},{9,1... | collective-permute-start | bytes 1572872 | tf_op jit(solution)/shard_map/ppermute | solution.py:14
  49.3 15.2 %collective-permute-start.18 = (f32[512,256]{1,0:T(8,128)S(1)}, f32[512,256]{1,0:T(8,128)S(1)}, u32[]{:S(2)}, u32[]{:S(2)}) collective-permute-start(f32[512,256]{1,0:T(8,128)S(1)} %collective-permute-done.2.refs_0_), channel_id=1, source_target_pairs={{0,1},{1,0},{2,3},{3,2},{4,5},{5,4},{6,7},{7,6},{8,9},{9,8},{10,11... | collective-permute-start | bytes 1572872 | tf_op jit(solution)/shard_map/ppermute | solution.py:14
  53.4 7.7 %collective-permute-start.15 = (f32[360,256]{1,0:T(8,128)S(1)}, f32[360,256]{1,0:T(8,128)S(1)}, u32[]{:S(2)}, u32[]{:S(2)}) collective-permute-start(f32[360,256]{1,0:T(8,128)S(1)} %collective-permute-done.8.refs_0_.s2), channel_id=1, source_target_pairs={{0,1},{1,0},{2,3},{3,2},{4,5},{5,4},{6,7},{7,6},{8,9},{9,8},{10,11... | collective-permute-start | bytes 1105928 | tf_op jit(solution)/shard_map/ppermute | solution.py:14
  53.4 11.0 %collective-permute-start.12 = (f32[360,256]{1,0:T(8,128)S(1)}, f32[360,256]{1,0:T(8,128)S(1)}, u32[]{:S(2)}, u32[]{:S(2)}) collective-permute-start(f32[360,256]{1,0:T(8,128)S(1)} %collective-permute-done.8.refs_0_.s2), channel_id=1, source_target_pairs={{0,4},{4,0},{8,12},{12,8},{1,5},{5,1},{9,13},{13,9},{2,6},{6,2},{1... | collective-permute-start | bytes 1105928 | tf_op jit(solution)/shard_map/ppermute | solution.py:14
  55.2 17.0 %collective-permute-start.17 = (f32[512,256]{1,0:T(8,128)S(1)}, f32[512,256]{1,0:T(8,128)S(1)}, u32[]{:S(2)}, u32[]{:S(2)}) collective-permute-start(f32[512,256]{1,0:T(8,128)S(1)} %collective-permute-done.1.refs_0_), channel_id=1, source_target_pairs={{0,2},{2,0},{1,3},{3,1},{4,6},{6,4},{5,7},{7,5},{8,10},{10,8},{9,1... | collective-permute-start | bytes 1572872 | tf_op jit(solution)/shard_map/ppermute | solution.py:14
  61.2 12.8 %collective-permute-start.20 = (f32[256,512]{1,0:T(8,128)S(1)}, f32[256,512]{1,0:T(8,128)S(1)}, u32[]{:S(2)}, u32[]{:S(2)}) collective-permute-start(f32[256,512]{1,0:T(8,128)S(1)} %collective-permute-done.13.refs_0_), channel_id=1, source_target_pairs={{0,1},{1,0},{2,3},{3,2},{4,5},{5,4},{6,7},{7,6},{8,9},{9,8},{10,11... | collective-permute-start | bytes 1572872 | tf_op jit(solution)/shard_map/ppermute | solution.py:14
  61.2 14.6 %collective-permute-start.24 = (f32[512,256]{1,0:T(8,128)S(1)}, f32[512,256]{1,0:T(8,128)S(1)}, u32[]{:S(2)}, u32[]{:S(2)}) collective-permute-start(f32[512,256]{1,0:T(8,128)S(1)} %collective-permute-done.2.refs_0_), channel_id=1, source_target_pairs={{0,4},{4,0},{8,12},{12,8},{1,5},{5,1},{9,13},{13,9},{2,6},{6,2},{1... | collective-permute-start | bytes 1572872 | tf_op jit(solution)/shard_map/ppermute | solution.py:14
  64.4 7.7 %collective-permute-start.16 = (f32[360,256]{1,0:T(8,128)S(1)}, f32[360,256]{1,0:T(8,128)S(1)}, u32[]{:S(2)}, u32[]{:S(2)}) collective-permute-start(f32[360,256]{1,0:T(8,128)S(1)} %collective-permute-done.5.refs_0_.s1), channel_id=1, source_target_pairs={{0,1},{1,0},{2,3},{3,2},{4,5},{5,4},{6,7},{7,6},{8,9},{9,8},{10,11... | collective-permute-start | bytes 1105928 | tf_op jit(solution)/shard_map/ppermute | solution.py:14
  64.4 8.9 %collective-permute-start.19 = (f32[360,256]{1,0:T(8,128)S(1)}, f32[360,256]{1,0:T(8,128)S(1)}, u32[]{:S(2)}, u32[]{:S(2)}) collective-permute-start(f32[360,256]{1,0:T(8,128)S(1)} %collective-permute-done.12.refs_0_.s3), channel_id=1, source_target_pairs={{0,1},{1,0},{2,3},{3,2},{4,5},{5,4},{6,7},{7,6},{8,9},{9,8},{10,11... | collective-permute-start | bytes 1105928 | tf_op jit(solution)/shard_map/ppermute | solution.py:14
  72.2 3.6 %collective-permute-start.22 = (f32[512,256]{1,0:T(8,128)S(1)}, f32[512,256]{1,0:T(8,128)S(1)}, u32[]{:S(2)}, u32[]{:S(2)}) collective-permute-start(f32[512,256]{1,0:T(8,128)S(1)} %collective-permute-done.7.refs_0_), channel_id=1, source_target_pairs={{0,1},{1,0},{2,3},{3,2},{4,5},{5,4},{6,7},{7,6},{8,9},{9,8},{10,11... | collective-permute-start | bytes 1572872 | tf_op jit(solution)/shard_map/ppermute | solution.py:14
  72.2 4.3 %collective-permute-start.21 = (f32[512,256]{1,0:T(8,128)S(1)}, f32[512,256]{1,0:T(8,128)S(1)}, u32[]{:S(2)}, u32[]{:S(2)}) collective-permute-start(f32[512,256]{1,0:T(8,128)S(1)} %collective-permute-done.6.refs_0_), channel_id=1, source_target_pairs={{0,1},{1,0},{2,3},{3,2},{4,5},{5,4},{6,7},{7,6},{8,9},{9,8},{10,11... | collective-permute-start | bytes 1572872 | tf_op jit(solution)/shard_map/ppermute | solution.py:14
  73.3 3.9 %collective-permute-start.23 = (f32[512,256]{1,0:T(8,128)S(1)}, f32[512,256]{1,0:T(8,128)S(1)}, u32[]{:S(2)}, u32[]{:S(2)}) collective-permute-start(f32[512,256]{1,0:T(8,128)S(1)} %collective-permute-done.17.refs_28_), channel_id=1, source_target_pairs={{0,1},{1,0},{2,3},{3,2},{4,5},{5,4},{6,7},{7,6},{8,9},{9,8},{10,11... | collective-permute-start | bytes 1572872 | tf_op jit(solution)/shard_map/ppermute | solution.py:14
  75.7 1.9 %collective-permute-start.25 = (f32[512,256]{1,0:T(8,128)S(1)}, f32[512,256]{1,0:T(8,128)S(1)}, u32[]{:S(2)}, u32[]{:S(2)}) collective-permute-start(f32[512,256]{1,0:T(8,128)S(1)} %collective-permute-done.24.refs_30_), channel_id=1, source_target_pairs={{0,1},{1,0},{2,3},{3,2},{4,5},{5,4},{6,7},{7,6},{8,9},{9,8},{10,11... | collective-permute-start | bytes 1572872 | tf_op jit(solution)/shard_map/ppermute | solution.py:14
  (3 other events, 16.3 us)

commit v8 on v7

--- a/solution.py
+++ b/solution.py
@@ -14,6 +14,12 @@
     return lax.ppermute(value, axis, pairs)
 
 
+def couple_across(couple):
+    columns, cores = lax.axis_size("gx"), lax.axis_size("gz")
+    pairs = [(column * cores + column % 2, (column ^ 1) * cores + column % 2) for column in range(columns)]
+    return lax.ppermute(couple, ("gx", "gz"), pairs)
+
+
 def after(value, *earlier):
     return lax.optimization_barrier((value,) + earlier)[0]
 
@@ -35,18 +41,18 @@
 
 PLAN = (
     ("take", "Cx"), ("send", "Rx"), ("send", "By"), ("edge", "E"),
-    ("take", "Ly"), ("send", "Ey"),
-    ("take", "Lx"), ("send", "Bx"), ("swap", "E"),
+    ("take", "Ly"), ("send", "Bx"), ("send", "Ey"),
+    ("take", "Lx"), ("swap", "E"),
     ("take", "By", "L"), ("send", "Ry"), ("swap", "Ly"),
     ("take", "Rx", "R", "B"), ("send", "Ex"), ("swap", "Lx"), ("split", "E"),
-    ("take", "Ey"), ("send", "Ld"), ("split", "Ly"),
-    ("take", "Bx", "E"), ("send", "Ed"), ("swap", "By"), ("swap", "Rx"), ("split", "Rx"),
-    ("take", "Ry", "Ly"), ("send", "Rd"), ("swap", "Ey"), ("swap", "Bx"), ("split", "Lx"),
+    ("take", "Ey", "E"), ("send", "Ld"), ("split", "Ly"),
+    ("take", "Bx", "Ly"), ("send", "Ed"), ("swap", "By"), ("swap", "Rx"), ("split", "Rx"),
+    ("take", "Ry"), ("send", "Rd"), ("swap", "Ey"), ("swap", "Bx"), ("split", "Lx"),
     ("take", "Ex", "Rx"), ("send", "Bd"),
-    ("take", "Ld", "Lx"), ("swap", "Ry"), ("swap", "Ld"), ("split", "By"), ("split", "Ey"), ("split", "Bx"),
-    ("take", "Ed", "Ey"), ("swap", "Ex"), ("swap", "Ed"), ("split", "Ry"), ("split", "Ex"), ("split", "Ld"),
-    ("take", "Rd", "By"), ("swap", "Rd"), ("split", "Ed"),
-    ("take", "Bd", "Ex", "Ld", "Ed"), ("swap", "Bd"),
+    ("take", "Ld", "Lx"), ("swap", "Ry"), ("swap", "Ex"), ("swap", "Ld"), ("split", "By"), ("split", "Ey"), ("split", "Bx"), ("split", "Ex"),
+    ("take", "Ed", "Ey"), ("swap", "Ed"), ("split", "Ry"), ("split", "Ld"),
+    ("take", "Rd", "By", "Ex"), ("swap", "Rd"), ("split", "Ed"), ("lead", "lead"),
+    ("take", "Bd", "Ld", "Ed", "lead"), ("swap", "Bd"),
 )
 
 
@@ -90,18 +96,16 @@
 
 
 def edge_state_kernel(place, mine, other, pair_cols, cells, one, two, mass, weight, edge_ref, weight_ref):
-    half = mine.shape[0]
     rows, width = one.shape
-    for step, couple in enumerate((mine, other)):
-        start = ((place[0] % 2) ^ step) * half
-        edge_ref[pl.ds(pl.multiple_of(start, half), half), :] = exact_dot(couple[...], pair_cols[...])
+    couple = jnp.where(place[0] % 2 == place[1], mine[...], other[...])
+    edge_ref[:width, :] = exact_dot(couple, pair_cols[...])
     cell = column_of(cells[...].astype(F32))
     number = lax.broadcasted_iota(jnp.int32, (rows, width), 1)
     chosen = [(cell == (number + place[2 + side]).astype(F32)).astype(F32) for side in range(2)]
     picked = exact_dot(jnp.concatenate(chosen, axis=1), pair_cols[...])
     for index, value in enumerate((one[...], two[...], picked)):
-        edge_ref[2 * half + index * rows:2 * half + (index + 1) * rows, :] = value
-    edge_ref[2 * half + 3 * rows:, :] = jnp.broadcast_to(mass[...], (8, width))
+        edge_ref[width + index * rows:width + (index + 1) * rows, :] = value
+    edge_ref[width + 3 * rows:, :] = jnp.broadcast_to(mass[...], (8, width))
     weight_ref[...] = weight[...]
 
 
@@ -145,12 +149,10 @@
 
 def edge_kernel(place, *refs):
     pieces, (high_ref, low_ref) = refs[:-2], refs[-2:]
-    rows = pieces[0].shape[1] // 2
+    width = high_ref.shape[1]
     for part, piece in enumerate(pieces):
-        for bit in range(2):
-            start = (bit ^ (place[0] % 2)) * 2 * rows + (place[1] ^ part) * rows
-            where = (pl.ds(pl.multiple_of(start, rows), rows), slice(None))
-            store_split(high_ref, low_ref, where, piece[bit * rows:(bit + 1) * rows, :])
+        start = (place[1] ^ part ^ (place[0] % 2)) * width
+        store_split(high_ref, low_ref, (pl.ds(pl.multiple_of(start, width), width), slice(None)), piece[:width, :])
 
 
 def split_call(kernel, place, rows, *pieces):
@@ -187,14 +189,14 @@
     return jnp.concatenate([product(left, panels[2 * tile][...], panels[2 * tile + 1][...]) for tile in range(4)], axis=1)
 
 
-def forward_two(half, two, scale, lift, root):
+def quad_sums(half, two, scale, lift):
     width = lift[0].shape[1]
 
     def column_block(block, part):
         return jnp.concatenate([lift[2 * tile + part][block * width:(block + 1) * width, :] for tile in range(4)], axis=0)
 
     sums = jnp.concatenate([product(half, column_block(block, 0), column_block(block, 1)) for block in range(4)], axis=1)
-    return tall(sums + two * scale, root)
+    return sums + two * scale
 
 
 def below(tiles, rows, index, count):
@@ -202,7 +204,15 @@
     return jnp.concatenate([tile[start:start + count, :] for tile in tiles], axis=1)
 
 
-def march_kernel(s0, s1, s2, s3, weight, place, *refs):
+def lead_kernel(s0, s1, s2, s3, weight, *refs):
+    edge, lift, (half_ref, sums_ref) = refs[:8], refs[8:16], refs[16:]
+    tiles, rows = (s0, s1, s2, s3), half_ref.shape[0]
+    one, two, picked, scale = [below(tiles, rows, index, count) for index, count in enumerate((rows, rows, rows, 1))]
+    half_ref[...] = forward_half(one, picked, weight[0:1, :], edge)
+    sums_ref[...] = quad_sums(half_ref[...], two, scale, lift)
+
+
+def march_kernel(s0, s1, s2, s3, weight, half_start, sums_start, place, *refs):
     edge, lift, root, back = refs[:8], refs[8:16], refs[16:22], refs[22:28]
     root_mine, root_other, back_mine, back_other, one_ref, two_ref = refs[28:34]
     rows, width = one_ref.shape
@@ -210,16 +220,14 @@
     split_tall(place, (root_mine, root_other), *refs[34:36])
     split_tall(place, (back_mine, back_other), *refs[36:38])
     root, back = root + refs[34:36], back + refs[36:38]
-    one, two, picked, scale = [below(tiles, rows, index, count) for index, count in enumerate((rows, rows, rows, 1))]
-    half = forward_half(one, picked, weight[0:1, :], edge)
-    two = forward_two(half, two, scale, lift, root)
+    picked, scale = below(tiles, rows, 2, rows), below(tiles, rows, 3, 1)
 
     def advance(step, carry):
         half, two = carry
         half = forward_half(half - tall(two, back), picked, weight[pl.ds(step, 1), :], edge)
-        return half, forward_two(half, two, scale, lift, root)
-
-    half, two = lax.fori_loop(1, weight.shape[0], advance, (half, two))
+        return half, tall(quad_sums(half, two, scale, lift), root)
+
+    half, two = lax.fori_loop(1, weight.shape[0], advance, (half_start[...], tall(sums_start[...], root)))
     one_ref[...] = half[:, :width] - product(two, back[0][...], back[1][...])
     two_ref[...] = two[:, :width]
 
@@ -248,8 +256,8 @@
     first_cell = ((column - x_bit) * lax.axis_size("gy") + row) * width
     place = jnp.stack([2 * y_bit + x_bit, core, first_cell, first_cell + lax.axis_size("gy") * width]).astype(jnp.int32)
 
-    couple_half, lift_half = cut_call(place, (couple, lift), ((width // 2, 2 * width), (width, 2 * width)))
-    value = {"Cx": from_partner(couple_half, "gx"), "Ly": from_partner(lift_half, "gy"), "Lx": from_partner(lift_half, "gx")}
+    (lift_half,) = cut_call(place, (lift,), ((width, 2 * width),))
+    value = {"Cx": couple_across(couple), "Ly": from_partner(lift_half, "gy"), "Lx": from_partner(lift_half, "gx")}
     back_half, root_half = cut_call(after(place, value["Cx"]), (back, root), ((2 * width, width),) * 2)
     own = {"L": lift_half, "B": back_half, "R": root_half}
     kernels = {"L": (wide_kernel, 4 * width), "R": (tall_kernel, 4 * width), "B": (tall_kernel, 4 * width), "E": (edge_kernel, 2 * width)}
@@ -268,7 +276,7 @@
             own["E"], weight = edge_call(
                 width + 3 * rows + 8,
                 place,
-                couple_half,
+                couple,
                 value["Cx"],
                 pair_cols,
                 probe_cells[None, :],
@@ -284,24 +292,32 @@
             value[name] = from_partner(after(source, token), "g" + axis)
         elif verb == "swap":
             other[name] = from_partner(after(value[name], token), "gz")
+        elif verb == "lead":
+            states = (own["E"], value["Ex"], value["Ey"], value["Ed"], weight)
+            early = [panel for tile in ("E", "Ex", "Ey", "Ed", "L", "Lx", "Ly", "Ld") for panel in ready[tile]]
+            ready[name] = pl.pallas_call(
+                lead_kernel,
+                in_specs=[pl.BlockSpec(memory_space=pltpu.VMEM)] * (5 + len(early)),
+                out_specs=(pl.BlockSpec(memory_space=pltpu.VMEM),) * 2,
+                out_shape=(jax.ShapeDtypeStruct((rows, 4 * width), F32),) * 2,
+                cost_estimate=CHEAP,
+                compiler_params=pltpu.CompilerParams(vmem_limit_bytes=6 * 2**20),
+            )(*states, *early)
         else:
             kernel, size = kernels[kind]
             ready[name] = split_call(kernel, after(place, token), size, value[name], other[name])
 
     vmem, smem = pl.BlockSpec(memory_space=pltpu.VMEM), pl.BlockSpec(memory_space=pltpu.SMEM)
-    panels = ()
-    for kind, tiles in (("E", ("", "x", "y", "d")), ("L", ("", "x", "y", "d")), ("R", ("", "x", "y")), ("B", ("", "x", "y"))):
-        for tile in tiles:
-            panels += ready[kind + tile]
-    panels += (value["Rd"], other["Rd"], value["Bd"], other["Bd"])
+    late = [panel for tile in ("R", "Rx", "Ry", "B", "Bx", "By") for panel in ready[tile]]
+    late += [value["Rd"], other["Rd"], value["Bd"], other["Bd"]]
     one, two = pl.pallas_call(
         march_kernel,
-        in_specs=[vmem] * 5 + [smem] + [vmem] * len(panels),
+        in_specs=[vmem] * 7 + [smem] + [vmem] * (len(early) + len(late)),
         out_specs=(vmem, vmem),
         out_shape=(jax.ShapeDtypeStruct((rows, width), F32),) * 2,
         scratch_shapes=[pltpu.VMEM((4 * width, width), BF16)] * 4,
         compiler_params=pltpu.CompilerParams(vmem_limit_bytes=12 * 2**20),
-    )(own["E"], value["Ex"], value["Ey"], value["Ed"], weight, place, *panels)
+    )(*states, *ready["lead"], place, *early, *late)
     return (one[None, None], two[None, None])
 
 

time: 103 us -> 105 us (1.019)
  starting transfers between devices: 23.3 us -> 26.2 us
    ppermute x26 -> x25, waiting for transfers between devices: 38.9 us -> 30.5 us  [from_partner(): return lax.ppermute(value, axis, pairs)]
    ppermute x0 -> x1, waiting for transfers between devices: none -> 7.4 us  [couple_across(): return lax.ppermute(couple, ('gx', 'gz'), pairs)]
    ppermute x0 -> x1, starting transfers between devices: none -> 4.96 us  [couple_across(): return lax.ppermute(couple, ('gx', 'gz'), pairs)]
    ppermute x26 -> x25, starting transfers between devices: 23.3 us -> 21.3 us  [from_partner(): return lax.ppermute(value, axis, pairs)]
    pallas_call x1 -> x2, Pallas kernels: 25 us -> 25.1 us  [the longest x1 23.9 us: shards(): pl.pallas_call(march_kernel, in_specs=[vmem] * 7 + [smem] + [vmem] * (len...]
  transfers between devices with their start and end apart: 26 -> 26, of which waited for: 14 -> 10; matrix products, arithmetic and copies ran while one was open for 0% -> 0% of each run, Pallas kernels for 12% -> 15%
where the time goes in v8:
time: 105 us
  Pallas kernels  39.5 us (38%)
  waiting for transfers between devices  37.9 us (36%)
  starting transfers between devices  26.2 us (25%)
    ppermute x25, waiting for transfers between devices, from_partner(): return lax.ppermute(value, axis, pairs)  30.5 us
    pallas_call x1, Pallas kernels, shards(): pl.pallas_call(march_kernel, in_specs=[vmem] * 7 + [smem] + [vmem] * (len...  23.9 us
    ppermute x25, starting transfers between devices, from_partner(): return lax.ppermute(value, axis, pairs)  21.3 us
    pallas_call x14, Pallas kernels, split_call(): pl.pallas_call(kernel, in_specs=[pl.BlockSpec(memory_space=pltpu.SMEM)] +...  9.57 us
    ppermute x1, waiting for transfers between devices, couple_across(): return lax.ppermute(couple, ('gx', 'gz'), pairs)  7.4 us
    ppermute x1, starting transfers between devices, couple_across(): return lax.ppermute(couple, ('gx', 'gz'), pairs)  4.96 us
    pallas_call x2, Pallas kernels, cut_call(): pl.pallas_call(cut_kernel, in_specs=[pl.BlockSpec(memory_space=pltpu.SMEM...  3.36 us
  transfers between devices with their start and end apart: 26, of which 10 were waited for; matrix products, arithmetic and copies ran while one was open for 0% of the time, Pallas kernels for 15%

profile of v8, /device:TPU:0, one launch (start us, length us, event | category | flops | bytes accessed | tf_op | source)
XLA Modules:
  0.0 104.7 jit_solution(3734930455336880753)
XLA Ops:
  0.6 5.0 %collective-permute-start = (f32[256,512]{1,0:T(8,128)}, f32[256,512]{1,0:T(8,128)S(1)}, u32[]{:S(2)}, u32[]{:S(2)}) collective-permute-start(f32[256,512]{1,0:T(8,128)} %bitcast.21), channel_id=1, source_target_pairs={{0,4},{5,1},{8,12},{13,9},{2,6},{7,3},{10,14},{15,11},{16,20},{21,... | collective-permute-start | bytes 1572872 | tf_op jit(solution)/shard_map/ppermute | solution.py:20
  5.7 1.6 %shard_map.115 = f32[256,512]{1,0:T(8,128)S(1)} custom-call(s32[4]{0:T(128)S(1)} %pad_add_fusion.place, f32[256,1024]{1,0:T(8,128)} %bitcast.19), custom_call_target="tpu_custom_call" | custom-call | flops 1 | bytes 1 | tf_op jit(solution)/shard_map/pallas_call | solution.py:81
  7.3 1.6 %collective-permute-start.4 = (f32[256,512]{1,0:T(8,128)S(1)}, f32[256,512]{1,0:T(8,128)S(1)}, u32[]{:S(2)}, u32[]{:S(2)}) collective-permute-start(f32[256,512]{1,0:T(8,128)S(1)} %shard_map.115), channel_id=1, source_target_pairs={{0,2},{2,0},{1,3},{3,1},{4,6},{6,4},{5,7},{7,5},{8,10},{10,8},{9,1... | collective-permute-start | bytes 1572872 | tf_op jit(solution)/shard_map/ppermute | solution.py:14
  8.9 7.4 %collective-permute-done.other = f32[256,512]{1,0:T(8,128)S(1)} collective-permute-done((f32[256,512]{1,0:T(8,128)}, f32[256,512]{1,0:T(8,128)S(1)}, u32[]{:S(2)}, u32[]{:S(2)}) %collective-permute-start) | collective-permute-done | bytes 524320 | tf_op jit(solution)/shard_map/ppermute | solution.py:20
  16.3 1.8 %shard_map.114 = (f32[512,256]{1,0:T(8,128)S(1)}, f32[512,256]{1,0:T(8,128)S(1)}) custom-call(s32[4]{0:T(128)S(1)} %pad_add_fusion.place, f32[1024,256]{1,0:T(8,128)} %bitcast.15, f32[1024,256]{1,0:T(8,128)} %bitcast.17), custom_call_target="tpu_custom_call" | custom-call | flops 1 | bytes 1 | tf_op jit(solution)/shard_map/pallas_call | solution.py:81
  18.1 2.8 %collective-permute-start.2 = (f32[512,256]{1,0:T(8,128)S(1)}, f32[512,256]{1,0:T(8,128)S(1)}, u32[]{:S(2)}, u32[]{:S(2)}) collective-permute-start(f32[512,256]{1,0:T(8,128)S(1)} %get-tuple-element.100), channel_id=1, source_target_pairs={{0,2},{2,0},{1,3},{3,1},{4,6},{6,4},{5,7},{7,5},{8,10},{10,8},{9,1... | collective-permute-start | bytes 1572872 | tf_op jit(solution)/shard_map/ppermute | solution.py:14
  20.9 2.4 %collective-permute-start.1 = (f32[512,256]{1,0:T(8,128)S(1)}, f32[512,256]{1,0:T(8,128)S(1)}, u32[]{:S(2)}, u32[]{:S(2)}) collective-permute-start(f32[512,256]{1,0:T(8,128)S(1)} %get-tuple-element.99), channel_id=1, source_target_pairs={{0,4},{4,0},{8,12},{12,8},{1,5},{5,1},{9,13},{13,9},{2,6},{6,2},{1... | collective-permute-start | bytes 1572872 | tf_op jit(solution)/shard_map/ppermute | solution.py:14
  23.3 1.4 %shard_map.113 = (f32[360,256]{1,0:T(8,128)S(1)}, f32[9,32]{1,0:T(8,128)S(1)}) custom-call(s32[4]{0:T(128)S(1)} %pad_add_fusion.place, f32[256,512]{1,0:T(8,128)S(1)} %bitcast.22, f32[256,512]{1,0:T(8,128)S(1)} %collective-permute-done.other, f32[512,256]{1,0:T(8,128)S(1)} %bitcast.23, s32[1,32]{1,0:T(1,128)S(1)} %bitcast.27, f32[32,256]{1,0:T(8,128)S(1)} %bitcast.24, ...), custom_call_target="tpu_custom_call" | custom-call | flops 1 | bytes 1 | tf_op jit(solution)/shard_map/pallas_call | solution.py:115
  24.9 2.5 %collective-permute-done.3.refs_0_ = f32[256,512]{1,0:T(8,128)S(1)} collective-permute-done((f32[256,512]{1,0:T(8,128)S(1)}, f32[256,512]{1,0:T(8,128)S(1)}, u32[]{:S(2)}, u32[]{:S(2)}) %collective-permute-start.3) | collective-permute-done | bytes 524320 | tf_op jit(solution)/shard_map/ppermute | solution.py:14
  27.4 0.7 shard_map.116
  28.1 5.6 %collective-permute-done.2.refs_0_ = f32[512,256]{1,0:T(8,128)S(1)} collective-permute-done((f32[512,256]{1,0:T(8,128)S(1)}, f32[512,256]{1,0:T(8,128)S(1)}, u32[]{:S(2)}, u32[]{:S(2)}) %collective-permute-start.2) | collective-permute-done | bytes 524320 | tf_op jit(solution)/shard_map/ppermute | solution.py:14
  33.7 2.4 %collective-permute-start.7 = (f32[512,256]{1,0:T(8,128)S(1)}, f32[512,256]{1,0:T(8,128)S(1)}, u32[]{:S(2)}, u32[]{:S(2)}) collective-permute-start(f32[512,256]{1,0:T(8,128)S(1)} %get-tuple-element.100), channel_id=1, source_target_pairs={{0,4},{4,0},{8,12},{12,8},{1,5},{5,1},{9,13},{13,9},{2,6},{6,2},{1... | collective-permute-start | bytes 1572872 | tf_op jit(solution)/shard_map/ppermute | solution.py:14
  36.1 1.8 %collective-permute-start.6 = (f32[512,256]{1,0:T(8,128)S(1)}, f32[512,256]{1,0:T(8,128)S(1)}, u32[]{:S(2)}, u32[]{:S(2)}) collective-permute-start(f32[512,256]{1,0:T(8,128)S(1)} %get-tuple-element.99), channel_id=1, source_target_pairs={{0,2},{2,0},{1,3},{3,1},{4,6},{6,4},{5,7},{7,5},{8,10},{10,8},{9,1... | collective-permute-start | bytes 1572872 | tf_op jit(solution)/shard_map/ppermute | solution.py:14
  38.6 0.7 shard_map.117
  39.4 1.4 %collective-permute-start.5 = (f32[360,256]{1,0:T(8,128)S(1)}, f32[360,256]{1,0:T(8,128)S(1)}, u32[]{:S(2)}, u32[]{:S(2)}) collective-permute-start(f32[360,256]{1,0:T(8,128)S(1)} %get-tuple-element.103.refs_0_.s0), channel_id=1, source_target_pairs={{0,4},{4,0},{8,12},{12,8},{1,5},{5,1},{9,13},{13,9},{2,6},{6,2},{1... | collective-permute-start | bytes 1105928 | tf_op jit(solution)/shard_map/ppermute | solution.py:14
  41.5 0.7 shard_map.120
  42.2 6.7 %collective-permute-done.7.refs_0_ = f32[512,256]{1,0:T(8,128)S(1)} collective-permute-done((f32[512,256]{1,0:T(8,128)S(1)}, f32[512,256]{1,0:T(8,128)S(1)}, u32[]{:S(2)}, u32[]{:S(2)}) %collective-permute-start.7) | collective-permute-done | bytes 524320 | tf_op jit(solution)/shard_map/ppermute | solution.py:14
  48.9 1.8 %collective-permute-start.13 = (f32[256,512]{1,0:T(8,128)S(1)}, f32[256,512]{1,0:T(8,128)S(1)}, u32[]{:S(2)}, u32[]{:S(2)}) collective-permute-start(f32[256,512]{1,0:T(8,128)S(1)} %collective-permute-done.3.refs_0_), channel_id=1, source_target_pairs={{0,2},{2,0},{1,3},{3,1},{4,6},{6,4},{5,7},{7,5},{8,10},{10,8},{9,1... | collective-permute-start | bytes 1572872 | tf_op jit(solution)/shard_map/ppermute | solution.py:14
  50.9 5.7 %collective-permute-done.5.refs_0_.s1 = f32[360,256]{1,0:T(8,128)S(1)} collective-permute-done((f32[360,256]{1,0:T(8,128)S(1)}, f32[360,256]{1,0:T(8,128)S(1)}, u32[]{:S(2)}, u32[]{:S(2)}) %collective-permute-start.5) | collective-permute-done | bytes 368672 | tf_op jit(solution)/shard_map/ppermute | solution.py:14
  56.6 1.7 %collective-permute-start.12 = (f32[360,256]{1,0:T(8,128)S(1)}, f32[360,256]{1,0:T(8,128)S(1)}, u32[]{:S(2)}, u32[]{:S(2)}) collective-permute-start(f32[360,256]{1,0:T(8,128)S(1)} %collective-permute-done.8.refs_0_.s2), channel_id=1, source_target_pairs={{0,4},{4,0},{8,12},{12,8},{1,5},{5,1},{9,13},{13,9},{2,6},{6,2},{1... | collective-permute-start | bytes 1105928 | tf_op jit(solution)/shard_map/ppermute | solution.py:14
  58.4 0.7 shard_map.122
  59.1 1.8 %collective-permute-start.17 = (f32[512,256]{1,0:T(8,128)S(1)}, f32[512,256]{1,0:T(8,128)S(1)}, u32[]{:S(2)}, u32[]{:S(2)}) collective-permute-start(f32[512,256]{1,0:T(8,128)S(1)} %collective-permute-done.1.refs_0_), channel_id=1, source_target_pairs={{0,2},{2,0},{1,3},{3,1},{4,6},{6,4},{5,7},{7,5},{8,10},{10,8},{9,1... | collective-permute-start | bytes 1572872 | tf_op jit(solution)/shard_map/ppermute | solution.py:14
  61.6 2.0 %collective-permute-done.13.refs_0_ = f32[256,512]{1,0:T(8,128)S(1)} collective-permute-done((f32[256,512]{1,0:T(8,128)S(1)}, f32[256,512]{1,0:T(8,128)S(1)}, u32[]{:S(2)}, u32[]{:S(2)}) %collective-permute-start.13) | collective-permute-done | bytes 524320 | tf_op jit(solution)/shard_map/ppermute | solution.py:14
  63.6 1.9 %collective-permute-start.24 = (f32[512,256]{1,0:T(8,128)S(1)}, f32[512,256]{1,0:T(8,128)S(1)}, u32[]{:S(2)}, u32[]{:S(2)}) collective-permute-start(f32[512,256]{1,0:T(8,128)S(1)} %collective-permute-done.2.refs_0_), channel_id=1, source_target_pairs={{0,4},{4,0},{8,12},{12,8},{1,5},{5,1},{9,13},{13,9},{2,6},{6,2},{1... | collective-permute-start | bytes 1572872 | tf_op jit(solution)/shard_map/ppermute | solution.py:14
  65.6 2.4 %collective-permute-done.12.refs_0_.s3 = f32[360,256]{1,0:T(8,128)S(1)} collective-permute-done((f32[360,256]{1,0:T(8,128)S(1)}, f32[360,256]{1,0:T(8,128)S(1)}, u32[]{:S(2)}, u32[]{:S(2)}) %collective-permute-start.12) | collective-permute-done | bytes 368672 | tf_op jit(solution)/shard_map/ppermute | solution.py:14
  69.2 0.7 shard_map.125
  70.6 3.8 %collective-permute-done.17.refs_28_ = f32[512,256]{1,0:T(8,128)S(1)} collective-permute-done((f32[512,256]{1,0:T(8,128)S(1)}, f32[512,256]{1,0:T(8,128)S(1)}, u32[]{:S(2)}, u32[]{:S(2)}) %collective-permute-start.17) | collective-permute-done | bytes 524320 | tf_op jit(solution)/shard_map/ppermute | solution.py:14
  75.6 0.7 shard_map.127
  76.4 1.2 %shard_map.128 = (f32[32,1024]{1,0:T(8,128)S(1)}, f32[32,1024]{1,0:T(8,128)S(1)}) custom-call(f32[360,256]{1,0:T(8,128)S(1)} %get-tuple-element.103.refs_0_.s0, f32[360,256]{1,0:T(8,128)S(1)} %collective-permute-done.5.refs_0_.s1, f32[360,256]{1,0:T(8,128)S(1)} %collective-permute-done.8.refs_0_.s2, f32[360,256]{1,0:T(8,128)S(1)} %collective-permute-done.12.refs_0_.s3, ...), custom_call_target="tpu_custom_call" | custom-call | flops 1 | bytes 1 | tf_op jit(solution)/shard_map/pallas_call | solution.py:298
  77.6 1.3 %collective-permute-done.24.refs_30_ = f32[512,256]{1,0:T(8,128)S(1)} collective-permute-done((f32[512,256]{1,0:T(8,128)S(1)}, f32[512,256]{1,0:T(8,128)S(1)}, u32[]{:S(2)}, u32[]{:S(2)}) %collective-permute-start.24) | collective-permute-done | bytes 524320 | tf_op jit(solution)/shard_map/ppermute | solution.py:14
  78.9 0.7 shard_map.130
  80.8 23.9 %shard_map.131 = (f32[32,256]{1,0:T(8,128)}, f32[32,256]{1,0:T(8,128)}) custom-call(f32[360,256]{1,0:T(8,128)S(1)} %get-tuple-element.103.refs_0_.s0, f32[360,256]{1,0:T(8,128)S(1)} %collective-permute-done.5.refs_0_.s1, f32[360,256]{1,0:T(8,128)S(1)} %collective-permute-done.8.refs_0_.s2, f32[360,256]{1,0:T(8,128)S(1)} %collective-permute-done.12.refs_0_.s3, ...), custom_call_target="tpu_custom_call" | custom-call | tf_op jit(solution)/shard_map/pallas_call | solution.py:313
  (60 shorter events, 6.9 us)
Async XLA Ops:
  0.6 15.6 %collective-permute-start = (f32[256,512]{1,0:T(8,128)}, f32[256,512]{1,0:T(8,128)S(1)}, u32[]{:S(2)}, u32[]{:S(2)}) collective-permute-start(f32[256,512]{1,0:T(8,128)} %bitcast.21), channel_id=1, source_target_pairs={{0,4},{5,1},{8,12},{13,9},{2,6},{7,3},{10,14},{15,11},{16,20},{21,... | collective-permute-start | bytes 1572872 | tf_op jit(solution)/shard_map/ppermute | solution.py:20
  7.3 17.4 %collective-permute-start.4 = (f32[256,512]{1,0:T(8,128)S(1)}, f32[256,512]{1,0:T(8,128)S(1)}, u32[]{:S(2)}, u32[]{:S(2)}) collective-permute-start(f32[256,512]{1,0:T(8,128)S(1)} %shard_map.115), channel_id=1, source_target_pairs={{0,2},{2,0},{1,3},{3,1},{4,6},{6,4},{5,7},{7,5},{8,10},{10,8},{9,1... | collective-permute-start | bytes 1572872 | tf_op jit(solution)/shard_map/ppermute | solution.py:14
  8.9 18.5 %collective-permute-start.3 = (f32[256,512]{1,0:T(8,128)S(1)}, f32[256,512]{1,0:T(8,128)S(1)}, u32[]{:S(2)}, u32[]{:S(2)}) collective-permute-start(f32[256,512]{1,0:T(8,128)S(1)} %shard_map.115), channel_id=1, source_target_pairs={{0,4},{4,0},{8,12},{12,8},{1,5},{5,1},{9,13},{13,9},{2,6},{6,2},{1... | collective-permute-start | bytes 1572872 | tf_op jit(solution)/shard_map/ppermute | solution.py:14
  16.3 7.0 %copy-start.7 = (f32[9,32]{1,0:T(8,128)S(1)}, f32[9,32]{1,0:T(8,128)}, u32[]{:S(2)}) copy-start(f32[9,32]{1,0:T(8,128)} %weight.1) | copy-start | bytes 3460
  16.3 7.0 %copy-start.8 = (f32[1,1,256]{2,1,0:T(1,128)S(1)}, f32[1,1,256]{2,1,0:T(1,128)}, u32[]{:S(2)}) copy-start(f32[1,1,256]{2,1,0:T(1,128)} %param.17) | copy-start | bytes 3076
  16.3 7.0 %copy-start.9 = (s32[32]{0:T(128)S(1)}, s32[32]{0:T(128)}, u32[]{:S(2)}) copy-start(s32[32]{0:T(128)} %param.18) | copy-start | bytes 388
  18.1 9.3 %copy-start.2 = (f32[1,1,256,1024]{3,2,1,0:T(8,128)S(1)}, f32[1,1,256,1024]{3,2,1,0:T(8,128)}, u32[]{:S(2)}) copy-start(f32[1,1,256,1024]{3,2,1,0:T(8,128)} %param.14) | copy-start | bytes 3145732
  18.1 15.6 %collective-permute-start.2 = (f32[512,256]{1,0:T(8,128)S(1)}, f32[512,256]{1,0:T(8,128)S(1)}, u32[]{:S(2)}, u32[]{:S(2)}) collective-permute-start(f32[512,256]{1,0:T(8,128)S(1)} %get-tuple-element.100), channel_id=1, source_target_pairs={{0,2},{2,0},{1,3},{3,1},{4,6},{6,4},{5,7},{7,5},{8,10},{10,8},{9,1... | collective-permute-start | bytes 1572872 | tf_op jit(solution)/shard_map/ppermute | solution.py:14
  20.9 15.2 %collective-permute-start.1 = (f32[512,256]{1,0:T(8,128)S(1)}, f32[512,256]{1,0:T(8,128)S(1)}, u32[]{:S(2)}, u32[]{:S(2)}) collective-permute-start(f32[512,256]{1,0:T(8,128)S(1)} %get-tuple-element.99), channel_id=1, source_target_pairs={{0,4},{4,0},{8,12},{12,8},{1,5},{5,1},{9,13},{13,9},{2,6},{6,2},{1... | collective-permute-start | bytes 1572872 | tf_op jit(solution)/shard_map/ppermute | solution.py:14
  23.3 14.6 %copy-start = (f32[1,1,1024,256]{3,2,1,0:T(8,128)S(1)}, f32[1,1,1024,256]{3,2,1,0:T(8,128)}, u32[]{:S(2)}) copy-start(f32[1,1,1024,256]{3,2,1,0:T(8,128)} %param.16) | copy-start | bytes 3145732
  24.8 13.8 %copy-start.1 = (f32[1,1,1024,256]{3,2,1,0:T(8,128)S(1)}, f32[1,1,1024,256]{3,2,1,0:T(8,128)}, u32[]{:S(2)}) copy-start(f32[1,1,1024,256]{3,2,1,0:T(8,128)} %param.15) | copy-start | bytes 3145732
  24.8 14.6 %collective-permute-start.8 = (f32[360,256]{1,0:T(8,128)S(1)}, f32[360,256]{1,0:T(8,128)S(1)}, u32[]{:S(2)}, u32[]{:S(2)}) collective-permute-start(f32[360,256]{1,0:T(8,128)S(1)} %get-tuple-element.103.refs_0_.s0), channel_id=1, source_target_pairs={{0,2},{2,0},{1,3},{3,1},{4,6},{6,4},{5,7},{7,5},{8,10},{10,8},{9,1... | collective-permute-start | bytes 1105928 | tf_op jit(solution)/shard_map/ppermute | solution.py:14
  27.4 12.0 %collective-permute-start.9 = (f32[360,256]{1,0:T(8,128)S(1)}, f32[360,256]{1,0:T(8,128)S(1)}, u32[]{:S(2)}, u32[]{:S(2)}) collective-permute-start(f32[360,256]{1,0:T(8,128)S(1)} %get-tuple-element.103.refs_0_.s0), channel_id=1, source_target_pairs={{0,1},{1,0},{2,3},{3,2},{4,5},{5,4},{6,7},{7,6},{8,9},{9,8},{10,11... | collective-permute-start | bytes 1105928 | tf_op jit(solution)/shard_map/ppermute | solution.py:14
  33.7 7.8 %collective-permute-start.10 = (f32[256,512]{1,0:T(8,128)S(1)}, f32[256,512]{1,0:T(8,128)S(1)}, u32[]{:S(2)}, u32[]{:S(2)}) collective-permute-start(f32[256,512]{1,0:T(8,128)S(1)} %collective-permute-done.4.refs_0_), channel_id=1, source_target_pairs={{0,1},{1,0},{2,3},{3,2},{4,5},{5,4},{6,7},{7,6},{8,9},{9,8},{10,11... | collective-permute-start | bytes 1572872 | tf_op jit(solution)/shard_map/ppermute | solution.py:14
  33.7 15.2 %collective-permute-start.7 = (f32[512,256]{1,0:T(8,128)S(1)}, f32[512,256]{1,0:T(8,128)S(1)}, u32[]{:S(2)}, u32[]{:S(2)}) collective-permute-start(f32[512,256]{1,0:T(8,128)S(1)} %get-tuple-element.100), channel_id=1, source_target_pairs={{0,4},{4,0},{8,12},{12,8},{1,5},{5,1},{9,13},{13,9},{2,6},{6,2},{1... | collective-permute-start | bytes 1572872 | tf_op jit(solution)/shard_map/ppermute | solution.py:14
  36.1 14.5 %collective-permute-start.6 = (f32[512,256]{1,0:T(8,128)S(1)}, f32[512,256]{1,0:T(8,128)S(1)}, u32[]{:S(2)}, u32[]{:S(2)}) collective-permute-start(f32[512,256]{1,0:T(8,128)S(1)} %get-tuple-element.99), channel_id=1, source_target_pairs={{0,2},{2,0},{1,3},{3,1},{4,6},{6,4},{5,7},{7,5},{8,10},{10,8},{9,1... | collective-permute-start | bytes 1572872 | tf_op jit(solution)/shard_map/ppermute | solution.py:14
  39.3 17.3 %collective-permute-start.14 = (f32[256,512]{1,0:T(8,128)S(1)}, f32[256,512]{1,0:T(8,128)S(1)}, u32[]{:S(2)}, u32[]{:S(2)}) collective-permute-start(f32[256,512]{1,0:T(8,128)S(1)} %collective-permute-done.3.refs_0_), channel_id=1, source_target_pairs={{0,1},{1,0},{2,3},{3,2},{4,5},{5,4},{6,7},{7,6},{8,9},{9,8},{10,11... | collective-permute-start | bytes 1572872 | tf_op jit(solution)/shard_map/ppermute | solution.py:14
  39.4 17.2 %collective-permute-start.5 = (f32[360,256]{1,0:T(8,128)S(1)}, f32[360,256]{1,0:T(8,128)S(1)}, u32[]{:S(2)}, u32[]{:S(2)}) collective-permute-start(f32[360,256]{1,0:T(8,128)S(1)} %get-tuple-element.103.refs_0_.s0), channel_id=1, source_target_pairs={{0,4},{4,0},{8,12},{12,8},{1,5},{5,1},{9,13},{13,9},{2,6},{6,2},{1... | collective-permute-start | bytes 1105928 | tf_op jit(solution)/shard_map/ppermute | solution.py:14
  48.9 10.2 %collective-permute-start.11 = (f32[512,256]{1,0:T(8,128)S(1)}, f32[512,256]{1,0:T(8,128)S(1)}, u32[]{:S(2)}, u32[]{:S(2)}) collective-permute-start(f32[512,256]{1,0:T(8,128)S(1)} %collective-permute-done.1.refs_0_), channel_id=1, source_target_pairs={{0,1},{1,0},{2,3},{3,2},{4,5},{5,4},{6,7},{7,6},{8,9},{9,8},{10,11... | collective-permute-start | bytes 1572872 | tf_op jit(solution)/shard_map/ppermute | solution.py:14
  48.9 14.7 %collective-permute-start.13 = (f32[256,512]{1,0:T(8,128)S(1)}, f32[256,512]{1,0:T(8,128)S(1)}, u32[]{:S(2)}, u32[]{:S(2)}) collective-permute-start(f32[256,512]{1,0:T(8,128)S(1)} %collective-permute-done.3.refs_0_), channel_id=1, source_target_pairs={{0,2},{2,0},{1,3},{3,1},{4,6},{6,4},{5,7},{7,5},{8,10},{10,8},{9,1... | collective-permute-start | bytes 1572872 | tf_op jit(solution)/shard_map/ppermute | solution.py:14
  50.7 18.0 %collective-permute-start.18 = (f32[512,256]{1,0:T(8,128)S(1)}, f32[512,256]{1,0:T(8,128)S(1)}, u32[]{:S(2)}, u32[]{:S(2)}) collective-permute-start(f32[512,256]{1,0:T(8,128)S(1)} %collective-permute-done.2.refs_0_), channel_id=1, source_target_pairs={{0,1},{1,0},{2,3},{3,2},{4,5},{5,4},{6,7},{7,6},{8,9},{9,8},{10,11... | collective-permute-start | bytes 1572872 | tf_op jit(solution)/shard_map/ppermute | solution.py:14
  56.6 7.0 %collective-permute-start.15 = (f32[360,256]{1,0:T(8,128)S(1)}, f32[360,256]{1,0:T(8,128)S(1)}, u32[]{:S(2)}, u32[]{:S(2)}) collective-permute-start(f32[360,256]{1,0:T(8,128)S(1)} %collective-permute-done.8.refs_0_.s2), channel_id=1, source_target_pairs={{0,1},{1,0},{2,3},{3,2},{4,5},{5,4},{6,7},{7,6},{8,9},{9,8},{10,11... | collective-permute-start | bytes 1105928 | tf_op jit(solution)/shard_map/ppermute | solution.py:14
  56.6 11.4 %collective-permute-start.12 = (f32[360,256]{1,0:T(8,128)S(1)}, f32[360,256]{1,0:T(8,128)S(1)}, u32[]{:S(2)}, u32[]{:S(2)}) collective-permute-start(f32[360,256]{1,0:T(8,128)S(1)} %collective-permute-done.8.refs_0_.s2), channel_id=1, source_target_pairs={{0,4},{4,0},{8,12},{12,8},{1,5},{5,1},{9,13},{13,9},{2,6},{6,2},{1... | collective-permute-start | bytes 1105928 | tf_op jit(solution)/shard_map/ppermute | solution.py:14
  59.1 15.4 %collective-permute-start.17 = (f32[512,256]{1,0:T(8,128)S(1)}, f32[512,256]{1,0:T(8,128)S(1)}, u32[]{:S(2)}, u32[]{:S(2)}) collective-permute-start(f32[512,256]{1,0:T(8,128)S(1)} %collective-permute-done.1.refs_0_), channel_id=1, source_target_pairs={{0,2},{2,0},{1,3},{3,1},{4,6},{6,4},{5,7},{7,5},{8,10},{10,8},{9,1... | collective-permute-start | bytes 1572872 | tf_op jit(solution)/shard_map/ppermute | solution.py:14
  63.6 12.0 %collective-permute-start.20 = (f32[256,512]{1,0:T(8,128)S(1)}, f32[256,512]{1,0:T(8,128)S(1)}, u32[]{:S(2)}, u32[]{:S(2)}) collective-permute-start(f32[256,512]{1,0:T(8,128)S(1)} %collective-permute-done.13.refs_0_), channel_id=1, source_target_pairs={{0,1},{1,0},{2,3},{3,2},{4,5},{5,4},{6,7},{7,6},{8,9},{9,8},{10,11... | collective-permute-start | bytes 1572872 | tf_op jit(solution)/shard_map/ppermute | solution.py:14
  63.6 15.2 %collective-permute-start.24 = (f32[512,256]{1,0:T(8,128)S(1)}, f32[512,256]{1,0:T(8,128)S(1)}, u32[]{:S(2)}, u32[]{:S(2)}) collective-permute-start(f32[512,256]{1,0:T(8,128)S(1)} %collective-permute-done.2.refs_0_), channel_id=1, source_target_pairs={{0,4},{4,0},{8,12},{12,8},{1,5},{5,1},{9,13},{13,9},{2,6},{6,2},{1... | collective-permute-start | bytes 1572872 | tf_op jit(solution)/shard_map/ppermute | solution.py:14
  68.0 1.9 %collective-permute-start.16 = (f32[360,256]{1,0:T(8,128)S(1)}, f32[360,256]{1,0:T(8,128)S(1)}, u32[]{:S(2)}, u32[]{:S(2)}) collective-permute-start(f32[360,256]{1,0:T(8,128)S(1)} %collective-permute-done.5.refs_0_.s1), channel_id=1, source_target_pairs={{0,1},{1,0},{2,3},{3,2},{4,5},{5,4},{6,7},{7,6},{8,9},{9,8},{10,11... | collective-permute-start | bytes 1105928 | tf_op jit(solution)/shard_map/ppermute | solution.py:14
  68.6 5.8 %collective-permute-start.19 = (f32[360,256]{1,0:T(8,128)S(1)}, f32[360,256]{1,0:T(8,128)S(1)}, u32[]{:S(2)}, u32[]{:S(2)}) collective-permute-start(f32[360,256]{1,0:T(8,128)S(1)} %collective-permute-done.12.refs_0_.s3), channel_id=1, source_target_pairs={{0,1},{1,0},{2,3},{3,2},{4,5},{5,4},{6,7},{7,6},{8,9},{9,8},{10,11... | collective-permute-start | bytes 1105928 | tf_op jit(solution)/shard_map/ppermute | solution.py:14
  69.9 8.9 %collective-permute-start.22 = (f32[512,256]{1,0:T(8,128)S(1)}, f32[512,256]{1,0:T(8,128)S(1)}, u32[]{:S(2)}, u32[]{:S(2)}) collective-permute-start(f32[512,256]{1,0:T(8,128)S(1)} %collective-permute-done.7.refs_0_), channel_id=1, source_target_pairs={{0,1},{1,0},{2,3},{3,2},{4,5},{5,4},{6,7},{7,6},{8,9},{9,8},{10,11... | collective-permute-start | bytes 1572872 | tf_op jit(solution)/shard_map/ppermute | solution.py:14
  74.5 5.1 %collective-permute-start.21 = (f32[512,256]{1,0:T(8,128)S(1)}, f32[512,256]{1,0:T(8,128)S(1)}, u32[]{:S(2)}, u32[]{:S(2)}) collective-permute-start(f32[512,256]{1,0:T(8,128)S(1)} %collective-permute-done.6.refs_0_), channel_id=1, source_target_pairs={{0,1},{1,0},{2,3},{3,2},{4,5},{5,4},{6,7},{7,6},{8,9},{9,8},{10,11... | collective-permute-start | bytes 1572872 | tf_op jit(solution)/shard_map/ppermute | solution.py:14
  74.5 5.8 %collective-permute-start.23 = (f32[512,256]{1,0:T(8,128)S(1)}, f32[512,256]{1,0:T(8,128)S(1)}, u32[]{:S(2)}, u32[]{:S(2)}) collective-permute-start(f32[512,256]{1,0:T(8,128)S(1)} %collective-permute-done.17.refs_28_), channel_id=1, source_target_pairs={{0,1},{1,0},{2,3},{3,2},{4,5},{5,4},{6,7},{7,6},{8,9},{9,8},{10,11... | collective-permute-start | bytes 1572872 | tf_op jit(solution)/shard_map/ppermute | solution.py:14
  78.8 1.9 %collective-permute-start.25 = (f32[512,256]{1,0:T(8,128)S(1)}, f32[512,256]{1,0:T(8,128)S(1)}, u32[]{:S(2)}, u32[]{:S(2)}) collective-permute-start(f32[512,256]{1,0:T(8,128)S(1)} %collective-permute-done.24.refs_30_), channel_id=1, source_target_pairs={{0,1},{1,0},{2,3},{3,2},{4,5},{5,4},{6,7},{7,6},{8,9},{9,8},{10,11... | collective-permute-start | bytes 1572872 | tf_op jit(solution)/shard_map/ppermute | solution.py:14
  (4 other events, 28.0 us)

commit v9 on v8

--- a/solution.py
+++ b/solution.py
@@ -12,12 +12,6 @@
 def from_partner(value, axis):
     pairs = [(source, source ^ 1) for source in range(lax.axis_size(axis))]
     return lax.ppermute(value, axis, pairs)
-
-
-def couple_across(couple):
-    columns, cores = lax.axis_size("gx"), lax.axis_size("gz")
-    pairs = [(column * cores + column % 2, (column ^ 1) * cores + column % 2) for column in range(columns)]
-    return lax.ppermute(couple, ("gx", "gz"), pairs)
 
 
 def after(value, *earlier):
@@ -46,13 +40,13 @@
     ("take", "By", "L"), ("send", "Ry"), ("swap", "Ly"),
     ("take", "Rx", "R", "B"), ("send", "Ex"), ("swap", "Lx"), ("split", "E"),
     ("take", "Ey", "E"), ("send", "Ld"), ("split", "Ly"),
-    ("take", "Bx", "Ly"), ("send", "Ed"), ("swap", "By"), ("swap", "Rx"), ("split", "Rx"),
-    ("take", "Ry"), ("send", "Rd"), ("swap", "Ey"), ("swap", "Bx"), ("split", "Lx"),
+    ("take", "Bx", "Ly"), ("send", "Ed"), ("swap", "By"), ("swap", "Rx"), ("split", "By"), ("split", "Rx"),
+    ("take", "Ry"), ("send", "Rd"), ("swap", "Ey"), ("split", "Lx"),
     ("take", "Ex", "Rx"), ("send", "Bd"),
-    ("take", "Ld", "Lx"), ("swap", "Ry"), ("swap", "Ex"), ("swap", "Ld"), ("split", "By"), ("split", "Ey"), ("split", "Bx"), ("split", "Ex"),
-    ("take", "Ed", "Ey"), ("swap", "Ed"), ("split", "Ry"), ("split", "Ld"),
-    ("take", "Rd", "By", "Ex"), ("swap", "Rd"), ("split", "Ed"), ("lead", "lead"),
-    ("take", "Bd", "Ld", "Ed", "lead"), ("swap", "Bd"),
+    ("take", "Ld", "Lx"), ("swap", "Bx"), ("swap", "Ry"), ("swap", "Ex"), ("swap", "Ld"), ("split", "Ey"), ("split", "Ex"),
+    ("take", "Ed", "By", "Ey"), ("swap", "Ed"), ("split", "Ld"),
+    ("take", "Rd", "Ex"), ("swap", "Rd"), ("split", "Rd"), ("split", "Bx"), ("split", "Ed"), ("lead", "lead"),
+    ("take", "Bd", "Ld", "Ed", "lead"), ("swap", "Bd"), ("split", "Ry"), ("root", "root"),
 )
 
 
@@ -96,16 +90,18 @@
 
 
 def edge_state_kernel(place, mine, other, pair_cols, cells, one, two, mass, weight, edge_ref, weight_ref):
+    half = mine.shape[0]
     rows, width = one.shape
-    couple = jnp.where(place[0] % 2 == place[1], mine[...], other[...])
-    edge_ref[:width, :] = exact_dot(couple, pair_cols[...])
+    for step, couple in enumerate((mine, other)):
+        start = ((place[0] % 2) ^ step) * half
+        edge_ref[pl.ds(pl.multiple_of(start, half), half), :] = exact_dot(couple[...], pair_cols[...])
     cell = column_of(cells[...].astype(F32))
     number = lax.broadcasted_iota(jnp.int32, (rows, width), 1)
     chosen = [(cell == (number + place[2 + side]).astype(F32)).astype(F32) for side in range(2)]
     picked = exact_dot(jnp.concatenate(chosen, axis=1), pair_cols[...])
     for index, value in enumerate((one[...], two[...], picked)):
-        edge_ref[width + index * rows:width + (index + 1) * rows, :] = value
-    edge_ref[width + 3 * rows:, :] = jnp.broadcast_to(mass[...], (8, width))
+        edge_ref[2 * half + index * rows:2 * half + (index + 1) * rows, :] = value
+    edge_ref[2 * half + 3 * rows:, :] = jnp.broadcast_to(mass[...], (8, width))
     weight_ref[...] = weight[...]
 
 
@@ -149,10 +145,12 @@
 
 def edge_kernel(place, *refs):
     pieces, (high_ref, low_ref) = refs[:-2], refs[-2:]
-    width = high_ref.shape[1]
+    rows = pieces[0].shape[1] // 2
     for part, piece in enumerate(pieces):
-        start = (place[1] ^ part ^ (place[0] % 2)) * width
-        store_split(high_ref, low_ref, (pl.ds(pl.multiple_of(start, width), width), slice(None)), piece[:width, :])
+        for bit in range(2):
+            start = (bit ^ (place[0] % 2)) * 2 * rows + (place[1] ^ part) * rows
+            where = (pl.ds(pl.multiple_of(start, rows), rows), slice(None))
+            store_split(high_ref, low_ref, where, piece[bit * rows:(bit + 1) * rows, :])
 
 
 def split_call(kernel, place, rows, *pieces):
@@ -212,14 +210,17 @@
     sums_ref[...] = quad_sums(half_ref[...], two, scale, lift)
 
 
-def march_kernel(s0, s1, s2, s3, weight, half_start, sums_start, place, *refs):
-    edge, lift, root, back = refs[:8], refs[8:16], refs[16:22], refs[22:28]
-    root_mine, root_other, back_mine, back_other, one_ref, two_ref = refs[28:34]
+def root_kernel(sums, *refs):
+    refs[-1][...] = tall(sums[...], refs[:-1])
+
+
+def march_kernel(s0, s1, s2, s3, weight, half_start, two_start, place, *refs):
+    edge, lift, root, back = refs[:8], refs[8:16], refs[16:24], refs[24:30]
+    mine, other, one_ref, two_ref, last_high, last_low = refs[30:]
     rows, width = one_ref.shape
     tiles = (s0, s1, s2, s3)
-    split_tall(place, (root_mine, root_other), *refs[34:36])
-    split_tall(place, (back_mine, back_other), *refs[36:38])
-    root, back = root + refs[34:36], back + refs[36:38]
+    split_tall(place, (mine, other), last_high, last_low)
+    back = back + (last_high, last_low)
     picked, scale = below(tiles, rows, 2, rows), below(tiles, rows, 3, 1)
 
     def advance(step, carry):
@@ -227,7 +228,7 @@
         half = forward_half(half - tall(two, back), picked, weight[pl.ds(step, 1), :], edge)
         return half, tall(quad_sums(half, two, scale, lift), root)
 
-    half, two = lax.fori_loop(1, weight.shape[0], advance, (half_start[...], tall(sums_start[...], root)))
+    half, two = lax.fori_loop(1, weight.shape[0], advance, (half_start[...], two_start[...]))
     one_ref[...] = half[:, :width] - product(two, back[0][...], back[1][...])
     two_ref[...] = two[:, :width]
 
@@ -256,8 +257,8 @@
     first_cell = ((column - x_bit) * lax.axis_size("gy") + row) * width
     place = jnp.stack([2 * y_bit + x_bit, core, first_cell, first_cell + lax.axis_size("gy") * width]).astype(jnp.int32)
 
-    (lift_half,) = cut_call(place, (lift,), ((width, 2 * width),))
-    value = {"Cx": couple_across(couple), "Ly": from_partner(lift_half, "gy"), "Lx": from_partner(lift_half, "gx")}
+    couple_half, lift_half = cut_call(place, (couple, lift), ((width // 2, 2 * width), (width, 2 * width)))
+    value = {"Cx": from_partner(couple_half, "gx"), "Ly": from_partner(lift_half, "gy"), "Lx": from_partner(lift_half, "gx")}
     back_half, root_half = cut_call(after(place, value["Cx"]), (back, root), ((2 * width, width),) * 2)
     own = {"L": lift_half, "B": back_half, "R": root_half}
     kernels = {"L": (wide_kernel, 4 * width), "R": (tall_kernel, 4 * width), "B": (tall_kernel, 4 * width), "E": (edge_kernel, 2 * width)}
@@ -276,7 +277,7 @@
             own["E"], weight = edge_call(
                 width + 3 * rows + 8,
                 place,
-                couple,
+                couple_half,
                 value["Cx"],
                 pair_cols,
                 probe_cells[None, :],
@@ -303,21 +304,30 @@
                 cost_estimate=CHEAP,
                 compiler_params=pltpu.CompilerParams(vmem_limit_bytes=6 * 2**20),
             )(*states, *early)
+        elif verb == "root":
+            roots = [panel for tile in ("R", "Rx", "Ry", "Rd") for panel in ready[tile]]
+            two = pl.pallas_call(
+                root_kernel,
+                in_specs=[pl.BlockSpec(memory_space=pltpu.VMEM)] * (1 + len(roots)),
+                out_specs=pl.BlockSpec(memory_space=pltpu.VMEM),
+                out_shape=jax.ShapeDtypeStruct((rows, 4 * width), F32),
+                cost_estimate=CHEAP,
+                compiler_params=pltpu.CompilerParams(vmem_limit_bytes=6 * 2**20),
+            )(ready["lead"][1], *roots)
         else:
             kernel, size = kernels[kind]
             ready[name] = split_call(kernel, after(place, token), size, value[name], other[name])
 
     vmem, smem = pl.BlockSpec(memory_space=pltpu.VMEM), pl.BlockSpec(memory_space=pltpu.SMEM)
-    late = [panel for tile in ("R", "Rx", "Ry", "B", "Bx", "By") for panel in ready[tile]]
-    late += [value["Rd"], other["Rd"], value["Bd"], other["Bd"]]
+    late = [panel for tile in ("B", "Bx", "By") for panel in ready[tile]] + [value["Bd"], other["Bd"]]
     one, two = pl.pallas_call(
         march_kernel,
-        in_specs=[vmem] * 7 + [smem] + [vmem] * (len(early) + len(late)),
+        in_specs=[vmem] * 7 + [smem] + [vmem] * (len(early) + len(roots) + len(late)),
         out_specs=(vmem, vmem),
         out_shape=(jax.ShapeDtypeStruct((rows, width), F32),) * 2,
-        scratch_shapes=[pltpu.VMEM((4 * width, width), BF16)] * 4,
+        scratch_shapes=[pltpu.VMEM((4 * width, width), BF16)] * 2,
         compiler_params=pltpu.CompilerParams(vmem_limit_bytes=12 * 2**20),
-    )(*states, *ready["lead"], place, *early, *late)
+    )(*states, ready["lead"][0], two, place, *early, *roots, *late)
     return (one[None, None], two[None, None])
 
 

time: 105 us -> 102 us (0.971)
  starting transfers between devices: 26.2 us -> 19.6 us
  waiting for transfers between devices: 37.9 us -> 41.3 us
    ppermute x25 -> x26, waiting for transfers between devices: 30.5 us -> 41.3 us  [from_partner(): return lax.ppermute(value, axis, pairs)]
    ppermute x1 -> x0, waiting for transfers between devices: 7.4 us -> none  [couple_across(): return lax.ppermute(couple, ('gx', 'gz'), pairs)]
    ppermute x1 -> x0, starting transfers between devices: 4.96 us -> none  [couple_across(): return lax.ppermute(couple, ('gx', 'gz'), pairs)]
    ppermute x25 -> x26, starting transfers between devices: 21.3 us -> 19.6 us  [from_partner(): return lax.ppermute(value, axis, pairs)]
    pallas_call x14 -> x15, Pallas kernels: 9.57 us -> 10.2 us  [split_call(): pl.pallas_call(kernel, in_specs=[pl.BlockSpec(memory_space=pltpu.SMEM)] +...]
  transfers between devices with their start and end apart: 26 -> 26, of which waited for: 10 -> 13; matrix products, arithmetic and copies ran while one was open for 0% -> 0% of each run, Pallas kernels for 15% -> 15%
where the time goes in v9:
time: 102 us
  waiting for transfers between devices  41.3 us (40%)
  Pallas kernels  40.1 us (39%)
  starting transfers between devices  19.6 us (19%)
    ppermute x26, waiting for transfers between devices, from_partner(): return lax.ppermute(value, axis, pairs)  41.3 us
    pallas_call x1, Pallas kernels, shards(): pl.pallas_call(march_kernel, in_specs=[vmem] * 7 + [smem] + [vmem] * (len...  23 us
    ppermute x26, starting transfers between devices, from_partner(): return lax.ppermute(value, axis, pairs)  19.6 us
    pallas_call x15, Pallas kernels, split_call(): pl.pallas_call(kernel, in_specs=[pl.BlockSpec(memory_space=pltpu.SMEM)] +...  10.2 us
    pallas_call x2, Pallas kernels, cut_call(): pl.pallas_call(cut_kernel, in_specs=[pl.BlockSpec(memory_space=pltpu.SMEM...  3.45 us
  transfers between devices with their start and end apart: 26, of which 13 were waited for; matrix products, arithmetic and copies ran while one was open for 0% of the time, Pallas kernels for 15%

profile of v9, /device:TPU:0, one launch (start us, length us, event | category | flops | bytes accessed | tf_op | source)
XLA Modules:
  0.0 102.0 jit_solution(10356138341779210884)
XLA Ops:
  0.7 1.7 %shard_map.113 = (f32[128,512]{1,0:T(8,128)S(1)}, f32[256,512]{1,0:T(8,128)S(1)}) custom-call(s32[4]{0:T(128)S(1)} %pad_add_fusion.place, f32[256,512]{1,0:T(8,128)} %bitcast.26, f32[256,1024]{1,0:T(8,128)} %bitcast.19), custom_call_target="tpu_custom_call" | custom-call | flops 1 | bytes 1 | tf_op jit(solution)/shard_map/pallas_call | solution.py:75
  2.4 3.1 %collective-permute-start = (f32[128,512]{1,0:T(8,128)S(1)}, f32[128,512]{1,0:T(8,128)S(1)}, u32[]{:S(2)}, u32[]{:S(2)}) collective-permute-start(f32[128,512]{1,0:T(8,128)S(1)} %get-tuple-element.88.mine), channel_id=1, source_target_pairs={{0,4},{4,0},{8,12},{12,8},{1,5},{5,1},{9,13},{13,9},{2,6},{6,2},{1... | collective-permute-start | bytes 786440 | tf_op jit(solution)/shard_map/ppermute | solution.py:14
  5.5 1.5 %collective-permute-start.4 = (f32[256,512]{1,0:T(8,128)S(1)}, f32[256,512]{1,0:T(8,128)S(1)}, u32[]{:S(2)}, u32[]{:S(2)}) collective-permute-start(f32[256,512]{1,0:T(8,128)S(1)} %get-tuple-element.96), channel_id=1, source_target_pairs={{0,2},{2,0},{1,3},{3,1},{4,6},{6,4},{5,7},{7,5},{8,10},{10,8},{9,1... | collective-permute-start | bytes 1572872 | tf_op jit(solution)/shard_map/ppermute | solution.py:14
  7.5 5.2 %collective-permute-done.other = f32[128,512]{1,0:T(8,128)S(1)} collective-permute-done((f32[128,512]{1,0:T(8,128)S(1)}, f32[128,512]{1,0:T(8,128)S(1)}, u32[]{:S(2)}, u32[]{:S(2)}) %collective-permute-start) | collective-permute-done | bytes 262176 | tf_op jit(solution)/shard_map/ppermute | solution.py:14
  12.7 1.8 %shard_map.115 = (f32[512,256]{1,0:T(8,128)S(1)}, f32[512,256]{1,0:T(8,128)S(1)}) custom-call(s32[4]{0:T(128)S(1)} %pad_add_fusion.place, f32[1024,256]{1,0:T(8,128)} %bitcast.17, f32[1024,256]{1,0:T(8,128)} %bitcast.15), custom_call_target="tpu_custom_call" | custom-call | flops 1 | bytes 1 | tf_op jit(solution)/shard_map/pallas_call | solution.py:75
  14.5 2.0 %collective-permute-start.2 = (f32[512,256]{1,0:T(8,128)S(1)}, f32[512,256]{1,0:T(8,128)S(1)}, u32[]{:S(2)}, u32[]{:S(2)}) collective-permute-start(f32[512,256]{1,0:T(8,128)S(1)} %get-tuple-element.107), channel_id=1, source_target_pairs={{0,2},{2,0},{1,3},{3,1},{4,6},{6,4},{5,7},{7,5},{8,10},{10,8},{9,1... | collective-permute-start | bytes 1572872 | tf_op jit(solution)/shard_map/ppermute | solution.py:14
  16.5 1.6 %collective-permute-start.1 = (f32[512,256]{1,0:T(8,128)S(1)}, f32[512,256]{1,0:T(8,128)S(1)}, u32[]{:S(2)}, u32[]{:S(2)}) collective-permute-start(f32[512,256]{1,0:T(8,128)S(1)} %get-tuple-element.106), channel_id=1, source_target_pairs={{0,4},{4,0},{8,12},{12,8},{1,5},{5,1},{9,13},{13,9},{2,6},{6,2},{1... | collective-permute-start | bytes 1572872 | tf_op jit(solution)/shard_map/ppermute | solution.py:14
  18.1 1.5 %shard_map.114 = (f32[360,256]{1,0:T(8,128)S(1)}, f32[9,32]{1,0:T(8,128)S(1)}) custom-call(s32[4]{0:T(128)S(1)} %pad_add_fusion.place, f32[128,512]{1,0:T(8,128)S(1)} %get-tuple-element.88.mine, f32[128,512]{1,0:T(8,128)S(1)} %collective-permute-done.other, f32[512,256]{1,0:T(8,128)S(1)} %bitcast.21, s32[1,32]{1,0:T(1,128)S(1)} %bitcast.25, ...), custom_call_target="tpu_custom_call" | custom-call | flops 1 | bytes 1 | tf_op jit(solution)/shard_map/pallas_call | solution.py:111
  19.6 0.7 collective-permute-done.4.refs_0_
  20.4 1.5 %collective-permute-start.8 = (f32[360,256]{1,0:T(8,128)S(1)}, f32[360,256]{1,0:T(8,128)S(1)}, u32[]{:S(2)}, u32[]{:S(2)}) collective-permute-start(f32[360,256]{1,0:T(8,128)S(1)} %get-tuple-element.110.refs_0_.s0), channel_id=1, source_target_pairs={{0,2},{2,0},{1,3},{3,1},{4,6},{6,4},{5,7},{7,5},{8,10},{10,8},{9,1... | collective-permute-start | bytes 1105928 | tf_op jit(solution)/shard_map/ppermute | solution.py:14
  21.9 2.0 %collective-permute-done.3.refs_0_ = f32[256,512]{1,0:T(8,128)S(1)} collective-permute-done((f32[256,512]{1,0:T(8,128)S(1)}, f32[256,512]{1,0:T(8,128)S(1)}, u32[]{:S(2)}, u32[]{:S(2)}) %collective-permute-start.3) | collective-permute-done | bytes 524320 | tf_op jit(solution)/shard_map/ppermute | solution.py:14
  24.6 7.0 %collective-permute-done.2.refs_0_ = f32[512,256]{1,0:T(8,128)S(1)} collective-permute-done((f32[512,256]{1,0:T(8,128)S(1)}, f32[512,256]{1,0:T(8,128)S(1)}, u32[]{:S(2)}, u32[]{:S(2)}) %collective-permute-start.2) | collective-permute-done | bytes 524320 | tf_op jit(solution)/shard_map/ppermute | solution.py:14
  31.6 2.9 %collective-permute-done.1.refs_0_ = f32[512,256]{1,0:T(8,128)S(1)} collective-permute-done((f32[512,256]{1,0:T(8,128)S(1)}, f32[512,256]{1,0:T(8,128)S(1)}, u32[]{:S(2)}, u32[]{:S(2)}) %collective-permute-start.1) | collective-permute-done | bytes 524320 | tf_op jit(solution)/shard_map/ppermute | solution.py:14
  34.5 1.4 %collective-permute-start.6 = (f32[512,256]{1,0:T(8,128)S(1)}, f32[512,256]{1,0:T(8,128)S(1)}, u32[]{:S(2)}, u32[]{:S(2)}) collective-permute-start(f32[512,256]{1,0:T(8,128)S(1)} %get-tuple-element.106), channel_id=1, source_target_pairs={{0,2},{2,0},{1,3},{3,1},{4,6},{6,4},{5,7},{7,5},{8,10},{10,8},{9,1... | collective-permute-start | bytes 1572872 | tf_op jit(solution)/shard_map/ppermute | solution.py:14
  37.4 2.1 %collective-permute-done.8.refs_0_.s2 = f32[360,256]{1,0:T(8,128)S(1)} collective-permute-done((f32[360,256]{1,0:T(8,128)S(1)}, f32[360,256]{1,0:T(8,128)S(1)}, u32[]{:S(2)}, u32[]{:S(2)}) %collective-permute-start.8) | collective-permute-done | bytes 368672 | tf_op jit(solution)/shard_map/ppermute | solution.py:14
  40.6 0.7 shard_map.120
  41.3 5.1 %collective-permute-done.7.refs_0_ = f32[512,256]{1,0:T(8,128)S(1)} collective-permute-done((f32[512,256]{1,0:T(8,128)S(1)}, f32[512,256]{1,0:T(8,128)S(1)}, u32[]{:S(2)}, u32[]{:S(2)}) %collective-permute-start.7) | collective-permute-done | bytes 524320 | tf_op jit(solution)/shard_map/ppermute | solution.py:14
  46.3 1.5 %collective-permute-start.13 = (f32[256,512]{1,0:T(8,128)S(1)}, f32[256,512]{1,0:T(8,128)S(1)}, u32[]{:S(2)}, u32[]{:S(2)}) collective-permute-start(f32[256,512]{1,0:T(8,128)S(1)} %collective-permute-done.3.refs_0_), channel_id=1, source_target_pairs={{0,2},{2,0},{1,3},{3,1},{4,6},{6,4},{5,7},{7,5},{8,10},{10,8},{9,1... | collective-permute-start | bytes 1572872 | tf_op jit(solution)/shard_map/ppermute | solution.py:14
  47.8 1.5 %collective-permute-done.6.refs_0_ = f32[512,256]{1,0:T(8,128)S(1)} collective-permute-done((f32[512,256]{1,0:T(8,128)S(1)}, f32[512,256]{1,0:T(8,128)S(1)}, u32[]{:S(2)}, u32[]{:S(2)}) %collective-permute-start.6) | collective-permute-done | bytes 524320 | tf_op jit(solution)/shard_map/ppermute | solution.py:14
  49.3 4.6 %collective-permute-done.5.refs_0_.s1 = f32[360,256]{1,0:T(8,128)S(1)} collective-permute-done((f32[360,256]{1,0:T(8,128)S(1)}, f32[360,256]{1,0:T(8,128)S(1)}, u32[]{:S(2)}, u32[]{:S(2)}) %collective-permute-start.5) | collective-permute-done | bytes 368672 | tf_op jit(solution)/shard_map/ppermute | solution.py:14
  53.8 1.3 %collective-permute-start.12 = (f32[360,256]{1,0:T(8,128)S(1)}, f32[360,256]{1,0:T(8,128)S(1)}, u32[]{:S(2)}, u32[]{:S(2)}) collective-permute-start(f32[360,256]{1,0:T(8,128)S(1)} %collective-permute-done.8.refs_0_.s2), channel_id=1, source_target_pairs={{0,4},{4,0},{8,12},{12,8},{1,5},{5,1},{9,13},{13,9},{2,6},{6,2},{1... | collective-permute-start | bytes 1105928 | tf_op jit(solution)/shard_map/ppermute | solution.py:14
  55.9 1.6 %collective-permute-start.18 = (f32[512,256]{1,0:T(8,128)S(1)}, f32[512,256]{1,0:T(8,128)S(1)}, u32[]{:S(2)}, u32[]{:S(2)}) collective-permute-start(f32[512,256]{1,0:T(8,128)S(1)} %collective-permute-done.1.refs_0_), channel_id=1, source_target_pairs={{0,2},{2,0},{1,3},{3,1},{4,6},{6,4},{5,7},{7,5},{8,10},{10,8},{9,1... | collective-permute-start | bytes 1572872 | tf_op jit(solution)/shard_map/ppermute | solution.py:14
  58.2 2.9 %collective-permute-done.13.refs_0_ = f32[256,512]{1,0:T(8,128)S(1)} collective-permute-done((f32[256,512]{1,0:T(8,128)S(1)}, f32[256,512]{1,0:T(8,128)S(1)}, u32[]{:S(2)}, u32[]{:S(2)}) %collective-permute-start.13) | collective-permute-done | bytes 524320 | tf_op jit(solution)/shard_map/ppermute | solution.py:14
  61.0 1.9 %collective-permute-start.21 = (f32[512,256]{1,0:T(8,128)S(1)}, f32[512,256]{1,0:T(8,128)S(1)}, u32[]{:S(2)}, u32[]{:S(2)}) collective-permute-start(f32[512,256]{1,0:T(8,128)S(1)} %collective-permute-done.2.refs_0_), channel_id=1, source_target_pairs={{0,4},{4,0},{8,12},{12,8},{1,5},{5,1},{9,13},{13,9},{2,6},{6,2},{1... | collective-permute-start | bytes 1572872 | tf_op jit(solution)/shard_map/ppermute | solution.py:14
  66.4 5.5 %collective-permute-done.18.refs_0_ = f32[512,256]{1,0:T(8,128)S(1)} collective-permute-done((f32[512,256]{1,0:T(8,128)S(1)}, f32[512,256]{1,0:T(8,128)S(1)}, u32[]{:S(2)}, u32[]{:S(2)}) %collective-permute-start.18) | collective-permute-done | bytes 524320 | tf_op jit(solution)/shard_map/ppermute | solution.py:14
  73.0 0.7 shard_map.127
  73.7 1.2 %shard_map.128 = (f32[32,1024]{1,0:T(8,128)S(1)}, f32[32,1024]{1,0:T(8,128)S(1)}) custom-call(f32[360,256]{1,0:T(8,128)S(1)} %get-tuple-element.110.refs_0_.s0, f32[360,256]{1,0:T(8,128)S(1)} %collective-permute-done.5.refs_0_.s1, f32[360,256]{1,0:T(8,128)S(1)} %collective-permute-done.8.refs_0_.s2, f32[360,256]{1,0:T(8,128)S(1)} %collective-permute-done.12.refs_0_.s3, ...), custom_call_target="tpu_custom_call" | custom-call | flops 1 | bytes 1 | tf_op jit(solution)/shard_map/pallas_call | solution.py:299
  75.0 1.1 %collective-permute-done.21.refs_30_ = f32[512,256]{1,0:T(8,128)S(1)} collective-permute-done((f32[512,256]{1,0:T(8,128)S(1)}, f32[512,256]{1,0:T(8,128)S(1)}, u32[]{:S(2)}, u32[]{:S(2)}) %collective-permute-start.21) | collective-permute-done | bytes 524320 | tf_op jit(solution)/shard_map/ppermute | solution.py:14
  76.1 0.7 shard_map.132
  76.8 0.7 shard_map.129
  78.2 0.8 shard_map.131.two_start
  79.1 23.0 %shard_map.133 = (f32[32,256]{1,0:T(8,128)}, f32[32,256]{1,0:T(8,128)}) custom-call(f32[360,256]{1,0:T(8,128)S(1)} %get-tuple-element.110.refs_0_.s0, f32[360,256]{1,0:T(8,128)S(1)} %collective-permute-done.5.refs_0_.s1, f32[360,256]{1,0:T(8,128)S(1)} %collective-permute-done.8.refs_0_.s2, f32[360,256]{1,0:T(8,128)S(1)} %collective-permute-done.12.refs_0_.s3, ...), custom_call_target="tpu_custom_call" | custom-call | tf_op jit(solution)/shard_map/pallas_call | solution.py:323
  (60 shorter events, 10.4 us)
Async XLA Ops:
  2.4 10.2 %collective-permute-start = (f32[128,512]{1,0:T(8,128)S(1)}, f32[128,512]{1,0:T(8,128)S(1)}, u32[]{:S(2)}, u32[]{:S(2)}) collective-permute-start(f32[128,512]{1,0:T(8,128)S(1)} %get-tuple-element.88.mine), channel_id=1, source_target_pairs={{0,4},{4,0},{8,12},{12,8},{1,5},{5,1},{9,13},{13,9},{2,6},{6,2},{1... | collective-permute-start | bytes 786440 | tf_op jit(solution)/shard_map/ppermute | solution.py:14
  5.5 14.8 %collective-permute-start.4 = (f32[256,512]{1,0:T(8,128)S(1)}, f32[256,512]{1,0:T(8,128)S(1)}, u32[]{:S(2)}, u32[]{:S(2)}) collective-permute-start(f32[256,512]{1,0:T(8,128)S(1)} %get-tuple-element.96), channel_id=1, source_target_pairs={{0,2},{2,0},{1,3},{3,1},{4,6},{6,4},{5,7},{7,5},{8,10},{10,8},{9,1... | collective-permute-start | bytes 1572872 | tf_op jit(solution)/shard_map/ppermute | solution.py:14
  7.0 16.9 %collective-permute-start.3 = (f32[256,512]{1,0:T(8,128)S(1)}, f32[256,512]{1,0:T(8,128)S(1)}, u32[]{:S(2)}, u32[]{:S(2)}) collective-permute-start(f32[256,512]{1,0:T(8,128)S(1)} %get-tuple-element.96), channel_id=1, source_target_pairs={{0,4},{4,0},{8,12},{12,8},{1,5},{5,1},{9,13},{13,9},{2,6},{6,2},{1... | collective-permute-start | bytes 1572872 | tf_op jit(solution)/shard_map/ppermute | solution.py:14
  12.7 5.4 %copy-start.5 = (f32[1,1,32,256]{3,2,1,0:T(8,128)S(1)}, f32[1,1,32,256]{3,2,1,0:T(8,128)}, u32[]{:S(2)}) copy-start(f32[1,1,32,256]{3,2,1,0:T(8,128)} %param.11) | copy-start | bytes 98308
  12.7 5.4 %copy-start.6 = (f32[9,32]{1,0:T(8,128)S(1)}, f32[9,32]{1,0:T(8,128)}, u32[]{:S(2)}) copy-start(f32[9,32]{1,0:T(8,128)} %weight.1) | copy-start | bytes 3460
  12.7 5.4 %copy-start.7 = (f32[1,1,256]{2,1,0:T(1,128)S(1)}, f32[1,1,256]{2,1,0:T(1,128)}, u32[]{:S(2)}) copy-start(f32[1,1,256]{2,1,0:T(1,128)} %param.17) | copy-start | bytes 3076
  14.5 9.4 %copy-start.2 = (f32[1,1,256,1024]{3,2,1,0:T(8,128)S(1)}, f32[1,1,256,1024]{3,2,1,0:T(8,128)}, u32[]{:S(2)}) copy-start(f32[1,1,256,1024]{3,2,1,0:T(8,128)} %param.14) | copy-start | bytes 3145732
  14.5 17.1 %collective-permute-start.2 = (f32[512,256]{1,0:T(8,128)S(1)}, f32[512,256]{1,0:T(8,128)S(1)}, u32[]{:S(2)}, u32[]{:S(2)}) collective-permute-start(f32[512,256]{1,0:T(8,128)S(1)} %get-tuple-element.107), channel_id=1, source_target_pairs={{0,2},{2,0},{1,3},{3,1},{4,6},{6,4},{5,7},{7,5},{8,10},{10,8},{9,1... | collective-permute-start | bytes 1572872 | tf_op jit(solution)/shard_map/ppermute | solution.py:14
  16.5 18.0 %collective-permute-start.1 = (f32[512,256]{1,0:T(8,128)S(1)}, f32[512,256]{1,0:T(8,128)S(1)}, u32[]{:S(2)}, u32[]{:S(2)}) collective-permute-start(f32[512,256]{1,0:T(8,128)S(1)} %get-tuple-element.106), channel_id=1, source_target_pairs={{0,4},{4,0},{8,12},{12,8},{1,5},{5,1},{9,13},{13,9},{2,6},{6,2},{1... | collective-permute-start | bytes 1572872 | tf_op jit(solution)/shard_map/ppermute | solution.py:14
  18.1 17.8 %copy-start = (f32[1,1,1024,256]{3,2,1,0:T(8,128)S(1)}, f32[1,1,1024,256]{3,2,1,0:T(8,128)}, u32[]{:S(2)}) copy-start(f32[1,1,1024,256]{3,2,1,0:T(8,128)} %param.15) | copy-start | bytes 3145732
  20.4 16.3 %copy-start.1 = (f32[1,1,1024,256]{3,2,1,0:T(8,128)S(1)}, f32[1,1,1024,256]{3,2,1,0:T(8,128)}, u32[]{:S(2)}) copy-start(f32[1,1,1024,256]{3,2,1,0:T(8,128)} %param.16) | copy-start | bytes 3145732
  20.4 19.1 %collective-permute-start.8 = (f32[360,256]{1,0:T(8,128)S(1)}, f32[360,256]{1,0:T(8,128)S(1)}, u32[]{:S(2)}, u32[]{:S(2)}) collective-permute-start(f32[360,256]{1,0:T(8,128)S(1)} %get-tuple-element.110.refs_0_.s0), channel_id=1, source_target_pairs={{0,2},{2,0},{1,3},{3,1},{4,6},{6,4},{5,7},{7,5},{8,10},{10,8},{9,1... | collective-permute-start | bytes 1105928 | tf_op jit(solution)/shard_map/ppermute | solution.py:14
  23.9 15.6 %collective-permute-start.9 = (f32[360,256]{1,0:T(8,128)S(1)}, f32[360,256]{1,0:T(8,128)S(1)}, u32[]{:S(2)}, u32[]{:S(2)}) collective-permute-start(f32[360,256]{1,0:T(8,128)S(1)} %get-tuple-element.110.refs_0_.s0), channel_id=1, source_target_pairs={{0,1},{1,0},{2,3},{3,2},{4,5},{5,4},{6,7},{7,6},{8,9},{9,8},{10,11... | collective-permute-start | bytes 1105928 | tf_op jit(solution)/shard_map/ppermute | solution.py:14
  31.6 8.9 %collective-permute-start.10 = (f32[256,512]{1,0:T(8,128)S(1)}, f32[256,512]{1,0:T(8,128)S(1)}, u32[]{:S(2)}, u32[]{:S(2)}) collective-permute-start(f32[256,512]{1,0:T(8,128)S(1)} %collective-permute-done.4.refs_0_), channel_id=1, source_target_pairs={{0,1},{1,0},{2,3},{3,2},{4,5},{5,4},{6,7},{7,6},{8,9},{9,8},{10,11... | collective-permute-start | bytes 1572872 | tf_op jit(solution)/shard_map/ppermute | solution.py:14
  31.6 14.7 %collective-permute-start.7 = (f32[512,256]{1,0:T(8,128)S(1)}, f32[512,256]{1,0:T(8,128)S(1)}, u32[]{:S(2)}, u32[]{:S(2)}) collective-permute-start(f32[512,256]{1,0:T(8,128)S(1)} %get-tuple-element.107), channel_id=1, source_target_pairs={{0,4},{4,0},{8,12},{12,8},{1,5},{5,1},{9,13},{13,9},{2,6},{6,2},{1... | collective-permute-start | bytes 1572872 | tf_op jit(solution)/shard_map/ppermute | solution.py:14
  34.5 14.7 %collective-permute-start.6 = (f32[512,256]{1,0:T(8,128)S(1)}, f32[512,256]{1,0:T(8,128)S(1)}, u32[]{:S(2)}, u32[]{:S(2)}) collective-permute-start(f32[512,256]{1,0:T(8,128)S(1)} %get-tuple-element.106), channel_id=1, source_target_pairs={{0,2},{2,0},{1,3},{3,1},{4,6},{6,4},{5,7},{7,5},{8,10},{10,8},{9,1... | collective-permute-start | bytes 1572872 | tf_op jit(solution)/shard_map/ppermute | solution.py:14
  39.5 14.3 %collective-permute-start.14 = (f32[256,512]{1,0:T(8,128)S(1)}, f32[256,512]{1,0:T(8,128)S(1)}, u32[]{:S(2)}, u32[]{:S(2)}) collective-permute-start(f32[256,512]{1,0:T(8,128)S(1)} %collective-permute-done.3.refs_0_), channel_id=1, source_target_pairs={{0,1},{1,0},{2,3},{3,2},{4,5},{5,4},{6,7},{7,6},{8,9},{9,8},{10,11... | collective-permute-start | bytes 1572872 | tf_op jit(solution)/shard_map/ppermute | solution.py:14
  39.5 14.3 %collective-permute-start.5 = (f32[360,256]{1,0:T(8,128)S(1)}, f32[360,256]{1,0:T(8,128)S(1)}, u32[]{:S(2)}, u32[]{:S(2)}) collective-permute-start(f32[360,256]{1,0:T(8,128)S(1)} %get-tuple-element.110.refs_0_.s0), channel_id=1, source_target_pairs={{0,4},{4,0},{8,12},{12,8},{1,5},{5,1},{9,13},{13,9},{2,6},{6,2},{1... | collective-permute-start | bytes 1105928 | tf_op jit(solution)/shard_map/ppermute | solution.py:14
  46.3 9.6 %collective-permute-start.11 = (f32[512,256]{1,0:T(8,128)S(1)}, f32[512,256]{1,0:T(8,128)S(1)}, u32[]{:S(2)}, u32[]{:S(2)}) collective-permute-start(f32[512,256]{1,0:T(8,128)S(1)} %collective-permute-done.1.refs_0_), channel_id=1, source_target_pairs={{0,1},{1,0},{2,3},{3,2},{4,5},{5,4},{6,7},{7,6},{8,9},{9,8},{10,11... | collective-permute-start | bytes 1572872 | tf_op jit(solution)/shard_map/ppermute | solution.py:14
  46.3 14.7 %collective-permute-start.13 = (f32[256,512]{1,0:T(8,128)S(1)}, f32[256,512]{1,0:T(8,128)S(1)}, u32[]{:S(2)}, u32[]{:S(2)}) collective-permute-start(f32[256,512]{1,0:T(8,128)S(1)} %collective-permute-done.3.refs_0_), channel_id=1, source_target_pairs={{0,2},{2,0},{1,3},{3,1},{4,6},{6,4},{5,7},{7,5},{8,10},{10,8},{9,1... | collective-permute-start | bytes 1572872 | tf_op jit(solution)/shard_map/ppermute | solution.py:14
  49.3 13.7 %collective-permute-start.15 = (f32[512,256]{1,0:T(8,128)S(1)}, f32[512,256]{1,0:T(8,128)S(1)}, u32[]{:S(2)}, u32[]{:S(2)}) collective-permute-start(f32[512,256]{1,0:T(8,128)S(1)} %collective-permute-done.2.refs_0_), channel_id=1, source_target_pairs={{0,1},{1,0},{2,3},{3,2},{4,5},{5,4},{6,7},{7,6},{8,9},{9,8},{10,11... | collective-permute-start | bytes 1572872 | tf_op jit(solution)/shard_map/ppermute | solution.py:14
  53.8 7.2 %collective-permute-start.16 = (f32[360,256]{1,0:T(8,128)S(1)}, f32[360,256]{1,0:T(8,128)S(1)}, u32[]{:S(2)}, u32[]{:S(2)}) collective-permute-start(f32[360,256]{1,0:T(8,128)S(1)} %collective-permute-done.8.refs_0_.s2), channel_id=1, source_target_pairs={{0,1},{1,0},{2,3},{3,2},{4,5},{5,4},{6,7},{7,6},{8,9},{9,8},{10,11... | collective-permute-start | bytes 1105928 | tf_op jit(solution)/shard_map/ppermute | solution.py:14
  53.8 11.4 %collective-permute-start.12 = (f32[360,256]{1,0:T(8,128)S(1)}, f32[360,256]{1,0:T(8,128)S(1)}, u32[]{:S(2)}, u32[]{:S(2)}) collective-permute-start(f32[360,256]{1,0:T(8,128)S(1)} %collective-permute-done.8.refs_0_.s2), channel_id=1, source_target_pairs={{0,4},{4,0},{8,12},{12,8},{1,5},{5,1},{9,13},{13,9},{2,6},{6,2},{1... | collective-permute-start | bytes 1105928 | tf_op jit(solution)/shard_map/ppermute | solution.py:14
  55.9 16.0 %collective-permute-start.18 = (f32[512,256]{1,0:T(8,128)S(1)}, f32[512,256]{1,0:T(8,128)S(1)}, u32[]{:S(2)}, u32[]{:S(2)}) collective-permute-start(f32[512,256]{1,0:T(8,128)S(1)} %collective-permute-done.1.refs_0_), channel_id=1, source_target_pairs={{0,2},{2,0},{1,3},{3,1},{4,6},{6,4},{5,7},{7,5},{8,10},{10,8},{9,1... | collective-permute-start | bytes 1572872 | tf_op jit(solution)/shard_map/ppermute | solution.py:14
  61.0 12.0 %collective-permute-start.20 = (f32[256,512]{1,0:T(8,128)S(1)}, f32[256,512]{1,0:T(8,128)S(1)}, u32[]{:S(2)}, u32[]{:S(2)}) collective-permute-start(f32[256,512]{1,0:T(8,128)S(1)} %collective-permute-done.13.refs_0_), channel_id=1, source_target_pairs={{0,1},{1,0},{2,3},{3,2},{4,5},{5,4},{6,7},{7,6},{8,9},{9,8},{10,11... | collective-permute-start | bytes 1572872 | tf_op jit(solution)/shard_map/ppermute | solution.py:14
  61.0 15.0 %collective-permute-start.21 = (f32[512,256]{1,0:T(8,128)S(1)}, f32[512,256]{1,0:T(8,128)S(1)}, u32[]{:S(2)}, u32[]{:S(2)}) collective-permute-start(f32[512,256]{1,0:T(8,128)S(1)} %collective-permute-done.2.refs_0_), channel_id=1, source_target_pairs={{0,4},{4,0},{8,12},{12,8},{1,5},{5,1},{9,13},{13,9},{2,6},{6,2},{1... | collective-permute-start | bytes 1572872 | tf_op jit(solution)/shard_map/ppermute | solution.py:14
  63.0 2.3 %collective-permute-start.17 = (f32[360,256]{1,0:T(8,128)S(1)}, f32[360,256]{1,0:T(8,128)S(1)}, u32[]{:S(2)}, u32[]{:S(2)}) collective-permute-start(f32[360,256]{1,0:T(8,128)S(1)} %collective-permute-done.5.refs_0_.s1), channel_id=1, source_target_pairs={{0,1},{1,0},{2,3},{3,2},{4,5},{5,4},{6,7},{7,6},{8,9},{9,8},{10,11... | collective-permute-start | bytes 1105928 | tf_op jit(solution)/shard_map/ppermute | solution.py:14
  65.2 6.7 %collective-permute-start.19 = (f32[360,256]{1,0:T(8,128)S(1)}, f32[360,256]{1,0:T(8,128)S(1)}, u32[]{:S(2)}, u32[]{:S(2)}) collective-permute-start(f32[360,256]{1,0:T(8,128)S(1)} %collective-permute-done.12.refs_0_.s3), channel_id=1, source_target_pairs={{0,1},{1,0},{2,3},{3,2},{4,5},{5,4},{6,7},{7,6},{8,9},{9,8},{10,11... | collective-permute-start | bytes 1105928 | tf_op jit(solution)/shard_map/ppermute | solution.py:14
  65.2 11.6 %collective-permute-start.22 = (f32[512,256]{1,0:T(8,128)S(1)}, f32[512,256]{1,0:T(8,128)S(1)}, u32[]{:S(2)}, u32[]{:S(2)}) collective-permute-start(f32[512,256]{1,0:T(8,128)S(1)} %collective-permute-done.6.refs_0_), channel_id=1, source_target_pairs={{0,1},{1,0},{2,3},{3,2},{4,5},{5,4},{6,7},{7,6},{8,9},{9,8},{10,11... | collective-permute-start | bytes 1572872 | tf_op jit(solution)/shard_map/ppermute | solution.py:14
  71.9 4.2 %collective-permute-start.24 = (f32[512,256]{1,0:T(8,128)S(1)}, f32[512,256]{1,0:T(8,128)S(1)}, u32[]{:S(2)}, u32[]{:S(2)}) collective-permute-start(f32[512,256]{1,0:T(8,128)S(1)} %collective-permute-done.7.refs_0_), channel_id=1, source_target_pairs={{0,1},{1,0},{2,3},{3,2},{4,5},{5,4},{6,7},{7,6},{8,9},{9,8},{10,11... | collective-permute-start | bytes 1572872 | tf_op jit(solution)/shard_map/ppermute | solution.py:14
  71.9 5.6 %collective-permute-start.23 = (f32[512,256]{1,0:T(8,128)S(1)}, f32[512,256]{1,0:T(8,128)S(1)}, u32[]{:S(2)}, u32[]{:S(2)}) collective-permute-start(f32[512,256]{1,0:T(8,128)S(1)} %collective-permute-done.18.refs_0_), channel_id=1, source_target_pairs={{0,1},{1,0},{2,3},{3,2},{4,5},{5,4},{6,7},{7,6},{8,9},{9,8},{10,11... | collective-permute-start | bytes 1572872 | tf_op jit(solution)/shard_map/ppermute | solution.py:14
  76.1 3.0 %collective-permute-start.25 = (f32[512,256]{1,0:T(8,128)S(1)}, f32[512,256]{1,0:T(8,128)S(1)}, u32[]{:S(2)}, u32[]{:S(2)}) collective-permute-start(f32[512,256]{1,0:T(8,128)S(1)} %collective-permute-done.21.refs_30_), channel_id=1, source_target_pairs={{0,1},{1,0},{2,3},{3,2},{4,5},{5,4},{6,7},{7,6},{8,9},{9,8},{10,11... | collective-permute-start | bytes 1572872 | tf_op jit(solution)/shard_map/ppermute | solution.py:14
  (3 other events, 16.3 us)

commit v10 on v9

--- a/solution.py
+++ b/solution.py
@@ -27,10 +27,12 @@
     return high, (value - high.astype(F32)).astype(BF16)
 
 
-def store_split(high_ref, low_ref, where, value):
-    high, low = halves_of(value)
-    high_ref[where] = high
-    low_ref[where] = low
+def store_split(high_ref, low_ref, start, piece, row, column, size):
+    step = 32
+    for offset in range(0, size, step):
+        value = piece[row + offset:row + offset + step, column:column + high_ref.shape[1]]
+        where = pl.ds(pl.multiple_of(start + offset, step), step)
+        high_ref[where, :], low_ref[where, :] = halves_of(value)
 
 
 PLAN = (
@@ -124,8 +126,7 @@
     for part, piece in enumerate(pieces):
         for block in range(blocks):
             number = block if len(pieces) == 1 else 2 * (place[1] ^ part) + block
-            rows = pl.ds(pl.multiple_of((number ^ place[0]) * width, width), width)
-            store_split(high_ref, low_ref, (rows, slice(None)), piece[block * width:(block + 1) * width, :])
+            store_split(high_ref, low_ref, (number ^ place[0]) * width, piece, block * width, 0, width)
 
 
 def tall_kernel(place, *refs):
@@ -139,8 +140,7 @@
     for part, piece in enumerate(pieces):
         for block in range(blocks):
             number = block if len(pieces) == 1 else 2 * (place[1] ^ part) + block
-            rows = pl.ds(pl.multiple_of((number ^ place[0]) * width, width), width)
-            store_split(high_ref, low_ref, (rows, slice(None)), piece[:, block * width:(block + 1) * width])
+            store_split(high_ref, low_ref, (number ^ place[0]) * width, piece, 0, block * width, width)
 
 
 def edge_kernel(place, *refs):
@@ -149,8 +149,7 @@
     for part, piece in enumerate(pieces):
         for bit in range(2):
             start = (bit ^ (place[0] % 2)) * 2 * rows + (place[1] ^ part) * rows
-            where = (pl.ds(pl.multiple_of(start, rows), rows), slice(None))
-            store_split(high_ref, low_ref, where, piece[bit * rows:(bit + 1) * rows, :])
+            store_split(high_ref, low_ref, start, piece, bit * rows, 0, rows)
 
 
 def split_call(kernel, place, rows, *pieces):

time: 102 us -> 102 us (level)
  no operation moved by 1% of the time
where the time goes in v10:
time: 102 us
  waiting for transfers between devices  41.7 us (41%)
  Pallas kernels  39.6 us (39%)
  starting transfers between devices  19.5 us (19%)
    ppermute x26, waiting for transfers between devices, from_partner(): return lax.ppermute(value, axis, pairs)  41.7 us
    pallas_call x1, Pallas kernels, shards(): pl.pallas_call(march_kernel, in_specs=[vmem] * 7 + [smem] + [vmem] * (len...  22.9 us
    ppermute x26, starting transfers between devices, from_partner(): return lax.ppermute(value, axis, pairs)  19.5 us
    pallas_call x15, Pallas kernels, split_call(): pl.pallas_call(kernel, in_specs=[pl.BlockSpec(memory_space=pltpu.SMEM)] +...  9.7 us
    pallas_call x2, Pallas kernels, cut_call(): pl.pallas_call(cut_kernel, in_specs=[pl.BlockSpec(memory_space=pltpu.SMEM...  3.45 us
  transfers between devices with their start and end apart: 26, of which 13 were waited for; matrix products, arithmetic and copies ran while one was open for 0% of the time, Pallas kernels for 15%

profile of v10, /device:TPU:0, one launch (start us, length us, event | category | flops | bytes accessed | tf_op | source)
XLA Modules:
  0.0 101.9 jit_solution(11124281116370043121)
XLA Ops:
  0.7 1.7 %shard_map.113 = (f32[128,512]{1,0:T(8,128)S(1)}, f32[256,512]{1,0:T(8,128)S(1)}) custom-call(s32[4]{0:T(128)S(1)} %pad_add_fusion.place, f32[256,512]{1,0:T(8,128)} %bitcast.26, f32[256,1024]{1,0:T(8,128)} %bitcast.19), custom_call_target="tpu_custom_call" | custom-call | flops 1 | bytes 1 | tf_op jit(solution)/shard_map/pallas_call | solution.py:77
  2.4 3.1 %collective-permute-start = (f32[128,512]{1,0:T(8,128)S(1)}, f32[128,512]{1,0:T(8,128)S(1)}, u32[]{:S(2)}, u32[]{:S(2)}) collective-permute-start(f32[128,512]{1,0:T(8,128)S(1)} %get-tuple-element.88.mine), channel_id=1, source_target_pairs={{0,4},{4,0},{8,12},{12,8},{1,5},{5,1},{9,13},{13,9},{2,6},{6,2},{1... | collective-permute-start | bytes 786440 | tf_op jit(solution)/shard_map/ppermute | solution.py:14
  5.5 1.5 %collective-permute-start.4 = (f32[256,512]{1,0:T(8,128)S(1)}, f32[256,512]{1,0:T(8,128)S(1)}, u32[]{:S(2)}, u32[]{:S(2)}) collective-permute-start(f32[256,512]{1,0:T(8,128)S(1)} %get-tuple-element.96), channel_id=1, source_target_pairs={{0,2},{2,0},{1,3},{3,1},{4,6},{6,4},{5,7},{7,5},{8,10},{10,8},{9,1... | collective-permute-start | bytes 1572872 | tf_op jit(solution)/shard_map/ppermute | solution.py:14
  7.5 5.2 %collective-permute-done.other = f32[128,512]{1,0:T(8,128)S(1)} collective-permute-done((f32[128,512]{1,0:T(8,128)S(1)}, f32[128,512]{1,0:T(8,128)S(1)}, u32[]{:S(2)}, u32[]{:S(2)}) %collective-permute-start) | collective-permute-done | bytes 262176 | tf_op jit(solution)/shard_map/ppermute | solution.py:14
  12.7 1.8 %shard_map.115 = (f32[512,256]{1,0:T(8,128)S(1)}, f32[512,256]{1,0:T(8,128)S(1)}) custom-call(s32[4]{0:T(128)S(1)} %pad_add_fusion.place, f32[1024,256]{1,0:T(8,128)} %bitcast.17, f32[1024,256]{1,0:T(8,128)} %bitcast.15), custom_call_target="tpu_custom_call" | custom-call | flops 1 | bytes 1 | tf_op jit(solution)/shard_map/pallas_call | solution.py:77
  14.5 2.0 %collective-permute-start.2 = (f32[512,256]{1,0:T(8,128)S(1)}, f32[512,256]{1,0:T(8,128)S(1)}, u32[]{:S(2)}, u32[]{:S(2)}) collective-permute-start(f32[512,256]{1,0:T(8,128)S(1)} %get-tuple-element.107), channel_id=1, source_target_pairs={{0,2},{2,0},{1,3},{3,1},{4,6},{6,4},{5,7},{7,5},{8,10},{10,8},{9,1... | collective-permute-start | bytes 1572872 | tf_op jit(solution)/shard_map/ppermute | solution.py:14
  16.5 1.6 %collective-permute-start.1 = (f32[512,256]{1,0:T(8,128)S(1)}, f32[512,256]{1,0:T(8,128)S(1)}, u32[]{:S(2)}, u32[]{:S(2)}) collective-permute-start(f32[512,256]{1,0:T(8,128)S(1)} %get-tuple-element.106), channel_id=1, source_target_pairs={{0,4},{4,0},{8,12},{12,8},{1,5},{5,1},{9,13},{13,9},{2,6},{6,2},{1... | collective-permute-start | bytes 1572872 | tf_op jit(solution)/shard_map/ppermute | solution.py:14
  18.1 1.5 %shard_map.114 = (f32[360,256]{1,0:T(8,128)S(1)}, f32[9,32]{1,0:T(8,128)S(1)}) custom-call(s32[4]{0:T(128)S(1)} %pad_add_fusion.place, f32[128,512]{1,0:T(8,128)S(1)} %get-tuple-element.88.mine, f32[128,512]{1,0:T(8,128)S(1)} %collective-permute-done.other, f32[512,256]{1,0:T(8,128)S(1)} %bitcast.21, s32[1,32]{1,0:T(1,128)S(1)} %bitcast.25, ...), custom_call_target="tpu_custom_call" | custom-call | flops 1 | bytes 1 | tf_op jit(solution)/shard_map/pallas_call | solution.py:113
  19.6 0.7 collective-permute-done.4.refs_0_
  20.4 1.5 %collective-permute-start.8 = (f32[360,256]{1,0:T(8,128)S(1)}, f32[360,256]{1,0:T(8,128)S(1)}, u32[]{:S(2)}, u32[]{:S(2)}) collective-permute-start(f32[360,256]{1,0:T(8,128)S(1)} %get-tuple-element.110.refs_0_.s0), channel_id=1, source_target_pairs={{0,2},{2,0},{1,3},{3,1},{4,6},{6,4},{5,7},{7,5},{8,10},{10,8},{9,1... | collective-permute-start | bytes 1105928 | tf_op jit(solution)/shard_map/ppermute | solution.py:14
  21.9 2.0 %collective-permute-done.3.refs_0_ = f32[256,512]{1,0:T(8,128)S(1)} collective-permute-done((f32[256,512]{1,0:T(8,128)S(1)}, f32[256,512]{1,0:T(8,128)S(1)}, u32[]{:S(2)}, u32[]{:S(2)}) %collective-permute-start.3) | collective-permute-done | bytes 524320 | tf_op jit(solution)/shard_map/ppermute | solution.py:14
  24.6 7.0 %collective-permute-done.2.refs_0_ = f32[512,256]{1,0:T(8,128)S(1)} collective-permute-done((f32[512,256]{1,0:T(8,128)S(1)}, f32[512,256]{1,0:T(8,128)S(1)}, u32[]{:S(2)}, u32[]{:S(2)}) %collective-permute-start.2) | collective-permute-done | bytes 524320 | tf_op jit(solution)/shard_map/ppermute | solution.py:14
  31.6 2.9 %collective-permute-done.1.refs_0_ = f32[512,256]{1,0:T(8,128)S(1)} collective-permute-done((f32[512,256]{1,0:T(8,128)S(1)}, f32[512,256]{1,0:T(8,128)S(1)}, u32[]{:S(2)}, u32[]{:S(2)}) %collective-permute-start.1) | collective-permute-done | bytes 524320 | tf_op jit(solution)/shard_map/ppermute | solution.py:14
  34.5 1.4 %collective-permute-start.6 = (f32[512,256]{1,0:T(8,128)S(1)}, f32[512,256]{1,0:T(8,128)S(1)}, u32[]{:S(2)}, u32[]{:S(2)}) collective-permute-start(f32[512,256]{1,0:T(8,128)S(1)} %get-tuple-element.106), channel_id=1, source_target_pairs={{0,2},{2,0},{1,3},{3,1},{4,6},{6,4},{5,7},{7,5},{8,10},{10,8},{9,1... | collective-permute-start | bytes 1572872 | tf_op jit(solution)/shard_map/ppermute | solution.py:14
  37.3 2.2 %collective-permute-done.8.refs_0_.s2 = f32[360,256]{1,0:T(8,128)S(1)} collective-permute-done((f32[360,256]{1,0:T(8,128)S(1)}, f32[360,256]{1,0:T(8,128)S(1)}, u32[]{:S(2)}, u32[]{:S(2)}) %collective-permute-start.8) | collective-permute-done | bytes 368672 | tf_op jit(solution)/shard_map/ppermute | solution.py:14
  40.5 0.7 shard_map.120
  41.1 5.2 %collective-permute-done.7.refs_0_ = f32[512,256]{1,0:T(8,128)S(1)} collective-permute-done((f32[512,256]{1,0:T(8,128)S(1)}, f32[512,256]{1,0:T(8,128)S(1)}, u32[]{:S(2)}, u32[]{:S(2)}) %collective-permute-start.7) | collective-permute-done | bytes 524320 | tf_op jit(solution)/shard_map/ppermute | solution.py:14
  46.3 1.5 %collective-permute-start.13 = (f32[256,512]{1,0:T(8,128)S(1)}, f32[256,512]{1,0:T(8,128)S(1)}, u32[]{:S(2)}, u32[]{:S(2)}) collective-permute-start(f32[256,512]{1,0:T(8,128)S(1)} %collective-permute-done.3.refs_0_), channel_id=1, source_target_pairs={{0,2},{2,0},{1,3},{3,1},{4,6},{6,4},{5,7},{7,5},{8,10},{10,8},{9,1... | collective-permute-start | bytes 1572872 | tf_op jit(solution)/shard_map/ppermute | solution.py:14
  47.8 1.5 %collective-permute-done.6.refs_0_ = f32[512,256]{1,0:T(8,128)S(1)} collective-permute-done((f32[512,256]{1,0:T(8,128)S(1)}, f32[512,256]{1,0:T(8,128)S(1)}, u32[]{:S(2)}, u32[]{:S(2)}) %collective-permute-start.6) | collective-permute-done | bytes 524320 | tf_op jit(solution)/shard_map/ppermute | solution.py:14
  49.3 4.6 %collective-permute-done.5.refs_0_.s1 = f32[360,256]{1,0:T(8,128)S(1)} collective-permute-done((f32[360,256]{1,0:T(8,128)S(1)}, f32[360,256]{1,0:T(8,128)S(1)}, u32[]{:S(2)}, u32[]{:S(2)}) %collective-permute-start.5) | collective-permute-done | bytes 368672 | tf_op jit(solution)/shard_map/ppermute | solution.py:14
  53.8 1.3 %collective-permute-start.12 = (f32[360,256]{1,0:T(8,128)S(1)}, f32[360,256]{1,0:T(8,128)S(1)}, u32[]{:S(2)}, u32[]{:S(2)}) collective-permute-start(f32[360,256]{1,0:T(8,128)S(1)} %collective-permute-done.8.refs_0_.s2), channel_id=1, source_target_pairs={{0,4},{4,0},{8,12},{12,8},{1,5},{5,1},{9,13},{13,9},{2,6},{6,2},{1... | collective-permute-start | bytes 1105928 | tf_op jit(solution)/shard_map/ppermute | solution.py:14
  55.9 1.6 %collective-permute-start.18 = (f32[512,256]{1,0:T(8,128)S(1)}, f32[512,256]{1,0:T(8,128)S(1)}, u32[]{:S(2)}, u32[]{:S(2)}) collective-permute-start(f32[512,256]{1,0:T(8,128)S(1)} %collective-permute-done.1.refs_0_), channel_id=1, source_target_pairs={{0,2},{2,0},{1,3},{3,1},{4,6},{6,4},{5,7},{7,5},{8,10},{10,8},{9,1... | collective-permute-start | bytes 1572872 | tf_op jit(solution)/shard_map/ppermute | solution.py:14
  58.1 3.0 %collective-permute-done.13.refs_0_ = f32[256,512]{1,0:T(8,128)S(1)} collective-permute-done((f32[256,512]{1,0:T(8,128)S(1)}, f32[256,512]{1,0:T(8,128)S(1)}, u32[]{:S(2)}, u32[]{:S(2)}) %collective-permute-start.13) | collective-permute-done | bytes 524320 | tf_op jit(solution)/shard_map/ppermute | solution.py:14
  61.0 1.9 %collective-permute-start.21 = (f32[512,256]{1,0:T(8,128)S(1)}, f32[512,256]{1,0:T(8,128)S(1)}, u32[]{:S(2)}, u32[]{:S(2)}) collective-permute-start(f32[512,256]{1,0:T(8,128)S(1)} %collective-permute-done.2.refs_0_), channel_id=1, source_target_pairs={{0,4},{4,0},{8,12},{12,8},{1,5},{5,1},{9,13},{13,9},{2,6},{6,2},{1... | collective-permute-start | bytes 1572872 | tf_op jit(solution)/shard_map/ppermute | solution.py:14
  64.5 0.7 collective-permute-done.12.refs_0_.s3
  66.4 5.5 %collective-permute-done.18.refs_0_ = f32[512,256]{1,0:T(8,128)S(1)} collective-permute-done((f32[512,256]{1,0:T(8,128)S(1)}, f32[512,256]{1,0:T(8,128)S(1)}, u32[]{:S(2)}, u32[]{:S(2)}) %collective-permute-start.18) | collective-permute-done | bytes 524320 | tf_op jit(solution)/shard_map/ppermute | solution.py:14
  73.0 0.7 shard_map.127
  73.7 1.2 %shard_map.128 = (f32[32,1024]{1,0:T(8,128)S(1)}, f32[32,1024]{1,0:T(8,128)S(1)}) custom-call(f32[360,256]{1,0:T(8,128)S(1)} %get-tuple-element.110.refs_0_.s0, f32[360,256]{1,0:T(8,128)S(1)} %collective-permute-done.5.refs_0_.s1, f32[360,256]{1,0:T(8,128)S(1)} %collective-permute-done.8.refs_0_.s2, f32[360,256]{1,0:T(8,128)S(1)} %collective-permute-done.12.refs_0_.s3, ...), custom_call_target="tpu_custom_call" | custom-call | flops 1 | bytes 1 | tf_op jit(solution)/shard_map/pallas_call | solution.py:298
  74.9 1.2 %collective-permute-done.21.refs_30_ = f32[512,256]{1,0:T(8,128)S(1)} collective-permute-done((f32[512,256]{1,0:T(8,128)S(1)}, f32[512,256]{1,0:T(8,128)S(1)}, u32[]{:S(2)}, u32[]{:S(2)}) %collective-permute-start.21) | collective-permute-done | bytes 524320 | tf_op jit(solution)/shard_map/ppermute | solution.py:14
  76.8 0.7 shard_map.129
  78.1 0.8 shard_map.131.two_start
  78.9 22.9 %shard_map.133 = (f32[32,256]{1,0:T(8,128)}, f32[32,256]{1,0:T(8,128)}) custom-call(f32[360,256]{1,0:T(8,128)S(1)} %get-tuple-element.110.refs_0_.s0, f32[360,256]{1,0:T(8,128)S(1)} %collective-permute-done.5.refs_0_.s1, f32[360,256]{1,0:T(8,128)S(1)} %collective-permute-done.8.refs_0_.s2, f32[360,256]{1,0:T(8,128)S(1)} %collective-permute-done.12.refs_0_.s3, ...), custom_call_target="tpu_custom_call" | custom-call | tf_op jit(solution)/shard_map/pallas_call | solution.py:322
  (60 shorter events, 10.0 us)
Async XLA Ops:
  2.4 10.2 %collective-permute-start = (f32[128,512]{1,0:T(8,128)S(1)}, f32[128,512]{1,0:T(8,128)S(1)}, u32[]{:S(2)}, u32[]{:S(2)}) collective-permute-start(f32[128,512]{1,0:T(8,128)S(1)} %get-tuple-element.88.mine), channel_id=1, source_target_pairs={{0,4},{4,0},{8,12},{12,8},{1,5},{5,1},{9,13},{13,9},{2,6},{6,2},{1... | collective-permute-start | bytes 786440 | tf_op jit(solution)/shard_map/ppermute | solution.py:14
  5.5 14.8 %collective-permute-start.4 = (f32[256,512]{1,0:T(8,128)S(1)}, f32[256,512]{1,0:T(8,128)S(1)}, u32[]{:S(2)}, u32[]{:S(2)}) collective-permute-start(f32[256,512]{1,0:T(8,128)S(1)} %get-tuple-element.96), channel_id=1, source_target_pairs={{0,2},{2,0},{1,3},{3,1},{4,6},{6,4},{5,7},{7,5},{8,10},{10,8},{9,1... | collective-permute-start | bytes 1572872 | tf_op jit(solution)/shard_map/ppermute | solution.py:14
  7.0 16.9 %collective-permute-start.3 = (f32[256,512]{1,0:T(8,128)S(1)}, f32[256,512]{1,0:T(8,128)S(1)}, u32[]{:S(2)}, u32[]{:S(2)}) collective-permute-start(f32[256,512]{1,0:T(8,128)S(1)} %get-tuple-element.96), channel_id=1, source_target_pairs={{0,4},{4,0},{8,12},{12,8},{1,5},{5,1},{9,13},{13,9},{2,6},{6,2},{1... | collective-permute-start | bytes 1572872 | tf_op jit(solution)/shard_map/ppermute | solution.py:14
  12.7 5.4 %copy-start.5 = (f32[1,1,32,256]{3,2,1,0:T(8,128)S(1)}, f32[1,1,32,256]{3,2,1,0:T(8,128)}, u32[]{:S(2)}) copy-start(f32[1,1,32,256]{3,2,1,0:T(8,128)} %param.11) | copy-start | bytes 98308
  12.7 5.4 %copy-start.6 = (f32[9,32]{1,0:T(8,128)S(1)}, f32[9,32]{1,0:T(8,128)}, u32[]{:S(2)}) copy-start(f32[9,32]{1,0:T(8,128)} %weight.1) | copy-start | bytes 3460
  12.7 5.4 %copy-start.7 = (f32[1,1,256]{2,1,0:T(1,128)S(1)}, f32[1,1,256]{2,1,0:T(1,128)}, u32[]{:S(2)}) copy-start(f32[1,1,256]{2,1,0:T(1,128)} %param.17) | copy-start | bytes 3076
  14.5 9.4 %copy-start.2 = (f32[1,1,256,1024]{3,2,1,0:T(8,128)S(1)}, f32[1,1,256,1024]{3,2,1,0:T(8,128)}, u32[]{:S(2)}) copy-start(f32[1,1,256,1024]{3,2,1,0:T(8,128)} %param.14) | copy-start | bytes 3145732
  14.5 17.1 %collective-permute-start.2 = (f32[512,256]{1,0:T(8,128)S(1)}, f32[512,256]{1,0:T(8,128)S(1)}, u32[]{:S(2)}, u32[]{:S(2)}) collective-permute-start(f32[512,256]{1,0:T(8,128)S(1)} %get-tuple-element.107), channel_id=1, source_target_pairs={{0,2},{2,0},{1,3},{3,1},{4,6},{6,4},{5,7},{7,5},{8,10},{10,8},{9,1... | collective-permute-start | bytes 1572872 | tf_op jit(solution)/shard_map/ppermute | solution.py:14
  16.5 18.0 %collective-permute-start.1 = (f32[512,256]{1,0:T(8,128)S(1)}, f32[512,256]{1,0:T(8,128)S(1)}, u32[]{:S(2)}, u32[]{:S(2)}) collective-permute-start(f32[512,256]{1,0:T(8,128)S(1)} %get-tuple-element.106), channel_id=1, source_target_pairs={{0,4},{4,0},{8,12},{12,8},{1,5},{5,1},{9,13},{13,9},{2,6},{6,2},{1... | collective-permute-start | bytes 1572872 | tf_op jit(solution)/shard_map/ppermute | solution.py:14
  18.1 17.8 %copy-start = (f32[1,1,1024,256]{3,2,1,0:T(8,128)S(1)}, f32[1,1,1024,256]{3,2,1,0:T(8,128)}, u32[]{:S(2)}) copy-start(f32[1,1,1024,256]{3,2,1,0:T(8,128)} %param.15) | copy-start | bytes 3145732
  20.4 16.3 %copy-start.1 = (f32[1,1,1024,256]{3,2,1,0:T(8,128)S(1)}, f32[1,1,1024,256]{3,2,1,0:T(8,128)}, u32[]{:S(2)}) copy-start(f32[1,1,1024,256]{3,2,1,0:T(8,128)} %param.16) | copy-start | bytes 3145732
  20.4 19.1 %collective-permute-start.8 = (f32[360,256]{1,0:T(8,128)S(1)}, f32[360,256]{1,0:T(8,128)S(1)}, u32[]{:S(2)}, u32[]{:S(2)}) collective-permute-start(f32[360,256]{1,0:T(8,128)S(1)} %get-tuple-element.110.refs_0_.s0), channel_id=1, source_target_pairs={{0,2},{2,0},{1,3},{3,1},{4,6},{6,4},{5,7},{7,5},{8,10},{10,8},{9,1... | collective-permute-start | bytes 1105928 | tf_op jit(solution)/shard_map/ppermute | solution.py:14
  23.9 15.6 %collective-permute-start.9 = (f32[360,256]{1,0:T(8,128)S(1)}, f32[360,256]{1,0:T(8,128)S(1)}, u32[]{:S(2)}, u32[]{:S(2)}) collective-permute-start(f32[360,256]{1,0:T(8,128)S(1)} %get-tuple-element.110.refs_0_.s0), channel_id=1, source_target_pairs={{0,1},{1,0},{2,3},{3,2},{4,5},{5,4},{6,7},{7,6},{8,9},{9,8},{10,11... | collective-permute-start | bytes 1105928 | tf_op jit(solution)/shard_map/ppermute | solution.py:14
  31.6 8.9 %collective-permute-start.10 = (f32[256,512]{1,0:T(8,128)S(1)}, f32[256,512]{1,0:T(8,128)S(1)}, u32[]{:S(2)}, u32[]{:S(2)}) collective-permute-start(f32[256,512]{1,0:T(8,128)S(1)} %collective-permute-done.4.refs_0_), channel_id=1, source_target_pairs={{0,1},{1,0},{2,3},{3,2},{4,5},{5,4},{6,7},{7,6},{8,9},{9,8},{10,11... | collective-permute-start | bytes 1572872 | tf_op jit(solution)/shard_map/ppermute | solution.py:14
  31.6 14.7 %collective-permute-start.7 = (f32[512,256]{1,0:T(8,128)S(1)}, f32[512,256]{1,0:T(8,128)S(1)}, u32[]{:S(2)}, u32[]{:S(2)}) collective-permute-start(f32[512,256]{1,0:T(8,128)S(1)} %get-tuple-element.107), channel_id=1, source_target_pairs={{0,4},{4,0},{8,12},{12,8},{1,5},{5,1},{9,13},{13,9},{2,6},{6,2},{1... | collective-permute-start | bytes 1572872 | tf_op jit(solution)/shard_map/ppermute | solution.py:14
  34.5 14.7 %collective-permute-start.6 = (f32[512,256]{1,0:T(8,128)S(1)}, f32[512,256]{1,0:T(8,128)S(1)}, u32[]{:S(2)}, u32[]{:S(2)}) collective-permute-start(f32[512,256]{1,0:T(8,128)S(1)} %get-tuple-element.106), channel_id=1, source_target_pairs={{0,2},{2,0},{1,3},{3,1},{4,6},{6,4},{5,7},{7,5},{8,10},{10,8},{9,1... | collective-permute-start | bytes 1572872 | tf_op jit(solution)/shard_map/ppermute | solution.py:14
  39.5 14.3 %collective-permute-start.14 = (f32[256,512]{1,0:T(8,128)S(1)}, f32[256,512]{1,0:T(8,128)S(1)}, u32[]{:S(2)}, u32[]{:S(2)}) collective-permute-start(f32[256,512]{1,0:T(8,128)S(1)} %collective-permute-done.3.refs_0_), channel_id=1, source_target_pairs={{0,1},{1,0},{2,3},{3,2},{4,5},{5,4},{6,7},{7,6},{8,9},{9,8},{10,11... | collective-permute-start | bytes 1572872 | tf_op jit(solution)/shard_map/ppermute | solution.py:14
  39.5 14.3 %collective-permute-start.5 = (f32[360,256]{1,0:T(8,128)S(1)}, f32[360,256]{1,0:T(8,128)S(1)}, u32[]{:S(2)}, u32[]{:S(2)}) collective-permute-start(f32[360,256]{1,0:T(8,128)S(1)} %get-tuple-element.110.refs_0_.s0), channel_id=1, source_target_pairs={{0,4},{4,0},{8,12},{12,8},{1,5},{5,1},{9,13},{13,9},{2,6},{6,2},{1... | collective-permute-start | bytes 1105928 | tf_op jit(solution)/shard_map/ppermute | solution.py:14
  46.3 9.5 %collective-permute-start.11 = (f32[512,256]{1,0:T(8,128)S(1)}, f32[512,256]{1,0:T(8,128)S(1)}, u32[]{:S(2)}, u32[]{:S(2)}) collective-permute-start(f32[512,256]{1,0:T(8,128)S(1)} %collective-permute-done.1.refs_0_), channel_id=1, source_target_pairs={{0,1},{1,0},{2,3},{3,2},{4,5},{5,4},{6,7},{7,6},{8,9},{9,8},{10,11... | collective-permute-start | bytes 1572872 | tf_op jit(solution)/shard_map/ppermute | solution.py:14
  46.3 14.7 %collective-permute-start.13 = (f32[256,512]{1,0:T(8,128)S(1)}, f32[256,512]{1,0:T(8,128)S(1)}, u32[]{:S(2)}, u32[]{:S(2)}) collective-permute-start(f32[256,512]{1,0:T(8,128)S(1)} %collective-permute-done.3.refs_0_), channel_id=1, source_target_pairs={{0,2},{2,0},{1,3},{3,1},{4,6},{6,4},{5,7},{7,5},{8,10},{10,8},{9,1... | collective-permute-start | bytes 1572872 | tf_op jit(solution)/shard_map/ppermute | solution.py:14
  49.3 13.7 %collective-permute-start.15 = (f32[512,256]{1,0:T(8,128)S(1)}, f32[512,256]{1,0:T(8,128)S(1)}, u32[]{:S(2)}, u32[]{:S(2)}) collective-permute-start(f32[512,256]{1,0:T(8,128)S(1)} %collective-permute-done.2.refs_0_), channel_id=1, source_target_pairs={{0,1},{1,0},{2,3},{3,2},{4,5},{5,4},{6,7},{7,6},{8,9},{9,8},{10,11... | collective-permute-start | bytes 1572872 | tf_op jit(solution)/shard_map/ppermute | solution.py:14
  53.8 7.2 %collective-permute-start.16 = (f32[360,256]{1,0:T(8,128)S(1)}, f32[360,256]{1,0:T(8,128)S(1)}, u32[]{:S(2)}, u32[]{:S(2)}) collective-permute-start(f32[360,256]{1,0:T(8,128)S(1)} %collective-permute-done.8.refs_0_.s2), channel_id=1, source_target_pairs={{0,1},{1,0},{2,3},{3,2},{4,5},{5,4},{6,7},{7,6},{8,9},{9,8},{10,11... | collective-permute-start | bytes 1105928 | tf_op jit(solution)/shard_map/ppermute | solution.py:14
  53.8 11.4 %collective-permute-start.12 = (f32[360,256]{1,0:T(8,128)S(1)}, f32[360,256]{1,0:T(8,128)S(1)}, u32[]{:S(2)}, u32[]{:S(2)}) collective-permute-start(f32[360,256]{1,0:T(8,128)S(1)} %collective-permute-done.8.refs_0_.s2), channel_id=1, source_target_pairs={{0,4},{4,0},{8,12},{12,8},{1,5},{5,1},{9,13},{13,9},{2,6},{6,2},{1... | collective-permute-start | bytes 1105928 | tf_op jit(solution)/shard_map/ppermute | solution.py:14
  55.9 16.0 %collective-permute-start.18 = (f32[512,256]{1,0:T(8,128)S(1)}, f32[512,256]{1,0:T(8,128)S(1)}, u32[]{:S(2)}, u32[]{:S(2)}) collective-permute-start(f32[512,256]{1,0:T(8,128)S(1)} %collective-permute-done.1.refs_0_), channel_id=1, source_target_pairs={{0,2},{2,0},{1,3},{3,1},{4,6},{6,4},{5,7},{7,5},{8,10},{10,8},{9,1... | collective-permute-start | bytes 1572872 | tf_op jit(solution)/shard_map/ppermute | solution.py:14
  61.0 12.0 %collective-permute-start.20 = (f32[256,512]{1,0:T(8,128)S(1)}, f32[256,512]{1,0:T(8,128)S(1)}, u32[]{:S(2)}, u32[]{:S(2)}) collective-permute-start(f32[256,512]{1,0:T(8,128)S(1)} %collective-permute-done.13.refs_0_), channel_id=1, source_target_pairs={{0,1},{1,0},{2,3},{3,2},{4,5},{5,4},{6,7},{7,6},{8,9},{9,8},{10,11... | collective-permute-start | bytes 1572872 | tf_op jit(solution)/shard_map/ppermute | solution.py:14
  61.0 15.0 %collective-permute-start.21 = (f32[512,256]{1,0:T(8,128)S(1)}, f32[512,256]{1,0:T(8,128)S(1)}, u32[]{:S(2)}, u32[]{:S(2)}) collective-permute-start(f32[512,256]{1,0:T(8,128)S(1)} %collective-permute-done.2.refs_0_), channel_id=1, source_target_pairs={{0,4},{4,0},{8,12},{12,8},{1,5},{5,1},{9,13},{13,9},{2,6},{6,2},{1... | collective-permute-start | bytes 1572872 | tf_op jit(solution)/shard_map/ppermute | solution.py:14
  63.0 2.3 %collective-permute-start.17 = (f32[360,256]{1,0:T(8,128)S(1)}, f32[360,256]{1,0:T(8,128)S(1)}, u32[]{:S(2)}, u32[]{:S(2)}) collective-permute-start(f32[360,256]{1,0:T(8,128)S(1)} %collective-permute-done.5.refs_0_.s1), channel_id=1, source_target_pairs={{0,1},{1,0},{2,3},{3,2},{4,5},{5,4},{6,7},{7,6},{8,9},{9,8},{10,11... | collective-permute-start | bytes 1105928 | tf_op jit(solution)/shard_map/ppermute | solution.py:14
  65.2 6.7 %collective-permute-start.19 = (f32[360,256]{1,0:T(8,128)S(1)}, f32[360,256]{1,0:T(8,128)S(1)}, u32[]{:S(2)}, u32[]{:S(2)}) collective-permute-start(f32[360,256]{1,0:T(8,128)S(1)} %collective-permute-done.12.refs_0_.s3), channel_id=1, source_target_pairs={{0,1},{1,0},{2,3},{3,2},{4,5},{5,4},{6,7},{7,6},{8,9},{9,8},{10,11... | collective-permute-start | bytes 1105928 | tf_op jit(solution)/shard_map/ppermute | solution.py:14
  65.2 11.5 %collective-permute-start.22 = (f32[512,256]{1,0:T(8,128)S(1)}, f32[512,256]{1,0:T(8,128)S(1)}, u32[]{:S(2)}, u32[]{:S(2)}) collective-permute-start(f32[512,256]{1,0:T(8,128)S(1)} %collective-permute-done.6.refs_0_), channel_id=1, source_target_pairs={{0,1},{1,0},{2,3},{3,2},{4,5},{5,4},{6,7},{7,6},{8,9},{9,8},{10,11... | collective-permute-start | bytes 1572872 | tf_op jit(solution)/shard_map/ppermute | solution.py:14
  71.9 4.2 %collective-permute-start.24 = (f32[512,256]{1,0:T(8,128)S(1)}, f32[512,256]{1,0:T(8,128)S(1)}, u32[]{:S(2)}, u32[]{:S(2)}) collective-permute-start(f32[512,256]{1,0:T(8,128)S(1)} %collective-permute-done.7.refs_0_), channel_id=1, source_target_pairs={{0,1},{1,0},{2,3},{3,2},{4,5},{5,4},{6,7},{7,6},{8,9},{9,8},{10,11... | collective-permute-start | bytes 1572872 | tf_op jit(solution)/shard_map/ppermute | solution.py:14
  71.9 5.5 %collective-permute-start.23 = (f32[512,256]{1,0:T(8,128)S(1)}, f32[512,256]{1,0:T(8,128)S(1)}, u32[]{:S(2)}, u32[]{:S(2)}) collective-permute-start(f32[512,256]{1,0:T(8,128)S(1)} %collective-permute-done.18.refs_0_), channel_id=1, source_target_pairs={{0,1},{1,0},{2,3},{3,2},{4,5},{5,4},{6,7},{7,6},{8,9},{9,8},{10,11... | collective-permute-start | bytes 1572872 | tf_op jit(solution)/shard_map/ppermute | solution.py:14
  76.1 2.9 %collective-permute-start.25 = (f32[512,256]{1,0:T(8,128)S(1)}, f32[512,256]{1,0:T(8,128)S(1)}, u32[]{:S(2)}, u32[]{:S(2)}) collective-permute-start(f32[512,256]{1,0:T(8,128)S(1)} %collective-permute-done.21.refs_30_), channel_id=1, source_target_pairs={{0,1},{1,0},{2,3},{3,2},{4,5},{5,4},{6,7},{7,6},{8,9},{9,8},{10,11... | collective-permute-start | bytes 1572872 | tf_op jit(solution)/shard_map/ppermute | solution.py:14
  (3 other events, 16.3 us)

commit v11 on v10

--- a/solution.py
+++ b/solution.py
@@ -47,8 +47,8 @@
     ("take", "Ex", "Rx"), ("send", "Bd"),
     ("take", "Ld", "Lx"), ("swap", "Bx"), ("swap", "Ry"), ("swap", "Ex"), ("swap", "Ld"), ("split", "Ey"), ("split", "Ex"),
     ("take", "Ed", "By", "Ey"), ("swap", "Ed"), ("split", "Ld"),
-    ("take", "Rd", "Ex"), ("swap", "Rd"), ("split", "Rd"), ("split", "Bx"), ("split", "Ed"), ("lead", "lead"),
-    ("take", "Bd", "Ld", "Ed", "lead"), ("swap", "Bd"), ("split", "Ry"), ("root", "root"),
+    ("take", "Rd", "Ex"), ("swap", "Rd"), ("split", "Bx"), ("split", "Ed"), ("lead", "lead"),
+    ("take", "Bd", "Ld", "Ed", "lead"), ("swap", "Bd"), ("split", "Ry"), ("split", "Rd"), ("root", "root"),
 )
 
 

time: 102 us -> 102 us (level)
  no operation moved by 1% of the time
where the time goes in v11:
time: 102 us
  waiting for transfers between devices  41.7 us (41%)
  Pallas kernels  39.6 us (39%)
  starting transfers between devices  19.5 us (19%)
    ppermute x26, waiting for transfers between devices, from_partner(): return lax.ppermute(value, axis, pairs)  41.7 us
    pallas_call x1, Pallas kernels, shards(): pl.pallas_call(march_kernel, in_specs=[vmem] * 7 + [smem] + [vmem] * (len...  22.9 us
    ppermute x26, starting transfers between devices, from_partner(): return lax.ppermute(value, axis, pairs)  19.5 us
    pallas_call x15, Pallas kernels, split_call(): pl.pallas_call(kernel, in_specs=[pl.BlockSpec(memory_space=pltpu.SMEM)] +...  9.7 us
    pallas_call x2, Pallas kernels, cut_call(): pl.pallas_call(cut_kernel, in_specs=[pl.BlockSpec(memory_space=pltpu.SMEM...  3.45 us
  transfers between devices with their start and end apart: 26, of which 13 were waited for; matrix products, arithmetic and copies ran while one was open for 0% of the time, Pallas kernels for 15%

profile of v11, /device:TPU:0, one launch (start us, length us, event | category | flops | bytes accessed | tf_op | source)
XLA Modules:
  0.0 101.9 jit_solution(11124281116370043121)
XLA Ops:
  0.7 1.7 %shard_map.113 = (f32[128,512]{1,0:T(8,128)S(1)}, f32[256,512]{1,0:T(8,128)S(1)}) custom-call(s32[4]{0:T(128)S(1)} %pad_add_fusion.place, f32[256,512]{1,0:T(8,128)} %bitcast.26, f32[256,1024]{1,0:T(8,128)} %bitcast.19), custom_call_target="tpu_custom_call" | custom-call | flops 1 | bytes 1 | tf_op jit(solution)/shard_map/pallas_call | solution.py:77
  2.4 3.1 %collective-permute-start = (f32[128,512]{1,0:T(8,128)S(1)}, f32[128,512]{1,0:T(8,128)S(1)}, u32[]{:S(2)}, u32[]{:S(2)}) collective-permute-start(f32[128,512]{1,0:T(8,128)S(1)} %get-tuple-element.88.mine), channel_id=1, source_target_pairs={{0,4},{4,0},{8,12},{12,8},{1,5},{5,1},{9,13},{13,9},{2,6},{6,2},{1... | collective-permute-start | bytes 786440 | tf_op jit(solution)/shard_map/ppermute | solution.py:14
  5.5 1.5 %collective-permute-start.4 = (f32[256,512]{1,0:T(8,128)S(1)}, f32[256,512]{1,0:T(8,128)S(1)}, u32[]{:S(2)}, u32[]{:S(2)}) collective-permute-start(f32[256,512]{1,0:T(8,128)S(1)} %get-tuple-element.96), channel_id=1, source_target_pairs={{0,2},{2,0},{1,3},{3,1},{4,6},{6,4},{5,7},{7,5},{8,10},{10,8},{9,1... | collective-permute-start | bytes 1572872 | tf_op jit(solution)/shard_map/ppermute | solution.py:14
  7.5 5.2 %collective-permute-done.other = f32[128,512]{1,0:T(8,128)S(1)} collective-permute-done((f32[128,512]{1,0:T(8,128)S(1)}, f32[128,512]{1,0:T(8,128)S(1)}, u32[]{:S(2)}, u32[]{:S(2)}) %collective-permute-start) | collective-permute-done | bytes 262176 | tf_op jit(solution)/shard_map/ppermute | solution.py:14
  12.7 1.8 %shard_map.115 = (f32[512,256]{1,0:T(8,128)S(1)}, f32[512,256]{1,0:T(8,128)S(1)}) custom-call(s32[4]{0:T(128)S(1)} %pad_add_fusion.place, f32[1024,256]{1,0:T(8,128)} %bitcast.17, f32[1024,256]{1,0:T(8,128)} %bitcast.15), custom_call_target="tpu_custom_call" | custom-call | flops 1 | bytes 1 | tf_op jit(solution)/shard_map/pallas_call | solution.py:77
  14.5 2.0 %collective-permute-start.2 = (f32[512,256]{1,0:T(8,128)S(1)}, f32[512,256]{1,0:T(8,128)S(1)}, u32[]{:S(2)}, u32[]{:S(2)}) collective-permute-start(f32[512,256]{1,0:T(8,128)S(1)} %get-tuple-element.107), channel_id=1, source_target_pairs={{0,2},{2,0},{1,3},{3,1},{4,6},{6,4},{5,7},{7,5},{8,10},{10,8},{9,1... | collective-permute-start | bytes 1572872 | tf_op jit(solution)/shard_map/ppermute | solution.py:14
  16.5 1.6 %collective-permute-start.1 = (f32[512,256]{1,0:T(8,128)S(1)}, f32[512,256]{1,0:T(8,128)S(1)}, u32[]{:S(2)}, u32[]{:S(2)}) collective-permute-start(f32[512,256]{1,0:T(8,128)S(1)} %get-tuple-element.106), channel_id=1, source_target_pairs={{0,4},{4,0},{8,12},{12,8},{1,5},{5,1},{9,13},{13,9},{2,6},{6,2},{1... | collective-permute-start | bytes 1572872 | tf_op jit(solution)/shard_map/ppermute | solution.py:14
  18.1 1.5 %shard_map.114 = (f32[360,256]{1,0:T(8,128)S(1)}, f32[9,32]{1,0:T(8,128)S(1)}) custom-call(s32[4]{0:T(128)S(1)} %pad_add_fusion.place, f32[128,512]{1,0:T(8,128)S(1)} %get-tuple-element.88.mine, f32[128,512]{1,0:T(8,128)S(1)} %collective-permute-done.other, f32[512,256]{1,0:T(8,128)S(1)} %bitcast.21, s32[1,32]{1,0:T(1,128)S(1)} %bitcast.25, ...), custom_call_target="tpu_custom_call" | custom-call | flops 1 | bytes 1 | tf_op jit(solution)/shard_map/pallas_call | solution.py:113
  19.6 0.7 collective-permute-done.4.refs_0_
  20.4 1.5 %collective-permute-start.8 = (f32[360,256]{1,0:T(8,128)S(1)}, f32[360,256]{1,0:T(8,128)S(1)}, u32[]{:S(2)}, u32[]{:S(2)}) collective-permute-start(f32[360,256]{1,0:T(8,128)S(1)} %get-tuple-element.110.refs_0_.s0), channel_id=1, source_target_pairs={{0,2},{2,0},{1,3},{3,1},{4,6},{6,4},{5,7},{7,5},{8,10},{10,8},{9,1... | collective-permute-start | bytes 1105928 | tf_op jit(solution)/shard_map/ppermute | solution.py:14
  21.9 2.0 %collective-permute-done.3.refs_0_ = f32[256,512]{1,0:T(8,128)S(1)} collective-permute-done((f32[256,512]{1,0:T(8,128)S(1)}, f32[256,512]{1,0:T(8,128)S(1)}, u32[]{:S(2)}, u32[]{:S(2)}) %collective-permute-start.3) | collective-permute-done | bytes 524320 | tf_op jit(solution)/shard_map/ppermute | solution.py:14
  24.6 7.0 %collective-permute-done.2.refs_0_ = f32[512,256]{1,0:T(8,128)S(1)} collective-permute-done((f32[512,256]{1,0:T(8,128)S(1)}, f32[512,256]{1,0:T(8,128)S(1)}, u32[]{:S(2)}, u32[]{:S(2)}) %collective-permute-start.2) | collective-permute-done | bytes 524320 | tf_op jit(solution)/shard_map/ppermute | solution.py:14
  31.6 2.9 %collective-permute-done.1.refs_0_ = f32[512,256]{1,0:T(8,128)S(1)} collective-permute-done((f32[512,256]{1,0:T(8,128)S(1)}, f32[512,256]{1,0:T(8,128)S(1)}, u32[]{:S(2)}, u32[]{:S(2)}) %collective-permute-start.1) | collective-permute-done | bytes 524320 | tf_op jit(solution)/shard_map/ppermute | solution.py:14
  34.5 1.4 %collective-permute-start.6 = (f32[512,256]{1,0:T(8,128)S(1)}, f32[512,256]{1,0:T(8,128)S(1)}, u32[]{:S(2)}, u32[]{:S(2)}) collective-permute-start(f32[512,256]{1,0:T(8,128)S(1)} %get-tuple-element.106), channel_id=1, source_target_pairs={{0,2},{2,0},{1,3},{3,1},{4,6},{6,4},{5,7},{7,5},{8,10},{10,8},{9,1... | collective-permute-start | bytes 1572872 | tf_op jit(solution)/shard_map/ppermute | solution.py:14
  37.3 2.2 %collective-permute-done.8.refs_0_.s2 = f32[360,256]{1,0:T(8,128)S(1)} collective-permute-done((f32[360,256]{1,0:T(8,128)S(1)}, f32[360,256]{1,0:T(8,128)S(1)}, u32[]{:S(2)}, u32[]{:S(2)}) %collective-permute-start.8) | collective-permute-done | bytes 368672 | tf_op jit(solution)/shard_map/ppermute | solution.py:14
  40.5 0.7 shard_map.120
  41.1 5.2 %collective-permute-done.7.refs_0_ = f32[512,256]{1,0:T(8,128)S(1)} collective-permute-done((f32[512,256]{1,0:T(8,128)S(1)}, f32[512,256]{1,0:T(8,128)S(1)}, u32[]{:S(2)}, u32[]{:S(2)}) %collective-permute-start.7) | collective-permute-done | bytes 524320 | tf_op jit(solution)/shard_map/ppermute | solution.py:14
  46.3 1.5 %collective-permute-start.13 = (f32[256,512]{1,0:T(8,128)S(1)}, f32[256,512]{1,0:T(8,128)S(1)}, u32[]{:S(2)}, u32[]{:S(2)}) collective-permute-start(f32[256,512]{1,0:T(8,128)S(1)} %collective-permute-done.3.refs_0_), channel_id=1, source_target_pairs={{0,2},{2,0},{1,3},{3,1},{4,6},{6,4},{5,7},{7,5},{8,10},{10,8},{9,1... | collective-permute-start | bytes 1572872 | tf_op jit(solution)/shard_map/ppermute | solution.py:14
  47.8 1.5 %collective-permute-done.6.refs_0_ = f32[512,256]{1,0:T(8,128)S(1)} collective-permute-done((f32[512,256]{1,0:T(8,128)S(1)}, f32[512,256]{1,0:T(8,128)S(1)}, u32[]{:S(2)}, u32[]{:S(2)}) %collective-permute-start.6) | collective-permute-done | bytes 524320 | tf_op jit(solution)/shard_map/ppermute | solution.py:14
  49.3 4.6 %collective-permute-done.5.refs_0_.s1 = f32[360,256]{1,0:T(8,128)S(1)} collective-permute-done((f32[360,256]{1,0:T(8,128)S(1)}, f32[360,256]{1,0:T(8,128)S(1)}, u32[]{:S(2)}, u32[]{:S(2)}) %collective-permute-start.5) | collective-permute-done | bytes 368672 | tf_op jit(solution)/shard_map/ppermute | solution.py:14
  53.8 1.3 %collective-permute-start.12 = (f32[360,256]{1,0:T(8,128)S(1)}, f32[360,256]{1,0:T(8,128)S(1)}, u32[]{:S(2)}, u32[]{:S(2)}) collective-permute-start(f32[360,256]{1,0:T(8,128)S(1)} %collective-permute-done.8.refs_0_.s2), channel_id=1, source_target_pairs={{0,4},{4,0},{8,12},{12,8},{1,5},{5,1},{9,13},{13,9},{2,6},{6,2},{1... | collective-permute-start | bytes 1105928 | tf_op jit(solution)/shard_map/ppermute | solution.py:14
  55.9 1.6 %collective-permute-start.18 = (f32[512,256]{1,0:T(8,128)S(1)}, f32[512,256]{1,0:T(8,128)S(1)}, u32[]{:S(2)}, u32[]{:S(2)}) collective-permute-start(f32[512,256]{1,0:T(8,128)S(1)} %collective-permute-done.1.refs_0_), channel_id=1, source_target_pairs={{0,2},{2,0},{1,3},{3,1},{4,6},{6,4},{5,7},{7,5},{8,10},{10,8},{9,1... | collective-permute-start | bytes 1572872 | tf_op jit(solution)/shard_map/ppermute | solution.py:14
  58.1 3.0 %collective-permute-done.13.refs_0_ = f32[256,512]{1,0:T(8,128)S(1)} collective-permute-done((f32[256,512]{1,0:T(8,128)S(1)}, f32[256,512]{1,0:T(8,128)S(1)}, u32[]{:S(2)}, u32[]{:S(2)}) %collective-permute-start.13) | collective-permute-done | bytes 524320 | tf_op jit(solution)/shard_map/ppermute | solution.py:14
  61.0 1.9 %collective-permute-start.21 = (f32[512,256]{1,0:T(8,128)S(1)}, f32[512,256]{1,0:T(8,128)S(1)}, u32[]{:S(2)}, u32[]{:S(2)}) collective-permute-start(f32[512,256]{1,0:T(8,128)S(1)} %collective-permute-done.2.refs_0_), channel_id=1, source_target_pairs={{0,4},{4,0},{8,12},{12,8},{1,5},{5,1},{9,13},{13,9},{2,6},{6,2},{1... | collective-permute-start | bytes 1572872 | tf_op jit(solution)/shard_map/ppermute | solution.py:14
  64.5 0.7 collective-permute-done.12.refs_0_.s3
  66.4 5.5 %collective-permute-done.18.refs_0_ = f32[512,256]{1,0:T(8,128)S(1)} collective-permute-done((f32[512,256]{1,0:T(8,128)S(1)}, f32[512,256]{1,0:T(8,128)S(1)}, u32[]{:S(2)}, u32[]{:S(2)}) %collective-permute-start.18) | collective-permute-done | bytes 524320 | tf_op jit(solution)/shard_map/ppermute | solution.py:14
  73.0 0.7 shard_map.127
  73.7 1.2 %shard_map.128 = (f32[32,1024]{1,0:T(8,128)S(1)}, f32[32,1024]{1,0:T(8,128)S(1)}) custom-call(f32[360,256]{1,0:T(8,128)S(1)} %get-tuple-element.110.refs_0_.s0, f32[360,256]{1,0:T(8,128)S(1)} %collective-permute-done.5.refs_0_.s1, f32[360,256]{1,0:T(8,128)S(1)} %collective-permute-done.8.refs_0_.s2, f32[360,256]{1,0:T(8,128)S(1)} %collective-permute-done.12.refs_0_.s3, ...), custom_call_target="tpu_custom_call" | custom-call | flops 1 | bytes 1 | tf_op jit(solution)/shard_map/pallas_call | solution.py:298
  74.9 1.2 %collective-permute-done.21.refs_30_ = f32[512,256]{1,0:T(8,128)S(1)} collective-permute-done((f32[512,256]{1,0:T(8,128)S(1)}, f32[512,256]{1,0:T(8,128)S(1)}, u32[]{:S(2)}, u32[]{:S(2)}) %collective-permute-start.21) | collective-permute-done | bytes 524320 | tf_op jit(solution)/shard_map/ppermute | solution.py:14
  76.8 0.7 shard_map.129
  78.1 0.8 shard_map.131.two_start
  78.9 22.9 %shard_map.133 = (f32[32,256]{1,0:T(8,128)}, f32[32,256]{1,0:T(8,128)}) custom-call(f32[360,256]{1,0:T(8,128)S(1)} %get-tuple-element.110.refs_0_.s0, f32[360,256]{1,0:T(8,128)S(1)} %collective-permute-done.5.refs_0_.s1, f32[360,256]{1,0:T(8,128)S(1)} %collective-permute-done.8.refs_0_.s2, f32[360,256]{1,0:T(8,128)S(1)} %collective-permute-done.12.refs_0_.s3, ...), custom_call_target="tpu_custom_call" | custom-call | tf_op jit(solution)/shard_map/pallas_call | solution.py:322
  (60 shorter events, 10.0 us)
Async XLA Ops:
  2.4 10.2 %collective-permute-start = (f32[128,512]{1,0:T(8,128)S(1)}, f32[128,512]{1,0:T(8,128)S(1)}, u32[]{:S(2)}, u32[]{:S(2)}) collective-permute-start(f32[128,512]{1,0:T(8,128)S(1)} %get-tuple-element.88.mine), channel_id=1, source_target_pairs={{0,4},{4,0},{8,12},{12,8},{1,5},{5,1},{9,13},{13,9},{2,6},{6,2},{1... | collective-permute-start | bytes 786440 | tf_op jit(solution)/shard_map/ppermute | solution.py:14
  5.5 14.8 %collective-permute-start.4 = (f32[256,512]{1,0:T(8,128)S(1)}, f32[256,512]{1,0:T(8,128)S(1)}, u32[]{:S(2)}, u32[]{:S(2)}) collective-permute-start(f32[256,512]{1,0:T(8,128)S(1)} %get-tuple-element.96), channel_id=1, source_target_pairs={{0,2},{2,0},{1,3},{3,1},{4,6},{6,4},{5,7},{7,5},{8,10},{10,8},{9,1... | collective-permute-start | bytes 1572872 | tf_op jit(solution)/shard_map/ppermute | solution.py:14
  7.0 16.9 %collective-permute-start.3 = (f32[256,512]{1,0:T(8,128)S(1)}, f32[256,512]{1,0:T(8,128)S(1)}, u32[]{:S(2)}, u32[]{:S(2)}) collective-permute-start(f32[256,512]{1,0:T(8,128)S(1)} %get-tuple-element.96), channel_id=1, source_target_pairs={{0,4},{4,0},{8,12},{12,8},{1,5},{5,1},{9,13},{13,9},{2,6},{6,2},{1... | collective-permute-start | bytes 1572872 | tf_op jit(solution)/shard_map/ppermute | solution.py:14
  12.7 5.4 %copy-start.5 = (f32[1,1,32,256]{3,2,1,0:T(8,128)S(1)}, f32[1,1,32,256]{3,2,1,0:T(8,128)}, u32[]{:S(2)}) copy-start(f32[1,1,32,256]{3,2,1,0:T(8,128)} %param.11) | copy-start | bytes 98308
  12.7 5.4 %copy-start.6 = (f32[9,32]{1,0:T(8,128)S(1)}, f32[9,32]{1,0:T(8,128)}, u32[]{:S(2)}) copy-start(f32[9,32]{1,0:T(8,128)} %weight.1) | copy-start | bytes 3460
  12.7 5.4 %copy-start.7 = (f32[1,1,256]{2,1,0:T(1,128)S(1)}, f32[1,1,256]{2,1,0:T(1,128)}, u32[]{:S(2)}) copy-start(f32[1,1,256]{2,1,0:T(1,128)} %param.17) | copy-start | bytes 3076
  14.5 9.4 %copy-start.2 = (f32[1,1,256,1024]{3,2,1,0:T(8,128)S(1)}, f32[1,1,256,1024]{3,2,1,0:T(8,128)}, u32[]{:S(2)}) copy-start(f32[1,1,256,1024]{3,2,1,0:T(8,128)} %param.14) | copy-start | bytes 3145732
  14.5 17.1 %collective-permute-start.2 = (f32[512,256]{1,0:T(8,128)S(1)}, f32[512,256]{1,0:T(8,128)S(1)}, u32[]{:S(2)}, u32[]{:S(2)}) collective-permute-start(f32[512,256]{1,0:T(8,128)S(1)} %get-tuple-element.107), channel_id=1, source_target_pairs={{0,2},{2,0},{1,3},{3,1},{4,6},{6,4},{5,7},{7,5},{8,10},{10,8},{9,1... | collective-permute-start | bytes 1572872 | tf_op jit(solution)/shard_map/ppermute | solution.py:14
  16.5 18.0 %collective-permute-start.1 = (f32[512,256]{1,0:T(8,128)S(1)}, f32[512,256]{1,0:T(8,128)S(1)}, u32[]{:S(2)}, u32[]{:S(2)}) collective-permute-start(f32[512,256]{1,0:T(8,128)S(1)} %get-tuple-element.106), channel_id=1, source_target_pairs={{0,4},{4,0},{8,12},{12,8},{1,5},{5,1},{9,13},{13,9},{2,6},{6,2},{1... | collective-permute-start | bytes 1572872 | tf_op jit(solution)/shard_map/ppermute | solution.py:14
  18.1 17.8 %copy-start = (f32[1,1,1024,256]{3,2,1,0:T(8,128)S(1)}, f32[1,1,1024,256]{3,2,1,0:T(8,128)}, u32[]{:S(2)}) copy-start(f32[1,1,1024,256]{3,2,1,0:T(8,128)} %param.15) | copy-start | bytes 3145732
  20.4 16.3 %copy-start.1 = (f32[1,1,1024,256]{3,2,1,0:T(8,128)S(1)}, f32[1,1,1024,256]{3,2,1,0:T(8,128)}, u32[]{:S(2)}) copy-start(f32[1,1,1024,256]{3,2,1,0:T(8,128)} %param.16) | copy-start | bytes 3145732
  20.4 19.1 %collective-permute-start.8 = (f32[360,256]{1,0:T(8,128)S(1)}, f32[360,256]{1,0:T(8,128)S(1)}, u32[]{:S(2)}, u32[]{:S(2)}) collective-permute-start(f32[360,256]{1,0:T(8,128)S(1)} %get-tuple-element.110.refs_0_.s0), channel_id=1, source_target_pairs={{0,2},{2,0},{1,3},{3,1},{4,6},{6,4},{5,7},{7,5},{8,10},{10,8},{9,1... | collective-permute-start | bytes 1105928 | tf_op jit(solution)/shard_map/ppermute | solution.py:14
  23.9 15.6 %collective-permute-start.9 = (f32[360,256]{1,0:T(8,128)S(1)}, f32[360,256]{1,0:T(8,128)S(1)}, u32[]{:S(2)}, u32[]{:S(2)}) collective-permute-start(f32[360,256]{1,0:T(8,128)S(1)} %get-tuple-element.110.refs_0_.s0), channel_id=1, source_target_pairs={{0,1},{1,0},{2,3},{3,2},{4,5},{5,4},{6,7},{7,6},{8,9},{9,8},{10,11... | collective-permute-start | bytes 1105928 | tf_op jit(solution)/shard_map/ppermute | solution.py:14
  31.6 8.9 %collective-permute-start.10 = (f32[256,512]{1,0:T(8,128)S(1)}, f32[256,512]{1,0:T(8,128)S(1)}, u32[]{:S(2)}, u32[]{:S(2)}) collective-permute-start(f32[256,512]{1,0:T(8,128)S(1)} %collective-permute-done.4.refs_0_), channel_id=1, source_target_pairs={{0,1},{1,0},{2,3},{3,2},{4,5},{5,4},{6,7},{7,6},{8,9},{9,8},{10,11... | collective-permute-start | bytes 1572872 | tf_op jit(solution)/shard_map/ppermute | solution.py:14
  31.6 14.7 %collective-permute-start.7 = (f32[512,256]{1,0:T(8,128)S(1)}, f32[512,256]{1,0:T(8,128)S(1)}, u32[]{:S(2)}, u32[]{:S(2)}) collective-permute-start(f32[512,256]{1,0:T(8,128)S(1)} %get-tuple-element.107), channel_id=1, source_target_pairs={{0,4},{4,0},{8,12},{12,8},{1,5},{5,1},{9,13},{13,9},{2,6},{6,2},{1... | collective-permute-start | bytes 1572872 | tf_op jit(solution)/shard_map/ppermute | solution.py:14
  34.5 14.7 %collective-permute-start.6 = (f32[512,256]{1,0:T(8,128)S(1)}, f32[512,256]{1,0:T(8,128)S(1)}, u32[]{:S(2)}, u32[]{:S(2)}) collective-permute-start(f32[512,256]{1,0:T(8,128)S(1)} %get-tuple-element.106), channel_id=1, source_target_pairs={{0,2},{2,0},{1,3},{3,1},{4,6},{6,4},{5,7},{7,5},{8,10},{10,8},{9,1... | collective-permute-start | bytes 1572872 | tf_op jit(solution)/shard_map/ppermute | solution.py:14
  39.5 14.3 %collective-permute-start.14 = (f32[256,512]{1,0:T(8,128)S(1)}, f32[256,512]{1,0:T(8,128)S(1)}, u32[]{:S(2)}, u32[]{:S(2)}) collective-permute-start(f32[256,512]{1,0:T(8,128)S(1)} %collective-permute-done.3.refs_0_), channel_id=1, source_target_pairs={{0,1},{1,0},{2,3},{3,2},{4,5},{5,4},{6,7},{7,6},{8,9},{9,8},{10,11... | collective-permute-start | bytes 1572872 | tf_op jit(solution)/shard_map/ppermute | solution.py:14
  39.5 14.3 %collective-permute-start.5 = (f32[360,256]{1,0:T(8,128)S(1)}, f32[360,256]{1,0:T(8,128)S(1)}, u32[]{:S(2)}, u32[]{:S(2)}) collective-permute-start(f32[360,256]{1,0:T(8,128)S(1)} %get-tuple-element.110.refs_0_.s0), channel_id=1, source_target_pairs={{0,4},{4,0},{8,12},{12,8},{1,5},{5,1},{9,13},{13,9},{2,6},{6,2},{1... | collective-permute-start | bytes 1105928 | tf_op jit(solution)/shard_map/ppermute | solution.py:14
  46.3 9.5 %collective-permute-start.11 = (f32[512,256]{1,0:T(8,128)S(1)}, f32[512,256]{1,0:T(8,128)S(1)}, u32[]{:S(2)}, u32[]{:S(2)}) collective-permute-start(f32[512,256]{1,0:T(8,128)S(1)} %collective-permute-done.1.refs_0_), channel_id=1, source_target_pairs={{0,1},{1,0},{2,3},{3,2},{4,5},{5,4},{6,7},{7,6},{8,9},{9,8},{10,11... | collective-permute-start | bytes 1572872 | tf_op jit(solution)/shard_map/ppermute | solution.py:14
  46.3 14.7 %collective-permute-start.13 = (f32[256,512]{1,0:T(8,128)S(1)}, f32[256,512]{1,0:T(8,128)S(1)}, u32[]{:S(2)}, u32[]{:S(2)}) collective-permute-start(f32[256,512]{1,0:T(8,128)S(1)} %collective-permute-done.3.refs_0_), channel_id=1, source_target_pairs={{0,2},{2,0},{1,3},{3,1},{4,6},{6,4},{5,7},{7,5},{8,10},{10,8},{9,1... | collective-permute-start | bytes 1572872 | tf_op jit(solution)/shard_map/ppermute | solution.py:14
  49.3 13.7 %collective-permute-start.15 = (f32[512,256]{1,0:T(8,128)S(1)}, f32[512,256]{1,0:T(8,128)S(1)}, u32[]{:S(2)}, u32[]{:S(2)}) collective-permute-start(f32[512,256]{1,0:T(8,128)S(1)} %collective-permute-done.2.refs_0_), channel_id=1, source_target_pairs={{0,1},{1,0},{2,3},{3,2},{4,5},{5,4},{6,7},{7,6},{8,9},{9,8},{10,11... | collective-permute-start | bytes 1572872 | tf_op jit(solution)/shard_map/ppermute | solution.py:14
  53.8 7.2 %collective-permute-start.16 = (f32[360,256]{1,0:T(8,128)S(1)}, f32[360,256]{1,0:T(8,128)S(1)}, u32[]{:S(2)}, u32[]{:S(2)}) collective-permute-start(f32[360,256]{1,0:T(8,128)S(1)} %collective-permute-done.8.refs_0_.s2), channel_id=1, source_target_pairs={{0,1},{1,0},{2,3},{3,2},{4,5},{5,4},{6,7},{7,6},{8,9},{9,8},{10,11... | collective-permute-start | bytes 1105928 | tf_op jit(solution)/shard_map/ppermute | solution.py:14
  53.8 11.4 %collective-permute-start.12 = (f32[360,256]{1,0:T(8,128)S(1)}, f32[360,256]{1,0:T(8,128)S(1)}, u32[]{:S(2)}, u32[]{:S(2)}) collective-permute-start(f32[360,256]{1,0:T(8,128)S(1)} %collective-permute-done.8.refs_0_.s2), channel_id=1, source_target_pairs={{0,4},{4,0},{8,12},{12,8},{1,5},{5,1},{9,13},{13,9},{2,6},{6,2},{1... | collective-permute-start | bytes 1105928 | tf_op jit(solution)/shard_map/ppermute | solution.py:14
  55.9 16.0 %collective-permute-start.18 = (f32[512,256]{1,0:T(8,128)S(1)}, f32[512,256]{1,0:T(8,128)S(1)}, u32[]{:S(2)}, u32[]{:S(2)}) collective-permute-start(f32[512,256]{1,0:T(8,128)S(1)} %collective-permute-done.1.refs_0_), channel_id=1, source_target_pairs={{0,2},{2,0},{1,3},{3,1},{4,6},{6,4},{5,7},{7,5},{8,10},{10,8},{9,1... | collective-permute-start | bytes 1572872 | tf_op jit(solution)/shard_map/ppermute | solution.py:14
  61.0 12.0 %collective-permute-start.20 = (f32[256,512]{1,0:T(8,128)S(1)}, f32[256,512]{1,0:T(8,128)S(1)}, u32[]{:S(2)}, u32[]{:S(2)}) collective-permute-start(f32[256,512]{1,0:T(8,128)S(1)} %collective-permute-done.13.refs_0_), channel_id=1, source_target_pairs={{0,1},{1,0},{2,3},{3,2},{4,5},{5,4},{6,7},{7,6},{8,9},{9,8},{10,11... | collective-permute-start | bytes 1572872 | tf_op jit(solution)/shard_map/ppermute | solution.py:14
  61.0 15.0 %collective-permute-start.21 = (f32[512,256]{1,0:T(8,128)S(1)}, f32[512,256]{1,0:T(8,128)S(1)}, u32[]{:S(2)}, u32[]{:S(2)}) collective-permute-start(f32[512,256]{1,0:T(8,128)S(1)} %collective-permute-done.2.refs_0_), channel_id=1, source_target_pairs={{0,4},{4,0},{8,12},{12,8},{1,5},{5,1},{9,13},{13,9},{2,6},{6,2},{1... | collective-permute-start | bytes 1572872 | tf_op jit(solution)/shard_map/ppermute | solution.py:14
  63.0 2.3 %collective-permute-start.17 = (f32[360,256]{1,0:T(8,128)S(1)}, f32[360,256]{1,0:T(8,128)S(1)}, u32[]{:S(2)}, u32[]{:S(2)}) collective-permute-start(f32[360,256]{1,0:T(8,128)S(1)} %collective-permute-done.5.refs_0_.s1), channel_id=1, source_target_pairs={{0,1},{1,0},{2,3},{3,2},{4,5},{5,4},{6,7},{7,6},{8,9},{9,8},{10,11... | collective-permute-start | bytes 1105928 | tf_op jit(solution)/shard_map/ppermute | solution.py:14
  65.2 6.7 %collective-permute-start.19 = (f32[360,256]{1,0:T(8,128)S(1)}, f32[360,256]{1,0:T(8,128)S(1)}, u32[]{:S(2)}, u32[]{:S(2)}) collective-permute-start(f32[360,256]{1,0:T(8,128)S(1)} %collective-permute-done.12.refs_0_.s3), channel_id=1, source_target_pairs={{0,1},{1,0},{2,3},{3,2},{4,5},{5,4},{6,7},{7,6},{8,9},{9,8},{10,11... | collective-permute-start | bytes 1105928 | tf_op jit(solution)/shard_map/ppermute | solution.py:14
  65.2 11.5 %collective-permute-start.22 = (f32[512,256]{1,0:T(8,128)S(1)}, f32[512,256]{1,0:T(8,128)S(1)}, u32[]{:S(2)}, u32[]{:S(2)}) collective-permute-start(f32[512,256]{1,0:T(8,128)S(1)} %collective-permute-done.6.refs_0_), channel_id=1, source_target_pairs={{0,1},{1,0},{2,3},{3,2},{4,5},{5,4},{6,7},{7,6},{8,9},{9,8},{10,11... | collective-permute-start | bytes 1572872 | tf_op jit(solution)/shard_map/ppermute | solution.py:14
  71.9 4.2 %collective-permute-start.24 = (f32[512,256]{1,0:T(8,128)S(1)}, f32[512,256]{1,0:T(8,128)S(1)}, u32[]{:S(2)}, u32[]{:S(2)}) collective-permute-start(f32[512,256]{1,0:T(8,128)S(1)} %collective-permute-done.7.refs_0_), channel_id=1, source_target_pairs={{0,1},{1,0},{2,3},{3,2},{4,5},{5,4},{6,7},{7,6},{8,9},{9,8},{10,11... | collective-permute-start | bytes 1572872 | tf_op jit(solution)/shard_map/ppermute | solution.py:14
  71.9 5.5 %collective-permute-start.23 = (f32[512,256]{1,0:T(8,128)S(1)}, f32[512,256]{1,0:T(8,128)S(1)}, u32[]{:S(2)}, u32[]{:S(2)}) collective-permute-start(f32[512,256]{1,0:T(8,128)S(1)} %collective-permute-done.18.refs_0_), channel_id=1, source_target_pairs={{0,1},{1,0},{2,3},{3,2},{4,5},{5,4},{6,7},{7,6},{8,9},{9,8},{10,11... | collective-permute-start | bytes 1572872 | tf_op jit(solution)/shard_map/ppermute | solution.py:14
  76.1 2.9 %collective-permute-start.25 = (f32[512,256]{1,0:T(8,128)S(1)}, f32[512,256]{1,0:T(8,128)S(1)}, u32[]{:S(2)}, u32[]{:S(2)}) collective-permute-start(f32[512,256]{1,0:T(8,128)S(1)} %collective-permute-done.21.refs_30_), channel_id=1, source_target_pairs={{0,1},{1,0},{2,3},{3,2},{4,5},{5,4},{6,7},{7,6},{8,9},{9,8},{10,11... | collective-permute-start | bytes 1572872 | tf_op jit(solution)/shard_map/ppermute | solution.py:14
  (3 other events, 16.3 us)
